TPU v7x, 256 devices: a whole 4x4x8 slice. The times are simulated.
256 devices in a mesh: cuts: 2 (over core), tile: 128 (over z, y, x).
Axes of the slice: x: 4, y: 4, z: 8, core: 2. Of those that a mesh axis runs over, the one named last changes fastest.
Arguments:
- object_slices: float32 [2, 2, 16384, 2048], P('cuts', None, 'tile'), may hold values from -1 to 1, as said below
- probe: float32 [2, 256, 256], replicated, may hold values from -4 to 4
- positions: int32 [256, 2], P('tile'), may hold values from 0 to 16128, as said below
- counts: int32 [128], P('tile'), may hold values from 1 to 2
- intensity: float32 [256, 256, 256], P('tile'), may hold values from 0 to 2
Outputs:
- object_grad: float32 [2, 2, 16384, 2048], P('cuts', None, 'tile')
Inputs may be any that keep to these rules, and one draw needn't show every extreme that they name: `positions`: slot s belongs to strip t = s // 2; its row offset lies between max(0, (t - 1) * 128) and min(t * 128, 16128), its column offset between 0 and 1792. `object_slices`: every object cell has a magnitude between 0.7 and 1.0.
All inputs are finite; a program needn't handle non-finite values.
Results may differ from a plain program's by a relative error of at most 0.00015.
Values sent between devices are 32-bit elements; how exact they have to be, the bound alone decides.
No kernel may reach another device: no remote copies, remote signals or barrier semaphores. Data moves between devices by JAX's collectives and lax.ppermute only.
A program may use at most 64 MiB of HBM per device.

v0:
```python
import numpy as np
import ml_dtypes

import jax
import jax.numpy as jnp
from jax import lax
from jax.experimental import pallas as pl
from jax.experimental.pallas import tpu as pltpu
from jax.sharding import PartitionSpec as P

WIN = 256
HALF = 128


def split_tables(real_part, imag_part):
    parts = []
    for values in (real_part, imag_part - real_part, real_part + imag_part):
        high = values.astype(ml_dtypes.bfloat16)
        low = (values - high.astype(np.float64)).astype(ml_dtypes.bfloat16)
        parts += [high, low]
    return np.stack(parts)


def build_tables():
    index = np.arange(WIN)
    turned = 2.0 * np.pi * ((index[:, None] * index[None, :]) % WIN) / WIN
    dft = (np.cos(turned) - 1j * np.sin(turned)) / np.sqrt(WIN)
    centred = (index + WIN // 2) % WIN - WIN // 2
    phase = np.pi * (centred * centred % (4 * WIN)) / (2 * WIN)
    prop = np.conj(dft) @ ((np.cos(phase) - 1j * np.sin(phase))[:, None] * dft)
    prop = 0.5 * (prop + prop.T)
    return split_tables(dft.real, dft.imag), split_tables(prop.real, prop.imag)


def split(value):
    high = value.astype(jnp.bfloat16)
    low = (value - high.astype(jnp.float32)).astype(jnp.bfloat16)
    return high, low


def dot(left, right):
    return jnp.dot(left, right, preferred_element_type=jnp.float32)


def product(field, table, which, from_left):
    high, low = split(field)
    table_high = table[2 * which]
    table_low = table[2 * which + 1]
    if from_left:
        return dot(table_high, high) + (dot(table_high, low) + dot(table_low, high))
    return dot(high, table_high) + (dot(low, table_high) + dot(high, table_low))


def complex_product(real, imag, table, conjugate, from_left):
    shared = product(real + imag, table, 0, from_left)
    if conjugate:
        first = product(real, table, 2, from_left)
        second = product(imag, table, 1, from_left)
        return shared + second, shared - first
    first = product(real, table, 1, from_left)
    second = product(imag, table, 2, from_left)
    return shared - second, shared + first


def sandwich(real, imag, table, conjugate):
    real, imag = complex_product(real, imag, table, conjugate, False)
    return complex_product(real, imag, table, conjugate, True)


def block(number):
    return pl.ds(pl.multiple_of(number * HALF, HALF), HALF)


def cut_piece(strip_ref, column, out_ref):
    first = lax.shift_right_logical(column, 7)
    offset = jnp.bitwise_and(column, HALF - 1)
    lanes = lax.broadcasted_iota(jnp.int32, (HALF, HALF), 1)
    mine = lanes >= offset
    third = jnp.minimum(first + 2, strip_ref.shape[-1] // HALF - 1)
    for part in range(2):
        out_ref[part, :, 0:HALF] = jnp.where(
            mine, strip_ref[0, part, :, block(first)], strip_ref[0, part, :, block(third)]
        )
        out_ref[part, :, HALF:WIN] = strip_ref[0, part, :, block(first + 1)]


def own_kernel(pos_ref, strip_ref, same_ref, cross_ref):
    core = lax.axis_index("cuts")
    cut_piece(strip_ref, pos_ref[core, 1], same_ref)
    cut_piece(strip_ref, pos_ref[1 - core, 1], cross_ref)


def halo_kernel(
    below_ref, above_ref, strip_ref, up_same_ref, up_cross_ref, down_same_ref, down_cross_ref
):
    core = lax.axis_index("cuts")
    cut_piece(strip_ref, above_ref[core, 1], up_same_ref)
    cut_piece(strip_ref, above_ref[1 - core, 1], up_cross_ref)
    cut_piece(strip_ref, below_ref[core, 1], down_same_ref)
    cut_piece(strip_ref, below_ref[1 - core, 1], down_cross_ref)


def slot_kernel(
    pos_ref,
    counts_ref,
    probe_ref,
    dft_ref,
    prop_ref,
    own_same_ref,
    own_cross_ref,
    low_same_ref,
    low_cross_ref,
    high_same_ref,
    high_cross_ref,
    intensity_ref,
    rim_same_ref,
    rim_cross_ref,
    mid_same_ref,
    mid_cross_ref,
    object_ref,
    grad_ref,
    measured_ref,
    sem,
):
    core = lax.axis_index("cuts")
    tile = lax.axis_index("tile")
    live = counts_ref[0] > core

    @pl.when(live)
    def _():
        fetch = pltpu.make_async_copy(intensity_ref.at[core], measured_ref, sem)
        fetch.start()
        shift_rows = pos_ref[core, 0] - (tile - 1) * HALF
        shift_cols = jnp.bitwise_and(pos_ref[core, 1], HALF - 1)
        rows = lax.broadcasted_iota(jnp.int32, (HALF, WIN), 0)
        from_low = rows >= shift_rows
        for part in range(2):
            object_ref[core, part, 0:HALF] = jnp.where(
                from_low, low_same_ref[part], high_same_ref[part]
            )
            object_ref[core, part, HALF:WIN] = own_same_ref[part]
            object_ref[1 - core, part, 0:HALF] = jnp.where(
                from_low, low_cross_ref[part], high_cross_ref[part]
            )
            object_ref[1 - core, part, HALF:WIN] = own_cross_ref[part]

        def rolled(part):
            return pltpu.roll(pltpu.roll(probe_ref[part], shift_rows, 0), shift_cols, 1)

        zero_re, zero_im = rolled(0), rolled(1)
        cell_re, cell_im = object_ref[0, 0], object_ref[0, 1]
        one_re, one_im = sandwich(
            zero_re * cell_re - zero_im * cell_im,
            zero_re * cell_im + zero_im * cell_re,
            prop_ref,
            False,
        )
        cell_re, cell_im = object_ref[1, 0], object_ref[1, 1]
        far_re, far_im = sandwich(
            one_re * cell_re - one_im * cell_im,
            one_re * cell_im + one_im * cell_re,
            dft_ref,
            False,
        )
        fetch.wait()
        residual = far_re * far_re + far_im * far_im - measured_ref[...]
        back_re, back_im = sandwich(far_re * residual, far_im * residual, dft_ref, True)
        grad_ref[1, 0] = one_re * back_re + one_im * back_im
        grad_ref[1, 1] = one_re * back_im - one_im * back_re
        back_re, back_im = sandwich(
            cell_re * back_re + cell_im * back_im,
            cell_re * back_im - cell_im * back_re,
            prop_ref,
            True,
        )
        grad_ref[0, 0] = zero_re * back_re + zero_im * back_im
        grad_ref[0, 1] = zero_re * back_im - zero_im * back_re

    @pl.when(jnp.logical_not(live))
    def _():
        grad_ref[...] = jnp.zeros_like(grad_ref)

    rim_same_ref[...] = grad_ref[core, :, 0:HALF]
    mid_same_ref[...] = grad_ref[core, :, HALF:WIN]
    rim_cross_ref[...] = grad_ref[1 - core, :, 0:HALF]
    mid_cross_ref[...] = grad_ref[1 - core, :, HALF:WIN]


def add_piece(out_ref, piece_ref, column, keep):
    first = lax.shift_right_logical(column, 7)
    offset = jnp.bitwise_and(column, HALF - 1)
    lanes = lax.broadcasted_iota(jnp.int32, (HALF, HALF), 1)
    mine = lanes >= offset
    third = jnp.minimum(first + 2, out_ref.shape[-1] // HALF - 1)
    for part in range(2):
        left = piece_ref[part, :, 0:HALF]
        right = piece_ref[part, :, HALF:WIN]
        if keep is not None:
            left = jnp.where(keep, left, 0.0)
            right = jnp.where(keep, right, 0.0)
        out_ref[0, part, :, block(first)] += jnp.where(mine, left, 0.0)
        out_ref[0, part, :, block(first + 1)] += right
        out_ref[0, part, :, block(third)] += jnp.where(mine, 0.0, left)


def collect_kernel(
    pos_ref,
    below_ref,
    above_ref,
    mid_same_ref,
    mid_cross_ref,
    up_same_ref,
    up_cross_ref,
    down_same_ref,
    down_cross_ref,
    out_ref,
):
    core = lax.axis_index("cuts")
    tile = lax.axis_index("tile")
    last = lax.axis_size("tile") - 1
    out_ref[...] = jnp.zeros_like(out_ref)
    add_piece(out_ref, mid_same_ref, pos_ref[core, 1], None)
    add_piece(out_ref, mid_cross_ref, pos_ref[1 - core, 1], None)
    rows = lax.broadcasted_iota(jnp.int32, (HALF, HALF), 0)
    below = jnp.where(tile == 0, last, tile - 1)
    above = jnp.where(tile == last, 0, tile + 1)
    for slot, piece_ref in ((core, up_same_ref), (1 - core, up_cross_ref)):
        shift_rows = below_ref[slot, 0] - (below - 1) * HALF
        add_piece(out_ref, piece_ref, below_ref[slot, 1], rows < shift_rows)
    for slot, piece_ref in ((core, down_same_ref), (1 - core, down_cross_ref)):
        shift_rows = above_ref[slot, 0] - (above - 1) * HALF
        add_piece(out_ref, piece_ref, above_ref[slot, 1], rows >= shift_rows)


SMEM = pl.BlockSpec(memory_space=pltpu.SMEM)
VMEM = pl.BlockSpec(memory_space=pltpu.VMEM)
ANY = pl.BlockSpec(memory_space=pl.ANY)


def cost(flops, moved):
    return pl.CostEstimate(flops=flops, bytes_accessed=moved, transcendentals=0)


def local(object_slices, probe, positions, counts, intensity):
    tiles = lax.axis_size("tile")

    def hop(value, swap, by):
        pairs = []
        for core in range(2):
            for tile in range(tiles):
                target = (core + swap) % 2 * tiles + (tile + by) % tiles
                pairs.append((core * tiles + tile, target))
        return lax.ppermute(value, ("cuts", "tile"), pairs)

    piece = jax.ShapeDtypeStruct((2, HALF, WIN), jnp.float32)
    dft, prop = build_tables()
    below = hop(positions, 0, 1)
    above = hop(positions, 0, -1)
    own_same, to_sibling = pl.pallas_call(
        own_kernel,
        out_shape=(piece,) * 2,
        in_specs=[SMEM, VMEM],
        out_specs=(VMEM,) * 2,
        cost_estimate=cost(0, 3 << 20),
        name="cut_own",
    )(positions, object_slices)
    up_same, up_cross, down_same, down_cross = pl.pallas_call(
        halo_kernel,
        out_shape=(piece,) * 4,
        in_specs=[SMEM, SMEM, VMEM],
        out_specs=(VMEM,) * 4,
        cost_estimate=cost(0, 3 << 20),
        name="cut_halo",
    )(below, above, object_slices)
    low_same = hop(up_same, 0, 1)
    high_same = hop(down_same, 0, -1)
    low_cross = hop(up_cross, 1, 1)
    high_cross = hop(down_cross, 1, -1)
    own_cross = hop(to_sibling, 1, 0)
    rim_same, rim_cross, mid_same, mid_cross = pl.pallas_call(
        slot_kernel,
        out_shape=(piece,) * 4,
        in_specs=[SMEM, SMEM] + [VMEM] * 9 + [ANY],
        out_specs=(VMEM,) * 4,
        scratch_shapes=[
            pltpu.VMEM((2, 2, WIN, WIN), jnp.float32),
            pltpu.VMEM((2, 2, WIN, WIN), jnp.float32),
            pltpu.VMEM((WIN, WIN), jnp.float32),
            pltpu.SemaphoreType.DMA,
        ],
        compiler_params=pltpu.CompilerParams(vmem_limit_bytes=32 << 20),
        cost_estimate=cost(72 * 2 * WIN**3, 6 << 20),
        name="slot",
    )(
        positions,
        counts,
        probe,
        jnp.asarray(dft),
        jnp.asarray(prop),
        own_same,
        own_cross,
        low_same,
        low_cross,
        high_same,
        high_cross,
        intensity,
    )
    got_up_same = hop(rim_same, 0, 1)
    got_down_same = hop(rim_same, 0, -1)
    got_up_cross = hop(rim_cross, 1, 1)
    got_down_cross = hop(rim_cross, 1, -1)
    got_mid = hop(mid_cross, 1, 0)
    return pl.pallas_call(
        collect_kernel,
        out_shape=jax.ShapeDtypeStruct(object_slices.shape, jnp.float32),
        in_specs=[SMEM] * 3 + [VMEM] * 6,
        out_specs=VMEM,
        compiler_params=pltpu.CompilerParams(vmem_limit_bytes=32 << 20),
        cost_estimate=cost(0, 4 << 20),
        name="collect",
    )(
        positions,
        below,
        above,
        mid_same,
        got_mid,
        got_up_same,
        got_up_cross,
        got_down_same,
        got_down_cross,
    )


def solution(mesh):
    in_specs = (
        P("cuts", None, "tile", None),
        P(),
        P("tile", None),
        P("tile"),
        P("tile", None, None),
    )
    out_specs = P("cuts", None, "tile", None)
    return jax.shard_map(local, mesh=mesh, in_specs=in_specs, out_specs=out_specs, check_vma=False)
```

profile of v0, /device:TPU:1, one launch (start us, length us, event | category | flops | bytes accessed | tf_op | source)
XLA Modules:
  0.0 79.5 jit_solution(13392127192999194761)
XLA Ops:
  0.0 0.0 copy-start.6
  0.0 0.0 copy-start.5
  0.0 11.1 %collective-permute-start.1 = (s32[2,2]{1,0:T(2,128)}, s32[2,2]{1,0:T(2,128)S(1)}, u32[]{:S(2)}, u32[]{:S(2)}) collective-permute-start(s32[2,2]{1,0:T(2,128)} %pos_ref.5), channel_id=1, source_target_pairs={{0,127},{1,0},{2,1},{3,2},{4,3},{5,4},{6,5},{7,6},{8,7},{9,8},{10,... | collective-permute-start | bytes 56 | tf_op jit(solution)/shard_map/ppermute | solution.py:253
  11.2 0.0 collective-permute-start
  11.2 2.5 %cut_own.1 = (f32[2,128,256]{2,1,0:T(8,128)}, f32[2,128,256]{2,1,0:T(8,128)}) custom-call(s32[2,2]{1,0:T(2,128)} %pos_ref.5, f32[1,2,128,2048]{3,2,1,0:T(8,128)} %strip_ref.3), custom_call_target="tpu_custom_call" | custom-call | bytes 3145728 | tf_op jit(solution)/shard_map/cut_own/pallas_call | solution.py:259
  13.7 1.0 %collective-permute-start.2 = (f32[2,128,256]{2,1,0:T(8,128)}, f32[2,128,256]{2,1,0:T(8,128)S(1)}, u32[]{:S(2)}, u32[]{:S(2)}) collective-permute-start(f32[2,128,256]{2,1,0:T(8,128)} %get-tuple-element.16), channel_id=1, source_target_pairs={{0,128},{1,129},{2,130},{3,131},{4,132},{5,133},{6,134},{7,135},{8... | collective-permute-start | bytes 786440 | tf_op jit(solution)/shard_map/ppermute | solution.py:253
  14.6 0.0 collective-permute-done.1.above_ref
  14.6 4.6 %collective-permute-done.below_ref = s32[2,2]{1,0:T(2,128)S(1)} collective-permute-done((s32[2,2]{1,0:T(2,128)}, s32[2,2]{1,0:T(2,128)S(1)}, u32[]{:S(2)}, u32[]{:S(2)}) %collective-permute-start) | collective-permute-done | bytes 48 | tf_op jit(solution)/shard_map/ppermute | solution.py:253
  19.2 0.6 copy-done.2
  19.8 2.8 %cut_halo.1 = (f32[2,128,256]{2,1,0:T(8,128)}, f32[2,128,256]{2,1,0:T(8,128)}, f32[2,128,256]{2,1,0:T(8,128)}, f32[2,128,256]{2,1,0:T(8,128)}) custom-call(s32[2,2]{1,0:T(2,128)} %copy-done.2, s32[2,2]{1,0:T(2,128)} %copy-done, f32[1,2,128,2048]{3,2,1,0:T(8,128)} %strip_ref.3), custom_call_target="tpu_custom_call" | custom-call | bytes 3145728 | tf_op jit(solution)/shard_map/cut_halo/pallas_call | solution.py:267
  22.6 0.0 collective-permute-start.3
  22.6 0.0 collective-permute-start.4
  22.6 8.9 %collective-permute-start.5 = (f32[2,128,256]{2,1,0:T(8,128)}, f32[2,128,256]{2,1,0:T(8,128)S(1)}, u32[]{:S(2)}, u32[]{:S(2)}) collective-permute-start(f32[2,128,256]{2,1,0:T(8,128)} %get-tuple-element.19), channel_id=1, source_target_pairs={{0,127},{1,0},{2,1},{3,2},{4,3},{5,4},{6,5},{7,6},{8,7},{9,8},{10,... | collective-permute-start | bytes 786440 | tf_op jit(solution)/shard_map/ppermute | solution.py:253
  31.5 0.3 collective-permute-start.6
  32.5 0.0 collective-permute-done.2.own_cross_ref
  32.5 1.5 %collective-permute-done.3.low_same_ref = f32[2,128,256]{2,1,0:T(8,128)S(1)} collective-permute-done((f32[2,128,256]{2,1,0:T(8,128)}, f32[2,128,256]{2,1,0:T(8,128)S(1)}, u32[]{:S(2)}, u32[]{:S(2)}) %collective-permute-start.3) | collective-permute-done | bytes 262176 | tf_op jit(solution)/shard_map/ppermute | solution.py:253
  33.9 8.0 %collective-permute-done.4.low_cross_ref = f32[2,128,256]{2,1,0:T(8,128)S(1)} collective-permute-done((f32[2,128,256]{2,1,0:T(8,128)}, f32[2,128,256]{2,1,0:T(8,128)S(1)}, u32[]{:S(2)}, u32[]{:S(2)}) %collective-permute-start.4) | collective-permute-done | bytes 262176 | tf_op jit(solution)/shard_map/ppermute | solution.py:253
  41.9 0.0 collective-permute-done.5.high_same_ref
  41.9 0.9 %collective-permute-done.6.high_cross_ref = f32[2,128,256]{2,1,0:T(8,128)S(1)} collective-permute-done((f32[2,128,256]{2,1,0:T(8,128)}, f32[2,128,256]{2,1,0:T(8,128)S(1)}, u32[]{:S(2)}, u32[]{:S(2)}) %collective-permute-start.6) | collective-permute-done | bytes 262176 | tf_op jit(solution)/shard_map/ppermute | solution.py:253
  42.8 0.7 slot.1
  43.6 6.1 %collective-permute-start.7 = (f32[2,128,256]{2,1,0:T(8,128)S(1)}, f32[2,128,256]{2,1,0:T(8,128)S(1)}, u32[]{:S(2)}, u32[]{:S(2)}) collective-permute-start(f32[2,128,256]{2,1,0:T(8,128)S(1)} %get-tuple-element.22), channel_id=1, source_target_pairs={{0,128},{1,129},{2,130},{3,131},{4,132},{5,133},{6,134},{7,135},{8... | collective-permute-start | bytes 786440 | tf_op jit(solution)/shard_map/ppermute | solution.py:253
  49.6 6.7 %collective-permute-start.10 = (f32[2,128,256]{2,1,0:T(8,128)S(1)}, f32[2,128,256]{2,1,0:T(8,128)S(1)}, u32[]{:S(2)}, u32[]{:S(2)}) collective-permute-start(f32[2,128,256]{2,1,0:T(8,128)S(1)} %get-tuple-element.23), channel_id=1, source_target_pairs={{0,127},{1,0},{2,1},{3,2},{4,3},{5,4},{6,5},{7,6},{8,7},{9,8},{10,... | collective-permute-start | bytes 786440 | tf_op jit(solution)/shard_map/ppermute | solution.py:253
  56.4 0.0 collective-permute-start.8
  56.4 7.4 %collective-permute-start.11 = (f32[2,128,256]{2,1,0:T(8,128)S(1)}, f32[2,128,256]{2,1,0:T(8,128)S(1)}, u32[]{:S(2)}, u32[]{:S(2)}) collective-permute-start(f32[2,128,256]{2,1,0:T(8,128)S(1)} %get-tuple-element.24), channel_id=1, source_target_pairs={{0,255},{1,128},{2,129},{3,130},{4,131},{5,132},{6,133},{7,134},{8... | collective-permute-start | bytes 786440 | tf_op jit(solution)/shard_map/ppermute | solution.py:253
  63.8 0.0 collective-permute-start.9
  63.8 0.0 collective-permute-done.7.mid_cross_ref
  63.8 0.0 collective-permute-done.10.down_same_ref
  63.8 5.5 %collective-permute-done.8.up_same_ref = f32[2,128,256]{2,1,0:T(8,128)S(1)} collective-permute-done((f32[2,128,256]{2,1,0:T(8,128)S(1)}, f32[2,128,256]{2,1,0:T(8,128)S(1)}, u32[]{:S(2)}, u32[]{:S(2)}) %collective-permute-start.8) | collective-permute-done | bytes 262176 | tf_op jit(solution)/shard_map/ppermute | solution.py:253
  69.3 0.5 collective-permute-done.11.down_cross_ref
  69.8 7.1 %collective-permute-done.9.up_cross_ref = f32[2,128,256]{2,1,0:T(8,128)S(1)} collective-permute-done((f32[2,128,256]{2,1,0:T(8,128)S(1)}, f32[2,128,256]{2,1,0:T(8,128)S(1)}, u32[]{:S(2)}, u32[]{:S(2)}) %collective-permute-start.9) | collective-permute-done | bytes 262176 | tf_op jit(solution)/shard_map/ppermute | solution.py:253
  77.0 0.0 copy-done.1
  77.0 2.5 %collect.1 = f32[1,2,128,2048]{3,2,1,0:T(8,128)} custom-call(s32[2,2]{1,0:T(2,128)S(1)} %copy-done.4, s32[2,2]{1,0:T(2,128)S(1)} %copy-done.3, s32[2,2]{1,0:T(2,128)S(1)} %copy-done.1, f32[2,128,256]{2,1,0:T(8,128)S(1)} %get-tuple-element.21.mid_same_ref, f32[2,128,256]{2,1,0:T(8,128)S(1)} %collective-permute-done.7.mid_cross_ref, ...), custom_call_target="tpu_custom_call" | custom-call | bytes 4194304 | tf_op jit(solution)/shard_map/collect/pallas_call | solution.py:313
  (16 shorter events, 0.0 us)
Async XLA Ops:
  0.0 42.8 %copy-start.8 = (bf16[6,256,256]{2,1,0:T(8,128)(2,1)S(1)}, bf16[6,256,256]{2,1,0:T(8,128)(2,1)}, u32[]{:S(2)}) copy-start(bf16[6,256,256]{2,1,0:T(8,128)(2,1)} %constant.5.clone.prop_ref) | copy-start | bytes 2359300
  0.0 42.8 %copy-start.9 = (bf16[6,256,256]{2,1,0:T(8,128)(2,1)S(1)}, bf16[6,256,256]{2,1,0:T(8,128)(2,1)}, u32[]{:S(2)}) copy-start(bf16[6,256,256]{2,1,0:T(8,128)(2,1)} %constant.4.clone.dft_ref) | copy-start | bytes 2359300
  0.0 42.8 %copy-start.4 = (s32[2,2]{1,0:T(2,128)S(1)}, s32[2,2]{1,0:T(2,128)}, u32[]{:S(2)}) copy-start(s32[2,2]{1,0:T(2,128)} %pos_ref.5) | copy-start | bytes 52
  0.0 42.8 %copy-start.6 = (f32[2,256,256]{2,1,0:T(8,128)S(1)}, f32[2,256,256]{2,1,0:T(8,128)}, u32[]{:S(2)}) copy-start(f32[2,256,256]{2,1,0:T(8,128)} %intensity_ref.1) | copy-start | bytes 1572868
  0.0 42.8 %copy-start.5 = (f32[2,256,256]{2,1,0:T(8,128)S(1)}, f32[2,256,256]{2,1,0:T(8,128)}, u32[]{:S(2)}) copy-start(f32[2,256,256]{2,1,0:T(8,128)} %probe_ref.1) | copy-start | bytes 1572868
  0.0 14.6 %collective-permute-start.1 = (s32[2,2]{1,0:T(2,128)}, s32[2,2]{1,0:T(2,128)S(1)}, u32[]{:S(2)}, u32[]{:S(2)}) collective-permute-start(s32[2,2]{1,0:T(2,128)} %pos_ref.5), channel_id=1, source_target_pairs={{0,127},{1,0},{2,1},{3,2},{4,3},{5,4},{6,5},{7,6},{8,7},{9,8},{10,... | collective-permute-start | bytes 56 | tf_op jit(solution)/shard_map/ppermute | solution.py:253
  11.2 8.1 %collective-permute-start = (s32[2,2]{1,0:T(2,128)}, s32[2,2]{1,0:T(2,128)S(1)}, u32[]{:S(2)}, u32[]{:S(2)}) collective-permute-start(s32[2,2]{1,0:T(2,128)} %pos_ref.5), channel_id=1, source_target_pairs={{0,1},{1,2},{2,3},{3,4},{4,5},{5,6},{6,7},{7,8},{8,9},{9,10},{10,1... | collective-permute-start | bytes 56 | tf_op jit(solution)/shard_map/ppermute | solution.py:253
  13.7 29.1 %copy-start.7 = (f32[2,128,256]{2,1,0:T(8,128)S(1)}, f32[2,128,256]{2,1,0:T(8,128)}, u32[]{:S(2)}) copy-start(f32[2,128,256]{2,1,0:T(8,128)} %get-tuple-element.15.own_same_ref) | copy-start | bytes 786436
  13.7 18.8 %collective-permute-start.2 = (f32[2,128,256]{2,1,0:T(8,128)}, f32[2,128,256]{2,1,0:T(8,128)S(1)}, u32[]{:S(2)}, u32[]{:S(2)}) collective-permute-start(f32[2,128,256]{2,1,0:T(8,128)} %get-tuple-element.16), channel_id=1, source_target_pairs={{0,128},{1,129},{2,130},{3,131},{4,132},{5,133},{6,134},{7,135},{8... | collective-permute-start | bytes 786440 | tf_op jit(solution)/shard_map/ppermute | solution.py:253
  14.6 4.6 %copy-start = (s32[2,2]{1,0:T(2,128)}, s32[2,2]{1,0:T(2,128)S(1)}, u32[]{:S(2)}) copy-start(s32[2,2]{1,0:T(2,128)S(1)} %collective-permute-done.1.above_ref) | copy-start | bytes 52
  19.2 0.6 copy-start.2
  22.6 11.3 %collective-permute-start.3 = (f32[2,128,256]{2,1,0:T(8,128)}, f32[2,128,256]{2,1,0:T(8,128)S(1)}, u32[]{:S(2)}, u32[]{:S(2)}) collective-permute-start(f32[2,128,256]{2,1,0:T(8,128)} %get-tuple-element.17), channel_id=1, source_target_pairs={{0,1},{1,2},{2,3},{3,4},{4,5},{5,6},{6,7},{7,8},{8,9},{9,10},{10,1... | collective-permute-start | bytes 786440 | tf_op jit(solution)/shard_map/ppermute | solution.py:253
  22.6 19.3 %collective-permute-start.4 = (f32[2,128,256]{2,1,0:T(8,128)}, f32[2,128,256]{2,1,0:T(8,128)S(1)}, u32[]{:S(2)}, u32[]{:S(2)}) collective-permute-start(f32[2,128,256]{2,1,0:T(8,128)} %get-tuple-element.18), channel_id=1, source_target_pairs={{0,129},{1,130},{2,131},{3,132},{4,133},{5,134},{6,135},{7,136},{8... | collective-permute-start | bytes 786440 | tf_op jit(solution)/shard_map/ppermute | solution.py:253
  22.6 19.3 %collective-permute-start.5 = (f32[2,128,256]{2,1,0:T(8,128)}, f32[2,128,256]{2,1,0:T(8,128)S(1)}, u32[]{:S(2)}, u32[]{:S(2)}) collective-permute-start(f32[2,128,256]{2,1,0:T(8,128)} %get-tuple-element.19), channel_id=1, source_target_pairs={{0,127},{1,0},{2,1},{3,2},{4,3},{5,4},{6,5},{7,6},{8,7},{9,8},{10,... | collective-permute-start | bytes 786440 | tf_op jit(solution)/shard_map/ppermute | solution.py:253
  31.5 11.3 %collective-permute-start.6 = (f32[2,128,256]{2,1,0:T(8,128)}, f32[2,128,256]{2,1,0:T(8,128)S(1)}, u32[]{:S(2)}, u32[]{:S(2)}) collective-permute-start(f32[2,128,256]{2,1,0:T(8,128)} %get-tuple-element.20), channel_id=1, source_target_pairs={{0,255},{1,128},{2,129},{3,130},{4,131},{5,132},{6,133},{7,134},{8... | collective-permute-start | bytes 786440 | tf_op jit(solution)/shard_map/ppermute | solution.py:253
  42.8 34.2 %copy-start.1 = (s32[2,2]{1,0:T(2,128)S(1)}, s32[2,2]{1,0:T(2,128)}, u32[]{:S(2)}) copy-start(s32[2,2]{1,0:T(2,128)} %copy-done) | copy-start | bytes 52
  42.8 34.2 %copy-start.3 = (s32[2,2]{1,0:T(2,128)S(1)}, s32[2,2]{1,0:T(2,128)}, u32[]{:S(2)}) copy-start(s32[2,2]{1,0:T(2,128)} %copy-done.2) | copy-start | bytes 52
  43.6 20.2 %collective-permute-start.7 = (f32[2,128,256]{2,1,0:T(8,128)S(1)}, f32[2,128,256]{2,1,0:T(8,128)S(1)}, u32[]{:S(2)}, u32[]{:S(2)}) collective-permute-start(f32[2,128,256]{2,1,0:T(8,128)S(1)} %get-tuple-element.22), channel_id=1, source_target_pairs={{0,128},{1,129},{2,130},{3,131},{4,132},{5,133},{6,134},{7,135},{8... | collective-permute-start | bytes 786440 | tf_op jit(solution)/shard_map/ppermute | solution.py:253
  49.6 14.2 %collective-permute-start.10 = (f32[2,128,256]{2,1,0:T(8,128)S(1)}, f32[2,128,256]{2,1,0:T(8,128)S(1)}, u32[]{:S(2)}, u32[]{:S(2)}) collective-permute-start(f32[2,128,256]{2,1,0:T(8,128)S(1)} %get-tuple-element.23), channel_id=1, source_target_pairs={{0,127},{1,0},{2,1},{3,2},{4,3},{5,4},{6,5},{7,6},{8,7},{9,8},{10,... | collective-permute-start | bytes 786440 | tf_op jit(solution)/shard_map/ppermute | solution.py:253
  56.4 13.0 %collective-permute-start.8 = (f32[2,128,256]{2,1,0:T(8,128)S(1)}, f32[2,128,256]{2,1,0:T(8,128)S(1)}, u32[]{:S(2)}, u32[]{:S(2)}) collective-permute-start(f32[2,128,256]{2,1,0:T(8,128)S(1)} %get-tuple-element.23), channel_id=1, source_target_pairs={{0,1},{1,2},{2,3},{3,4},{4,5},{5,6},{6,7},{7,8},{8,9},{9,10},{10,1... | collective-permute-start | bytes 786440 | tf_op jit(solution)/shard_map/ppermute | solution.py:253
  56.4 13.5 %collective-permute-start.11 = (f32[2,128,256]{2,1,0:T(8,128)S(1)}, f32[2,128,256]{2,1,0:T(8,128)S(1)}, u32[]{:S(2)}, u32[]{:S(2)}) collective-permute-start(f32[2,128,256]{2,1,0:T(8,128)S(1)} %get-tuple-element.24), channel_id=1, source_target_pairs={{0,255},{1,128},{2,129},{3,130},{4,131},{5,132},{6,133},{7,134},{8... | collective-permute-start | bytes 786440 | tf_op jit(solution)/shard_map/ppermute | solution.py:253
  63.8 13.2 %collective-permute-start.9 = (f32[2,128,256]{2,1,0:T(8,128)S(1)}, f32[2,128,256]{2,1,0:T(8,128)S(1)}, u32[]{:S(2)}, u32[]{:S(2)}) collective-permute-start(f32[2,128,256]{2,1,0:T(8,128)S(1)} %get-tuple-element.24), channel_id=1, source_target_pairs={{0,129},{1,130},{2,131},{3,132},{4,133},{5,134},{6,135},{7,136},{8... | collective-permute-start | bytes 786440 | tf_op jit(solution)/shard_map/ppermute | solution.py:253
where the time goes:
time: 79.6 us; the launch traced here: 79.5 us
  starting transfers between devices  41.5 us (52%)
  waiting for transfers between devices  28.1 us (35%)
  Pallas kernels  8.54 us (11%)
    ppermute x12, starting transfers between devices, hop(): return lax.ppermute(value, ('cuts', 'tile'), pairs)  41.5 us
    ppermute x12, waiting for transfers between devices, hop(): return lax.ppermute(value, ('cuts', 'tile'), pairs)  28.1 us
    pallas_call x1, Pallas kernels, local(): pl.pallas_call(halo_kernel, out_shape=(piece,) * 4, in_specs=[SMEM, SMEM,...  2.8 us
    pallas_call x1, Pallas kernels, local(): pl.pallas_call(own_kernel, out_shape=(piece,) * 2, in_specs=[SMEM, VMEM],...  2.52 us
    pallas_call x1, Pallas kernels, local(): pl.pallas_call(collect_kernel, out_shape=jax.ShapeDtypeStruct(object_slic...  2.51 us
  transfers between devices with their start and end apart: 12, of which 7 were waited for; matrix products, arithmetic and copies ran while one was open for 0% of the time, Pallas kernels for 7%

commit v1 on v0

--- a/solution.py
+++ b/solution.py
@@ -84,20 +84,32 @@
         out_ref[part, :, HALF:WIN] = strip_ref[0, part, :, block(first + 1)]
 
 
-def own_kernel(pos_ref, strip_ref, same_ref, cross_ref):
+def cut_partner_kernel(first_ref, second_ref, strip_ref, to_first_ref, to_second_ref):
+    for slot in range(2):
+        cut_piece(strip_ref, first_ref[slot, 1], to_first_ref.at[slot])
+        cut_piece(strip_ref, second_ref[slot, 1], to_second_ref.at[slot])
+
+
+def cut_own_kernel(pos_ref, strip_ref, after_ref, same_ref, cross_ref):
     core = lax.axis_index("cuts")
     cut_piece(strip_ref, pos_ref[core, 1], same_ref)
     cut_piece(strip_ref, pos_ref[1 - core, 1], cross_ref)
 
 
-def halo_kernel(
-    below_ref, above_ref, strip_ref, up_same_ref, up_cross_ref, down_same_ref, down_cross_ref
-):
-    core = lax.axis_index("cuts")
-    cut_piece(strip_ref, above_ref[core, 1], up_same_ref)
-    cut_piece(strip_ref, above_ref[1 - core, 1], up_cross_ref)
-    cut_piece(strip_ref, below_ref[core, 1], down_same_ref)
-    cut_piece(strip_ref, below_ref[1 - core, 1], down_cross_ref)
+def from_first(pos_ref, slot, shape):
+    tile = lax.axis_index("tile")
+    odd = jnp.bitwise_and(tile, 1)
+    shift_rows = pos_ref[slot, 0] - (tile - 1) * HALF
+    rows = lax.broadcasted_iota(jnp.int32, shape, 0)
+    sign = 2 * odd - 1
+    return sign * (rows - shift_rows) >= 1 - odd
+
+
+def merge_kernel(pos_ref, first_ref, second_ref, out_ref):
+    slot = 1 - lax.axis_index("cuts")
+    mask = from_first(pos_ref, slot, (HALF, WIN))
+    for part in range(2):
+        out_ref[part] = jnp.where(mask, first_ref[slot, part], second_ref[slot, part])
 
 
 def slot_kernel(
@@ -108,15 +120,12 @@
     prop_ref,
     own_same_ref,
     own_cross_ref,
-    low_same_ref,
-    low_cross_ref,
-    high_same_ref,
-    high_cross_ref,
+    first_ref,
+    second_ref,
+    rim_cross_ref,
     intensity_ref,
-    rim_same_ref,
-    rim_cross_ref,
-    mid_same_ref,
-    mid_cross_ref,
+    out_same_ref,
+    out_cross_ref,
     object_ref,
     grad_ref,
     measured_ref,
@@ -132,16 +141,13 @@
         fetch.start()
         shift_rows = pos_ref[core, 0] - (tile - 1) * HALF
         shift_cols = jnp.bitwise_and(pos_ref[core, 1], HALF - 1)
-        rows = lax.broadcasted_iota(jnp.int32, (HALF, WIN), 0)
-        from_low = rows >= shift_rows
+        mask = from_first(pos_ref, core, (HALF, WIN))
         for part in range(2):
             object_ref[core, part, 0:HALF] = jnp.where(
-                from_low, low_same_ref[part], high_same_ref[part]
+                mask, first_ref[core, part], second_ref[core, part]
             )
             object_ref[core, part, HALF:WIN] = own_same_ref[part]
-            object_ref[1 - core, part, 0:HALF] = jnp.where(
-                from_low, low_cross_ref[part], high_cross_ref[part]
-            )
+            object_ref[1 - core, part, 0:HALF] = rim_cross_ref[part]
             object_ref[1 - core, part, HALF:WIN] = own_cross_ref[part]
 
         def rolled(part):
@@ -180,10 +186,14 @@
     def _():
         grad_ref[...] = jnp.zeros_like(grad_ref)
 
-    rim_same_ref[...] = grad_ref[core, :, 0:HALF]
-    mid_same_ref[...] = grad_ref[core, :, HALF:WIN]
-    rim_cross_ref[...] = grad_ref[1 - core, :, 0:HALF]
-    mid_cross_ref[...] = grad_ref[1 - core, :, HALF:WIN]
+    out_same_ref[...] = grad_ref[core]
+    out_cross_ref[...] = grad_ref[1 - core]
+
+
+def pack_kernel(same_ref, cross_ref, out_ref):
+    core = lax.axis_index("cuts")
+    out_ref[core] = same_ref[:, 0:HALF]
+    out_ref[1 - core] = cross_ref[:, 0:HALF]
 
 
 def add_piece(out_ref, piece_ref, column, keep):
@@ -204,32 +214,24 @@
 
 
 def collect_kernel(
-    pos_ref,
-    below_ref,
-    above_ref,
-    mid_same_ref,
-    mid_cross_ref,
-    up_same_ref,
-    up_cross_ref,
-    down_same_ref,
-    down_cross_ref,
-    out_ref,
+    pos_ref, pos_first_ref, pos_second_ref, same_ref, cross_ref, first_ref, second_ref, out_ref
 ):
     core = lax.axis_index("cuts")
     tile = lax.axis_index("tile")
-    last = lax.axis_size("tile") - 1
+    odd = jnp.bitwise_and(tile, 1)
     out_ref[...] = jnp.zeros_like(out_ref)
-    add_piece(out_ref, mid_same_ref, pos_ref[core, 1], None)
-    add_piece(out_ref, mid_cross_ref, pos_ref[1 - core, 1], None)
+    add_piece(out_ref, same_ref.at[:, HALF:WIN], pos_ref[core, 1], None)
+    add_piece(out_ref, cross_ref.at[:, HALF:WIN], pos_ref[1 - core, 1], None)
     rows = lax.broadcasted_iota(jnp.int32, (HALF, HALF), 0)
-    below = jnp.where(tile == 0, last, tile - 1)
-    above = jnp.where(tile == last, 0, tile + 1)
-    for slot, piece_ref in ((core, up_same_ref), (1 - core, up_cross_ref)):
-        shift_rows = below_ref[slot, 0] - (below - 1) * HALF
-        add_piece(out_ref, piece_ref, below_ref[slot, 1], rows < shift_rows)
-    for slot, piece_ref in ((core, down_same_ref), (1 - core, down_cross_ref)):
-        shift_rows = above_ref[slot, 0] - (above - 1) * HALF
-        add_piece(out_ref, piece_ref, above_ref[slot, 1], rows >= shift_rows)
+    for nearby_ref, piece_ref, above in (
+        (pos_first_ref, first_ref, 1 - odd),
+        (pos_second_ref, second_ref, odd),
+    ):
+        sign = 2 * above - 1
+        for slot in range(2):
+            shift_rows = nearby_ref[slot, 0] - (tile + sign - 1) * HALF
+            keep = sign * (rows - shift_rows) >= 1 - above
+            add_piece(out_ref, piece_ref.at[slot], nearby_ref[slot, 1], keep)
 
 
 SMEM = pl.BlockSpec(memory_space=pltpu.SMEM)
@@ -244,51 +246,73 @@
 def local(object_slices, probe, positions, counts, intensity):
     tiles = lax.axis_size("tile")
 
-    def hop(value, swap, by):
-        pairs = []
-        for core in range(2):
-            for tile in range(tiles):
-                target = (core + swap) % 2 * tiles + (tile + by) % tiles
-                pairs.append((core * tiles + tile, target))
+    def exchange(value, partner):
+        pairs = [(core * tiles + tile, core * tiles + partner(tile)) for core in range(2) for tile in range(tiles)]
+        pairs = [pair for pair in pairs if pair[1] // tiles == pair[0] // tiles and pair[1] >= 0]
         return lax.ppermute(value, ("cuts", "tile"), pairs)
 
-    piece = jax.ShapeDtypeStruct((2, HALF, WIN), jnp.float32)
+    def first(value):
+        return exchange(value, lambda tile: tile ^ 1)
+
+    def second(value):
+        return exchange(value, lambda tile: ((tile + 1) ^ 1) - 1)
+
+    def sibling(value):
+        return lax.ppermute(value, "cuts", [(0, 1), (1, 0)])
+
+    def shape(*extent):
+        return jax.ShapeDtypeStruct(extent, jnp.float32)
+
+    piece = shape(2, HALF, WIN)
+    whole = shape(2, WIN, WIN)
+    both = shape(2, 2, HALF, WIN)
     dft, prop = build_tables()
-    below = hop(positions, 0, 1)
-    above = hop(positions, 0, -1)
-    own_same, to_sibling = pl.pallas_call(
-        own_kernel,
-        out_shape=(piece,) * 2,
-        in_specs=[SMEM, VMEM],
+    pos_second = second(positions)
+    pos_first = first(positions)
+    to_first, to_second = pl.pallas_call(
+        cut_partner_kernel,
+        out_shape=(both,) * 2,
+        in_specs=[SMEM, SMEM, VMEM],
         out_specs=(VMEM,) * 2,
         cost_estimate=cost(0, 3 << 20),
+        compiler_params=pltpu.CompilerParams(vmem_limit_bytes=8 << 20),
+        name="cut_partner",
+    )(pos_first, pos_second, object_slices)
+    got_second = second(to_second)
+    got_first = first(to_first)
+    own_same, to_sibling = pl.pallas_call(
+        cut_own_kernel,
+        out_shape=(piece,) * 2,
+        in_specs=[SMEM, VMEM, ANY],
+        out_specs=(VMEM,) * 2,
+        cost_estimate=cost(0, 3 << 20),
+        compiler_params=pltpu.CompilerParams(vmem_limit_bytes=8 << 20),
         name="cut_own",
-    )(positions, object_slices)
-    up_same, up_cross, down_same, down_cross = pl.pallas_call(
-        halo_kernel,
-        out_shape=(piece,) * 4,
-        in_specs=[SMEM, SMEM, VMEM],
-        out_specs=(VMEM,) * 4,
-        cost_estimate=cost(0, 3 << 20),
-        name="cut_halo",
-    )(below, above, object_slices)
-    low_same = hop(up_same, 0, 1)
-    high_same = hop(down_same, 0, -1)
-    low_cross = hop(up_cross, 1, 1)
-    high_cross = hop(down_cross, 1, -1)
-    own_cross = hop(to_sibling, 1, 0)
-    rim_same, rim_cross, mid_same, mid_cross = pl.pallas_call(
+    )(positions, object_slices, to_first)
+    own_cross = sibling(to_sibling)
+    rim_cross = sibling(
+        pl.pallas_call(
+            merge_kernel,
+            out_shape=piece,
+            in_specs=[SMEM, VMEM, VMEM],
+            out_specs=VMEM,
+            cost_estimate=cost(0, 1 << 20),
+            compiler_params=pltpu.CompilerParams(vmem_limit_bytes=8 << 20),
+        name="merge",
+        )(positions, got_first, got_second)
+    )
+    grad_same, grad_cross = pl.pallas_call(
         slot_kernel,
-        out_shape=(piece,) * 4,
-        in_specs=[SMEM, SMEM] + [VMEM] * 9 + [ANY],
-        out_specs=(VMEM,) * 4,
+        out_shape=(whole,) * 2,
+        in_specs=[SMEM, SMEM] + [VMEM] * 8 + [ANY],
+        out_specs=(VMEM,) * 2,
         scratch_shapes=[
             pltpu.VMEM((2, 2, WIN, WIN), jnp.float32),
             pltpu.VMEM((2, 2, WIN, WIN), jnp.float32),
             pltpu.VMEM((WIN, WIN), jnp.float32),
             pltpu.SemaphoreType.DMA,
         ],
-        compiler_params=pltpu.CompilerParams(vmem_limit_bytes=32 << 20),
+        compiler_params=pltpu.CompilerParams(vmem_limit_bytes=16 << 20),
         cost_estimate=cost(72 * 2 * WIN**3, 6 << 20),
         name="slot",
     )(
@@ -299,36 +323,32 @@
         jnp.asarray(prop),
         own_same,
         own_cross,
-        low_same,
-        low_cross,
-        high_same,
-        high_cross,
+        got_first,
+        got_second,
+        rim_cross,
         intensity,
     )
-    got_up_same = hop(rim_same, 0, 1)
-    got_down_same = hop(rim_same, 0, -1)
-    got_up_cross = hop(rim_cross, 1, 1)
-    got_down_cross = hop(rim_cross, 1, -1)
-    got_mid = hop(mid_cross, 1, 0)
+    grad_cross = sibling(grad_cross)
+    rims = pl.pallas_call(
+        pack_kernel,
+        out_shape=both,
+        in_specs=[VMEM, VMEM],
+        out_specs=VMEM,
+        cost_estimate=cost(0, 1 << 20),
+        compiler_params=pltpu.CompilerParams(vmem_limit_bytes=8 << 20),
+        name="pack",
+    )(grad_same, grad_cross)
+    back_second = second(rims)
+    back_first = first(rims)
     return pl.pallas_call(
         collect_kernel,
         out_shape=jax.ShapeDtypeStruct(object_slices.shape, jnp.float32),
-        in_specs=[SMEM] * 3 + [VMEM] * 6,
+        in_specs=[SMEM] * 3 + [VMEM] * 4,
         out_specs=VMEM,
-        compiler_params=pltpu.CompilerParams(vmem_limit_bytes=32 << 20),
+        compiler_params=pltpu.CompilerParams(vmem_limit_bytes=16 << 20),
         cost_estimate=cost(0, 4 << 20),
         name="collect",
-    )(
-        positions,
-        below,
-        above,
-        mid_same,
-        got_mid,
-        got_up_same,
-        got_up_cross,
-        got_down_same,
-        got_down_cross,
-    )
+    )(positions, pos_first, pos_second, grad_same, grad_cross, back_first, back_second)
 
 
 def solution(mesh):

time: 79.6 us -> 67.3 us (0.85)
  the two profiles are of different devices: /device:TPU:1 before, /device:TPU:129 now
where the time goes in v1:
time: 67.3 us; the launch traced here: 66.6 us
  starting transfers between devices  29.8 us (44%)
  waiting for transfers between devices  29 us (43%)
  Pallas kernels  5.3 us (8%)
  local copies, waits for them, and re-layouts  1.63 us (2%)
  between operations  0.8 us (1%)
    ppermute x6, waiting for transfers between devices, exchange(): return lax.ppermute(value, ('cuts', 'tile'), pairs)  27 us
    ppermute x6, starting transfers between devices, exchange(): return lax.ppermute(value, ('cuts', 'tile'), pairs)  19.5 us
    ppermute x3, starting transfers between devices, sibling(): return lax.ppermute(value, 'cuts', [(0, 1), (1, 0)])  10.3 us
    pallas_call x1, Pallas kernels, local(): pl.pallas_call(collect_kernel, out_shape=jax.ShapeDtypeStruct(object_slic...  2.52 us
    ppermute x3, waiting for transfers between devices, sibling(): return lax.ppermute(value, 'cuts', [(0, 1), (1, 0)])  2.04 us
    unnamed x14, local copies, waits for them, and re-layouts  1.63 us
  transfers between devices with their start and end apart: 9, of which 5 were waited for; matrix products, arithmetic and copies ran while one was open for 0% of the time, Pallas kernels for 2%

profile of v1, /device:TPU:129, one launch (start us, length us, event | category | flops | bytes accessed | tf_op | source)
XLA Modules:
  0.0 66.6 jit_solution(1007501001984729622)
XLA Ops:
  0.0 6.4 %collective-permute-start.1 = (s32[2,2]{1,0:T(2,128)}, s32[2,2]{1,0:T(2,128)S(1)}, u32[]{:S(2)}, u32[]{:S(2)}) collective-permute-start(s32[2,2]{1,0:T(2,128)} %pos_ref.7), channel_id=1, source_target_pairs={{1,2},{2,1},{3,4},{4,3},{5,6},{6,5},{7,8},{8,7},{9,10},{10,9},{11,... | collective-permute-start | bytes 56 | tf_op jit(solution)/shard_map/ppermute | solution.py:252
  6.4 0.1 collective-permute-start
  6.5 3.5 %collective-permute-done.1.second_ref.pos_second_ref = s32[2,2]{1,0:T(2,128)S(1)} collective-permute-done((s32[2,2]{1,0:T(2,128)}, s32[2,2]{1,0:T(2,128)S(1)}, u32[]{:S(2)}, u32[]{:S(2)}) %collective-permute-start.1) | collective-permute-done | bytes 48 | tf_op jit(solution)/shard_map/ppermute | solution.py:252
  9.9 0.0 collective-permute-done.first_ref.pos_first_ref
  9.9 1.6 %copy-done = f32[1,2,128,2048]{3,2,1,0:T(8,128)S(1)} copy-done((f32[1,2,128,2048]{3,2,1,0:T(8,128)S(1)}, f32[1,2,128,2048]{3,2,1,0:T(8,128)}, u32[]{:S(2)}) %copy-start) | copy-done | bytes 2097176
  11.5 0.8 %cut_partner.1 = (f32[2,2,128,256]{3,2,1,0:T(8,128)S(1)}, f32[2,2,128,256]{3,2,1,0:T(8,128)S(1)}) custom-call(s32[2,2]{1,0:T(2,128)S(1)} %collective-permute-done.first_ref.pos_first_ref, s32[2,2]{1,0:T(2,128)S(1)} %collective-permute-done.1.second_ref.pos_second_ref, f32[1,2,128,2048]{3,2,1,0:T(8,128)S(1)} %copy-done), custom_call_target="tpu_custom_call" | custom-call | bytes 3145728 | tf_op jit(solution)/shard_map/cut_partner/pallas_call | solution.py:272
  12.3 0.0 copy-start.3
  12.3 0.0 copy-start.4
  12.3 0.0 copy-start.5
  12.4 0.0 copy-start.6
  12.4 6.5 %collective-permute-start.4 = (f32[2,2,128,256]{3,2,1,0:T(8,128)S(1)}, f32[2,2,128,256]{3,2,1,0:T(8,128)S(1)}, u32[]{:S(2)}, u32[]{:S(2)}) collective-permute-start(f32[2,2,128,256]{3,2,1,0:T(8,128)S(1)} %get-tuple-element.14), channel_id=1, source_target_pairs={{1,2},{2,1},{3,4},{4,3},{5,6},{6,5},{7,8},{8,7},{9,10},{10,9},{11,... | collective-permute-start | bytes 1572872 | tf_op jit(solution)/shard_map/ppermute | solution.py:252
  18.9 0.1 collective-permute-start.3
  19.0 0.0 copy-done.1
  19.0 0.0 copy-done.2
  19.0 0.7 %cut_own.1 = (f32[2,128,256]{2,1,0:T(8,128)S(1)}, f32[2,128,256]{2,1,0:T(8,128)S(1)}) custom-call(s32[2,2]{1,0:T(2,128)S(1)} %copy-done.2, f32[1,2,128,2048]{3,2,1,0:T(8,128)S(1)} %copy-done.1, f32[2,2,128,256]{3,2,1,0:T(8,128)S(1)} %get-tuple-element.11.after_ref), custom_call_target="tpu_custom_call" | custom-call | bytes 3145728 | tf_op jit(solution)/shard_map/cut_own/pallas_call | solution.py:283
  19.7 2.2 %collective-permute-start.2 = (f32[2,128,256]{2,1,0:T(8,128)S(1)}, f32[2,128,256]{2,1,0:T(8,128)S(1)}, u32[]{:S(2)}, u32[]{:S(2)}) collective-permute-start(f32[2,128,256]{2,1,0:T(8,128)S(1)} %get-tuple-element.13), channel_id=1, source_target_pairs={{0,128},{128,0},{1,129},{129,1},{2,130},{130,2},{3,131},{131,3},{4... | collective-permute-start | bytes 786440 | tf_op jit(solution)/shard_map/ppermute | solution.py:261
  21.9 9.5 %collective-permute-done.4.second_ref = f32[2,2,128,256]{3,2,1,0:T(8,128)S(1)} collective-permute-done((f32[2,2,128,256]{3,2,1,0:T(8,128)S(1)}, f32[2,2,128,256]{3,2,1,0:T(8,128)S(1)}, u32[]{:S(2)}, u32[]{:S(2)}) %collective-permute-start.4) | collective-permute-done | bytes 524320 | tf_op jit(solution)/shard_map/ppermute | solution.py:252
  31.4 0.0 collective-permute-done.3.first_ref
  31.4 0.6 merge.1
  32.0 2.8 %collective-permute-start.5 = (f32[2,128,256]{2,1,0:T(8,128)S(1)}, f32[2,128,256]{2,1,0:T(8,128)S(1)}, u32[]{:S(2)}, u32[]{:S(2)}) collective-permute-start(f32[2,128,256]{2,1,0:T(8,128)S(1)} %merge.1), channel_id=1, source_target_pairs={{0,128},{128,0},{1,129},{129,1},{2,130},{130,2},{3,131},{131,3},{4... | collective-permute-start | bytes 786440 | tf_op jit(solution)/shard_map/ppermute | solution.py:261
  35.5 0.0 collective-permute-done.2.own_cross_ref
  35.5 0.5 collective-permute-done.5.rim_cross_ref
  36.0 0.0 copy-done.3
  36.0 0.0 copy-done.5
  36.0 0.7 %slot.1 = (f32[2,256,256]{2,1,0:T(8,128)S(1)}, f32[2,256,256]{2,1,0:T(8,128)S(1)}) custom-call(s32[2,2]{1,0:T(2,128)S(1)} %copy-done.2, s32[1]{0:T(128)S(6)} %copy.8.counts_ref, f32[2,256,256]{2,1,0:T(8,128)S(1)} %copy-done.3, bf16[6,256,256]{2,1,0:T(8,128)(2,1)S(1)} %copy-done.6, bf16[6,256,256]{2,1,0:T(8,128)(2,1)S(1)} %copy-done.5, ...), custom_call_target="tpu_custom_call" | custom-call | flops 2415919104 | bytes 6291456 | tf_op jit(solution)/shard_map/slot/pallas_call | solution.py:304
  36.7 5.2 %collective-permute-start.6 = (f32[2,256,256]{2,1,0:T(8,128)S(1)}, f32[2,256,256]{2,1,0:T(8,128)S(1)}, u32[]{:S(2)}, u32[]{:S(2)}) collective-permute-start(f32[2,256,256]{2,1,0:T(8,128)S(1)} %get-tuple-element.16), channel_id=1, source_target_pairs={{0,128},{128,0},{1,129},{129,1},{2,130},{130,2},{3,131},{131,3},{4... | collective-permute-start | bytes 1572872 | tf_op jit(solution)/shard_map/ppermute | solution.py:261
  42.0 1.5 %collective-permute-done.6.cross_ref = f32[2,256,256]{2,1,0:T(8,128)S(1)} collective-permute-done((f32[2,256,256]{2,1,0:T(8,128)S(1)}, f32[2,256,256]{2,1,0:T(8,128)S(1)}, u32[]{:S(2)}, u32[]{:S(2)}) %collective-permute-start.6) | collective-permute-done | bytes 524320 | tf_op jit(solution)/shard_map/ppermute | solution.py:261
  43.6 6.4 %collective-permute-start.8 = (f32[2,2,128,256]{3,2,1,0:T(8,128)S(1)}, f32[2,2,128,256]{3,2,1,0:T(8,128)S(1)}, u32[]{:S(2)}, u32[]{:S(2)}) collective-permute-start(f32[2,2,128,256]{3,2,1,0:T(8,128)S(1)} %pack.1), channel_id=1, source_target_pairs={{1,2},{2,1},{3,4},{4,3},{5,6},{6,5},{7,8},{8,7},{9,10},{10,9},{11,... | collective-permute-start | bytes 1572872 | tf_op jit(solution)/shard_map/ppermute | solution.py:252
  50.0 0.1 collective-permute-start.7
  50.1 14.0 %collective-permute-done.8.second_ref = f32[2,2,128,256]{3,2,1,0:T(8,128)S(1)} collective-permute-done((f32[2,2,128,256]{3,2,1,0:T(8,128)S(1)}, f32[2,2,128,256]{3,2,1,0:T(8,128)S(1)}, u32[]{:S(2)}, u32[]{:S(2)}) %collective-permute-start.8) | collective-permute-done | bytes 524320 | tf_op jit(solution)/shard_map/ppermute | solution.py:252
  64.0 0.0 collective-permute-done.7.first_ref
  64.0 2.5 %collect.1 = f32[1,2,128,2048]{3,2,1,0:T(8,128)} custom-call(s32[2,2]{1,0:T(2,128)S(1)} %copy-done.2, s32[2,2]{1,0:T(2,128)S(1)} %collective-permute-done.first_ref.pos_first_ref, s32[2,2]{1,0:T(2,128)S(1)} %collective-permute-done.1.second_ref.pos_second_ref, f32[2,256,256]{2,1,0:T(8,128)S(1)} %get-tuple-element.15.same_ref, ...), custom_call_target="tpu_custom_call" | custom-call | bytes 4194304 | tf_op jit(solution)/shard_map/collect/pallas_call | solution.py:343
  (6 shorter events, 0.1 us)
Async XLA Ops:
  0.0 9.9 %collective-permute-start.1 = (s32[2,2]{1,0:T(2,128)}, s32[2,2]{1,0:T(2,128)S(1)}, u32[]{:S(2)}, u32[]{:S(2)}) collective-permute-start(s32[2,2]{1,0:T(2,128)} %pos_ref.7), channel_id=1, source_target_pairs={{1,2},{2,1},{3,4},{4,3},{5,6},{6,5},{7,8},{8,7},{9,10},{10,9},{11,... | collective-permute-start | bytes 56 | tf_op jit(solution)/shard_map/ppermute | solution.py:252
  6.4 3.6 %collective-permute-start = (s32[2,2]{1,0:T(2,128)}, s32[2,2]{1,0:T(2,128)S(1)}, u32[]{:S(2)}, u32[]{:S(2)}) collective-permute-start(s32[2,2]{1,0:T(2,128)} %pos_ref.7), channel_id=1, source_target_pairs={{0,1},{1,0},{2,3},{3,2},{4,5},{5,4},{6,7},{7,6},{8,9},{9,8},{10,11... | collective-permute-start | bytes 56 | tf_op jit(solution)/shard_map/ppermute | solution.py:252
  9.9 1.6 %copy-start = (f32[1,2,128,2048]{3,2,1,0:T(8,128)S(1)}, f32[1,2,128,2048]{3,2,1,0:T(8,128)}, u32[]{:S(2)}) copy-start(f32[1,2,128,2048]{3,2,1,0:T(8,128)} %strip_ref.3) | copy-start | bytes 6291460
  11.5 7.5 %copy-start.1 = (f32[1,2,128,2048]{3,2,1,0:T(8,128)S(1)}, f32[1,2,128,2048]{3,2,1,0:T(8,128)}, u32[]{:S(2)}) copy-start(f32[1,2,128,2048]{3,2,1,0:T(8,128)} %strip_ref.3) | copy-start | bytes 6291460
  11.5 7.5 %copy-start.2 = (s32[2,2]{1,0:T(2,128)S(1)}, s32[2,2]{1,0:T(2,128)}, u32[]{:S(2)}) copy-start(s32[2,2]{1,0:T(2,128)} %pos_ref.7) | copy-start | bytes 52
  12.3 23.7 %copy-start.3 = (f32[2,256,256]{2,1,0:T(8,128)S(1)}, f32[2,256,256]{2,1,0:T(8,128)}, u32[]{:S(2)}) copy-start(f32[2,256,256]{2,1,0:T(8,128)} %probe_ref.1) | copy-start | bytes 1572868
  12.3 23.7 %copy-start.4 = (f32[2,256,256]{2,1,0:T(8,128)S(1)}, f32[2,256,256]{2,1,0:T(8,128)}, u32[]{:S(2)}) copy-start(f32[2,256,256]{2,1,0:T(8,128)} %intensity_ref.1) | copy-start | bytes 1572868
  12.3 23.7 %copy-start.5 = (bf16[6,256,256]{2,1,0:T(8,128)(2,1)S(1)}, bf16[6,256,256]{2,1,0:T(8,128)(2,1)}, u32[]{:S(2)}) copy-start(bf16[6,256,256]{2,1,0:T(8,128)(2,1)} %constant.5.clone.prop_ref) | copy-start | bytes 2359300
  12.4 23.7 %copy-start.6 = (bf16[6,256,256]{2,1,0:T(8,128)(2,1)S(1)}, bf16[6,256,256]{2,1,0:T(8,128)(2,1)}, u32[]{:S(2)}) copy-start(bf16[6,256,256]{2,1,0:T(8,128)(2,1)} %constant.4.clone.dft_ref) | copy-start | bytes 2359300
  12.4 19.0 %collective-permute-start.4 = (f32[2,2,128,256]{3,2,1,0:T(8,128)S(1)}, f32[2,2,128,256]{3,2,1,0:T(8,128)S(1)}, u32[]{:S(2)}, u32[]{:S(2)}) collective-permute-start(f32[2,2,128,256]{3,2,1,0:T(8,128)S(1)} %get-tuple-element.14), channel_id=1, source_target_pairs={{1,2},{2,1},{3,4},{4,3},{5,6},{6,5},{7,8},{8,7},{9,10},{10,9},{11,... | collective-permute-start | bytes 1572872 | tf_op jit(solution)/shard_map/ppermute | solution.py:252
  18.9 12.5 %collective-permute-start.3 = (f32[2,2,128,256]{3,2,1,0:T(8,128)S(1)}, f32[2,2,128,256]{3,2,1,0:T(8,128)S(1)}, u32[]{:S(2)}, u32[]{:S(2)}) collective-permute-start(f32[2,2,128,256]{3,2,1,0:T(8,128)S(1)} %get-tuple-element.11.after_ref), channel_id=1, source_target_pairs={{0,1},{1,0},{2,3},{3,2},{4,5},{5,4},{6,7},{7,6},{8,9},{9,8},{10,11... | collective-permute-start | bytes 1572872 | tf_op jit(solution)/shard_map/ppermute | solution.py:252
  19.7 15.8 %collective-permute-start.2 = (f32[2,128,256]{2,1,0:T(8,128)S(1)}, f32[2,128,256]{2,1,0:T(8,128)S(1)}, u32[]{:S(2)}, u32[]{:S(2)}) collective-permute-start(f32[2,128,256]{2,1,0:T(8,128)S(1)} %get-tuple-element.13), channel_id=1, source_target_pairs={{0,128},{128,0},{1,129},{129,1},{2,130},{130,2},{3,131},{131,3},{4... | collective-permute-start | bytes 786440 | tf_op jit(solution)/shard_map/ppermute | solution.py:261
  32.0 4.0 %collective-permute-start.5 = (f32[2,128,256]{2,1,0:T(8,128)S(1)}, f32[2,128,256]{2,1,0:T(8,128)S(1)}, u32[]{:S(2)}, u32[]{:S(2)}) collective-permute-start(f32[2,128,256]{2,1,0:T(8,128)S(1)} %merge.1), channel_id=1, source_target_pairs={{0,128},{128,0},{1,129},{129,1},{2,130},{130,2},{3,131},{131,3},{4... | collective-permute-start | bytes 786440 | tf_op jit(solution)/shard_map/ppermute | solution.py:261
  36.7 6.8 %collective-permute-start.6 = (f32[2,256,256]{2,1,0:T(8,128)S(1)}, f32[2,256,256]{2,1,0:T(8,128)S(1)}, u32[]{:S(2)}, u32[]{:S(2)}) collective-permute-start(f32[2,256,256]{2,1,0:T(8,128)S(1)} %get-tuple-element.16), channel_id=1, source_target_pairs={{0,128},{128,0},{1,129},{129,1},{2,130},{130,2},{3,131},{131,3},{4... | collective-permute-start | bytes 1572872 | tf_op jit(solution)/shard_map/ppermute | solution.py:261
  43.6 20.5 %collective-permute-start.8 = (f32[2,2,128,256]{3,2,1,0:T(8,128)S(1)}, f32[2,2,128,256]{3,2,1,0:T(8,128)S(1)}, u32[]{:S(2)}, u32[]{:S(2)}) collective-permute-start(f32[2,2,128,256]{3,2,1,0:T(8,128)S(1)} %pack.1), channel_id=1, source_target_pairs={{1,2},{2,1},{3,4},{4,3},{5,6},{6,5},{7,8},{8,7},{9,10},{10,9},{11,... | collective-permute-start | bytes 1572872 | tf_op jit(solution)/shard_map/ppermute | solution.py:252
  50.0 14.1 %collective-permute-start.7 = (f32[2,2,128,256]{3,2,1,0:T(8,128)S(1)}, f32[2,2,128,256]{3,2,1,0:T(8,128)S(1)}, u32[]{:S(2)}, u32[]{:S(2)}) collective-permute-start(f32[2,2,128,256]{3,2,1,0:T(8,128)S(1)} %pack.1), channel_id=1, source_target_pairs={{0,1},{1,0},{2,3},{3,2},{4,5},{5,4},{6,7},{7,6},{8,9},{9,8},{10,11... | collective-permute-start | bytes 1572872 | tf_op jit(solution)/shard_map/ppermute | solution.py:252

commit v2 on v0

v2 whole, which is shorter than its diff:
```python
import numpy as np
import ml_dtypes

import jax
import jax.numpy as jnp
from jax import lax
from jax.experimental import pallas as pl
from jax.experimental.pallas import tpu as pltpu
from jax.sharding import PartitionSpec as P

WIN = 256
HALF = 128


def split_tables(real_part, imag_part):
    parts = []
    for values in (real_part, imag_part - real_part, real_part + imag_part):
        high = values.astype(ml_dtypes.bfloat16)
        low = (values - high.astype(np.float64)).astype(ml_dtypes.bfloat16)
        parts += [high, low]
    return np.stack(parts)


def build_tables():
    index = np.arange(WIN)
    turned = 2.0 * np.pi * ((index[:, None] * index[None, :]) % WIN) / WIN
    dft = (np.cos(turned) - 1j * np.sin(turned)) / np.sqrt(WIN)
    centred = (index + WIN // 2) % WIN - WIN // 2
    phase = np.pi * (centred * centred % (4 * WIN)) / (2 * WIN)
    prop = np.conj(dft) @ ((np.cos(phase) - 1j * np.sin(phase))[:, None] * dft)
    prop = 0.5 * (prop + prop.T)
    return split_tables(dft.real, dft.imag), split_tables(prop.real, prop.imag)


def split(value):
    high = value.astype(jnp.bfloat16)
    low = (value - high.astype(jnp.float32)).astype(jnp.bfloat16)
    return high, low


def dot(left, right):
    return jnp.dot(left, right, preferred_element_type=jnp.float32)


def product(field, table, which, from_left):
    high, low = split(field)
    table_high = table[2 * which]
    table_low = table[2 * which + 1]
    if from_left:
        return dot(table_high, high) + (dot(table_high, low) + dot(table_low, high))
    return dot(high, table_high) + (dot(low, table_high) + dot(high, table_low))


def complex_product(real, imag, table, conjugate, from_left):
    shared = product(real + imag, table, 0, from_left)
    if conjugate:
        first = product(real, table, 2, from_left)
        second = product(imag, table, 1, from_left)
        return shared + second, shared - first
    first = product(real, table, 1, from_left)
    second = product(imag, table, 2, from_left)
    return shared - second, shared + first


def sandwich(real, imag, table, conjugate):
    real, imag = complex_product(real, imag, table, conjugate, False)
    return complex_product(real, imag, table, conjugate, True)


def block(number):
    return pl.ds(pl.multiple_of(number * HALF, HALF), HALF)


def cut_piece(strip_ref, column, out_ref):
    first = lax.shift_right_logical(column, 7)
    offset = jnp.bitwise_and(column, HALF - 1)
    lanes = lax.broadcasted_iota(jnp.int32, (HALF, HALF), 1)
    mine = lanes >= offset
    third = jnp.minimum(first + 2, strip_ref.shape[-1] // HALF - 1)
    for part in range(2):
        out_ref[part, :, 0:HALF] = jnp.where(
            mine, strip_ref[0, part, :, block(first)], strip_ref[0, part, :, block(third)]
        )
        out_ref[part, :, HALF:WIN] = strip_ref[0, part, :, block(first + 1)]


def cut_kernel(
    below_ref, above_ref, own_ref, other_ref, up_zero_ref, down_zero_ref, up_one_ref, down_one_ref
):
    @pl.when(lax.axis_index("cuts") == 1)
    def _():
        for slot in range(2):
            cut_piece(other_ref, above_ref[slot, 1], up_zero_ref.at[slot])
            cut_piece(other_ref, below_ref[slot, 1], down_zero_ref.at[slot])
        for slot in range(2):
            cut_piece(own_ref, above_ref[slot, 1], up_one_ref.at[slot])
            cut_piece(own_ref, below_ref[slot, 1], down_one_ref.at[slot])


def slot_kernel(
    pos_ref,
    counts_ref,
    probe_ref,
    dft_ref,
    prop_ref,
    own_ref,
    other_ref,
    low_zero_ref,
    high_zero_ref,
    low_one_ref,
    high_one_ref,
    intensity_ref,
    rim_zero_ref,
    rim_one_ref,
    mid_zero_ref,
    mid_one_ref,
    object_ref,
):
    tile = lax.axis_index("tile")
    live_slots = jnp.where(lax.axis_index("cuts") == 0, counts_ref[0], 0)

    @pl.loop(0, live_slots)
    def _(slot):
        shift_rows = pos_ref[slot, 0] - (tile - 1) * HALF
        column = pos_ref[slot, 1]
        shift_cols = jnp.bitwise_and(column, HALF - 1)
        from_low = lax.broadcasted_iota(jnp.int32, (HALF, WIN), 0) >= shift_rows
        for layer, (strip_ref, low_ref, high_ref) in enumerate(
            ((own_ref, low_zero_ref, high_zero_ref), (other_ref, low_one_ref, high_one_ref))
        ):
            for part in range(2):
                object_ref[layer, part, 0:HALF] = jnp.where(
                    from_low, low_ref[slot, part], high_ref[slot, part]
                )
            cut_piece(strip_ref, column, object_ref.at[layer, :, HALF:WIN])

        def rolled(part):
            return pltpu.roll(pltpu.roll(probe_ref[part], shift_rows, 0), shift_cols, 1)

        zero_re, zero_im = rolled(0), rolled(1)
        cell_re, cell_im = object_ref[0, 0], object_ref[0, 1]
        one_re, one_im = sandwich(
            zero_re * cell_re - zero_im * cell_im,
            zero_re * cell_im + zero_im * cell_re,
            prop_ref,
            False,
        )
        cell_re, cell_im = object_ref[1, 0], object_ref[1, 1]
        far_re, far_im = sandwich(
            one_re * cell_re - one_im * cell_im,
            one_re * cell_im + one_im * cell_re,
            dft_ref,
            False,
        )
        residual = far_re * far_re + far_im * far_im - intensity_ref[slot]
        back_re, back_im = sandwich(far_re * residual, far_im * residual, dft_ref, True)
        for part, value in (
            (0, one_re * back_re + one_im * back_im),
            (1, one_re * back_im - one_im * back_re),
        ):
            rim_one_ref[slot, part] = value[0:HALF]
            mid_one_ref[slot, part] = value[HALF:WIN]
        back_re, back_im = sandwich(
            cell_re * back_re + cell_im * back_im,
            cell_re * back_im - cell_im * back_re,
            prop_ref,
            True,
        )
        for part, value in (
            (0, zero_re * back_re + zero_im * back_im),
            (1, zero_re * back_im - zero_im * back_re),
        ):
            rim_zero_ref[slot, part] = value[0:HALF]
            mid_zero_ref[slot, part] = value[HALF:WIN]

    @pl.when(live_slots == 1)
    def _():
        for ref in (rim_zero_ref, rim_one_ref, mid_zero_ref, mid_one_ref):
            ref[1] = jnp.zeros_like(ref[1])


def add_piece(out_ref, piece_ref, column, keep):
    first = lax.shift_right_logical(column, 7)
    offset = jnp.bitwise_and(column, HALF - 1)
    lanes = lax.broadcasted_iota(jnp.int32, (HALF, HALF), 1)
    mine = lanes >= offset
    third = jnp.minimum(first + 2, out_ref.shape[-1] // HALF - 1)
    for part in range(2):
        left = piece_ref[part, :, 0:HALF]
        right = piece_ref[part, :, HALF:WIN]
        if keep is not None:
            left = jnp.where(keep, left, 0.0)
            right = jnp.where(keep, right, 0.0)
        out_ref[0, part, :, block(first)] += jnp.where(mine, left, 0.0)
        out_ref[0, part, :, block(first + 1)] += right
        out_ref[0, part, :, block(third)] += jnp.where(mine, 0.0, left)


def collect_kernel(
    pos_ref,
    below_ref,
    above_ref,
    below_copy_ref,
    above_copy_ref,
    mid_zero_ref,
    up_zero_ref,
    down_zero_ref,
    mid_one_ref,
    up_one_ref,
    down_one_ref,
    out_ref,
):
    core = lax.axis_index("cuts")
    tile = lax.axis_index("tile")
    out_ref[...] = jnp.zeros_like(out_ref)
    rows = lax.broadcasted_iota(jnp.int32, (HALF, HALF), 0)

    def gather(lower_ref, upper_ref, mid_ref, up_ref, down_ref):
        for slot in range(2):
            add_piece(out_ref, mid_ref.at[slot], pos_ref[slot, 1], None)
            keep = rows < lower_ref[slot, 0] - (tile - 2) * HALF
            add_piece(out_ref, up_ref.at[slot], lower_ref[slot, 1], keep)
            keep = rows >= upper_ref[slot, 0] - tile * HALF
            add_piece(out_ref, down_ref.at[slot], upper_ref[slot, 1], keep)

    @pl.when(core == 0)
    def _():
        gather(below_copy_ref, above_copy_ref, mid_zero_ref, up_zero_ref, down_zero_ref)

    @pl.when(core == 1)
    def _():
        gather(below_ref, above_ref, mid_one_ref, up_one_ref, down_one_ref)


SMEM = pl.BlockSpec(memory_space=pltpu.SMEM)
VMEM = pl.BlockSpec(memory_space=pltpu.VMEM)
ANY = pl.BlockSpec(memory_space=pl.ANY)


LIMIT = 12 << 20


def local(object_slices, probe, positions, counts, intensity):
    tiles = lax.axis_size("tile")

    def send(value, source, target, by):
        pairs = []
        for tile in range(tiles):
            if 0 <= tile + by < tiles:
                pairs.append((source * tiles + tile, target * tiles + tile + by))
        return lax.ppermute(value, ("cuts", "tile"), pairs)

    def kernel(body, name, out_shape, in_specs, flops, moved, scratch=(), out_specs=None):
        return pl.pallas_call(
            body,
            out_shape=out_shape,
            in_specs=in_specs,
            out_specs=VMEM if out_specs is None else out_specs,
            scratch_shapes=scratch,
            compiler_params=pltpu.CompilerParams(vmem_limit_bytes=LIMIT),
            cost_estimate=pl.CostEstimate(flops=flops, bytes_accessed=moved, transcendentals=0),
            name=name,
        )

    pieces = jax.ShapeDtypeStruct((2, 2, HALF, WIN), jnp.float32)
    dft, prop = build_tables()
    other_slice = lax.ppermute(object_slices, "cuts", [(0, 1), (1, 0)])
    below = send(positions, 0, 1, 1)
    above = send(positions, 0, 1, -1)
    up_zero, down_zero, up_one, down_one = kernel(
        cut_kernel, "cut", (pieces,) * 4, [SMEM] * 2 + [VMEM] * 2, 0, 4 << 20, (), (VMEM,) * 4
    )(below, above, object_slices, other_slice)
    low_zero = send(up_zero, 1, 0, 1)
    high_zero = send(down_zero, 1, 0, -1)
    low_one = send(up_one, 1, 0, 1)
    high_one = send(down_one, 1, 0, -1)
    below_copy = send(below, 1, 0, 0)
    above_copy = send(above, 1, 0, 0)
    rim_zero, rim_one, mid_zero, mid_one = kernel(
        slot_kernel,
        "slot",
        (pieces,) * 4,
        [SMEM] * 2 + [VMEM] * 10,
        72 * 2 * WIN**3,
        6 << 20,
        (pltpu.VMEM((2, 2, WIN, WIN), jnp.float32),),
        (VMEM,) * 4,
    )(
        positions,
        counts,
        probe,
        jnp.asarray(dft),
        jnp.asarray(prop),
        object_slices,
        other_slice,
        low_zero,
        high_zero,
        low_one,
        high_one,
        intensity,
    )
    back_up_one = send(rim_one, 0, 1, 1)
    back_down_one = send(rim_one, 0, 1, -1)
    back_up_zero = send(rim_zero, 0, 0, 1)
    back_down_zero = send(rim_zero, 0, 0, -1)
    mid_one = send(mid_one, 0, 1, 0)
    return kernel(
        collect_kernel,
        "collect",
        jax.ShapeDtypeStruct(object_slices.shape, jnp.float32),
        [SMEM] * 5 + [VMEM] * 6,
        0,
        4 << 20,
    )(
        positions,
        below,
        above,
        below_copy,
        above_copy,
        mid_zero,
        back_up_zero,
        back_down_zero,
        mid_one,
        back_up_one,
        back_down_one,
    )


def solution(mesh):
    in_specs = (
        P("cuts", None, "tile", None),
        P(),
        P("tile", None),
        P("tile"),
        P("tile", None, None),
    )
    out_specs = P("cuts", None, "tile", None)
    return jax.shard_map(local, mesh=mesh, in_specs=in_specs, out_specs=out_specs, check_vma=False)
```

time: 79.6 us -> 68.2 us (0.86)
  the two profiles are of different devices: /device:TPU:1 before, /device:TPU:128 now
where the time goes in v2:
time: 68.2 us; the launch traced here: 67.5 us
  waiting for transfers between devices  27.8 us (41%)
  starting transfers between devices  27.7 us (41%)
  Pallas kernels  8.41 us (12%)
  local copies, waits for them, and re-layouts  2.74 us (4%)
  between operations  0.85 us (1%)
    ppermute x13, waiting for transfers between devices, send(): return lax.ppermute(value, ('cuts', 'tile'), pairs)  27.8 us
    ppermute x13, starting transfers between devices, send(): return lax.ppermute(value, ('cuts', 'tile'), pairs)  27.7 us
    pallas_call x1, Pallas kernels, local(): kernel(slot_kernel, 'slot', (pieces,) * 4, [SMEM] * 2 + [VMEM] * 10, 72 *...  5.3 us
    unnamed x14, local copies, waits for them, and re-layouts  2.74 us
    pallas_call x1, Pallas kernels, local(): kernel(collect_kernel, 'collect', jax.ShapeDtypeStruct(object_slices.shap...  2.53 us
  transfers between devices with their start and end apart: 14, of which 5 were waited for; matrix products, arithmetic and copies ran while one was open for 0% of the time, Pallas kernels for 8%

profile of v2, /device:TPU:128, one launch (start us, length us, event | category | flops | bytes accessed | tf_op | source)
XLA Modules:
  0.0 67.5 jit_solution(7411487932896896628)
XLA Ops:
  0.0 0.0 collective-permute-start.4
  0.0 3.5 %collective-permute-start = (s32[2,2]{1,0:T(2,128)}, s32[2,2]{1,0:T(2,128)S(1)}, u32[]{:S(2)}, u32[]{:S(2)}) collective-permute-start(s32[2,2]{1,0:T(2,128)} %pos_ref.3), channel_id=1, source_target_pairs={{0,129},{1,130},{2,131},{3,132},{4,133},{5,134},{6,135},{7,136},{8... | collective-permute-start | bytes 56 | tf_op jit(solution)/shard_map/ppermute | solution.py:251
  3.5 4.6 %collective-permute-start.1 = (s32[2,2]{1,0:T(2,128)}, s32[2,2]{1,0:T(2,128)S(1)}, u32[]{:S(2)}, u32[]{:S(2)}) collective-permute-start(s32[2,2]{1,0:T(2,128)} %pos_ref.3), channel_id=1, source_target_pairs={{1,128},{2,129},{3,130},{4,131},{5,132},{6,133},{7,134},{8,135},{9... | collective-permute-start | bytes 56 | tf_op jit(solution)/shard_map/ppermute | solution.py:251
  8.1 0.0 collective-permute-done.below_ref
  8.1 1.5 %collective-permute-done.1.above_ref = s32[2,2]{1,0:T(2,128)S(1)} collective-permute-done((s32[2,2]{1,0:T(2,128)}, s32[2,2]{1,0:T(2,128)S(1)}, u32[]{:S(2)}, u32[]{:S(2)}) %collective-permute-start.1) | collective-permute-done | bytes 48 | tf_op jit(solution)/shard_map/ppermute | solution.py:251
  9.6 0.0 collective-permute-done.4.other_ref
  9.6 1.6 %copy-done = f32[1,2,128,2048]{3,2,1,0:T(8,128)S(1)} copy-done((f32[1,2,128,2048]{3,2,1,0:T(8,128)S(1)}, f32[1,2,128,2048]{3,2,1,0:T(8,128)}, u32[]{:S(2)}) %copy-start) | copy-done | bytes 2097176
  11.2 0.0 copy-start.5
  11.2 0.6 cut.1
  11.8 1.4 %collective-permute-start.5 = (f32[2,2,128,256]{3,2,1,0:T(8,128)S(1)}, f32[2,2,128,256]{3,2,1,0:T(8,128)S(1)}, u32[]{:S(2)}, u32[]{:S(2)}) collective-permute-start(f32[2,2,128,256]{3,2,1,0:T(8,128)S(1)} %get-tuple-element.13), channel_id=1, source_target_pairs={{128,1},{129,2},{130,3},{131,4},{132,5},{133,6},{134,7},{135,8},{1... | collective-permute-start | bytes 1572872 | tf_op jit(solution)/shard_map/ppermute | solution.py:251
  13.2 1.3 %collective-permute-start.6 = (f32[2,2,128,256]{3,2,1,0:T(8,128)S(1)}, f32[2,2,128,256]{3,2,1,0:T(8,128)S(1)}, u32[]{:S(2)}, u32[]{:S(2)}) collective-permute-start(f32[2,2,128,256]{3,2,1,0:T(8,128)S(1)} %get-tuple-element.14), channel_id=1, source_target_pairs={{129,0},{130,1},{131,2},{132,3},{133,4},{134,5},{135,6},{136,7},{1... | collective-permute-start | bytes 1572872 | tf_op jit(solution)/shard_map/ppermute | solution.py:251
  14.5 1.3 %collective-permute-start.7 = (f32[2,2,128,256]{3,2,1,0:T(8,128)S(1)}, f32[2,2,128,256]{3,2,1,0:T(8,128)S(1)}, u32[]{:S(2)}, u32[]{:S(2)}) collective-permute-start(f32[2,2,128,256]{3,2,1,0:T(8,128)S(1)} %get-tuple-element.15), channel_id=1, source_target_pairs={{128,1},{129,2},{130,3},{131,4},{132,5},{133,6},{134,7},{135,8},{1... | collective-permute-start | bytes 1572872 | tf_op jit(solution)/shard_map/ppermute | solution.py:251
  15.8 1.3 %collective-permute-start.8 = (f32[2,2,128,256]{3,2,1,0:T(8,128)S(1)}, f32[2,2,128,256]{3,2,1,0:T(8,128)S(1)}, u32[]{:S(2)}, u32[]{:S(2)}) collective-permute-start(f32[2,2,128,256]{3,2,1,0:T(8,128)S(1)} %get-tuple-element.16), channel_id=1, source_target_pairs={{129,0},{130,1},{131,2},{132,3},{133,4},{134,5},{135,6},{136,7},{1... | collective-permute-start | bytes 1572872 | tf_op jit(solution)/shard_map/ppermute | solution.py:251
  17.7 1.3 %collective-permute-start.2 = (s32[2,2]{1,0:T(2,128)S(1)}, s32[2,2]{1,0:T(2,128)S(1)}, u32[]{:S(2)}, u32[]{:S(2)}) collective-permute-start(s32[2,2]{1,0:T(2,128)S(1)} %collective-permute-done.below_ref), channel_id=1, source_target_pairs={{128,0},{129,1},{130,2},{131,3},{132,4},{133,5},{134,6},{135,7},{1... | collective-permute-start | bytes 56 | tf_op jit(solution)/shard_map/ppermute | solution.py:251
  19.0 8.8 %collective-permute-done.5.low_zero_ref = f32[2,2,128,256]{3,2,1,0:T(8,128)S(1)} collective-permute-done((f32[2,2,128,256]{3,2,1,0:T(8,128)S(1)}, f32[2,2,128,256]{3,2,1,0:T(8,128)S(1)}, u32[]{:S(2)}, u32[]{:S(2)}) %collective-permute-start.5) | collective-permute-done | bytes 524320 | tf_op jit(solution)/shard_map/ppermute | solution.py:251
  27.8 1.3 %collective-permute-start.3 = (s32[2,2]{1,0:T(2,128)S(1)}, s32[2,2]{1,0:T(2,128)S(1)}, u32[]{:S(2)}, u32[]{:S(2)}) collective-permute-start(s32[2,2]{1,0:T(2,128)S(1)} %collective-permute-done.1.above_ref), channel_id=1, source_target_pairs={{128,0},{129,1},{130,2},{131,3},{132,4},{133,5},{134,6},{135,7},{1... | collective-permute-start | bytes 56 | tf_op jit(solution)/shard_map/ppermute | solution.py:251
  29.1 0.0 collective-permute-done.6.high_zero_ref
  29.1 4.3 %collective-permute-done.7.low_one_ref = f32[2,2,128,256]{3,2,1,0:T(8,128)S(1)} collective-permute-done((f32[2,2,128,256]{3,2,1,0:T(8,128)S(1)}, f32[2,2,128,256]{3,2,1,0:T(8,128)S(1)}, u32[]{:S(2)}, u32[]{:S(2)}) %collective-permute-start.7) | collective-permute-done | bytes 524320 | tf_op jit(solution)/shard_map/ppermute | solution.py:251
  33.5 0.0 copy-start.6
  33.5 1.1 %copy-done.6 = bf16[6,256,256]{2,1,0:T(8,128)(2,1)S(1)} copy-done((bf16[6,256,256]{2,1,0:T(8,128)(2,1)S(1)}, bf16[6,256,256]{2,1,0:T(8,128)(2,1)}, u32[]{:S(2)}) %copy-start.6) | copy-done | bytes 786456
  34.6 5.3 %slot.1 = (f32[2,2,128,256]{3,2,1,0:T(8,128)S(1)}, f32[2,2,128,256]{3,2,1,0:T(8,128)S(1)}, f32[2,2,128,256]{3,2,1,0:T(8,128)S(1)}, f32[2,2,128,256]{3,2,1,0:T(8,128)S(1)}) custom-call(s32[2,2]{1,0:T(2,128)S(1)} %copy-done.2, s32[1]{0:T(128)S(6)} %copy.8.counts_ref, f32[2,256,256]{2,1,0:T(8,128)S(1)} %copy-done.3, bf16[6,256,256]{2,1,0:T(8,128)(2,1)S(1)} %copy-done.5, ...), custom_call_target="tpu_custom_call" | custom-call | flops 2415919104 | bytes 6291456 | tf_op jit(solution)/shard_map/slot/pallas_call | solution.py:279
  39.9 1.3 %collective-permute-start.12 = (f32[2,2,128,256]{3,2,1,0:T(8,128)S(1)}, f32[2,2,128,256]{3,2,1,0:T(8,128)S(1)}, u32[]{:S(2)}, u32[]{:S(2)}) collective-permute-start(f32[2,2,128,256]{3,2,1,0:T(8,128)S(1)} %get-tuple-element.20), channel_id=1, source_target_pairs={{0,129},{1,130},{2,131},{3,132},{4,133},{5,134},{6,135},{7,136},{8... | collective-permute-start | bytes 1572872 | tf_op jit(solution)/shard_map/ppermute | solution.py:251
  41.3 1.3 %collective-permute-start.13 = (f32[2,2,128,256]{3,2,1,0:T(8,128)S(1)}, f32[2,2,128,256]{3,2,1,0:T(8,128)S(1)}, u32[]{:S(2)}, u32[]{:S(2)}) collective-permute-start(f32[2,2,128,256]{3,2,1,0:T(8,128)S(1)} %get-tuple-element.20), channel_id=1, source_target_pairs={{1,128},{2,129},{3,130},{4,131},{5,132},{6,133},{7,134},{8,135},{9... | collective-permute-start | bytes 1572872 | tf_op jit(solution)/shard_map/ppermute | solution.py:251
  42.6 5.9 %collective-permute-start.10 = (f32[2,2,128,256]{3,2,1,0:T(8,128)S(1)}, f32[2,2,128,256]{3,2,1,0:T(8,128)S(1)}, u32[]{:S(2)}, u32[]{:S(2)}) collective-permute-start(f32[2,2,128,256]{3,2,1,0:T(8,128)S(1)} %get-tuple-element.18), channel_id=1, source_target_pairs={{1,0},{2,1},{3,2},{4,3},{5,4},{6,5},{7,6},{8,7},{9,8},{10,9},{11,1... | collective-permute-start | bytes 1572872 | tf_op jit(solution)/shard_map/ppermute | solution.py:251
  48.5 0.0 collective-permute-done.2.below_copy_ref
  48.5 1.9 %collective-permute-start.9 = (f32[2,2,128,256]{3,2,1,0:T(8,128)S(1)}, f32[2,2,128,256]{3,2,1,0:T(8,128)S(1)}, u32[]{:S(2)}, u32[]{:S(2)}) collective-permute-start(f32[2,2,128,256]{3,2,1,0:T(8,128)S(1)} %get-tuple-element.18), channel_id=1, source_target_pairs={{0,1},{1,2},{2,3},{3,4},{4,5},{5,6},{6,7},{7,8},{8,9},{9,10},{10,1... | collective-permute-start | bytes 1572872 | tf_op jit(solution)/shard_map/ppermute | solution.py:251
  50.4 0.0 collective-permute-done.3.above_copy_ref
  50.4 1.3 %collective-permute-start.11 = (f32[2,2,128,256]{3,2,1,0:T(8,128)S(1)}, f32[2,2,128,256]{3,2,1,0:T(8,128)S(1)}, u32[]{:S(2)}, u32[]{:S(2)}) collective-permute-start(f32[2,2,128,256]{3,2,1,0:T(8,128)S(1)} %get-tuple-element.19), channel_id=1, source_target_pairs={{0,128},{1,129},{2,130},{3,131},{4,132},{5,133},{6,134},{7,135},{8... | collective-permute-start | bytes 1572872 | tf_op jit(solution)/shard_map/ppermute | solution.py:251
  51.8 3.4 %collective-permute-done.10.down_zero_ref = f32[2,2,128,256]{3,2,1,0:T(8,128)S(1)} collective-permute-done((f32[2,2,128,256]{3,2,1,0:T(8,128)S(1)}, f32[2,2,128,256]{3,2,1,0:T(8,128)S(1)}, u32[]{:S(2)}, u32[]{:S(2)}) %collective-permute-start.10) | collective-permute-done | bytes 524320 | tf_op jit(solution)/shard_map/ppermute | solution.py:251
  55.2 9.8 %collective-permute-done.9.up_zero_ref = f32[2,2,128,256]{3,2,1,0:T(8,128)S(1)} collective-permute-done((f32[2,2,128,256]{3,2,1,0:T(8,128)S(1)}, f32[2,2,128,256]{3,2,1,0:T(8,128)S(1)}, u32[]{:S(2)}, u32[]{:S(2)}) %collective-permute-start.9) | collective-permute-done | bytes 524320 | tf_op jit(solution)/shard_map/ppermute | solution.py:251
  65.0 0.0 collective-permute-done.11.mid_one_ref
  65.0 2.5 %collect.1 = f32[1,2,128,2048]{3,2,1,0:T(8,128)} custom-call(s32[2,2]{1,0:T(2,128)S(1)} %copy-done.2, s32[2,2]{1,0:T(2,128)S(1)} %collective-permute-done.below_ref, s32[2,2]{1,0:T(2,128)S(1)} %collective-permute-done.1.above_ref, s32[2,2]{1,0:T(2,128)S(1)} %collective-permute-done.2.below_copy_ref, s32[2,2]{1,0:T(2,128)S(1)} %collective-permute-done.3.above_copy_ref, ...), custom_call_target="tpu_custom_call" | custom-call | bytes 4194304 | tf_op jit(solution)/shard_map/collect/pallas_call | solution.py:307
  (13 shorter events, 0.0 us)
Async XLA Ops:
  0.0 9.6 %collective-permute-start.4 = (f32[1,2,128,2048]{3,2,1,0:T(8,128)}, f32[1,2,128,2048]{3,2,1,0:T(8,128)S(1)}, u32[]{:S(2)}, u32[]{:S(2)}) collective-permute-start(f32[1,2,128,2048]{3,2,1,0:T(8,128)} %own_ref.3), channel_id=1, source_target_pairs={{0,128},{128,0},{1,129},{129,1},{2,130},{130,2},{3,131},{131,3},{4... | collective-permute-start | bytes 6291464 | tf_op jit(solution)/shard_map/ppermute | solution.py:267
  0.0 8.1 %collective-permute-start = (s32[2,2]{1,0:T(2,128)}, s32[2,2]{1,0:T(2,128)S(1)}, u32[]{:S(2)}, u32[]{:S(2)}) collective-permute-start(s32[2,2]{1,0:T(2,128)} %pos_ref.3), channel_id=1, source_target_pairs={{0,129},{1,130},{2,131},{3,132},{4,133},{5,134},{6,135},{7,136},{8... | collective-permute-start | bytes 56 | tf_op jit(solution)/shard_map/ppermute | solution.py:251
  3.5 6.1 %collective-permute-start.1 = (s32[2,2]{1,0:T(2,128)}, s32[2,2]{1,0:T(2,128)S(1)}, u32[]{:S(2)}, u32[]{:S(2)}) collective-permute-start(s32[2,2]{1,0:T(2,128)} %pos_ref.3), channel_id=1, source_target_pairs={{1,128},{2,129},{3,130},{4,131},{5,132},{6,133},{7,134},{8,135},{9... | collective-permute-start | bytes 56 | tf_op jit(solution)/shard_map/ppermute | solution.py:251
  9.6 1.6 %copy-start = (f32[1,2,128,2048]{3,2,1,0:T(8,128)S(1)}, f32[1,2,128,2048]{3,2,1,0:T(8,128)}, u32[]{:S(2)}) copy-start(f32[1,2,128,2048]{3,2,1,0:T(8,128)} %own_ref.3) | copy-start | bytes 6291460
  11.2 22.3 %copy-start.1 = (f32[1,2,128,2048]{3,2,1,0:T(8,128)S(1)}, f32[1,2,128,2048]{3,2,1,0:T(8,128)}, u32[]{:S(2)}) copy-start(f32[1,2,128,2048]{3,2,1,0:T(8,128)} %own_ref.3) | copy-start | bytes 6291460
  11.2 22.3 %copy-start.2 = (s32[2,2]{1,0:T(2,128)S(1)}, s32[2,2]{1,0:T(2,128)}, u32[]{:S(2)}) copy-start(s32[2,2]{1,0:T(2,128)} %pos_ref.3) | copy-start | bytes 52
  11.2 22.3 %copy-start.3 = (f32[2,256,256]{2,1,0:T(8,128)S(1)}, f32[2,256,256]{2,1,0:T(8,128)}, u32[]{:S(2)}) copy-start(f32[2,256,256]{2,1,0:T(8,128)} %probe_ref.1) | copy-start | bytes 1572868
  11.2 22.3 %copy-start.4 = (f32[2,256,256]{2,1,0:T(8,128)S(1)}, f32[2,256,256]{2,1,0:T(8,128)}, u32[]{:S(2)}) copy-start(f32[2,256,256]{2,1,0:T(8,128)} %intensity_ref.1) | copy-start | bytes 1572868
  11.2 22.3 %copy-start.5 = (bf16[6,256,256]{2,1,0:T(8,128)(2,1)S(1)}, bf16[6,256,256]{2,1,0:T(8,128)(2,1)}, u32[]{:S(2)}) copy-start(bf16[6,256,256]{2,1,0:T(8,128)(2,1)} %constant.4.clone.dft_ref) | copy-start | bytes 2359300
  11.8 16.1 %collective-permute-start.5 = (f32[2,2,128,256]{3,2,1,0:T(8,128)S(1)}, f32[2,2,128,256]{3,2,1,0:T(8,128)S(1)}, u32[]{:S(2)}, u32[]{:S(2)}) collective-permute-start(f32[2,2,128,256]{3,2,1,0:T(8,128)S(1)} %get-tuple-element.13), channel_id=1, source_target_pairs={{128,1},{129,2},{130,3},{131,4},{132,5},{133,6},{134,7},{135,8},{1... | collective-permute-start | bytes 1572872 | tf_op jit(solution)/shard_map/ppermute | solution.py:251
  13.2 15.9 %collective-permute-start.6 = (f32[2,2,128,256]{3,2,1,0:T(8,128)S(1)}, f32[2,2,128,256]{3,2,1,0:T(8,128)S(1)}, u32[]{:S(2)}, u32[]{:S(2)}) collective-permute-start(f32[2,2,128,256]{3,2,1,0:T(8,128)S(1)} %get-tuple-element.14), channel_id=1, source_target_pairs={{129,0},{130,1},{131,2},{132,3},{133,4},{134,5},{135,6},{136,7},{1... | collective-permute-start | bytes 1572872 | tf_op jit(solution)/shard_map/ppermute | solution.py:251
  14.5 18.9 %collective-permute-start.7 = (f32[2,2,128,256]{3,2,1,0:T(8,128)S(1)}, f32[2,2,128,256]{3,2,1,0:T(8,128)S(1)}, u32[]{:S(2)}, u32[]{:S(2)}) collective-permute-start(f32[2,2,128,256]{3,2,1,0:T(8,128)S(1)} %get-tuple-element.15), channel_id=1, source_target_pairs={{128,1},{129,2},{130,3},{131,4},{132,5},{133,6},{134,7},{135,8},{1... | collective-permute-start | bytes 1572872 | tf_op jit(solution)/shard_map/ppermute | solution.py:251
  15.8 17.7 %collective-permute-start.8 = (f32[2,2,128,256]{3,2,1,0:T(8,128)S(1)}, f32[2,2,128,256]{3,2,1,0:T(8,128)S(1)}, u32[]{:S(2)}, u32[]{:S(2)}) collective-permute-start(f32[2,2,128,256]{3,2,1,0:T(8,128)S(1)} %get-tuple-element.16), channel_id=1, source_target_pairs={{129,0},{130,1},{131,2},{132,3},{133,4},{134,5},{135,6},{136,7},{1... | collective-permute-start | bytes 1572872 | tf_op jit(solution)/shard_map/ppermute | solution.py:251
  17.7 30.8 %collective-permute-start.2 = (s32[2,2]{1,0:T(2,128)S(1)}, s32[2,2]{1,0:T(2,128)S(1)}, u32[]{:S(2)}, u32[]{:S(2)}) collective-permute-start(s32[2,2]{1,0:T(2,128)S(1)} %collective-permute-done.below_ref), channel_id=1, source_target_pairs={{128,0},{129,1},{130,2},{131,3},{132,4},{133,5},{134,6},{135,7},{1... | collective-permute-start | bytes 56 | tf_op jit(solution)/shard_map/ppermute | solution.py:251
  27.8 22.6 %collective-permute-start.3 = (s32[2,2]{1,0:T(2,128)S(1)}, s32[2,2]{1,0:T(2,128)S(1)}, u32[]{:S(2)}, u32[]{:S(2)}) collective-permute-start(s32[2,2]{1,0:T(2,128)S(1)} %collective-permute-done.1.above_ref), channel_id=1, source_target_pairs={{128,0},{129,1},{130,2},{131,3},{132,4},{133,5},{134,6},{135,7},{1... | collective-permute-start | bytes 56 | tf_op jit(solution)/shard_map/ppermute | solution.py:251
  33.5 1.1 %copy-start.6 = (bf16[6,256,256]{2,1,0:T(8,128)(2,1)S(1)}, bf16[6,256,256]{2,1,0:T(8,128)(2,1)}, u32[]{:S(2)}) copy-start(bf16[6,256,256]{2,1,0:T(8,128)(2,1)} %constant.5.clone.prop_ref) | copy-start | bytes 2359300
  39.9 15.2 %collective-permute-start.12 = (f32[2,2,128,256]{3,2,1,0:T(8,128)S(1)}, f32[2,2,128,256]{3,2,1,0:T(8,128)S(1)}, u32[]{:S(2)}, u32[]{:S(2)}) collective-permute-start(f32[2,2,128,256]{3,2,1,0:T(8,128)S(1)} %get-tuple-element.20), channel_id=1, source_target_pairs={{0,129},{1,130},{2,131},{3,132},{4,133},{5,134},{6,135},{7,136},{8... | collective-permute-start | bytes 1572872 | tf_op jit(solution)/shard_map/ppermute | solution.py:251
  41.3 13.9 %collective-permute-start.13 = (f32[2,2,128,256]{3,2,1,0:T(8,128)S(1)}, f32[2,2,128,256]{3,2,1,0:T(8,128)S(1)}, u32[]{:S(2)}, u32[]{:S(2)}) collective-permute-start(f32[2,2,128,256]{3,2,1,0:T(8,128)S(1)} %get-tuple-element.20), channel_id=1, source_target_pairs={{1,128},{2,129},{3,130},{4,131},{5,132},{6,133},{7,134},{8,135},{9... | collective-permute-start | bytes 1572872 | tf_op jit(solution)/shard_map/ppermute | solution.py:251
  42.6 12.6 %collective-permute-start.10 = (f32[2,2,128,256]{3,2,1,0:T(8,128)S(1)}, f32[2,2,128,256]{3,2,1,0:T(8,128)S(1)}, u32[]{:S(2)}, u32[]{:S(2)}) collective-permute-start(f32[2,2,128,256]{3,2,1,0:T(8,128)S(1)} %get-tuple-element.18), channel_id=1, source_target_pairs={{1,0},{2,1},{3,2},{4,3},{5,4},{6,5},{7,6},{8,7},{9,8},{10,9},{11,1... | collective-permute-start | bytes 1572872 | tf_op jit(solution)/shard_map/ppermute | solution.py:251
  48.5 16.5 %collective-permute-start.9 = (f32[2,2,128,256]{3,2,1,0:T(8,128)S(1)}, f32[2,2,128,256]{3,2,1,0:T(8,128)S(1)}, u32[]{:S(2)}, u32[]{:S(2)}) collective-permute-start(f32[2,2,128,256]{3,2,1,0:T(8,128)S(1)} %get-tuple-element.18), channel_id=1, source_target_pairs={{0,1},{1,2},{2,3},{3,4},{4,5},{5,6},{6,7},{7,8},{8,9},{9,10},{10,1... | collective-permute-start | bytes 1572872 | tf_op jit(solution)/shard_map/ppermute | solution.py:251
  50.4 14.6 %collective-permute-start.11 = (f32[2,2,128,256]{3,2,1,0:T(8,128)S(1)}, f32[2,2,128,256]{3,2,1,0:T(8,128)S(1)}, u32[]{:S(2)}, u32[]{:S(2)}) collective-permute-start(f32[2,2,128,256]{3,2,1,0:T(8,128)S(1)} %get-tuple-element.19), channel_id=1, source_target_pairs={{0,128},{1,129},{2,130},{3,131},{4,132},{5,133},{6,134},{7,135},{8... | collective-permute-start | bytes 1572872 | tf_op jit(solution)/shard_map/ppermute | solution.py:251

commit v3 on v2

--- a/solution.py
+++ b/solution.py
@@ -84,68 +84,93 @@
         out_ref[part, :, HALF:WIN] = strip_ref[0, part, :, block(first + 1)]
 
 
+def stage_kernel(strip_ref, out_ref, sem):
+    copy = pltpu.make_async_copy(strip_ref, out_ref, sem)
+    copy.start()
+    copy.wait()
+
+
+def is_odd():
+    return jnp.bitwise_and(lax.axis_index("tile"), 1)
+
+
 def cut_kernel(
-    below_ref, above_ref, own_ref, other_ref, up_zero_ref, down_zero_ref, up_one_ref, down_one_ref
+    first_ref, second_ref, own_ref, other_ref, up_zero_ref, down_zero_ref, up_one_ref, down_one_ref
 ):
     @pl.when(lax.axis_index("cuts") == 1)
     def _():
-        for slot in range(2):
-            cut_piece(other_ref, above_ref[slot, 1], up_zero_ref.at[slot])
-            cut_piece(other_ref, below_ref[slot, 1], down_zero_ref.at[slot])
-        for slot in range(2):
-            cut_piece(own_ref, above_ref[slot, 1], up_one_ref.at[slot])
-            cut_piece(own_ref, below_ref[slot, 1], down_one_ref.at[slot])
+        odd = is_odd() == 1
+        for strip_ref, up_ref, down_ref in (
+            (other_ref, up_zero_ref, down_zero_ref),
+            (own_ref, up_one_ref, down_one_ref),
+        ):
+            for slot in range(2):
+                first, second = first_ref[slot, 1], second_ref[slot, 1]
+                cut_piece(strip_ref, jnp.where(odd, second, first), up_ref.at[slot])
+                cut_piece(strip_ref, jnp.where(odd, first, second), down_ref.at[slot])
+
+
+def slots_of_core(counts_ref):
+    return jnp.where(lax.axis_index("cuts") == 0, counts_ref[0], 0)
+
+
+def fill_window(pos_ref, slot, strip_ref, low_ref, high_ref, window_ref):
+    shift_rows = pos_ref[slot, 0] - (lax.axis_index("tile") - 1) * HALF
+    column = pos_ref[slot, 1]
+    from_low = lax.broadcasted_iota(jnp.int32, (HALF, WIN), 0) >= shift_rows
+    for part in range(2):
+        window_ref[part, 0:HALF] = jnp.where(from_low, low_ref[slot, part], high_ref[slot, part])
+    cut_piece(strip_ref, column, window_ref.at[:, HALF:WIN])
+    return shift_rows, jnp.bitwise_and(column, HALF - 1)
+
+
+def enter_kernel(
+    pos_ref, counts_ref, probe_ref, table_ref, own_ref, low_ref, high_ref, wave_ref, window_ref
+):
+    @pl.loop(0, slots_of_core(counts_ref))
+    def _(slot):
+        shift_rows, shift_cols = fill_window(pos_ref, slot, own_ref, low_ref, high_ref, window_ref)
+
+        def rolled(part):
+            return pltpu.roll(pltpu.roll(probe_ref[part], shift_rows, 0), shift_cols, 1)
+
+        zero_re, zero_im = rolled(0), rolled(1)
+        wave_ref[slot, 0, 0] = zero_re
+        wave_ref[slot, 0, 1] = zero_im
+        cell_re, cell_im = window_ref[0], window_ref[1]
+        one_re, one_im = sandwich(
+            zero_re * cell_re - zero_im * cell_im,
+            zero_re * cell_im + zero_im * cell_re,
+            table_ref.at[1],
+            False,
+        )
+        wave_ref[slot, 1, 0] = one_re
+        wave_ref[slot, 1, 1] = one_im
 
 
 def slot_kernel(
     pos_ref,
     counts_ref,
-    probe_ref,
-    dft_ref,
-    prop_ref,
-    own_ref,
+    table_ref,
+    wave_ref,
     other_ref,
-    low_zero_ref,
-    high_zero_ref,
-    low_one_ref,
-    high_one_ref,
+    low_ref,
+    high_ref,
     intensity_ref,
     rim_zero_ref,
     rim_one_ref,
     mid_zero_ref,
     mid_one_ref,
-    object_ref,
+    window_ref,
 ):
-    tile = lax.axis_index("tile")
-    live_slots = jnp.where(lax.axis_index("cuts") == 0, counts_ref[0], 0)
+    live_slots = slots_of_core(counts_ref)
+    dft_ref, prop_ref = table_ref.at[0], table_ref.at[1]
 
     @pl.loop(0, live_slots)
     def _(slot):
-        shift_rows = pos_ref[slot, 0] - (tile - 1) * HALF
-        column = pos_ref[slot, 1]
-        shift_cols = jnp.bitwise_and(column, HALF - 1)
-        from_low = lax.broadcasted_iota(jnp.int32, (HALF, WIN), 0) >= shift_rows
-        for layer, (strip_ref, low_ref, high_ref) in enumerate(
-            ((own_ref, low_zero_ref, high_zero_ref), (other_ref, low_one_ref, high_one_ref))
-        ):
-            for part in range(2):
-                object_ref[layer, part, 0:HALF] = jnp.where(
-                    from_low, low_ref[slot, part], high_ref[slot, part]
-                )
-            cut_piece(strip_ref, column, object_ref.at[layer, :, HALF:WIN])
-
-        def rolled(part):
-            return pltpu.roll(pltpu.roll(probe_ref[part], shift_rows, 0), shift_cols, 1)
-
-        zero_re, zero_im = rolled(0), rolled(1)
-        cell_re, cell_im = object_ref[0, 0], object_ref[0, 1]
-        one_re, one_im = sandwich(
-            zero_re * cell_re - zero_im * cell_im,
-            zero_re * cell_im + zero_im * cell_re,
-            prop_ref,
-            False,
-        )
-        cell_re, cell_im = object_ref[1, 0], object_ref[1, 1]
+        fill_window(pos_ref, slot, other_ref, low_ref, high_ref, window_ref)
+        cell_re, cell_im = window_ref[0], window_ref[1]
+        one_re, one_im = wave_ref[slot, 1, 0], wave_ref[slot, 1, 1]
         far_re, far_im = sandwich(
             one_re * cell_re - one_im * cell_im,
             one_re * cell_im + one_im * cell_re,
@@ -166,6 +191,7 @@
             prop_ref,
             True,
         )
+        zero_re, zero_im = wave_ref[slot, 0, 0], wave_ref[slot, 0, 1]
         for part, value in (
             (0, zero_re * back_re + zero_im * back_im),
             (1, zero_re * back_im - zero_im * back_re),
@@ -198,13 +224,13 @@
 
 def collect_kernel(
     pos_ref,
-    below_ref,
-    above_ref,
-    below_copy_ref,
-    above_copy_ref,
+    first_ref,
+    second_ref,
+    first_copy_ref,
+    second_copy_ref,
     mid_zero_ref,
-    up_zero_ref,
-    down_zero_ref,
+    first_zero_ref,
+    second_zero_ref,
     mid_one_ref,
     up_one_ref,
     down_one_ref,
@@ -212,24 +238,34 @@
 ):
     core = lax.axis_index("cuts")
     tile = lax.axis_index("tile")
+    odd = is_odd()
     out_ref[...] = jnp.zeros_like(out_ref)
     rows = lax.broadcasted_iota(jnp.int32, (HALF, HALF), 0)
 
-    def gather(lower_ref, upper_ref, mid_ref, up_ref, down_ref):
-        for slot in range(2):
-            add_piece(out_ref, mid_ref.at[slot], pos_ref[slot, 1], None)
-            keep = rows < lower_ref[slot, 0] - (tile - 2) * HALF
-            add_piece(out_ref, up_ref.at[slot], lower_ref[slot, 1], keep)
-            keep = rows >= upper_ref[slot, 0] - tile * HALF
-            add_piece(out_ref, down_ref.at[slot], upper_ref[slot, 1], keep)
+    def add(piece_ref, slot, row, column, above):
+        sign = 2 * above - 1
+        keep = sign * (rows - (row - (tile + sign - 1) * HALF)) >= 1 - above
+        add_piece(out_ref, piece_ref.at[slot], column, keep)
 
     @pl.when(core == 0)
     def _():
-        gather(below_copy_ref, above_copy_ref, mid_zero_ref, up_zero_ref, down_zero_ref)
+        for slot in range(2):
+            add_piece(out_ref, mid_zero_ref.at[slot], pos_ref[slot, 1], None)
+            row, column = first_copy_ref[slot, 0], first_copy_ref[slot, 1]
+            add(first_zero_ref, slot, row, column, 1 - odd)
+            row, column = second_copy_ref[slot, 0], second_copy_ref[slot, 1]
+            add(second_zero_ref, slot, row, column, odd)
 
     @pl.when(core == 1)
     def _():
-        gather(below_ref, above_ref, mid_one_ref, up_one_ref, down_one_ref)
+        for slot in range(2):
+            add_piece(out_ref, mid_one_ref.at[slot], pos_ref[slot, 1], None)
+            first = first_ref[slot, 0], first_ref[slot, 1]
+            second = second_ref[slot, 0], second_ref[slot, 1]
+            below = [jnp.where(odd == 1, one, two) for one, two in zip(first, second)]
+            above = [jnp.where(odd == 1, two, one) for one, two in zip(first, second)]
+            add(up_one_ref, slot, *below, 0)
+            add(down_one_ref, slot, *above, 1)
 
 
 SMEM = pl.BlockSpec(memory_space=pltpu.SMEM)
@@ -249,6 +285,17 @@
             if 0 <= tile + by < tiles:
                 pairs.append((source * tiles + tile, target * tiles + tile + by))
         return lax.ppermute(value, ("cuts", "tile"), pairs)
+
+    def swap(value, cores, partner):
+        pairs = [(tile, partner(tile)) for tile in range(tiles) if 0 <= partner(tile) < tiles]
+        pairs = [(core * tiles + one, core * tiles + two) for core in cores for one, two in pairs]
+        return lax.ppermute(value, ("cuts", "tile"), pairs)
+
+    def first(tile):
+        return tile ^ 1
+
+    def second(tile):
+        return ((tile + 1) ^ 1) - 1
 
     def kernel(body, name, out_shape, in_specs, flops, moved, scratch=(), out_specs=None):
         return pl.pallas_call(
@@ -263,63 +310,57 @@
         )
 
     pieces = jax.ShapeDtypeStruct((2, 2, HALF, WIN), jnp.float32)
-    dft, prop = build_tables()
+    tables = jnp.asarray(np.stack(build_tables()))
     other_slice = lax.ppermute(object_slices, "cuts", [(0, 1), (1, 0)])
-    below = send(positions, 0, 1, 1)
-    above = send(positions, 0, 1, -1)
+    pos_second = swap(positions, (1,), second)
+    pos_first = swap(positions, (1,), first)
+    strip = jax.ShapeDtypeStruct(object_slices.shape, jnp.float32)
+    own_slice = kernel(
+        stage_kernel, "stage", strip, [ANY], 0, 4 << 20, (pltpu.SemaphoreType.DMA,)
+    )(object_slices)
     up_zero, down_zero, up_one, down_one = kernel(
         cut_kernel, "cut", (pieces,) * 4, [SMEM] * 2 + [VMEM] * 2, 0, 4 << 20, (), (VMEM,) * 4
-    )(below, above, object_slices, other_slice)
+    )(pos_first, pos_second, own_slice, other_slice)
     low_zero = send(up_zero, 1, 0, 1)
     high_zero = send(down_zero, 1, 0, -1)
     low_one = send(up_one, 1, 0, 1)
     high_one = send(down_one, 1, 0, -1)
-    below_copy = send(below, 1, 0, 0)
-    above_copy = send(above, 1, 0, 0)
+    second_copy = send(pos_second, 1, 0, 0)
+    first_copy = send(pos_first, 1, 0, 0)
+    window = (pltpu.VMEM((2, WIN, WIN), jnp.float32),)
+    wave = kernel(
+        enter_kernel,
+        "enter",
+        jax.ShapeDtypeStruct((2, 2, 2, WIN, WIN), jnp.float32),
+        [SMEM] * 2 + [VMEM] * 5,
+        18 * 2 * WIN**3,
+        3 << 20,
+        window,
+    )(positions, counts, probe, tables, own_slice, low_zero, high_zero)
     rim_zero, rim_one, mid_zero, mid_one = kernel(
         slot_kernel,
         "slot",
         (pieces,) * 4,
-        [SMEM] * 2 + [VMEM] * 10,
-        72 * 2 * WIN**3,
+        [SMEM] * 2 + [VMEM] * 6,
+        54 * 2 * WIN**3,
         6 << 20,
-        (pltpu.VMEM((2, 2, WIN, WIN), jnp.float32),),
+        window,
         (VMEM,) * 4,
-    )(
-        positions,
-        counts,
-        probe,
-        jnp.asarray(dft),
-        jnp.asarray(prop),
-        object_slices,
-        other_slice,
-        low_zero,
-        high_zero,
-        low_one,
-        high_one,
-        intensity,
-    )
+    )(positions, counts, tables, wave, other_slice, low_one, high_one, intensity)
     back_up_one = send(rim_one, 0, 1, 1)
     back_down_one = send(rim_one, 0, 1, -1)
-    back_up_zero = send(rim_zero, 0, 0, 1)
-    back_down_zero = send(rim_zero, 0, 0, -1)
+    back_second = swap(rim_zero, (0,), second)
+    back_first = swap(rim_zero, (0,), first)
     mid_one = send(mid_one, 0, 1, 0)
-    return kernel(
-        collect_kernel,
-        "collect",
-        jax.ShapeDtypeStruct(object_slices.shape, jnp.float32),
-        [SMEM] * 5 + [VMEM] * 6,
-        0,
-        4 << 20,
-    )(
+    return kernel(collect_kernel, "collect", strip, [SMEM] * 5 + [VMEM] * 6, 0, 4 << 20)(
         positions,
-        below,
-        above,
-        below_copy,
-        above_copy,
+        pos_first,
+        pos_second,
+        first_copy,
+        second_copy,
         mid_zero,
-        back_up_zero,
-        back_down_zero,
+        back_first,
+        back_second,
         mid_one,
         back_up_one,
         back_down_one,

time: 68.2 us -> 59.7 us (0.88)
  starting transfers between devices: 27.7 us -> 21.7 us
  waiting for transfers between devices: 27.8 us -> 25.5 us
  local copies, waits for them, and re-layouts: 2.74 us -> 1.61 us
  Pallas kernels: 8.41 us -> 9.29 us
    ppermute x13 -> x9, starting transfers between devices: 27.7 us -> 11.8 us  [send(): return lax.ppermute(value, ('cuts', 'tile'), pairs)]
    ppermute x13 -> x9, waiting for transfers between devices: 27.8 us -> 16.5 us  [send(): return lax.ppermute(value, ('cuts', 'tile'), pairs)]
    ppermute x0 -> x4, starting transfers between devices: none -> 9.82 us  [swap(): return lax.ppermute(value, ('cuts', 'tile'), pairs)]
    ppermute x0 -> x4, waiting for transfers between devices: none -> 7.8 us  [swap(): return lax.ppermute(value, ('cuts', 'tile'), pairs)]
    ppermute x1, waiting for transfers between devices: 0.01 us -> 1.23 us  [local(): other_slice = lax.ppermute(object_slices, 'cuts', [(0, 1), (1, 0)])]
    unnamed x14 -> x10, local copies, waits for them, and re-layouts: 2.74 us -> 1.61 us
    pallas_call x2 -> x4, Pallas kernels: 7.83 us -> 8.72 us  [the longest x1 4.05 us: local(): kernel(slot_kernel, 'slot', (pieces,) * 4, [SMEM] * 2 + [VMEM] * 6, 54 *...]
  transfers between devices with their start and end apart: 14 -> 14, of which waited for: 5 -> 5; matrix products, arithmetic and copies ran while one was open for 0% -> 0% of each run, Pallas kernels for 8% -> 10%
where the time goes in v3:
time: 59.7 us; the launch traced here: 59 us
  waiting for transfers between devices  25.5 us (43%)
  starting transfers between devices  21.7 us (36%)
  Pallas kernels  9.29 us (16%)
  local copies, waits for them, and re-layouts  1.61 us (3%)
  between operations  0.89 us (1%)
    ppermute x9, waiting for transfers between devices, send(): return lax.ppermute(value, ('cuts', 'tile'), pairs)  16.5 us
    ppermute x9, starting transfers between devices, send(): return lax.ppermute(value, ('cuts', 'tile'), pairs)  11.8 us
    ppermute x4, starting transfers between devices, swap(): return lax.ppermute(value, ('cuts', 'tile'), pairs)  9.82 us
    ppermute x4, waiting for transfers between devices, swap(): return lax.ppermute(value, ('cuts', 'tile'), pairs)  7.8 us
    pallas_call x1, Pallas kernels, local(): kernel(slot_kernel, 'slot', (pieces,) * 4, [SMEM] * 2 + [VMEM] * 6, 54 *...  4.05 us
    pallas_call x1, Pallas kernels, local(): kernel(collect_kernel, 'collect', strip, [SMEM] * 5 + [VMEM] * 6, 0, 4 <<...  2.56 us
    pallas_call x1, Pallas kernels, local(): kernel(enter_kernel, 'enter', jax.ShapeDtypeStruct((2, 2, 2, WIN, WIN), j...  1.96 us
    unnamed x10, local copies, waits for them, and re-layouts  1.61 us
  transfers between devices with their start and end apart: 14, of which 5 were waited for; matrix products, arithmetic and copies ran while one was open for 0% of the time, Pallas kernels for 10%

profile of v3, /device:TPU:128, one launch (start us, length us, event | category | flops | bytes accessed | tf_op | source)
XLA Modules:
  0.0 59.0 jit_solution(283018583997456403)
XLA Ops:
  0.0 0.0 collective-permute-start.4
  0.0 0.7 %collective-permute-start = (s32[2,2]{1,0:T(2,128)}, s32[2,2]{1,0:T(2,128)S(1)}, u32[]{:S(2)}, u32[]{:S(2)}) collective-permute-start(s32[2,2]{1,0:T(2,128)} %pos_ref.5), channel_id=1, source_target_pairs={{128,129},{129,128},{130,131},{131,130},{132,133},{133,132},{134,1... | collective-permute-start | bytes 56 | tf_op jit(solution)/shard_map/ppermute | solution.py:292
  0.7 0.7 %collective-permute-start.1 = (s32[2,2]{1,0:T(2,128)}, s32[2,2]{1,0:T(2,128)S(1)}, u32[]{:S(2)}, u32[]{:S(2)}) collective-permute-start(s32[2,2]{1,0:T(2,128)} %pos_ref.5), channel_id=1, source_target_pairs={{129,130},{130,129},{131,132},{132,131},{133,134},{134,133},{135,1... | collective-permute-start | bytes 56 | tf_op jit(solution)/shard_map/ppermute | solution.py:292
  1.3 1.6 %copy-done.1 = f32[1,2,128,2048]{3,2,1,0:T(8,128)S(1)} copy-done((f32[1,2,128,2048]{3,2,1,0:T(8,128)S(1)}, f32[1,2,128,2048]{3,2,1,0:T(8,128)}, u32[]{:S(2)}) %copy-start.1) | copy-done | bytes 2097176
  2.9 0.1 stage.1.own_ref
  3.1 0.0 copy-start
  3.1 0.0 copy-start.2
  3.1 0.0 copy-start.4
  3.1 0.0 collective-permute-done.1.second_ref
  3.1 1.2 %collective-permute-done.4.other_ref = f32[1,2,128,2048]{3,2,1,0:T(8,128)S(1)} collective-permute-done((f32[1,2,128,2048]{3,2,1,0:T(8,128)}, f32[1,2,128,2048]{3,2,1,0:T(8,128)S(1)}, u32[]{:S(2)}, u32[]{:S(2)}) %collective-permute-start.4) | collective-permute-done | bytes 2097184 | tf_op jit(solution)/shard_map/ppermute | solution.py:314
  4.4 0.6 cut.1
  5.0 1.3 %collective-permute-start.5 = (f32[2,2,128,256]{3,2,1,0:T(8,128)S(1)}, f32[2,2,128,256]{3,2,1,0:T(8,128)S(1)}, u32[]{:S(2)}, u32[]{:S(2)}) collective-permute-start(f32[2,2,128,256]{3,2,1,0:T(8,128)S(1)} %get-tuple-element.13), channel_id=1, source_target_pairs={{128,1},{129,2},{130,3},{131,4},{132,5},{133,6},{134,7},{135,8},{1... | collective-permute-start | bytes 1572872 | tf_op jit(solution)/shard_map/ppermute | solution.py:287
  6.3 1.3 %collective-permute-start.6 = (f32[2,2,128,256]{3,2,1,0:T(8,128)S(1)}, f32[2,2,128,256]{3,2,1,0:T(8,128)S(1)}, u32[]{:S(2)}, u32[]{:S(2)}) collective-permute-start(f32[2,2,128,256]{3,2,1,0:T(8,128)S(1)} %get-tuple-element.14), channel_id=1, source_target_pairs={{129,0},{130,1},{131,2},{132,3},{133,4},{134,5},{135,6},{136,7},{1... | collective-permute-start | bytes 1572872 | tf_op jit(solution)/shard_map/ppermute | solution.py:287
  7.6 1.3 %collective-permute-start.7 = (f32[2,2,128,256]{3,2,1,0:T(8,128)S(1)}, f32[2,2,128,256]{3,2,1,0:T(8,128)S(1)}, u32[]{:S(2)}, u32[]{:S(2)}) collective-permute-start(f32[2,2,128,256]{3,2,1,0:T(8,128)S(1)} %get-tuple-element.15), channel_id=1, source_target_pairs={{128,1},{129,2},{130,3},{131,4},{132,5},{133,6},{134,7},{135,8},{1... | collective-permute-start | bytes 1572872 | tf_op jit(solution)/shard_map/ppermute | solution.py:287
  8.9 1.3 %collective-permute-start.8 = (f32[2,2,128,256]{3,2,1,0:T(8,128)S(1)}, f32[2,2,128,256]{3,2,1,0:T(8,128)S(1)}, u32[]{:S(2)}, u32[]{:S(2)}) collective-permute-start(f32[2,2,128,256]{3,2,1,0:T(8,128)S(1)} %get-tuple-element.16), channel_id=1, source_target_pairs={{129,0},{130,1},{131,2},{132,3},{133,4},{134,5},{135,6},{136,7},{1... | collective-permute-start | bytes 1572872 | tf_op jit(solution)/shard_map/ppermute | solution.py:287
  10.8 0.0 copy-start.3
  10.8 1.4 %collective-permute-start.2 = (s32[2,2]{1,0:T(2,128)S(1)}, s32[2,2]{1,0:T(2,128)S(1)}, u32[]{:S(2)}, u32[]{:S(2)}) collective-permute-start(s32[2,2]{1,0:T(2,128)S(1)} %collective-permute-done.first_ref), channel_id=1, source_target_pairs={{128,0},{129,1},{130,2},{131,3},{132,4},{133,5},{134,6},{135,7},{1... | collective-permute-start | bytes 56 | tf_op jit(solution)/shard_map/ppermute | solution.py:287
  12.2 14.2 %collective-permute-done.5.low_ref = f32[2,2,128,256]{3,2,1,0:T(8,128)S(1)} collective-permute-done((f32[2,2,128,256]{3,2,1,0:T(8,128)S(1)}, f32[2,2,128,256]{3,2,1,0:T(8,128)S(1)}, u32[]{:S(2)}, u32[]{:S(2)}) %collective-permute-start.5) | collective-permute-done | bytes 524320 | tf_op jit(solution)/shard_map/ppermute | solution.py:287
  26.4 1.3 %collective-permute-start.3 = (s32[2,2]{1,0:T(2,128)S(1)}, s32[2,2]{1,0:T(2,128)S(1)}, u32[]{:S(2)}, u32[]{:S(2)}) collective-permute-start(s32[2,2]{1,0:T(2,128)S(1)} %collective-permute-done.1.second_ref), channel_id=1, source_target_pairs={{128,0},{129,1},{130,2},{131,3},{132,4},{133,5},{134,6},{135,7},{1... | collective-permute-start | bytes 56 | tf_op jit(solution)/shard_map/ppermute | solution.py:287
  27.7 2.0 %enter.1.wave_ref = f32[2,2,2,256,256]{4,3,2,1,0:T(8,128)S(1)} custom-call(s32[2,2]{1,0:T(2,128)S(1)} %copy-done.4, s32[1]{0:T(128)S(6)} %copy.7.counts_ref, f32[2,256,256]{2,1,0:T(8,128)S(1)} %copy-done.2, bf16[2,6,256,256]{3,2,1,0:T(8,128)(2,1)S(1)} %copy-done, f32[1,2,128,2048]{3,2,1,0:T(8,128)S(1)} %stage.1.own_ref, ...), custom_call_target="tpu_custom_call" | custom-call | flops 603979776 | bytes 3145728 | tf_op jit(solution)/shard_map/enter/pallas_call | solution.py:331
  29.7 2.3 %collective-permute-done.7.low_ref = f32[2,2,128,256]{3,2,1,0:T(8,128)S(1)} collective-permute-done((f32[2,2,128,256]{3,2,1,0:T(8,128)S(1)}, f32[2,2,128,256]{3,2,1,0:T(8,128)S(1)}, u32[]{:S(2)}, u32[]{:S(2)}) %collective-permute-start.7) | collective-permute-done | bytes 524320 | tf_op jit(solution)/shard_map/ppermute | solution.py:287
  32.0 4.1 %slot.1 = (f32[2,2,128,256]{3,2,1,0:T(8,128)S(1)}, f32[2,2,128,256]{3,2,1,0:T(8,128)S(1)}, f32[2,2,128,256]{3,2,1,0:T(8,128)S(1)}, f32[2,2,128,256]{3,2,1,0:T(8,128)S(1)}) custom-call(s32[2,2]{1,0:T(2,128)S(1)} %copy-done.4, s32[1]{0:T(128)S(6)} %copy.7.counts_ref, bf16[2,6,256,256]{3,2,1,0:T(8,128)(2,1)S(1)} %copy-done, ...), custom_call_target="tpu_custom_call" | custom-call | flops 1811939328 | bytes 6291456 | tf_op jit(solution)/shard_map/slot/pallas_call | solution.py:340
  36.1 1.3 %collective-permute-start.12 = (f32[2,2,128,256]{3,2,1,0:T(8,128)S(1)}, f32[2,2,128,256]{3,2,1,0:T(8,128)S(1)}, u32[]{:S(2)}, u32[]{:S(2)}) collective-permute-start(f32[2,2,128,256]{3,2,1,0:T(8,128)S(1)} %get-tuple-element.20), channel_id=1, source_target_pairs={{0,129},{1,130},{2,131},{3,132},{4,133},{5,134},{6,135},{7,136},{8... | collective-permute-start | bytes 1572872 | tf_op jit(solution)/shard_map/ppermute | solution.py:287
  37.4 1.3 %collective-permute-start.13 = (f32[2,2,128,256]{3,2,1,0:T(8,128)S(1)}, f32[2,2,128,256]{3,2,1,0:T(8,128)S(1)}, u32[]{:S(2)}, u32[]{:S(2)}) collective-permute-start(f32[2,2,128,256]{3,2,1,0:T(8,128)S(1)} %get-tuple-element.20), channel_id=1, source_target_pairs={{1,128},{2,129},{3,130},{4,131},{5,132},{6,133},{7,134},{8,135},{9... | collective-permute-start | bytes 1572872 | tf_op jit(solution)/shard_map/ppermute | solution.py:287
  38.8 6.6 %collective-permute-start.10 = (f32[2,2,128,256]{3,2,1,0:T(8,128)S(1)}, f32[2,2,128,256]{3,2,1,0:T(8,128)S(1)}, u32[]{:S(2)}, u32[]{:S(2)}) collective-permute-start(f32[2,2,128,256]{3,2,1,0:T(8,128)S(1)} %get-tuple-element.18), channel_id=1, source_target_pairs={{1,2},{2,1},{3,4},{4,3},{5,6},{6,5},{7,8},{8,7},{9,10},{10,9},{11,... | collective-permute-start | bytes 1572872 | tf_op jit(solution)/shard_map/ppermute | solution.py:292
  45.4 1.9 %collective-permute-start.9 = (f32[2,2,128,256]{3,2,1,0:T(8,128)S(1)}, f32[2,2,128,256]{3,2,1,0:T(8,128)S(1)}, u32[]{:S(2)}, u32[]{:S(2)}) collective-permute-start(f32[2,2,128,256]{3,2,1,0:T(8,128)S(1)} %get-tuple-element.18), channel_id=1, source_target_pairs={{0,1},{1,0},{2,3},{3,2},{4,5},{5,4},{6,7},{7,6},{8,9},{9,8},{10,11... | collective-permute-start | bytes 1572872 | tf_op jit(solution)/shard_map/ppermute | solution.py:292
  47.3 1.3 %collective-permute-start.11 = (f32[2,2,128,256]{3,2,1,0:T(8,128)S(1)}, f32[2,2,128,256]{3,2,1,0:T(8,128)S(1)}, u32[]{:S(2)}, u32[]{:S(2)}) collective-permute-start(f32[2,2,128,256]{3,2,1,0:T(8,128)S(1)} %get-tuple-element.19), channel_id=1, source_target_pairs={{0,128},{1,129},{2,130},{3,131},{4,132},{5,133},{6,134},{7,135},{8... | collective-permute-start | bytes 1572872 | tf_op jit(solution)/shard_map/ppermute | solution.py:287
  48.6 6.6 %collective-permute-done.10.second_zero_ref = f32[2,2,128,256]{3,2,1,0:T(8,128)S(1)} collective-permute-done((f32[2,2,128,256]{3,2,1,0:T(8,128)S(1)}, f32[2,2,128,256]{3,2,1,0:T(8,128)S(1)}, u32[]{:S(2)}, u32[]{:S(2)}) %collective-permute-start.10) | collective-permute-done | bytes 524320 | tf_op jit(solution)/shard_map/ppermute | solution.py:292
  55.3 0.0 collective-permute-done.12.up_one_ref
  55.3 0.0 collective-permute-done.13.down_one_ref
  55.3 1.2 %collective-permute-done.9.first_zero_ref = f32[2,2,128,256]{3,2,1,0:T(8,128)S(1)} collective-permute-done((f32[2,2,128,256]{3,2,1,0:T(8,128)S(1)}, f32[2,2,128,256]{3,2,1,0:T(8,128)S(1)}, u32[]{:S(2)}, u32[]{:S(2)}) %collective-permute-start.9) | collective-permute-done | bytes 524320 | tf_op jit(solution)/shard_map/ppermute | solution.py:292
  56.5 2.6 %collect.1 = f32[1,2,128,2048]{3,2,1,0:T(8,128)} custom-call(s32[2,2]{1,0:T(2,128)S(1)} %copy-done.4, s32[2,2]{1,0:T(2,128)S(1)} %collective-permute-done.first_ref, s32[2,2]{1,0:T(2,128)S(1)} %collective-permute-done.1.second_ref, s32[2,2]{1,0:T(2,128)S(1)} %collective-permute-done.2.first_copy_ref, s32[2,2]{1,0:T(2,128)S(1)} %collective-permute-done.3.second_copy_ref, ...), custom_call_target="tpu_custom_call" | custom-call | bytes 4194304 | tf_op jit(solution)/shard_map/collect/pallas_call | solution.py:355
  (11 shorter events, 0.0 us)
Async XLA Ops:
  0.0 4.4 %collective-permute-start.4 = (f32[1,2,128,2048]{3,2,1,0:T(8,128)}, f32[1,2,128,2048]{3,2,1,0:T(8,128)S(1)}, u32[]{:S(2)}, u32[]{:S(2)}) collective-permute-start(f32[1,2,128,2048]{3,2,1,0:T(8,128)} %strip_ref.1), channel_id=1, source_target_pairs={{0,128},{128,0},{1,129},{129,1},{2,130},{130,2},{3,131},{131,3},{4... | collective-permute-start | bytes 6291464 | tf_op jit(solution)/shard_map/ppermute | solution.py:314
  0.0 3.1 %collective-permute-start = (s32[2,2]{1,0:T(2,128)}, s32[2,2]{1,0:T(2,128)S(1)}, u32[]{:S(2)}, u32[]{:S(2)}) collective-permute-start(s32[2,2]{1,0:T(2,128)} %pos_ref.5), channel_id=1, source_target_pairs={{128,129},{129,128},{130,131},{131,130},{132,133},{133,132},{134,1... | collective-permute-start | bytes 56 | tf_op jit(solution)/shard_map/ppermute | solution.py:292
  0.7 2.5 %collective-permute-start.1 = (s32[2,2]{1,0:T(2,128)}, s32[2,2]{1,0:T(2,128)S(1)}, u32[]{:S(2)}, u32[]{:S(2)}) collective-permute-start(s32[2,2]{1,0:T(2,128)} %pos_ref.5), channel_id=1, source_target_pairs={{129,130},{130,129},{131,132},{132,131},{133,134},{134,133},{135,1... | collective-permute-start | bytes 56 | tf_op jit(solution)/shard_map/ppermute | solution.py:292
  1.3 1.6 %copy-start.1 = (f32[1,2,128,2048]{3,2,1,0:T(8,128)S(1)}, f32[1,2,128,2048]{3,2,1,0:T(8,128)}, u32[]{:S(2)}) copy-start(f32[1,2,128,2048]{3,2,1,0:T(8,128)} %strip_ref.1) | copy-start | bytes 6291460
  3.1 24.6 %copy-start = (bf16[2,6,256,256]{3,2,1,0:T(8,128)(2,1)S(1)}, bf16[2,6,256,256]{3,2,1,0:T(8,128)(2,1)}, u32[]{:S(2)}) copy-start(bf16[2,6,256,256]{3,2,1,0:T(8,128)(2,1)} %constant.2.clone.table_ref) | copy-start | bytes 4718596
  3.1 24.6 %copy-start.2 = (f32[2,256,256]{2,1,0:T(8,128)S(1)}, f32[2,256,256]{2,1,0:T(8,128)}, u32[]{:S(2)}) copy-start(f32[2,256,256]{2,1,0:T(8,128)} %probe_ref.1) | copy-start | bytes 1572868
  3.1 24.6 %copy-start.4 = (s32[2,2]{1,0:T(2,128)S(1)}, s32[2,2]{1,0:T(2,128)}, u32[]{:S(2)}) copy-start(s32[2,2]{1,0:T(2,128)} %pos_ref.5) | copy-start | bytes 52
  5.0 21.5 %collective-permute-start.5 = (f32[2,2,128,256]{3,2,1,0:T(8,128)S(1)}, f32[2,2,128,256]{3,2,1,0:T(8,128)S(1)}, u32[]{:S(2)}, u32[]{:S(2)}) collective-permute-start(f32[2,2,128,256]{3,2,1,0:T(8,128)S(1)} %get-tuple-element.13), channel_id=1, source_target_pairs={{128,1},{129,2},{130,3},{131,4},{132,5},{133,6},{134,7},{135,8},{1... | collective-permute-start | bytes 1572872 | tf_op jit(solution)/shard_map/ppermute | solution.py:287
  6.3 21.5 %collective-permute-start.6 = (f32[2,2,128,256]{3,2,1,0:T(8,128)S(1)}, f32[2,2,128,256]{3,2,1,0:T(8,128)S(1)}, u32[]{:S(2)}, u32[]{:S(2)}) collective-permute-start(f32[2,2,128,256]{3,2,1,0:T(8,128)S(1)} %get-tuple-element.14), channel_id=1, source_target_pairs={{129,0},{130,1},{131,2},{132,3},{133,4},{134,5},{135,6},{136,7},{1... | collective-permute-start | bytes 1572872 | tf_op jit(solution)/shard_map/ppermute | solution.py:287
  7.6 24.5 %collective-permute-start.7 = (f32[2,2,128,256]{3,2,1,0:T(8,128)S(1)}, f32[2,2,128,256]{3,2,1,0:T(8,128)S(1)}, u32[]{:S(2)}, u32[]{:S(2)}) collective-permute-start(f32[2,2,128,256]{3,2,1,0:T(8,128)S(1)} %get-tuple-element.15), channel_id=1, source_target_pairs={{128,1},{129,2},{130,3},{131,4},{132,5},{133,6},{134,7},{135,8},{1... | collective-permute-start | bytes 1572872 | tf_op jit(solution)/shard_map/ppermute | solution.py:287
  8.9 23.2 %collective-permute-start.8 = (f32[2,2,128,256]{3,2,1,0:T(8,128)S(1)}, f32[2,2,128,256]{3,2,1,0:T(8,128)S(1)}, u32[]{:S(2)}, u32[]{:S(2)}) collective-permute-start(f32[2,2,128,256]{3,2,1,0:T(8,128)S(1)} %get-tuple-element.16), channel_id=1, source_target_pairs={{129,0},{130,1},{131,2},{132,3},{133,4},{134,5},{135,6},{136,7},{1... | collective-permute-start | bytes 1572872 | tf_op jit(solution)/shard_map/ppermute | solution.py:287
  10.8 21.2 %copy-start.3 = (f32[2,256,256]{2,1,0:T(8,128)S(1)}, f32[2,256,256]{2,1,0:T(8,128)}, u32[]{:S(2)}) copy-start(f32[2,256,256]{2,1,0:T(8,128)} %intensity_ref.1) | copy-start | bytes 1572868
  10.8 34.6 %collective-permute-start.2 = (s32[2,2]{1,0:T(2,128)S(1)}, s32[2,2]{1,0:T(2,128)S(1)}, u32[]{:S(2)}, u32[]{:S(2)}) collective-permute-start(s32[2,2]{1,0:T(2,128)S(1)} %collective-permute-done.first_ref), channel_id=1, source_target_pairs={{128,0},{129,1},{130,2},{131,3},{132,4},{133,5},{134,6},{135,7},{1... | collective-permute-start | bytes 56 | tf_op jit(solution)/shard_map/ppermute | solution.py:287
  26.4 20.9 %collective-permute-start.3 = (s32[2,2]{1,0:T(2,128)S(1)}, s32[2,2]{1,0:T(2,128)S(1)}, u32[]{:S(2)}, u32[]{:S(2)}) collective-permute-start(s32[2,2]{1,0:T(2,128)S(1)} %collective-permute-done.1.second_ref), channel_id=1, source_target_pairs={{128,0},{129,1},{130,2},{131,3},{132,4},{133,5},{134,6},{135,7},{1... | collective-permute-start | bytes 56 | tf_op jit(solution)/shard_map/ppermute | solution.py:287
  36.1 19.2 %collective-permute-start.12 = (f32[2,2,128,256]{3,2,1,0:T(8,128)S(1)}, f32[2,2,128,256]{3,2,1,0:T(8,128)S(1)}, u32[]{:S(2)}, u32[]{:S(2)}) collective-permute-start(f32[2,2,128,256]{3,2,1,0:T(8,128)S(1)} %get-tuple-element.20), channel_id=1, source_target_pairs={{0,129},{1,130},{2,131},{3,132},{4,133},{5,134},{6,135},{7,136},{8... | collective-permute-start | bytes 1572872 | tf_op jit(solution)/shard_map/ppermute | solution.py:287
  37.4 17.8 %collective-permute-start.13 = (f32[2,2,128,256]{3,2,1,0:T(8,128)S(1)}, f32[2,2,128,256]{3,2,1,0:T(8,128)S(1)}, u32[]{:S(2)}, u32[]{:S(2)}) collective-permute-start(f32[2,2,128,256]{3,2,1,0:T(8,128)S(1)} %get-tuple-element.20), channel_id=1, source_target_pairs={{1,128},{2,129},{3,130},{4,131},{5,132},{6,133},{7,134},{8,135},{9... | collective-permute-start | bytes 1572872 | tf_op jit(solution)/shard_map/ppermute | solution.py:287
  38.8 16.5 %collective-permute-start.10 = (f32[2,2,128,256]{3,2,1,0:T(8,128)S(1)}, f32[2,2,128,256]{3,2,1,0:T(8,128)S(1)}, u32[]{:S(2)}, u32[]{:S(2)}) collective-permute-start(f32[2,2,128,256]{3,2,1,0:T(8,128)S(1)} %get-tuple-element.18), channel_id=1, source_target_pairs={{1,2},{2,1},{3,4},{4,3},{5,6},{6,5},{7,8},{8,7},{9,10},{10,9},{11,... | collective-permute-start | bytes 1572872 | tf_op jit(solution)/shard_map/ppermute | solution.py:292
  45.4 11.1 %collective-permute-start.9 = (f32[2,2,128,256]{3,2,1,0:T(8,128)S(1)}, f32[2,2,128,256]{3,2,1,0:T(8,128)S(1)}, u32[]{:S(2)}, u32[]{:S(2)}) collective-permute-start(f32[2,2,128,256]{3,2,1,0:T(8,128)S(1)} %get-tuple-element.18), channel_id=1, source_target_pairs={{0,1},{1,0},{2,3},{3,2},{4,5},{5,4},{6,7},{7,6},{8,9},{9,8},{10,11... | collective-permute-start | bytes 1572872 | tf_op jit(solution)/shard_map/ppermute | solution.py:292
  47.3 9.1 %collective-permute-start.11 = (f32[2,2,128,256]{3,2,1,0:T(8,128)S(1)}, f32[2,2,128,256]{3,2,1,0:T(8,128)S(1)}, u32[]{:S(2)}, u32[]{:S(2)}) collective-permute-start(f32[2,2,128,256]{3,2,1,0:T(8,128)S(1)} %get-tuple-element.19), channel_id=1, source_target_pairs={{0,128},{1,129},{2,130},{3,131},{4,132},{5,133},{6,134},{7,135},{8... | collective-permute-start | bytes 1572872 | tf_op jit(solution)/shard_map/ppermute | solution.py:287

commit v4 on v3

--- a/solution.py
+++ b/solution.py
@@ -84,52 +84,57 @@
         out_ref[part, :, HALF:WIN] = strip_ref[0, part, :, block(first + 1)]
 
 
-def stage_kernel(strip_ref, out_ref, sem):
+def stage_kernel(pos_ref, strip_ref, pos_out_ref, out_ref, sem):
     copy = pltpu.make_async_copy(strip_ref, out_ref, sem)
     copy.start()
+    for slot in range(2):
+        for entry in range(2):
+            pos_out_ref[slot, entry] = pos_ref[slot, entry]
     copy.wait()
 
 
-def is_odd():
-    return jnp.bitwise_and(lax.axis_index("tile"), 1)
-
-
-def cut_kernel(
-    first_ref, second_ref, own_ref, other_ref, up_zero_ref, down_zero_ref, up_one_ref, down_one_ref
-):
+def cut_kernel(pos_ref, strip_ref, after_ref, out_ref):
     @pl.when(lax.axis_index("cuts") == 1)
     def _():
-        odd = is_odd() == 1
-        for strip_ref, up_ref, down_ref in (
-            (other_ref, up_zero_ref, down_zero_ref),
-            (own_ref, up_one_ref, down_one_ref),
-        ):
-            for slot in range(2):
-                first, second = first_ref[slot, 1], second_ref[slot, 1]
-                cut_piece(strip_ref, jnp.where(odd, second, first), up_ref.at[slot])
-                cut_piece(strip_ref, jnp.where(odd, first, second), down_ref.at[slot])
+        for slot in range(2):
+            cut_piece(strip_ref, pos_ref[slot, 1], out_ref.at[slot])
 
 
 def slots_of_core(counts_ref):
     return jnp.where(lax.axis_index("cuts") == 0, counts_ref[0], 0)
 
 
-def fill_window(pos_ref, slot, strip_ref, low_ref, high_ref, window_ref):
-    shift_rows = pos_ref[slot, 0] - (lax.axis_index("tile") - 1) * HALF
+def fill_window(pos_ref, slot, strip_ref, first_ref, second_ref, window_ref):
+    tile = lax.axis_index("tile")
+    odd = jnp.bitwise_and(tile, 1)
+    shift_rows = pos_ref[slot, 0] - (tile - 1) * HALF
     column = pos_ref[slot, 1]
-    from_low = lax.broadcasted_iota(jnp.int32, (HALF, WIN), 0) >= shift_rows
+    rows = lax.broadcasted_iota(jnp.int32, (HALF, WIN), 0)
+    from_first = (2 * odd - 1) * (rows - shift_rows) >= 1 - odd
     for part in range(2):
-        window_ref[part, 0:HALF] = jnp.where(from_low, low_ref[slot, part], high_ref[slot, part])
+        window_ref[part, 0:HALF] = jnp.where(
+            from_first, first_ref[slot, part], second_ref[slot, part]
+        )
     cut_piece(strip_ref, column, window_ref.at[:, HALF:WIN])
     return shift_rows, jnp.bitwise_and(column, HALF - 1)
 
 
 def enter_kernel(
-    pos_ref, counts_ref, probe_ref, table_ref, own_ref, low_ref, high_ref, wave_ref, window_ref
+    pos_ref,
+    counts_ref,
+    probe_ref,
+    table_ref,
+    own_ref,
+    second_ref,
+    first_ref,
+    second_copy_ref,
+    first_copy_ref,
+    wave_ref,
+    window_ref,
 ):
     @pl.loop(0, slots_of_core(counts_ref))
     def _(slot):
-        shift_rows, shift_cols = fill_window(pos_ref, slot, own_ref, low_ref, high_ref, window_ref)
+        shift_rows, shift_cols = fill_window(pos_ref, slot, own_ref, first_ref, second_ref, window_ref)
 
         def rolled(part):
             return pltpu.roll(pltpu.roll(probe_ref[part], shift_rows, 0), shift_cols, 1)
@@ -154,8 +159,8 @@
     table_ref,
     wave_ref,
     other_ref,
-    low_ref,
-    high_ref,
+    second_ref,
+    first_ref,
     intensity_ref,
     rim_zero_ref,
     rim_one_ref,
@@ -168,7 +173,7 @@
 
     @pl.loop(0, live_slots)
     def _(slot):
-        fill_window(pos_ref, slot, other_ref, low_ref, high_ref, window_ref)
+        fill_window(pos_ref, slot, other_ref, first_ref, second_ref, window_ref)
         cell_re, cell_im = window_ref[0], window_ref[1]
         one_re, one_im = wave_ref[slot, 1, 0], wave_ref[slot, 1, 1]
         far_re, far_im = sandwich(
@@ -224,48 +229,49 @@
 
 def collect_kernel(
     pos_ref,
+    second_ref,
     first_ref,
-    second_ref,
+    second_copy_ref,
     first_copy_ref,
-    second_copy_ref,
     mid_zero_ref,
+    second_zero_ref,
     first_zero_ref,
-    second_zero_ref,
+    second_one_ref,
+    first_one_ref,
     mid_one_ref,
-    up_one_ref,
-    down_one_ref,
     out_ref,
 ):
     core = lax.axis_index("cuts")
     tile = lax.axis_index("tile")
-    odd = is_odd()
+    odd = jnp.bitwise_and(tile, 1)
     out_ref[...] = jnp.zeros_like(out_ref)
     rows = lax.broadcasted_iota(jnp.int32, (HALF, HALF), 0)
 
-    def add(piece_ref, slot, row, column, above):
-        sign = 2 * above - 1
-        keep = sign * (rows - (row - (tile + sign - 1) * HALF)) >= 1 - above
-        add_piece(out_ref, piece_ref.at[slot], column, keep)
+    def gather(mid_ref, *nearby):
+        for slot in range(2):
+            add_piece(out_ref, mid_ref.at[slot], pos_ref[slot, 1], None)
+        for piece_ref, place_ref, above in nearby:
+            sign = 2 * above - 1
+            for slot in range(2):
+                shift_rows = place_ref[slot, 0] - (tile + sign - 1) * HALF
+                keep = sign * (rows - shift_rows) >= 1 - above
+                add_piece(out_ref, piece_ref.at[slot], place_ref[slot, 1], keep)
 
     @pl.when(core == 0)
     def _():
-        for slot in range(2):
-            add_piece(out_ref, mid_zero_ref.at[slot], pos_ref[slot, 1], None)
-            row, column = first_copy_ref[slot, 0], first_copy_ref[slot, 1]
-            add(first_zero_ref, slot, row, column, 1 - odd)
-            row, column = second_copy_ref[slot, 0], second_copy_ref[slot, 1]
-            add(second_zero_ref, slot, row, column, odd)
+        gather(
+            mid_zero_ref,
+            (second_zero_ref, second_copy_ref, odd),
+            (first_zero_ref, first_copy_ref, 1 - odd),
+        )
 
     @pl.when(core == 1)
     def _():
-        for slot in range(2):
-            add_piece(out_ref, mid_one_ref.at[slot], pos_ref[slot, 1], None)
-            first = first_ref[slot, 0], first_ref[slot, 1]
-            second = second_ref[slot, 0], second_ref[slot, 1]
-            below = [jnp.where(odd == 1, one, two) for one, two in zip(first, second)]
-            above = [jnp.where(odd == 1, two, one) for one, two in zip(first, second)]
-            add(up_one_ref, slot, *below, 0)
-            add(down_one_ref, slot, *above, 1)
+        gather(
+            mid_one_ref,
+            (second_one_ref, second_ref, odd),
+            (first_one_ref, first_ref, 1 - odd),
+        )
 
 
 SMEM = pl.BlockSpec(memory_space=pltpu.SMEM)
@@ -279,23 +285,19 @@
 def local(object_slices, probe, positions, counts, intensity):
     tiles = lax.axis_size("tile")
 
-    def send(value, source, target, by):
-        pairs = []
-        for tile in range(tiles):
-            if 0 <= tile + by < tiles:
-                pairs.append((source * tiles + tile, target * tiles + tile + by))
-        return lax.ppermute(value, ("cuts", "tile"), pairs)
-
-    def swap(value, cores, partner):
-        pairs = [(tile, partner(tile)) for tile in range(tiles) if 0 <= partner(tile) < tiles]
-        pairs = [(core * tiles + one, core * tiles + two) for core in cores for one, two in pairs]
-        return lax.ppermute(value, ("cuts", "tile"), pairs)
-
     def first(tile):
         return tile ^ 1
 
     def second(tile):
         return ((tile + 1) ^ 1) - 1
+
+    def same(tile):
+        return tile
+
+    def send(value, source, target, partner):
+        pairs = [(tile, partner(tile)) for tile in range(tiles) if 0 <= partner(tile) < tiles]
+        pairs = [(source * tiles + one, target * tiles + two) for one, two in pairs]
+        return lax.ppermute(value, ("cuts", "tile"), pairs)
 
     def kernel(body, name, out_shape, in_specs, flops, moved, scratch=(), out_specs=None):
         return pl.pallas_call(
@@ -310,33 +312,45 @@
         )
 
     pieces = jax.ShapeDtypeStruct((2, 2, HALF, WIN), jnp.float32)
+    strip = jax.ShapeDtypeStruct(object_slices.shape, jnp.float32)
+    window = (pltpu.VMEM((2, WIN, WIN), jnp.float32),)
     tables = jnp.asarray(np.stack(build_tables()))
     other_slice = lax.ppermute(object_slices, "cuts", [(0, 1), (1, 0)])
-    pos_second = swap(positions, (1,), second)
-    pos_first = swap(positions, (1,), first)
-    strip = jax.ShapeDtypeStruct(object_slices.shape, jnp.float32)
-    own_slice = kernel(
-        stage_kernel, "stage", strip, [ANY], 0, 4 << 20, (pltpu.SemaphoreType.DMA,)
-    )(object_slices)
-    up_zero, down_zero, up_one, down_one = kernel(
-        cut_kernel, "cut", (pieces,) * 4, [SMEM] * 2 + [VMEM] * 2, 0, 4 << 20, (), (VMEM,) * 4
-    )(pos_first, pos_second, own_slice, other_slice)
-    low_zero = send(up_zero, 1, 0, 1)
-    high_zero = send(down_zero, 1, 0, -1)
-    low_one = send(up_one, 1, 0, 1)
-    high_one = send(down_one, 1, 0, -1)
-    second_copy = send(pos_second, 1, 0, 0)
-    first_copy = send(pos_first, 1, 0, 0)
-    window = (pltpu.VMEM((2, WIN, WIN), jnp.float32),)
+    pos_second = send(positions, 1, 1, second)
+    again, own_slice = kernel(
+        stage_kernel,
+        "stage",
+        (jax.ShapeDtypeStruct(positions.shape, positions.dtype), strip),
+        [SMEM, ANY],
+        0,
+        4 << 20,
+        (pltpu.SemaphoreType.DMA,),
+        (SMEM, VMEM),
+    )(positions, object_slices)
+    pos_first = send(again, 1, 1, first)
+
+    def cut(name, place, source, after):
+        return kernel(cut_kernel, name, pieces, [SMEM, VMEM, ANY], 0, 1 << 20)(place, source, after)
+
+    to_second_zero = cut("cut_second_zero", pos_second, other_slice, pos_first)
+    to_first_zero = cut("cut_first_zero", pos_first, other_slice, to_second_zero)
+    to_second_one = cut("cut_second_one", pos_second, own_slice, to_first_zero)
+    to_first_one = cut("cut_first_one", pos_first, own_slice, to_second_one)
+    second_zero = send(to_second_zero, 1, 0, second)
+    first_zero = send(to_first_zero, 1, 0, first)
+    second_one = send(to_second_one, 1, 0, second)
+    first_one = send(to_first_one, 1, 0, first)
+    second_copy = send(pos_second, 1, 0, same)
+    first_copy = send(pos_first, 1, 0, same)
     wave = kernel(
         enter_kernel,
         "enter",
         jax.ShapeDtypeStruct((2, 2, 2, WIN, WIN), jnp.float32),
-        [SMEM] * 2 + [VMEM] * 5,
+        [SMEM] * 2 + [VMEM] * 5 + [ANY] * 2,
         18 * 2 * WIN**3,
         3 << 20,
         window,
-    )(positions, counts, probe, tables, own_slice, low_zero, high_zero)
+    )(positions, counts, probe, tables, own_slice, second_zero, first_zero, second_copy, first_copy)
     rim_zero, rim_one, mid_zero, mid_one = kernel(
         slot_kernel,
         "slot",
@@ -346,24 +360,24 @@
         6 << 20,
         window,
         (VMEM,) * 4,
-    )(positions, counts, tables, wave, other_slice, low_one, high_one, intensity)
-    back_up_one = send(rim_one, 0, 1, 1)
-    back_down_one = send(rim_one, 0, 1, -1)
-    back_second = swap(rim_zero, (0,), second)
-    back_first = swap(rim_zero, (0,), first)
-    mid_one = send(mid_one, 0, 1, 0)
+    )(positions, counts, tables, wave, other_slice, second_one, first_one, intensity)
+    back_second_zero = send(rim_zero, 0, 1, second)
+    back_first_zero = send(rim_zero, 0, 1, first)
+    back_second_one = send(rim_one, 0, 1, second)
+    back_first_one = send(rim_one, 0, 1, first)
+    mid_one = send(mid_one, 0, 1, same)
     return kernel(collect_kernel, "collect", strip, [SMEM] * 5 + [VMEM] * 6, 0, 4 << 20)(
         positions,
+        pos_second,
         pos_first,
-        pos_second,
+        second_copy,
         first_copy,
-        second_copy,
         mid_zero,
-        back_first,
-        back_second,
+        send(back_second_zero, 1, 0, same),
+        send(back_first_zero, 1, 0, same),
+        back_second_one,
+        back_first_one,
         mid_one,
-        back_up_one,
-        back_down_one,
     )
 
 

time: 59.7 us -> 61 us (1.022)
  the two profiles are of different devices: /device:TPU:128 before, /device:TPU:225 now
where the time goes in v4:
time: 61 us; the launch traced here: 62.1 us
  starting transfers between devices  27.9 us (46%)
  waiting for transfers between devices  23.4 us (38%)
  Pallas kernels  7.67 us (13%)
  local copies, waits for them, and re-layouts  2.29 us (4%)
  between operations  0.92 us (2%)
    ppermute x15, starting transfers between devices, send(): return lax.ppermute(value, ('cuts', 'tile'), pairs)  27.2 us
    ppermute x15, waiting for transfers between devices, send(): return lax.ppermute(value, ('cuts', 'tile'), pairs)  23.3 us
    pallas_call x4, Pallas kernels, cut(): kernel(cut_kernel, name, pieces, [SMEM, VMEM, ANY], 0, 1 << 20)  2.67 us
    pallas_call x1, Pallas kernels, local(): kernel(collect_kernel, 'collect', strip, [SMEM] * 5 + [VMEM] * 6, 0, 4 <<...  2.56 us
    unnamed x12, local copies, waits for them, and re-layouts  2.29 us
    pallas_call x1, Pallas kernels, local(): kernel(stage_kernel, 'stage', (jax.ShapeDtypeStruct(positions.shape, posi...  1.3 us
  transfers between devices with their start and end apart: 16, of which 6 were waited for; matrix products, arithmetic and copies ran while one was open for 0% of the time, Pallas kernels for 5%

profile of v4, /device:TPU:225, one launch (start us, length us, event | category | flops | bytes accessed | tf_op | source)
XLA Modules:
  0.0 62.1 jit_solution(1160692698633444099)
XLA Ops:
  0.0 0.7 %collective-permute-start.4 = (f32[1,2,128,2048]{3,2,1,0:T(8,128)}, f32[1,2,128,2048]{3,2,1,0:T(8,128)S(1)}, u32[]{:S(2)}, u32[]{:S(2)}) collective-permute-start(f32[1,2,128,2048]{3,2,1,0:T(8,128)} %strip_ref.1), channel_id=1, source_target_pairs={{0,128},{128,0},{1,129},{129,1},{2,130},{130,2},{3,131},{131,3},{4... | collective-permute-start | bytes 6291464 | tf_op jit(solution)/shard_map/ppermute | solution.py:318
  0.7 7.3 %collective-permute-start = (s32[2,2]{1,0:T(2,128)}, s32[2,2]{1,0:T(2,128)S(1)}, u32[]{:S(2)}, u32[]{:S(2)}) collective-permute-start(s32[2,2]{1,0:T(2,128)} %pos_ref.7), channel_id=1, source_target_pairs={{129,130},{130,129},{131,132},{132,131},{133,134},{134,133},{135,1... | collective-permute-start | bytes 56 | tf_op jit(solution)/shard_map/ppermute | solution.py:300
  8.0 1.6 %copy-done.1 = f32[1,2,128,2048]{3,2,1,0:T(8,128)S(1)} copy-done((f32[1,2,128,2048]{3,2,1,0:T(8,128)S(1)}, f32[1,2,128,2048]{3,2,1,0:T(8,128)}, u32[]{:S(2)}) %copy-start.1) | copy-done | bytes 2097176
  9.6 0.7 %copy-done.4 = s32[2,2]{1,0:T(2,128)S(1)} copy-done((s32[2,2]{1,0:T(2,128)S(1)}, s32[2,2]{1,0:T(2,128)}, u32[]{:S(2)}) %copy-start.4) | copy-done | bytes 40
  10.2 1.3 %stage.1 = (s32[2,2]{1,0:T(2,128)S(1)}, f32[1,2,128,2048]{3,2,1,0:T(8,128)S(1)}) custom-call(s32[2,2]{1,0:T(2,128)S(1)} %copy-done.4, f32[1,2,128,2048]{3,2,1,0:T(8,128)S(1)} %copy-done.1), custom_call_target="tpu_custom_call" | custom-call | bytes 4194304 | tf_op jit(solution)/shard_map/stage/pallas_call | solution.py:320
  11.5 1.9 %collective-permute-start.1 = (s32[2,2]{1,0:T(2,128)S(1)}, s32[2,2]{1,0:T(2,128)S(1)}, u32[]{:S(2)}, u32[]{:S(2)}) collective-permute-start(s32[2,2]{1,0:T(2,128)S(1)} %get-tuple-element.11), channel_id=1, source_target_pairs={{128,129},{129,128},{130,131},{131,130},{132,133},{133,132},{134,1... | collective-permute-start | bytes 56 | tf_op jit(solution)/shard_map/ppermute | solution.py:300
  13.5 2.4 %collective-permute-done.1.after_ref.pos_ref.first_ref = s32[2,2]{1,0:T(2,128)S(1)} collective-permute-done((s32[2,2]{1,0:T(2,128)S(1)}, s32[2,2]{1,0:T(2,128)S(1)}, u32[]{:S(2)}, u32[]{:S(2)}) %collective-permute-start.1) | collective-permute-done | bytes 48 | tf_op jit(solution)/shard_map/ppermute | solution.py:300
  15.9 0.7 %cut_second_zero.1.after_ref = f32[2,2,128,256]{3,2,1,0:T(8,128)S(1)} custom-call(s32[2,2]{1,0:T(2,128)S(1)} %collective-permute-done.pos_ref.second_ref, f32[1,2,128,2048]{3,2,1,0:T(8,128)S(1)} %collective-permute-done.4.strip_ref.other_ref, s32[2,2]{1,0:T(2,128)S(1)} %collective-permute-done.1.after_ref.pos_ref.first_ref), custom_call_target="tpu_custom_call" | custom-call | bytes 1048576 | tf_op jit(solution)/shard_map/cut_second_zero/pallas_call | solution.py:333
  16.5 0.7 %cut_first_zero.1.after_ref = f32[2,2,128,256]{3,2,1,0:T(8,128)S(1)} custom-call(s32[2,2]{1,0:T(2,128)S(1)} %collective-permute-done.1.after_ref.pos_ref.first_ref, f32[1,2,128,2048]{3,2,1,0:T(8,128)S(1)} %collective-permute-done.4.strip_ref.other_ref, f32[2,2,128,256]{3,2,1,0:T(8,128)S(1)} %cut_second_zero.1.after_ref), custom_call_target="tpu_custom_call" | custom-call | bytes 1048576 | tf_op jit(solution)/shard_map/cut_first_zero/pallas_call | solution.py:333
  17.2 1.3 %collective-permute-start.6 = (f32[2,2,128,256]{3,2,1,0:T(8,128)S(1)}, f32[2,2,128,256]{3,2,1,0:T(8,128)S(1)}, u32[]{:S(2)}, u32[]{:S(2)}) collective-permute-start(f32[2,2,128,256]{3,2,1,0:T(8,128)S(1)} %cut_first_zero.1.after_ref), channel_id=1, source_target_pairs={{128,1},{129,0},{130,3},{131,2},{132,5},{133,4},{134,7},{135,6},{1... | collective-permute-start | bytes 1572872 | tf_op jit(solution)/shard_map/ppermute | solution.py:300
  18.5 1.3 %collective-permute-start.5 = (f32[2,2,128,256]{3,2,1,0:T(8,128)S(1)}, f32[2,2,128,256]{3,2,1,0:T(8,128)S(1)}, u32[]{:S(2)}, u32[]{:S(2)}) collective-permute-start(f32[2,2,128,256]{3,2,1,0:T(8,128)S(1)} %cut_second_zero.1.after_ref), channel_id=1, source_target_pairs={{129,2},{130,1},{131,4},{132,3},{133,6},{134,5},{135,8},{136,7},{1... | collective-permute-start | bytes 1572872 | tf_op jit(solution)/shard_map/ppermute | solution.py:300
  19.9 0.7 %cut_second_one.1.after_ref = f32[2,2,128,256]{3,2,1,0:T(8,128)S(1)} custom-call(s32[2,2]{1,0:T(2,128)S(1)} %collective-permute-done.pos_ref.second_ref, f32[1,2,128,2048]{3,2,1,0:T(8,128)S(1)} %get-tuple-element.12.own_ref.strip_ref, f32[2,2,128,256]{3,2,1,0:T(8,128)S(1)} %cut_first_zero.1.after_ref), custom_call_target="tpu_custom_call" | custom-call | bytes 1048576 | tf_op jit(solution)/shard_map/cut_second_one/pallas_call | solution.py:333
  20.6 0.7 %cut_first_one.1 = f32[2,2,128,256]{3,2,1,0:T(8,128)S(1)} custom-call(s32[2,2]{1,0:T(2,128)S(1)} %collective-permute-done.1.after_ref.pos_ref.first_ref, f32[1,2,128,2048]{3,2,1,0:T(8,128)S(1)} %get-tuple-element.12.own_ref.strip_ref, f32[2,2,128,256]{3,2,1,0:T(8,128)S(1)} %cut_second_one.1.after_ref), custom_call_target="tpu_custom_call" | custom-call | bytes 1048576 | tf_op jit(solution)/shard_map/cut_first_one/pallas_call | solution.py:333
  21.3 1.3 %collective-permute-start.8 = (f32[2,2,128,256]{3,2,1,0:T(8,128)S(1)}, f32[2,2,128,256]{3,2,1,0:T(8,128)S(1)}, u32[]{:S(2)}, u32[]{:S(2)}) collective-permute-start(f32[2,2,128,256]{3,2,1,0:T(8,128)S(1)} %cut_first_one.1), channel_id=1, source_target_pairs={{128,1},{129,0},{130,3},{131,2},{132,5},{133,4},{134,7},{135,6},{1... | collective-permute-start | bytes 1572872 | tf_op jit(solution)/shard_map/ppermute | solution.py:300
  22.6 1.3 %collective-permute-start.7 = (f32[2,2,128,256]{3,2,1,0:T(8,128)S(1)}, f32[2,2,128,256]{3,2,1,0:T(8,128)S(1)}, u32[]{:S(2)}, u32[]{:S(2)}) collective-permute-start(f32[2,2,128,256]{3,2,1,0:T(8,128)S(1)} %cut_second_one.1.after_ref), channel_id=1, source_target_pairs={{129,2},{130,1},{131,4},{132,3},{133,6},{134,5},{135,8},{136,7},{1... | collective-permute-start | bytes 1572872 | tf_op jit(solution)/shard_map/ppermute | solution.py:300
  24.6 1.4 %collective-permute-start.3 = (s32[2,2]{1,0:T(2,128)S(1)}, s32[2,2]{1,0:T(2,128)S(1)}, u32[]{:S(2)}, u32[]{:S(2)}) collective-permute-start(s32[2,2]{1,0:T(2,128)S(1)} %collective-permute-done.1.after_ref.pos_ref.first_ref), channel_id=1, source_target_pairs={{128,0},{129,1},{130,2},{131,3},{132,4},{133,5},{134,6},{135,7},{1... | collective-permute-start | bytes 56 | tf_op jit(solution)/shard_map/ppermute | solution.py:300
  26.0 0.8 %collective-permute-done.3.first_copy_ref = s32[2,2]{1,0:T(2,128)S(1)} collective-permute-done((s32[2,2]{1,0:T(2,128)S(1)}, s32[2,2]{1,0:T(2,128)S(1)}, u32[]{:S(2)}, u32[]{:S(2)}) %collective-permute-start.3) | collective-permute-done | bytes 48 | tf_op jit(solution)/shard_map/ppermute | solution.py:300
  26.8 2.2 %collective-permute-start.2 = (s32[2,2]{1,0:T(2,128)S(1)}, s32[2,2]{1,0:T(2,128)S(1)}, u32[]{:S(2)}, u32[]{:S(2)}) collective-permute-start(s32[2,2]{1,0:T(2,128)S(1)} %collective-permute-done.pos_ref.second_ref), channel_id=1, source_target_pairs={{128,0},{129,1},{130,2},{131,3},{132,4},{133,5},{134,6},{135,7},{1... | collective-permute-start | bytes 56 | tf_op jit(solution)/shard_map/ppermute | solution.py:300
  29.0 0.8 %collective-permute-done.2.second_copy_ref = s32[2,2]{1,0:T(2,128)S(1)} collective-permute-done((s32[2,2]{1,0:T(2,128)S(1)}, s32[2,2]{1,0:T(2,128)S(1)}, u32[]{:S(2)}, u32[]{:S(2)}) %collective-permute-start.2) | collective-permute-done | bytes 48 | tf_op jit(solution)/shard_map/ppermute | solution.py:300
  29.9 0.6 enter.1.wave_ref
  30.5 1.1 %collective-permute-done.7.second_ref = f32[2,2,128,256]{3,2,1,0:T(8,128)S(1)} collective-permute-done((f32[2,2,128,256]{3,2,1,0:T(8,128)S(1)}, f32[2,2,128,256]{3,2,1,0:T(8,128)S(1)}, u32[]{:S(2)}, u32[]{:S(2)}) %collective-permute-start.7) | collective-permute-done | bytes 524320 | tf_op jit(solution)/shard_map/ppermute | solution.py:300
  31.6 0.6 slot.1
  32.1 1.3 %collective-permute-start.9 = (f32[2,2,128,256]{3,2,1,0:T(8,128)S(1)}, f32[2,2,128,256]{3,2,1,0:T(8,128)S(1)}, u32[]{:S(2)}, u32[]{:S(2)}) collective-permute-start(f32[2,2,128,256]{3,2,1,0:T(8,128)S(1)} %get-tuple-element.14), channel_id=1, source_target_pairs={{1,130},{2,129},{3,132},{4,131},{5,134},{6,133},{7,136},{8,135},{9... | collective-permute-start | bytes 1572872 | tf_op jit(solution)/shard_map/ppermute | solution.py:300
  33.4 1.3 %collective-permute-start.11 = (f32[2,2,128,256]{3,2,1,0:T(8,128)S(1)}, f32[2,2,128,256]{3,2,1,0:T(8,128)S(1)}, u32[]{:S(2)}, u32[]{:S(2)}) collective-permute-start(f32[2,2,128,256]{3,2,1,0:T(8,128)S(1)} %get-tuple-element.14), channel_id=1, source_target_pairs={{0,129},{1,128},{2,131},{3,130},{4,133},{5,132},{6,135},{7,134},{8... | collective-permute-start | bytes 1572872 | tf_op jit(solution)/shard_map/ppermute | solution.py:300
  34.7 1.3 %collective-permute-start.13 = (f32[2,2,128,256]{3,2,1,0:T(8,128)S(1)}, f32[2,2,128,256]{3,2,1,0:T(8,128)S(1)}, u32[]{:S(2)}, u32[]{:S(2)}) collective-permute-start(f32[2,2,128,256]{3,2,1,0:T(8,128)S(1)} %get-tuple-element.15), channel_id=1, source_target_pairs={{1,130},{2,129},{3,132},{4,131},{5,134},{6,133},{7,136},{8,135},{9... | collective-permute-start | bytes 1572872 | tf_op jit(solution)/shard_map/ppermute | solution.py:300
  36.0 1.3 %collective-permute-start.14 = (f32[2,2,128,256]{3,2,1,0:T(8,128)S(1)}, f32[2,2,128,256]{3,2,1,0:T(8,128)S(1)}, u32[]{:S(2)}, u32[]{:S(2)}) collective-permute-start(f32[2,2,128,256]{3,2,1,0:T(8,128)S(1)} %get-tuple-element.15), channel_id=1, source_target_pairs={{0,129},{1,128},{2,131},{3,130},{4,133},{5,132},{6,135},{7,134},{8... | collective-permute-start | bytes 1572872 | tf_op jit(solution)/shard_map/ppermute | solution.py:300
  37.3 1.3 %collective-permute-start.15 = (f32[2,2,128,256]{3,2,1,0:T(8,128)S(1)}, f32[2,2,128,256]{3,2,1,0:T(8,128)S(1)}, u32[]{:S(2)}, u32[]{:S(2)}) collective-permute-start(f32[2,2,128,256]{3,2,1,0:T(8,128)S(1)} %get-tuple-element.16), channel_id=1, source_target_pairs={{0,128},{1,129},{2,130},{3,131},{4,132},{5,133},{6,134},{7,135},{8... | collective-permute-start | bytes 1572872 | tf_op jit(solution)/shard_map/ppermute | solution.py:300
  38.6 15.3 %collective-permute-done.9 = f32[2,2,128,256]{3,2,1,0:T(8,128)S(1)} collective-permute-done((f32[2,2,128,256]{3,2,1,0:T(8,128)S(1)}, f32[2,2,128,256]{3,2,1,0:T(8,128)S(1)}, u32[]{:S(2)}, u32[]{:S(2)}) %collective-permute-start.9) | collective-permute-done | bytes 524320 | tf_op jit(solution)/shard_map/ppermute | solution.py:300
  53.9 1.3 %collective-permute-start.10 = (f32[2,2,128,256]{3,2,1,0:T(8,128)S(1)}, f32[2,2,128,256]{3,2,1,0:T(8,128)S(1)}, u32[]{:S(2)}, u32[]{:S(2)}) collective-permute-start(f32[2,2,128,256]{3,2,1,0:T(8,128)S(1)} %collective-permute-done.9), channel_id=1, source_target_pairs={{128,0},{129,1},{130,2},{131,3},{132,4},{133,5},{134,6},{135,7},{1... | collective-permute-start | bytes 1572872 | tf_op jit(solution)/shard_map/ppermute | solution.py:300
  55.2 1.3 %collective-permute-start.12 = (f32[2,2,128,256]{3,2,1,0:T(8,128)S(1)}, f32[2,2,128,256]{3,2,1,0:T(8,128)S(1)}, u32[]{:S(2)}, u32[]{:S(2)}) collective-permute-start(f32[2,2,128,256]{3,2,1,0:T(8,128)S(1)} %collective-permute-done.11), channel_id=1, source_target_pairs={{128,0},{129,1},{130,2},{131,3},{132,4},{133,5},{134,6},{135,7},{1... | collective-permute-start | bytes 1572872 | tf_op jit(solution)/shard_map/ppermute | solution.py:300
  56.6 3.0 %collective-permute-done.13.second_one_ref = f32[2,2,128,256]{3,2,1,0:T(8,128)S(1)} collective-permute-done((f32[2,2,128,256]{3,2,1,0:T(8,128)S(1)}, f32[2,2,128,256]{3,2,1,0:T(8,128)S(1)}, u32[]{:S(2)}, u32[]{:S(2)}) %collective-permute-start.13) | collective-permute-done | bytes 524320 | tf_op jit(solution)/shard_map/ppermute | solution.py:300
  59.6 2.6 %collect.1 = f32[1,2,128,2048]{3,2,1,0:T(8,128)} custom-call(s32[2,2]{1,0:T(2,128)S(1)} %copy-done.5, s32[2,2]{1,0:T(2,128)S(1)} %collective-permute-done.pos_ref.second_ref, s32[2,2]{1,0:T(2,128)S(1)} %collective-permute-done.1.after_ref.pos_ref.first_ref, s32[2,2]{1,0:T(2,128)S(1)} %collective-permute-done.2.second_copy_ref, ...), custom_call_target="tpu_custom_call" | custom-call | bytes 4194304 | tf_op jit(solution)/shard_map/collect/pallas_call | solution.py:369
  (20 shorter events, 0.1 us)
Async XLA Ops:
  0.0 15.9 %collective-permute-start.4 = (f32[1,2,128,2048]{3,2,1,0:T(8,128)}, f32[1,2,128,2048]{3,2,1,0:T(8,128)S(1)}, u32[]{:S(2)}, u32[]{:S(2)}) collective-permute-start(f32[1,2,128,2048]{3,2,1,0:T(8,128)} %strip_ref.1), channel_id=1, source_target_pairs={{0,128},{128,0},{1,129},{129,1},{2,130},{130,2},{3,131},{131,3},{4... | collective-permute-start | bytes 6291464 | tf_op jit(solution)/shard_map/ppermute | solution.py:318
  0.7 15.2 %collective-permute-start = (s32[2,2]{1,0:T(2,128)}, s32[2,2]{1,0:T(2,128)S(1)}, u32[]{:S(2)}, u32[]{:S(2)}) collective-permute-start(s32[2,2]{1,0:T(2,128)} %pos_ref.7), channel_id=1, source_target_pairs={{129,130},{130,129},{131,132},{132,131},{133,134},{134,133},{135,1... | collective-permute-start | bytes 56 | tf_op jit(solution)/shard_map/ppermute | solution.py:300
  8.0 1.6 %copy-start.1 = (f32[1,2,128,2048]{3,2,1,0:T(8,128)S(1)}, f32[1,2,128,2048]{3,2,1,0:T(8,128)}, u32[]{:S(2)}) copy-start(f32[1,2,128,2048]{3,2,1,0:T(8,128)} %strip_ref.1) | copy-start | bytes 6291460
  9.5 0.7 %copy-start.4 = (s32[2,2]{1,0:T(2,128)S(1)}, s32[2,2]{1,0:T(2,128)}, u32[]{:S(2)}) copy-start(s32[2,2]{1,0:T(2,128)} %pos_ref.7) | copy-start | bytes 52
  11.5 4.3 %collective-permute-start.1 = (s32[2,2]{1,0:T(2,128)S(1)}, s32[2,2]{1,0:T(2,128)S(1)}, u32[]{:S(2)}, u32[]{:S(2)}) collective-permute-start(s32[2,2]{1,0:T(2,128)S(1)} %get-tuple-element.11), channel_id=1, source_target_pairs={{128,129},{129,128},{130,131},{131,130},{132,133},{133,132},{134,1... | collective-permute-start | bytes 56 | tf_op jit(solution)/shard_map/ppermute | solution.py:300
  17.2 12.6 %collective-permute-start.6 = (f32[2,2,128,256]{3,2,1,0:T(8,128)S(1)}, f32[2,2,128,256]{3,2,1,0:T(8,128)S(1)}, u32[]{:S(2)}, u32[]{:S(2)}) collective-permute-start(f32[2,2,128,256]{3,2,1,0:T(8,128)S(1)} %cut_first_zero.1.after_ref), channel_id=1, source_target_pairs={{128,1},{129,0},{130,3},{131,2},{132,5},{133,4},{134,7},{135,6},{1... | collective-permute-start | bytes 1572872 | tf_op jit(solution)/shard_map/ppermute | solution.py:300
  18.5 11.3 %collective-permute-start.5 = (f32[2,2,128,256]{3,2,1,0:T(8,128)S(1)}, f32[2,2,128,256]{3,2,1,0:T(8,128)S(1)}, u32[]{:S(2)}, u32[]{:S(2)}) collective-permute-start(f32[2,2,128,256]{3,2,1,0:T(8,128)S(1)} %cut_second_zero.1.after_ref), channel_id=1, source_target_pairs={{129,2},{130,1},{131,4},{132,3},{133,6},{134,5},{135,8},{136,7},{1... | collective-permute-start | bytes 1572872 | tf_op jit(solution)/shard_map/ppermute | solution.py:300
  20.5 9.3 %copy-start = (bf16[2,6,256,256]{3,2,1,0:T(8,128)(2,1)S(1)}, bf16[2,6,256,256]{3,2,1,0:T(8,128)(2,1)}, u32[]{:S(2)}) copy-start(bf16[2,6,256,256]{3,2,1,0:T(8,128)(2,1)} %constant.2.clone.table_ref) | copy-start | bytes 4718596
  20.6 9.3 %copy-start.2 = (f32[2,256,256]{2,1,0:T(8,128)S(1)}, f32[2,256,256]{2,1,0:T(8,128)}, u32[]{:S(2)}) copy-start(f32[2,256,256]{2,1,0:T(8,128)} %probe_ref.1) | copy-start | bytes 1572868
  20.6 9.3 %copy-start.5 = (s32[2,2]{1,0:T(2,128)S(1)}, s32[2,2]{1,0:T(2,128)}, u32[]{:S(2)}) copy-start(s32[2,2]{1,0:T(2,128)} %pos_ref.7) | copy-start | bytes 52
  21.3 9.2 %collective-permute-start.8 = (f32[2,2,128,256]{3,2,1,0:T(8,128)S(1)}, f32[2,2,128,256]{3,2,1,0:T(8,128)S(1)}, u32[]{:S(2)}, u32[]{:S(2)}) collective-permute-start(f32[2,2,128,256]{3,2,1,0:T(8,128)S(1)} %cut_first_one.1), channel_id=1, source_target_pairs={{128,1},{129,0},{130,3},{131,2},{132,5},{133,4},{134,7},{135,6},{1... | collective-permute-start | bytes 1572872 | tf_op jit(solution)/shard_map/ppermute | solution.py:300
  22.6 9.0 %collective-permute-start.7 = (f32[2,2,128,256]{3,2,1,0:T(8,128)S(1)}, f32[2,2,128,256]{3,2,1,0:T(8,128)S(1)}, u32[]{:S(2)}, u32[]{:S(2)}) collective-permute-start(f32[2,2,128,256]{3,2,1,0:T(8,128)S(1)} %cut_second_one.1.after_ref), channel_id=1, source_target_pairs={{129,2},{130,1},{131,4},{132,3},{133,6},{134,5},{135,8},{136,7},{1... | collective-permute-start | bytes 1572872 | tf_op jit(solution)/shard_map/ppermute | solution.py:300
  24.6 7.0 %copy-start.3 = (f32[2,256,256]{2,1,0:T(8,128)S(1)}, f32[2,256,256]{2,1,0:T(8,128)}, u32[]{:S(2)}) copy-start(f32[2,256,256]{2,1,0:T(8,128)} %intensity_ref.1) | copy-start | bytes 1572868
  24.6 2.2 %collective-permute-start.3 = (s32[2,2]{1,0:T(2,128)S(1)}, s32[2,2]{1,0:T(2,128)S(1)}, u32[]{:S(2)}, u32[]{:S(2)}) collective-permute-start(s32[2,2]{1,0:T(2,128)S(1)} %collective-permute-done.1.after_ref.pos_ref.first_ref), channel_id=1, source_target_pairs={{128,0},{129,1},{130,2},{131,3},{132,4},{133,5},{134,6},{135,7},{1... | collective-permute-start | bytes 56 | tf_op jit(solution)/shard_map/ppermute | solution.py:300
  26.8 3.0 %collective-permute-start.2 = (s32[2,2]{1,0:T(2,128)S(1)}, s32[2,2]{1,0:T(2,128)S(1)}, u32[]{:S(2)}, u32[]{:S(2)}) collective-permute-start(s32[2,2]{1,0:T(2,128)S(1)} %collective-permute-done.pos_ref.second_ref), channel_id=1, source_target_pairs={{128,0},{129,1},{130,2},{131,3},{132,4},{133,5},{134,6},{135,7},{1... | collective-permute-start | bytes 56 | tf_op jit(solution)/shard_map/ppermute | solution.py:300
  32.1 21.8 %collective-permute-start.9 = (f32[2,2,128,256]{3,2,1,0:T(8,128)S(1)}, f32[2,2,128,256]{3,2,1,0:T(8,128)S(1)}, u32[]{:S(2)}, u32[]{:S(2)}) collective-permute-start(f32[2,2,128,256]{3,2,1,0:T(8,128)S(1)} %get-tuple-element.14), channel_id=1, source_target_pairs={{1,130},{2,129},{3,132},{4,131},{5,134},{6,133},{7,136},{8,135},{9... | collective-permute-start | bytes 1572872 | tf_op jit(solution)/shard_map/ppermute | solution.py:300
  33.4 21.8 %collective-permute-start.11 = (f32[2,2,128,256]{3,2,1,0:T(8,128)S(1)}, f32[2,2,128,256]{3,2,1,0:T(8,128)S(1)}, u32[]{:S(2)}, u32[]{:S(2)}) collective-permute-start(f32[2,2,128,256]{3,2,1,0:T(8,128)S(1)} %get-tuple-element.14), channel_id=1, source_target_pairs={{0,129},{1,128},{2,131},{3,130},{4,133},{5,132},{6,135},{7,134},{8... | collective-permute-start | bytes 1572872 | tf_op jit(solution)/shard_map/ppermute | solution.py:300
  34.7 24.8 %collective-permute-start.13 = (f32[2,2,128,256]{3,2,1,0:T(8,128)S(1)}, f32[2,2,128,256]{3,2,1,0:T(8,128)S(1)}, u32[]{:S(2)}, u32[]{:S(2)}) collective-permute-start(f32[2,2,128,256]{3,2,1,0:T(8,128)S(1)} %get-tuple-element.15), channel_id=1, source_target_pairs={{1,130},{2,129},{3,132},{4,131},{5,134},{6,133},{7,136},{8,135},{9... | collective-permute-start | bytes 1572872 | tf_op jit(solution)/shard_map/ppermute | solution.py:300
  36.0 23.5 %collective-permute-start.14 = (f32[2,2,128,256]{3,2,1,0:T(8,128)S(1)}, f32[2,2,128,256]{3,2,1,0:T(8,128)S(1)}, u32[]{:S(2)}, u32[]{:S(2)}) collective-permute-start(f32[2,2,128,256]{3,2,1,0:T(8,128)S(1)} %get-tuple-element.15), channel_id=1, source_target_pairs={{0,129},{1,128},{2,131},{3,130},{4,133},{5,132},{6,135},{7,134},{8... | collective-permute-start | bytes 1572872 | tf_op jit(solution)/shard_map/ppermute | solution.py:300
  37.3 22.2 %collective-permute-start.15 = (f32[2,2,128,256]{3,2,1,0:T(8,128)S(1)}, f32[2,2,128,256]{3,2,1,0:T(8,128)S(1)}, u32[]{:S(2)}, u32[]{:S(2)}) collective-permute-start(f32[2,2,128,256]{3,2,1,0:T(8,128)S(1)} %get-tuple-element.16), channel_id=1, source_target_pairs={{0,128},{1,129},{2,130},{3,131},{4,132},{5,133},{6,134},{7,135},{8... | collective-permute-start | bytes 1572872 | tf_op jit(solution)/shard_map/ppermute | solution.py:300
  53.9 5.6 %collective-permute-start.10 = (f32[2,2,128,256]{3,2,1,0:T(8,128)S(1)}, f32[2,2,128,256]{3,2,1,0:T(8,128)S(1)}, u32[]{:S(2)}, u32[]{:S(2)}) collective-permute-start(f32[2,2,128,256]{3,2,1,0:T(8,128)S(1)} %collective-permute-done.9), channel_id=1, source_target_pairs={{128,0},{129,1},{130,2},{131,3},{132,4},{133,5},{134,6},{135,7},{1... | collective-permute-start | bytes 1572872 | tf_op jit(solution)/shard_map/ppermute | solution.py:300
  55.2 4.3 %collective-permute-start.12 = (f32[2,2,128,256]{3,2,1,0:T(8,128)S(1)}, f32[2,2,128,256]{3,2,1,0:T(8,128)S(1)}, u32[]{:S(2)}, u32[]{:S(2)}) collective-permute-start(f32[2,2,128,256]{3,2,1,0:T(8,128)S(1)} %collective-permute-done.11), channel_id=1, source_target_pairs={{128,0},{129,1},{130,2},{131,3},{132,4},{133,5},{134,6},{135,7},{1... | collective-permute-start | bytes 1572872 | tf_op jit(solution)/shard_map/ppermute | solution.py:300

commit v5 on v4

--- a/solution.py
+++ b/solution.py
@@ -84,20 +84,19 @@
         out_ref[part, :, HALF:WIN] = strip_ref[0, part, :, block(first + 1)]
 
 
-def stage_kernel(pos_ref, strip_ref, pos_out_ref, out_ref, sem):
+def stage_kernel(strip_ref, out_ref, sem):
     copy = pltpu.make_async_copy(strip_ref, out_ref, sem)
     copy.start()
-    for slot in range(2):
-        for entry in range(2):
-            pos_out_ref[slot, entry] = pos_ref[slot, entry]
     copy.wait()
 
 
-def cut_kernel(pos_ref, strip_ref, after_ref, out_ref):
+def cut_kernel(first_ref, second_ref, strip_ref, to_first_ref, to_second_ref):
     @pl.when(lax.axis_index("cuts") == 1)
     def _():
         for slot in range(2):
-            cut_piece(strip_ref, pos_ref[slot, 1], out_ref.at[slot])
+            cut_piece(strip_ref, first_ref[slot, 1], to_first_ref.at[slot])
+        for slot in range(2):
+            cut_piece(strip_ref, second_ref[slot, 1], to_second_ref.at[slot])
 
 
 def slots_of_core(counts_ref):
@@ -110,7 +109,7 @@
     shift_rows = pos_ref[slot, 0] - (tile - 1) * HALF
     column = pos_ref[slot, 1]
     rows = lax.broadcasted_iota(jnp.int32, (HALF, WIN), 0)
-    from_first = (2 * odd - 1) * (rows - shift_rows) >= 1 - odd
+    from_first = (1 - 2 * odd) * (rows - shift_rows) >= odd
     for part in range(2):
         window_ref[part, 0:HALF] = jnp.where(
             from_first, first_ref[slot, part], second_ref[slot, part]
@@ -125,10 +124,10 @@
     probe_ref,
     table_ref,
     own_ref,
+    first_ref,
     second_ref,
-    first_ref,
+    first_copy_ref,
     second_copy_ref,
-    first_copy_ref,
     wave_ref,
     window_ref,
 ):
@@ -159,8 +158,8 @@
     table_ref,
     wave_ref,
     other_ref,
+    first_ref,
     second_ref,
-    first_ref,
     intensity_ref,
     rim_zero_ref,
     rim_one_ref,
@@ -229,15 +228,15 @@
 
 def collect_kernel(
     pos_ref,
+    first_ref,
     second_ref,
-    first_ref,
+    first_copy_ref,
     second_copy_ref,
-    first_copy_ref,
     mid_zero_ref,
+    first_zero_ref,
     second_zero_ref,
-    first_zero_ref,
+    first_one_ref,
     second_one_ref,
-    first_one_ref,
     mid_one_ref,
     out_ref,
 ):
@@ -261,16 +260,16 @@
     def _():
         gather(
             mid_zero_ref,
-            (second_zero_ref, second_copy_ref, odd),
-            (first_zero_ref, first_copy_ref, 1 - odd),
+            (first_zero_ref, first_copy_ref, odd),
+            (second_zero_ref, second_copy_ref, 1 - odd),
         )
 
     @pl.when(core == 1)
     def _():
         gather(
             mid_one_ref,
-            (second_one_ref, second_ref, odd),
-            (first_one_ref, first_ref, 1 - odd),
+            (first_one_ref, first_ref, odd),
+            (second_one_ref, second_ref, 1 - odd),
         )
 
 
@@ -286,10 +285,10 @@
     tiles = lax.axis_size("tile")
 
     def first(tile):
+        return ((tile + 1) ^ 1) - 1
+
+    def second(tile):
         return tile ^ 1
-
-    def second(tile):
-        return ((tile + 1) ^ 1) - 1
 
     def same(tile):
         return tile
@@ -316,28 +315,21 @@
     window = (pltpu.VMEM((2, WIN, WIN), jnp.float32),)
     tables = jnp.asarray(np.stack(build_tables()))
     other_slice = lax.ppermute(object_slices, "cuts", [(0, 1), (1, 0)])
+    pos_first = send(positions, 1, 1, first)
     pos_second = send(positions, 1, 1, second)
-    again, own_slice = kernel(
-        stage_kernel,
-        "stage",
-        (jax.ShapeDtypeStruct(positions.shape, positions.dtype), strip),
-        [SMEM, ANY],
-        0,
-        4 << 20,
-        (pltpu.SemaphoreType.DMA,),
-        (SMEM, VMEM),
-    )(positions, object_slices)
-    pos_first = send(again, 1, 1, first)
-
-    def cut(name, place, source, after):
-        return kernel(cut_kernel, name, pieces, [SMEM, VMEM, ANY], 0, 1 << 20)(place, source, after)
-
-    to_second_zero = cut("cut_second_zero", pos_second, other_slice, pos_first)
-    to_first_zero = cut("cut_first_zero", pos_first, other_slice, to_second_zero)
-    to_second_one = cut("cut_second_one", pos_second, own_slice, to_first_zero)
-    to_first_one = cut("cut_first_one", pos_first, own_slice, to_second_one)
+    own_slice = kernel(
+        stage_kernel, "stage", strip, [ANY], 0, 4 << 20, (pltpu.SemaphoreType.DMA,)
+    )(object_slices)
+
+    def cut(name, source):
+        return kernel(
+            cut_kernel, name, (pieces,) * 2, [SMEM] * 2 + [VMEM], 0, 2 << 20, (), (VMEM,) * 2
+        )(pos_first, pos_second, source)
+
+    to_first_zero, to_second_zero = cut("cut_zero", other_slice)
     second_zero = send(to_second_zero, 1, 0, second)
     first_zero = send(to_first_zero, 1, 0, first)
+    to_first_one, to_second_one = cut("cut_one", own_slice)
     second_one = send(to_second_one, 1, 0, second)
     first_one = send(to_first_one, 1, 0, first)
     second_copy = send(pos_second, 1, 0, same)
@@ -350,7 +342,7 @@
         18 * 2 * WIN**3,
         3 << 20,
         window,
-    )(positions, counts, probe, tables, own_slice, second_zero, first_zero, second_copy, first_copy)
+    )(positions, counts, probe, tables, own_slice, first_zero, second_zero, first_copy, second_copy)
     rim_zero, rim_one, mid_zero, mid_one = kernel(
         slot_kernel,
         "slot",
@@ -360,23 +352,23 @@
         6 << 20,
         window,
         (VMEM,) * 4,
-    )(positions, counts, tables, wave, other_slice, second_one, first_one, intensity)
+    )(positions, counts, tables, wave, other_slice, first_one, second_one, intensity)
+    back_first_zero = send(rim_zero, 0, 1, first)
     back_second_zero = send(rim_zero, 0, 1, second)
-    back_first_zero = send(rim_zero, 0, 1, first)
+    back_first_one = send(rim_one, 0, 1, first)
     back_second_one = send(rim_one, 0, 1, second)
-    back_first_one = send(rim_one, 0, 1, first)
     mid_one = send(mid_one, 0, 1, same)
     return kernel(collect_kernel, "collect", strip, [SMEM] * 5 + [VMEM] * 6, 0, 4 << 20)(
         positions,
+        pos_first,
         pos_second,
-        pos_first,
+        first_copy,
         second_copy,
-        first_copy,
         mid_zero,
+        send(back_first_zero, 1, 0, same),
         send(back_second_zero, 1, 0, same),
-        send(back_first_zero, 1, 0, same),
+        back_first_one,
         back_second_one,
-        back_first_one,
         mid_one,
     )
 

time: 61 us -> 54.1 us (0.89)
  the two profiles are of different devices: /device:TPU:225 before, /device:TPU:129 now
where the time goes in v5:
time: 54.1 us; the launch traced here: 53.7 us
  starting transfers between devices  27 us (50%)
  waiting for transfers between devices  20.4 us (38%)
  Pallas kernels  5.4 us (10%)
  between operations  0.89 us (2%)
    ppermute x15, starting transfers between devices, send(): return lax.ppermute(value, ('cuts', 'tile'), pairs)  26.3 us
    ppermute x15, waiting for transfers between devices, send(): return lax.ppermute(value, ('cuts', 'tile'), pairs)  20.4 us
    pallas_call x1, Pallas kernels, local(): kernel(collect_kernel, 'collect', strip, [SMEM] * 5 + [VMEM] * 6, 0, 4 <<...  2.56 us
    pallas_call x2, Pallas kernels, cut(): kernel(cut_kernel, name, (pieces,) * 2, [SMEM] * 2 + [VMEM], 0, 2 << 20,...  1.56 us
  transfers between devices with their start and end apart: 16, of which 8 were waited for; matrix products, arithmetic and copies ran while one was open for 0% of the time, Pallas kernels for 3%

profile of v5, /device:TPU:129, one launch (start us, length us, event | category | flops | bytes accessed | tf_op | source)
XLA Modules:
  0.0 53.7 jit_solution(1496251941466658069)
XLA Ops:
  0.0 0.7 %collective-permute-start.4 = (f32[1,2,128,2048]{3,2,1,0:T(8,128)}, f32[1,2,128,2048]{3,2,1,0:T(8,128)S(1)}, u32[]{:S(2)}, u32[]{:S(2)}) collective-permute-start(f32[1,2,128,2048]{3,2,1,0:T(8,128)} %strip_ref.1), channel_id=1, source_target_pairs={{0,128},{128,0},{1,129},{129,1},{2,130},{130,2},{3,131},{131,3},{4... | collective-permute-start | bytes 6291464 | tf_op jit(solution)/shard_map/ppermute | solution.py:317
  0.7 6.4 %collective-permute-start = (s32[2,2]{1,0:T(2,128)}, s32[2,2]{1,0:T(2,128)S(1)}, u32[]{:S(2)}, u32[]{:S(2)}) collective-permute-start(s32[2,2]{1,0:T(2,128)} %pos_ref.5), channel_id=1, source_target_pairs={{129,130},{130,129},{131,132},{132,131},{133,134},{134,133},{135,1... | collective-permute-start | bytes 56 | tf_op jit(solution)/shard_map/ppermute | solution.py:299
  7.1 1.9 %collective-permute-start.1 = (s32[2,2]{1,0:T(2,128)}, s32[2,2]{1,0:T(2,128)S(1)}, u32[]{:S(2)}, u32[]{:S(2)}) collective-permute-start(s32[2,2]{1,0:T(2,128)} %pos_ref.5), channel_id=1, source_target_pairs={{128,129},{129,128},{130,131},{131,130},{132,133},{133,132},{134,1... | collective-permute-start | bytes 56 | tf_op jit(solution)/shard_map/ppermute | solution.py:299
  9.0 1.6 %collective-permute-done.first_ref = s32[2,2]{1,0:T(2,128)S(1)} collective-permute-done((s32[2,2]{1,0:T(2,128)}, s32[2,2]{1,0:T(2,128)S(1)}, u32[]{:S(2)}, u32[]{:S(2)}) %collective-permute-start) | collective-permute-done | bytes 48 | tf_op jit(solution)/shard_map/ppermute | solution.py:299
  10.6 1.0 %collective-permute-done.1.second_ref = s32[2,2]{1,0:T(2,128)S(1)} collective-permute-done((s32[2,2]{1,0:T(2,128)}, s32[2,2]{1,0:T(2,128)S(1)}, u32[]{:S(2)}, u32[]{:S(2)}) %collective-permute-start.1) | collective-permute-done | bytes 48 | tf_op jit(solution)/shard_map/ppermute | solution.py:299
  11.6 0.8 %cut_zero.1 = (f32[2,2,128,256]{3,2,1,0:T(8,128)S(1)}, f32[2,2,128,256]{3,2,1,0:T(8,128)S(1)}) custom-call(s32[2,2]{1,0:T(2,128)S(1)} %collective-permute-done.first_ref, s32[2,2]{1,0:T(2,128)S(1)} %collective-permute-done.1.second_ref, f32[1,2,128,2048]{3,2,1,0:T(8,128)S(1)} %collective-permute-done.4.strip_ref.other_ref), custom_call_target="tpu_custom_call" | custom-call | bytes 2097152 | tf_op jit(solution)/shard_map/cut_zero/pallas_call | solution.py:325
  12.4 1.3 %collective-permute-start.5 = (f32[2,2,128,256]{3,2,1,0:T(8,128)S(1)}, f32[2,2,128,256]{3,2,1,0:T(8,128)S(1)}, u32[]{:S(2)}, u32[]{:S(2)}) collective-permute-start(f32[2,2,128,256]{3,2,1,0:T(8,128)S(1)} %get-tuple-element.13), channel_id=1, source_target_pairs={{129,2},{130,1},{131,4},{132,3},{133,6},{134,5},{135,8},{136,7},{1... | collective-permute-start | bytes 1572872 | tf_op jit(solution)/shard_map/ppermute | solution.py:299
  13.7 1.3 %collective-permute-start.6 = (f32[2,2,128,256]{3,2,1,0:T(8,128)S(1)}, f32[2,2,128,256]{3,2,1,0:T(8,128)S(1)}, u32[]{:S(2)}, u32[]{:S(2)}) collective-permute-start(f32[2,2,128,256]{3,2,1,0:T(8,128)S(1)} %get-tuple-element.14), channel_id=1, source_target_pairs={{128,1},{129,0},{130,3},{131,2},{132,5},{133,4},{134,7},{135,6},{1... | collective-permute-start | bytes 1572872 | tf_op jit(solution)/shard_map/ppermute | solution.py:299
  15.0 0.2 stage.1.own_ref.strip_ref
  15.2 0.0 copy-start
  15.2 0.0 copy-start.2
  15.2 0.8 %cut_one.1 = (f32[2,2,128,256]{3,2,1,0:T(8,128)S(1)}, f32[2,2,128,256]{3,2,1,0:T(8,128)S(1)}) custom-call(s32[2,2]{1,0:T(2,128)S(1)} %collective-permute-done.first_ref, s32[2,2]{1,0:T(2,128)S(1)} %collective-permute-done.1.second_ref, f32[1,2,128,2048]{3,2,1,0:T(8,128)S(1)} %stage.1.own_ref.strip_ref), custom_call_target="tpu_custom_call" | custom-call | bytes 2097152 | tf_op jit(solution)/shard_map/cut_one/pallas_call | solution.py:325
  16.0 1.3 %collective-permute-start.7 = (f32[2,2,128,256]{3,2,1,0:T(8,128)S(1)}, f32[2,2,128,256]{3,2,1,0:T(8,128)S(1)}, u32[]{:S(2)}, u32[]{:S(2)}) collective-permute-start(f32[2,2,128,256]{3,2,1,0:T(8,128)S(1)} %get-tuple-element.15), channel_id=1, source_target_pairs={{129,2},{130,1},{131,4},{132,3},{133,6},{134,5},{135,8},{136,7},{1... | collective-permute-start | bytes 1572872 | tf_op jit(solution)/shard_map/ppermute | solution.py:299
  17.4 1.3 %collective-permute-start.8 = (f32[2,2,128,256]{3,2,1,0:T(8,128)S(1)}, f32[2,2,128,256]{3,2,1,0:T(8,128)S(1)}, u32[]{:S(2)}, u32[]{:S(2)}) collective-permute-start(f32[2,2,128,256]{3,2,1,0:T(8,128)S(1)} %get-tuple-element.16), channel_id=1, source_target_pairs={{128,1},{129,0},{130,3},{131,2},{132,5},{133,4},{134,7},{135,6},{1... | collective-permute-start | bytes 1572872 | tf_op jit(solution)/shard_map/ppermute | solution.py:299
  19.4 1.4 %collective-permute-start.2 = (s32[2,2]{1,0:T(2,128)S(1)}, s32[2,2]{1,0:T(2,128)S(1)}, u32[]{:S(2)}, u32[]{:S(2)}) collective-permute-start(s32[2,2]{1,0:T(2,128)S(1)} %collective-permute-done.first_ref), channel_id=1, source_target_pairs={{128,0},{129,1},{130,2},{131,3},{132,4},{133,5},{134,6},{135,7},{1... | collective-permute-start | bytes 56 | tf_op jit(solution)/shard_map/ppermute | solution.py:299
  20.8 0.8 %collective-permute-done.2.first_copy_ref = s32[2,2]{1,0:T(2,128)S(1)} collective-permute-done((s32[2,2]{1,0:T(2,128)S(1)}, s32[2,2]{1,0:T(2,128)S(1)}, u32[]{:S(2)}, u32[]{:S(2)}) %collective-permute-start.2) | collective-permute-done | bytes 48 | tf_op jit(solution)/shard_map/ppermute | solution.py:299
  21.6 2.2 %collective-permute-start.3 = (s32[2,2]{1,0:T(2,128)S(1)}, s32[2,2]{1,0:T(2,128)S(1)}, u32[]{:S(2)}, u32[]{:S(2)}) collective-permute-start(s32[2,2]{1,0:T(2,128)S(1)} %collective-permute-done.1.second_ref), channel_id=1, source_target_pairs={{128,0},{129,1},{130,2},{131,3},{132,4},{133,5},{134,6},{135,7},{1... | collective-permute-start | bytes 56 | tf_op jit(solution)/shard_map/ppermute | solution.py:299
  23.8 0.8 %collective-permute-done.3.second_copy_ref = s32[2,2]{1,0:T(2,128)S(1)} collective-permute-done((s32[2,2]{1,0:T(2,128)S(1)}, s32[2,2]{1,0:T(2,128)S(1)}, u32[]{:S(2)}, u32[]{:S(2)}) %collective-permute-start.3) | collective-permute-done | bytes 48 | tf_op jit(solution)/shard_map/ppermute | solution.py:299
  24.6 0.6 %enter.1.wave_ref = f32[2,2,2,256,256]{4,3,2,1,0:T(8,128)S(1)} custom-call(s32[2,2]{1,0:T(2,128)S(1)} %copy-done.4, s32[1]{0:T(128)S(6)} %copy.7.counts_ref, f32[2,256,256]{2,1,0:T(8,128)S(1)} %copy-done.2, bf16[2,6,256,256]{3,2,1,0:T(8,128)(2,1)S(1)} %copy-done, f32[1,2,128,2048]{3,2,1,0:T(8,128)S(1)} %stage.1.own_ref.strip_ref, ...), custom_call_target="tpu_custom_call" | custom-call | flops 603979776 | bytes 3145728 | tf_op jit(solution)/shard_map/enter/pallas_call | solution.py:337
  25.2 0.2 collective-permute-done.7.first_ref
  25.4 1.3 %collective-permute-done.8.second_ref = f32[2,2,128,256]{3,2,1,0:T(8,128)S(1)} collective-permute-done((f32[2,2,128,256]{3,2,1,0:T(8,128)S(1)}, f32[2,2,128,256]{3,2,1,0:T(8,128)S(1)}, u32[]{:S(2)}, u32[]{:S(2)}) %collective-permute-start.8) | collective-permute-done | bytes 524320 | tf_op jit(solution)/shard_map/ppermute | solution.py:299
  26.7 0.6 %slot.1 = (f32[2,2,128,256]{3,2,1,0:T(8,128)S(1)}, f32[2,2,128,256]{3,2,1,0:T(8,128)S(1)}, f32[2,2,128,256]{3,2,1,0:T(8,128)S(1)}, f32[2,2,128,256]{3,2,1,0:T(8,128)S(1)}) custom-call(s32[2,2]{1,0:T(2,128)S(1)} %copy-done.4, s32[1]{0:T(128)S(6)} %copy.7.counts_ref, bf16[2,6,256,256]{3,2,1,0:T(8,128)(2,1)S(1)} %copy-done, ...), custom_call_target="tpu_custom_call" | custom-call | flops 1811939328 | bytes 6291456 | tf_op jit(solution)/shard_map/slot/pallas_call | solution.py:346
  27.3 1.3 %collective-permute-start.9 = (f32[2,2,128,256]{3,2,1,0:T(8,128)S(1)}, f32[2,2,128,256]{3,2,1,0:T(8,128)S(1)}, u32[]{:S(2)}, u32[]{:S(2)}) collective-permute-start(f32[2,2,128,256]{3,2,1,0:T(8,128)S(1)} %get-tuple-element.18), channel_id=1, source_target_pairs={{1,130},{2,129},{3,132},{4,131},{5,134},{6,133},{7,136},{8,135},{9... | collective-permute-start | bytes 1572872 | tf_op jit(solution)/shard_map/ppermute | solution.py:299
  28.6 1.3 %collective-permute-start.11 = (f32[2,2,128,256]{3,2,1,0:T(8,128)S(1)}, f32[2,2,128,256]{3,2,1,0:T(8,128)S(1)}, u32[]{:S(2)}, u32[]{:S(2)}) collective-permute-start(f32[2,2,128,256]{3,2,1,0:T(8,128)S(1)} %get-tuple-element.18), channel_id=1, source_target_pairs={{0,129},{1,128},{2,131},{3,130},{4,133},{5,132},{6,135},{7,134},{8... | collective-permute-start | bytes 1572872 | tf_op jit(solution)/shard_map/ppermute | solution.py:299
  29.9 1.3 %collective-permute-start.13 = (f32[2,2,128,256]{3,2,1,0:T(8,128)S(1)}, f32[2,2,128,256]{3,2,1,0:T(8,128)S(1)}, u32[]{:S(2)}, u32[]{:S(2)}) collective-permute-start(f32[2,2,128,256]{3,2,1,0:T(8,128)S(1)} %get-tuple-element.19), channel_id=1, source_target_pairs={{1,130},{2,129},{3,132},{4,131},{5,134},{6,133},{7,136},{8,135},{9... | collective-permute-start | bytes 1572872 | tf_op jit(solution)/shard_map/ppermute | solution.py:299
  31.2 1.3 %collective-permute-start.14 = (f32[2,2,128,256]{3,2,1,0:T(8,128)S(1)}, f32[2,2,128,256]{3,2,1,0:T(8,128)S(1)}, u32[]{:S(2)}, u32[]{:S(2)}) collective-permute-start(f32[2,2,128,256]{3,2,1,0:T(8,128)S(1)} %get-tuple-element.19), channel_id=1, source_target_pairs={{0,129},{1,128},{2,131},{3,130},{4,133},{5,132},{6,135},{7,134},{8... | collective-permute-start | bytes 1572872 | tf_op jit(solution)/shard_map/ppermute | solution.py:299
  32.5 1.3 %collective-permute-start.15 = (f32[2,2,128,256]{3,2,1,0:T(8,128)S(1)}, f32[2,2,128,256]{3,2,1,0:T(8,128)S(1)}, u32[]{:S(2)}, u32[]{:S(2)}) collective-permute-start(f32[2,2,128,256]{3,2,1,0:T(8,128)S(1)} %get-tuple-element.20), channel_id=1, source_target_pairs={{0,128},{1,129},{2,130},{3,131},{4,132},{5,133},{6,134},{7,135},{8... | collective-permute-start | bytes 1572872 | tf_op jit(solution)/shard_map/ppermute | solution.py:299
  33.8 11.7 %collective-permute-done.9 = f32[2,2,128,256]{3,2,1,0:T(8,128)S(1)} collective-permute-done((f32[2,2,128,256]{3,2,1,0:T(8,128)S(1)}, f32[2,2,128,256]{3,2,1,0:T(8,128)S(1)}, u32[]{:S(2)}, u32[]{:S(2)}) %collective-permute-start.9) | collective-permute-done | bytes 524320 | tf_op jit(solution)/shard_map/ppermute | solution.py:299
  45.5 1.3 %collective-permute-start.10 = (f32[2,2,128,256]{3,2,1,0:T(8,128)S(1)}, f32[2,2,128,256]{3,2,1,0:T(8,128)S(1)}, u32[]{:S(2)}, u32[]{:S(2)}) collective-permute-start(f32[2,2,128,256]{3,2,1,0:T(8,128)S(1)} %collective-permute-done.9), channel_id=1, source_target_pairs={{128,0},{129,1},{130,2},{131,3},{132,4},{133,5},{134,6},{135,7},{1... | collective-permute-start | bytes 1572872 | tf_op jit(solution)/shard_map/ppermute | solution.py:299
  46.9 1.3 %collective-permute-start.12 = (f32[2,2,128,256]{3,2,1,0:T(8,128)S(1)}, f32[2,2,128,256]{3,2,1,0:T(8,128)S(1)}, u32[]{:S(2)}, u32[]{:S(2)}) collective-permute-start(f32[2,2,128,256]{3,2,1,0:T(8,128)S(1)} %collective-permute-done.11), channel_id=1, source_target_pairs={{128,0},{129,1},{130,2},{131,3},{132,4},{133,5},{134,6},{135,7},{1... | collective-permute-start | bytes 1572872 | tf_op jit(solution)/shard_map/ppermute | solution.py:299
  48.2 3.0 %collective-permute-done.13.first_one_ref = f32[2,2,128,256]{3,2,1,0:T(8,128)S(1)} collective-permute-done((f32[2,2,128,256]{3,2,1,0:T(8,128)S(1)}, f32[2,2,128,256]{3,2,1,0:T(8,128)S(1)}, u32[]{:S(2)}, u32[]{:S(2)}) %collective-permute-start.13) | collective-permute-done | bytes 524320 | tf_op jit(solution)/shard_map/ppermute | solution.py:299
  51.2 2.6 %collect.1 = f32[1,2,128,2048]{3,2,1,0:T(8,128)} custom-call(s32[2,2]{1,0:T(2,128)S(1)} %copy-done.4, s32[2,2]{1,0:T(2,128)S(1)} %collective-permute-done.first_ref, s32[2,2]{1,0:T(2,128)S(1)} %collective-permute-done.1.second_ref, s32[2,2]{1,0:T(2,128)S(1)} %collective-permute-done.2.first_copy_ref, s32[2,2]{1,0:T(2,128)S(1)} %collective-permute-done.3.second_copy_ref, ...), custom_call_target="tpu_custom_call" | custom-call | bytes 4194304 | tf_op jit(solution)/shard_map/collect/pallas_call | solution.py:361
  (16 shorter events, 0.0 us)
Async XLA Ops:
  0.0 15.0 %copy-start.1 = (f32[1,2,128,2048]{3,2,1,0:T(8,128)S(1)}, f32[1,2,128,2048]{3,2,1,0:T(8,128)}, u32[]{:S(2)}) copy-start(f32[1,2,128,2048]{3,2,1,0:T(8,128)} %strip_ref.1) | copy-start | bytes 6291460
  0.0 11.6 %collective-permute-start.4 = (f32[1,2,128,2048]{3,2,1,0:T(8,128)}, f32[1,2,128,2048]{3,2,1,0:T(8,128)S(1)}, u32[]{:S(2)}, u32[]{:S(2)}) collective-permute-start(f32[1,2,128,2048]{3,2,1,0:T(8,128)} %strip_ref.1), channel_id=1, source_target_pairs={{0,128},{128,0},{1,129},{129,1},{2,130},{130,2},{3,131},{131,3},{4... | collective-permute-start | bytes 6291464 | tf_op jit(solution)/shard_map/ppermute | solution.py:317
  0.7 9.9 %collective-permute-start = (s32[2,2]{1,0:T(2,128)}, s32[2,2]{1,0:T(2,128)S(1)}, u32[]{:S(2)}, u32[]{:S(2)}) collective-permute-start(s32[2,2]{1,0:T(2,128)} %pos_ref.5), channel_id=1, source_target_pairs={{129,130},{130,129},{131,132},{132,131},{133,134},{134,133},{135,1... | collective-permute-start | bytes 56 | tf_op jit(solution)/shard_map/ppermute | solution.py:299
  7.1 4.5 %collective-permute-start.1 = (s32[2,2]{1,0:T(2,128)}, s32[2,2]{1,0:T(2,128)S(1)}, u32[]{:S(2)}, u32[]{:S(2)}) collective-permute-start(s32[2,2]{1,0:T(2,128)} %pos_ref.5), channel_id=1, source_target_pairs={{128,129},{129,128},{130,131},{131,130},{132,133},{133,132},{134,1... | collective-permute-start | bytes 56 | tf_op jit(solution)/shard_map/ppermute | solution.py:299
  12.4 12.2 %collective-permute-start.5 = (f32[2,2,128,256]{3,2,1,0:T(8,128)S(1)}, f32[2,2,128,256]{3,2,1,0:T(8,128)S(1)}, u32[]{:S(2)}, u32[]{:S(2)}) collective-permute-start(f32[2,2,128,256]{3,2,1,0:T(8,128)S(1)} %get-tuple-element.13), channel_id=1, source_target_pairs={{129,2},{130,1},{131,4},{132,3},{133,6},{134,5},{135,8},{136,7},{1... | collective-permute-start | bytes 1572872 | tf_op jit(solution)/shard_map/ppermute | solution.py:299
  13.7 10.9 %collective-permute-start.6 = (f32[2,2,128,256]{3,2,1,0:T(8,128)S(1)}, f32[2,2,128,256]{3,2,1,0:T(8,128)S(1)}, u32[]{:S(2)}, u32[]{:S(2)}) collective-permute-start(f32[2,2,128,256]{3,2,1,0:T(8,128)S(1)} %get-tuple-element.14), channel_id=1, source_target_pairs={{128,1},{129,0},{130,3},{131,2},{132,5},{133,4},{134,7},{135,6},{1... | collective-permute-start | bytes 1572872 | tf_op jit(solution)/shard_map/ppermute | solution.py:299
  15.2 9.4 %copy-start = (bf16[2,6,256,256]{3,2,1,0:T(8,128)(2,1)S(1)}, bf16[2,6,256,256]{3,2,1,0:T(8,128)(2,1)}, u32[]{:S(2)}) copy-start(bf16[2,6,256,256]{3,2,1,0:T(8,128)(2,1)} %constant.2.clone.table_ref) | copy-start | bytes 4718596
  15.2 9.4 %copy-start.2 = (f32[2,256,256]{2,1,0:T(8,128)S(1)}, f32[2,256,256]{2,1,0:T(8,128)}, u32[]{:S(2)}) copy-start(f32[2,256,256]{2,1,0:T(8,128)} %probe_ref.1) | copy-start | bytes 1572868
  15.2 9.4 %copy-start.4 = (s32[2,2]{1,0:T(2,128)S(1)}, s32[2,2]{1,0:T(2,128)}, u32[]{:S(2)}) copy-start(s32[2,2]{1,0:T(2,128)} %pos_ref.5) | copy-start | bytes 52
  16.0 9.4 %collective-permute-start.7 = (f32[2,2,128,256]{3,2,1,0:T(8,128)S(1)}, f32[2,2,128,256]{3,2,1,0:T(8,128)S(1)}, u32[]{:S(2)}, u32[]{:S(2)}) collective-permute-start(f32[2,2,128,256]{3,2,1,0:T(8,128)S(1)} %get-tuple-element.15), channel_id=1, source_target_pairs={{129,2},{130,1},{131,4},{132,3},{133,6},{134,5},{135,8},{136,7},{1... | collective-permute-start | bytes 1572872 | tf_op jit(solution)/shard_map/ppermute | solution.py:299
  17.4 9.4 %collective-permute-start.8 = (f32[2,2,128,256]{3,2,1,0:T(8,128)S(1)}, f32[2,2,128,256]{3,2,1,0:T(8,128)S(1)}, u32[]{:S(2)}, u32[]{:S(2)}) collective-permute-start(f32[2,2,128,256]{3,2,1,0:T(8,128)S(1)} %get-tuple-element.16), channel_id=1, source_target_pairs={{128,1},{129,0},{130,3},{131,2},{132,5},{133,4},{134,7},{135,6},{1... | collective-permute-start | bytes 1572872 | tf_op jit(solution)/shard_map/ppermute | solution.py:299
  19.3 7.4 %copy-start.3 = (f32[2,256,256]{2,1,0:T(8,128)S(1)}, f32[2,256,256]{2,1,0:T(8,128)}, u32[]{:S(2)}) copy-start(f32[2,256,256]{2,1,0:T(8,128)} %intensity_ref.1) | copy-start | bytes 1572868
  19.4 2.2 %collective-permute-start.2 = (s32[2,2]{1,0:T(2,128)S(1)}, s32[2,2]{1,0:T(2,128)S(1)}, u32[]{:S(2)}, u32[]{:S(2)}) collective-permute-start(s32[2,2]{1,0:T(2,128)S(1)} %collective-permute-done.first_ref), channel_id=1, source_target_pairs={{128,0},{129,1},{130,2},{131,3},{132,4},{133,5},{134,6},{135,7},{1... | collective-permute-start | bytes 56 | tf_op jit(solution)/shard_map/ppermute | solution.py:299
  21.6 3.0 %collective-permute-start.3 = (s32[2,2]{1,0:T(2,128)S(1)}, s32[2,2]{1,0:T(2,128)S(1)}, u32[]{:S(2)}, u32[]{:S(2)}) collective-permute-start(s32[2,2]{1,0:T(2,128)S(1)} %collective-permute-done.1.second_ref), channel_id=1, source_target_pairs={{128,0},{129,1},{130,2},{131,3},{132,4},{133,5},{134,6},{135,7},{1... | collective-permute-start | bytes 56 | tf_op jit(solution)/shard_map/ppermute | solution.py:299
  27.3 18.2 %collective-permute-start.9 = (f32[2,2,128,256]{3,2,1,0:T(8,128)S(1)}, f32[2,2,128,256]{3,2,1,0:T(8,128)S(1)}, u32[]{:S(2)}, u32[]{:S(2)}) collective-permute-start(f32[2,2,128,256]{3,2,1,0:T(8,128)S(1)} %get-tuple-element.18), channel_id=1, source_target_pairs={{1,130},{2,129},{3,132},{4,131},{5,134},{6,133},{7,136},{8,135},{9... | collective-permute-start | bytes 1572872 | tf_op jit(solution)/shard_map/ppermute | solution.py:299
  28.6 18.2 %collective-permute-start.11 = (f32[2,2,128,256]{3,2,1,0:T(8,128)S(1)}, f32[2,2,128,256]{3,2,1,0:T(8,128)S(1)}, u32[]{:S(2)}, u32[]{:S(2)}) collective-permute-start(f32[2,2,128,256]{3,2,1,0:T(8,128)S(1)} %get-tuple-element.18), channel_id=1, source_target_pairs={{0,129},{1,128},{2,131},{3,130},{4,133},{5,132},{6,135},{7,134},{8... | collective-permute-start | bytes 1572872 | tf_op jit(solution)/shard_map/ppermute | solution.py:299
  29.9 21.2 %collective-permute-start.13 = (f32[2,2,128,256]{3,2,1,0:T(8,128)S(1)}, f32[2,2,128,256]{3,2,1,0:T(8,128)S(1)}, u32[]{:S(2)}, u32[]{:S(2)}) collective-permute-start(f32[2,2,128,256]{3,2,1,0:T(8,128)S(1)} %get-tuple-element.19), channel_id=1, source_target_pairs={{1,130},{2,129},{3,132},{4,131},{5,134},{6,133},{7,136},{8,135},{9... | collective-permute-start | bytes 1572872 | tf_op jit(solution)/shard_map/ppermute | solution.py:299
  31.2 19.9 %collective-permute-start.14 = (f32[2,2,128,256]{3,2,1,0:T(8,128)S(1)}, f32[2,2,128,256]{3,2,1,0:T(8,128)S(1)}, u32[]{:S(2)}, u32[]{:S(2)}) collective-permute-start(f32[2,2,128,256]{3,2,1,0:T(8,128)S(1)} %get-tuple-element.19), channel_id=1, source_target_pairs={{0,129},{1,128},{2,131},{3,130},{4,133},{5,132},{6,135},{7,134},{8... | collective-permute-start | bytes 1572872 | tf_op jit(solution)/shard_map/ppermute | solution.py:299
  32.5 18.6 %collective-permute-start.15 = (f32[2,2,128,256]{3,2,1,0:T(8,128)S(1)}, f32[2,2,128,256]{3,2,1,0:T(8,128)S(1)}, u32[]{:S(2)}, u32[]{:S(2)}) collective-permute-start(f32[2,2,128,256]{3,2,1,0:T(8,128)S(1)} %get-tuple-element.20), channel_id=1, source_target_pairs={{0,128},{1,129},{2,130},{3,131},{4,132},{5,133},{6,134},{7,135},{8... | collective-permute-start | bytes 1572872 | tf_op jit(solution)/shard_map/ppermute | solution.py:299
  45.5 5.6 %collective-permute-start.10 = (f32[2,2,128,256]{3,2,1,0:T(8,128)S(1)}, f32[2,2,128,256]{3,2,1,0:T(8,128)S(1)}, u32[]{:S(2)}, u32[]{:S(2)}) collective-permute-start(f32[2,2,128,256]{3,2,1,0:T(8,128)S(1)} %collective-permute-done.9), channel_id=1, source_target_pairs={{128,0},{129,1},{130,2},{131,3},{132,4},{133,5},{134,6},{135,7},{1... | collective-permute-start | bytes 1572872 | tf_op jit(solution)/shard_map/ppermute | solution.py:299
  46.9 4.3 %collective-permute-start.12 = (f32[2,2,128,256]{3,2,1,0:T(8,128)S(1)}, f32[2,2,128,256]{3,2,1,0:T(8,128)S(1)}, u32[]{:S(2)}, u32[]{:S(2)}) collective-permute-start(f32[2,2,128,256]{3,2,1,0:T(8,128)S(1)} %collective-permute-done.11), channel_id=1, source_target_pairs={{128,0},{129,1},{130,2},{131,3},{132,4},{133,5},{134,6},{135,7},{1... | collective-permute-start | bytes 1572872 | tf_op jit(solution)/shard_map/ppermute | solution.py:299

commit v6 on v5

--- a/solution.py
+++ b/solution.py
@@ -10,6 +10,7 @@
 
 WIN = 256
 HALF = 128
+CHUNK = 64
 
 
 def split_tables(real_part, imag_part):
@@ -45,10 +46,10 @@
 def product(field, table, which, from_left):
     high, low = split(field)
     table_high = table[2 * which]
-    table_low = table[2 * which + 1]
+    tables = [table_high, table_high, table[2 * which + 1]]
     if from_left:
-        return dot(table_high, high) + (dot(table_high, low) + dot(table_low, high))
-    return dot(high, table_high) + (dot(low, table_high) + dot(high, table_low))
+        return dot(jnp.concatenate(tables, axis=1), jnp.concatenate([high, low, high], axis=0))
+    return dot(jnp.concatenate([high, low, high], axis=1), jnp.concatenate(tables, axis=0))
 
 
 def complex_product(real, imag, table, conjugate, from_left):
@@ -212,18 +213,16 @@
 def add_piece(out_ref, piece_ref, column, keep):
     first = lax.shift_right_logical(column, 7)
     offset = jnp.bitwise_and(column, HALF - 1)
-    lanes = lax.broadcasted_iota(jnp.int32, (HALF, HALF), 1)
-    mine = lanes >= offset
+    mine = lax.broadcasted_iota(jnp.int32, (CHUNK, HALF), 1) >= offset
     third = jnp.minimum(first + 2, out_ref.shape[-1] // HALF - 1)
-    for part in range(2):
-        left = piece_ref[part, :, 0:HALF]
-        right = piece_ref[part, :, HALF:WIN]
-        if keep is not None:
-            left = jnp.where(keep, left, 0.0)
-            right = jnp.where(keep, right, 0.0)
-        out_ref[0, part, :, block(first)] += jnp.where(mine, left, 0.0)
-        out_ref[0, part, :, block(first + 1)] += right
-        out_ref[0, part, :, block(third)] += jnp.where(mine, 0.0, left)
+    left = piece_ref[:, 0:HALF]
+    right = piece_ref[:, HALF:WIN]
+    if keep is not None:
+        left = jnp.where(keep, left, 0.0)
+        right = jnp.where(keep, right, 0.0)
+    out_ref[:, block(first)] += jnp.where(mine, left, 0.0)
+    out_ref[:, block(first + 1)] += right
+    out_ref[:, block(third)] += jnp.where(mine, 0.0, left)
 
 
 def collect_kernel(
@@ -239,22 +238,37 @@
     second_one_ref,
     mid_one_ref,
     out_ref,
+    sum_ref,
+    sem,
 ):
     core = lax.axis_index("cuts")
     tile = lax.axis_index("tile")
     odd = jnp.bitwise_and(tile, 1)
-    out_ref[...] = jnp.zeros_like(out_ref)
-    rows = lax.broadcasted_iota(jnp.int32, (HALF, HALF), 0)
+    rows = lax.broadcasted_iota(jnp.int32, (CHUNK, HALF), 0)
 
     def gather(mid_ref, *nearby):
-        for slot in range(2):
-            add_piece(out_ref, mid_ref.at[slot], pos_ref[slot, 1], None)
-        for piece_ref, place_ref, above in nearby:
-            sign = 2 * above - 1
-            for slot in range(2):
-                shift_rows = place_ref[slot, 0] - (tile + sign - 1) * HALF
-                keep = sign * (rows - shift_rows) >= 1 - above
-                add_piece(out_ref, piece_ref.at[slot], place_ref[slot, 1], keep)
+        copies = []
+        for part in range(2):
+            for top in range(0, HALF, CHUNK):
+                here = pl.ds(top, CHUNK)
+                total = sum_ref.at[part, here]
+                total[...] = jnp.zeros(total.shape, jnp.float32)
+                for slot in range(2):
+                    add_piece(total, mid_ref.at[slot, part, here], pos_ref[slot, 1], None)
+                for piece_ref, place_ref, above in nearby:
+                    sign = 2 * above - 1
+                    for slot in range(2):
+                        shift_rows = place_ref[slot, 0] - (tile + sign - 1) * HALF - top
+                        keep = sign * (rows - shift_rows) >= 1 - above
+                        piece = piece_ref.at[slot, part, here]
+                        add_piece(total, piece, place_ref[slot, 1], keep)
+                copy = pltpu.make_async_copy(
+                    total, out_ref.at[0, part, here], sem.at[len(copies)]
+                )
+                copy.start()
+                copies.append(copy)
+        for copy in copies:
+            copy.wait()
 
     @pl.when(core == 0)
     def _():
@@ -358,7 +372,16 @@
     back_first_one = send(rim_one, 0, 1, first)
     back_second_one = send(rim_one, 0, 1, second)
     mid_one = send(mid_one, 0, 1, same)
-    return kernel(collect_kernel, "collect", strip, [SMEM] * 5 + [VMEM] * 6, 0, 4 << 20)(
+    return kernel(
+        collect_kernel,
+        "collect",
+        strip,
+        [SMEM] * 5 + [VMEM] * 6,
+        0,
+        4 << 20,
+        (pltpu.VMEM(strip.shape[1:], jnp.float32), pltpu.SemaphoreType.DMA((2 * HALF // CHUNK,))),
+        ANY,
+    )(
         positions,
         pos_first,
         pos_second,

time: 54.1 us -> 53.7 us (level)
  no operation moved by 1% of the time
where the time goes in v6:
time: 53.7 us; the launch traced here: 53.3 us
  starting transfers between devices  27 us (50%)
  waiting for transfers between devices  20.4 us (38%)
  Pallas kernels  5.01 us (9%)
  between operations  0.89 us (2%)
    ppermute x15, starting transfers between devices, send(): return lax.ppermute(value, ('cuts', 'tile'), pairs)  26.3 us
    ppermute x15, waiting for transfers between devices, send(): return lax.ppermute(value, ('cuts', 'tile'), pairs)  20.4 us
    pallas_call x1, Pallas kernels, local(): kernel(collect_kernel, 'collect', strip, [SMEM] * 5 + [VMEM] * 6, 0, 4 <<...  2.16 us
    pallas_call x2, Pallas kernels, cut(): kernel(cut_kernel, name, (pieces,) * 2, [SMEM] * 2 + [VMEM], 0, 2 << 20,...  1.56 us
  transfers between devices with their start and end apart: 16, of which 8 were waited for; matrix products, arithmetic and copies ran while one was open for 0% of the time, Pallas kernels for 3%

profile of v6, /device:TPU:129, one launch (start us, length us, event | category | flops | bytes accessed | tf_op | source)
XLA Modules:
  0.0 53.3 jit_solution(4899953323174356306)
XLA Ops:
  0.0 0.7 %collective-permute-start.4 = (f32[1,2,128,2048]{3,2,1,0:T(8,128)}, f32[1,2,128,2048]{3,2,1,0:T(8,128)S(1)}, u32[]{:S(2)}, u32[]{:S(2)}) collective-permute-start(f32[1,2,128,2048]{3,2,1,0:T(8,128)} %strip_ref.1), channel_id=1, source_target_pairs={{0,128},{128,0},{1,129},{129,1},{2,130},{130,2},{3,131},{131,3},{4... | collective-permute-start | bytes 6291464 | tf_op jit(solution)/shard_map/ppermute | solution.py:331
  0.7 6.4 %collective-permute-start = (s32[2,2]{1,0:T(2,128)}, s32[2,2]{1,0:T(2,128)S(1)}, u32[]{:S(2)}, u32[]{:S(2)}) collective-permute-start(s32[2,2]{1,0:T(2,128)} %pos_ref.5), channel_id=1, source_target_pairs={{129,130},{130,129},{131,132},{132,131},{133,134},{134,133},{135,1... | collective-permute-start | bytes 56 | tf_op jit(solution)/shard_map/ppermute | solution.py:313
  7.1 1.9 %collective-permute-start.1 = (s32[2,2]{1,0:T(2,128)}, s32[2,2]{1,0:T(2,128)S(1)}, u32[]{:S(2)}, u32[]{:S(2)}) collective-permute-start(s32[2,2]{1,0:T(2,128)} %pos_ref.5), channel_id=1, source_target_pairs={{128,129},{129,128},{130,131},{131,130},{132,133},{133,132},{134,1... | collective-permute-start | bytes 56 | tf_op jit(solution)/shard_map/ppermute | solution.py:313
  9.0 1.6 %collective-permute-done.first_ref = s32[2,2]{1,0:T(2,128)S(1)} collective-permute-done((s32[2,2]{1,0:T(2,128)}, s32[2,2]{1,0:T(2,128)S(1)}, u32[]{:S(2)}, u32[]{:S(2)}) %collective-permute-start) | collective-permute-done | bytes 48 | tf_op jit(solution)/shard_map/ppermute | solution.py:313
  10.6 1.0 %collective-permute-done.1.second_ref = s32[2,2]{1,0:T(2,128)S(1)} collective-permute-done((s32[2,2]{1,0:T(2,128)}, s32[2,2]{1,0:T(2,128)S(1)}, u32[]{:S(2)}, u32[]{:S(2)}) %collective-permute-start.1) | collective-permute-done | bytes 48 | tf_op jit(solution)/shard_map/ppermute | solution.py:313
  11.6 0.8 %cut_zero.1 = (f32[2,2,128,256]{3,2,1,0:T(8,128)S(1)}, f32[2,2,128,256]{3,2,1,0:T(8,128)S(1)}) custom-call(s32[2,2]{1,0:T(2,128)S(1)} %collective-permute-done.first_ref, s32[2,2]{1,0:T(2,128)S(1)} %collective-permute-done.1.second_ref, f32[1,2,128,2048]{3,2,1,0:T(8,128)S(1)} %collective-permute-done.4.strip_ref.other_ref), custom_call_target="tpu_custom_call" | custom-call | bytes 2097152 | tf_op jit(solution)/shard_map/cut_zero/pallas_call | solution.py:339
  12.4 1.3 %collective-permute-start.5 = (f32[2,2,128,256]{3,2,1,0:T(8,128)S(1)}, f32[2,2,128,256]{3,2,1,0:T(8,128)S(1)}, u32[]{:S(2)}, u32[]{:S(2)}) collective-permute-start(f32[2,2,128,256]{3,2,1,0:T(8,128)S(1)} %get-tuple-element.13), channel_id=1, source_target_pairs={{129,2},{130,1},{131,4},{132,3},{133,6},{134,5},{135,8},{136,7},{1... | collective-permute-start | bytes 1572872 | tf_op jit(solution)/shard_map/ppermute | solution.py:313
  13.7 1.3 %collective-permute-start.6 = (f32[2,2,128,256]{3,2,1,0:T(8,128)S(1)}, f32[2,2,128,256]{3,2,1,0:T(8,128)S(1)}, u32[]{:S(2)}, u32[]{:S(2)}) collective-permute-start(f32[2,2,128,256]{3,2,1,0:T(8,128)S(1)} %get-tuple-element.14), channel_id=1, source_target_pairs={{128,1},{129,0},{130,3},{131,2},{132,5},{133,4},{134,7},{135,6},{1... | collective-permute-start | bytes 1572872 | tf_op jit(solution)/shard_map/ppermute | solution.py:313
  15.0 0.2 stage.1.own_ref.strip_ref
  15.2 0.0 copy-start
  15.2 0.0 copy-start.2
  15.2 0.8 %cut_one.1 = (f32[2,2,128,256]{3,2,1,0:T(8,128)S(1)}, f32[2,2,128,256]{3,2,1,0:T(8,128)S(1)}) custom-call(s32[2,2]{1,0:T(2,128)S(1)} %collective-permute-done.first_ref, s32[2,2]{1,0:T(2,128)S(1)} %collective-permute-done.1.second_ref, f32[1,2,128,2048]{3,2,1,0:T(8,128)S(1)} %stage.1.own_ref.strip_ref), custom_call_target="tpu_custom_call" | custom-call | bytes 2097152 | tf_op jit(solution)/shard_map/cut_one/pallas_call | solution.py:339
  16.0 1.3 %collective-permute-start.7 = (f32[2,2,128,256]{3,2,1,0:T(8,128)S(1)}, f32[2,2,128,256]{3,2,1,0:T(8,128)S(1)}, u32[]{:S(2)}, u32[]{:S(2)}) collective-permute-start(f32[2,2,128,256]{3,2,1,0:T(8,128)S(1)} %get-tuple-element.15), channel_id=1, source_target_pairs={{129,2},{130,1},{131,4},{132,3},{133,6},{134,5},{135,8},{136,7},{1... | collective-permute-start | bytes 1572872 | tf_op jit(solution)/shard_map/ppermute | solution.py:313
  17.4 1.3 %collective-permute-start.8 = (f32[2,2,128,256]{3,2,1,0:T(8,128)S(1)}, f32[2,2,128,256]{3,2,1,0:T(8,128)S(1)}, u32[]{:S(2)}, u32[]{:S(2)}) collective-permute-start(f32[2,2,128,256]{3,2,1,0:T(8,128)S(1)} %get-tuple-element.16), channel_id=1, source_target_pairs={{128,1},{129,0},{130,3},{131,2},{132,5},{133,4},{134,7},{135,6},{1... | collective-permute-start | bytes 1572872 | tf_op jit(solution)/shard_map/ppermute | solution.py:313
  19.4 1.4 %collective-permute-start.2 = (s32[2,2]{1,0:T(2,128)S(1)}, s32[2,2]{1,0:T(2,128)S(1)}, u32[]{:S(2)}, u32[]{:S(2)}) collective-permute-start(s32[2,2]{1,0:T(2,128)S(1)} %collective-permute-done.first_ref), channel_id=1, source_target_pairs={{128,0},{129,1},{130,2},{131,3},{132,4},{133,5},{134,6},{135,7},{1... | collective-permute-start | bytes 56 | tf_op jit(solution)/shard_map/ppermute | solution.py:313
  20.8 0.8 %collective-permute-done.2.first_copy_ref = s32[2,2]{1,0:T(2,128)S(1)} collective-permute-done((s32[2,2]{1,0:T(2,128)S(1)}, s32[2,2]{1,0:T(2,128)S(1)}, u32[]{:S(2)}, u32[]{:S(2)}) %collective-permute-start.2) | collective-permute-done | bytes 48 | tf_op jit(solution)/shard_map/ppermute | solution.py:313
  21.6 2.2 %collective-permute-start.3 = (s32[2,2]{1,0:T(2,128)S(1)}, s32[2,2]{1,0:T(2,128)S(1)}, u32[]{:S(2)}, u32[]{:S(2)}) collective-permute-start(s32[2,2]{1,0:T(2,128)S(1)} %collective-permute-done.1.second_ref), channel_id=1, source_target_pairs={{128,0},{129,1},{130,2},{131,3},{132,4},{133,5},{134,6},{135,7},{1... | collective-permute-start | bytes 56 | tf_op jit(solution)/shard_map/ppermute | solution.py:313
  23.8 0.8 %collective-permute-done.3.second_copy_ref = s32[2,2]{1,0:T(2,128)S(1)} collective-permute-done((s32[2,2]{1,0:T(2,128)S(1)}, s32[2,2]{1,0:T(2,128)S(1)}, u32[]{:S(2)}, u32[]{:S(2)}) %collective-permute-start.3) | collective-permute-done | bytes 48 | tf_op jit(solution)/shard_map/ppermute | solution.py:313
  24.6 0.6 %enter.1.wave_ref = f32[2,2,2,256,256]{4,3,2,1,0:T(8,128)S(1)} custom-call(s32[2,2]{1,0:T(2,128)S(1)} %copy-done.4, s32[1]{0:T(128)S(6)} %copy.7.counts_ref, f32[2,256,256]{2,1,0:T(8,128)S(1)} %copy-done.2, bf16[2,6,256,256]{3,2,1,0:T(8,128)(2,1)S(1)} %copy-done, f32[1,2,128,2048]{3,2,1,0:T(8,128)S(1)} %stage.1.own_ref.strip_ref, ...), custom_call_target="tpu_custom_call" | custom-call | flops 603979776 | bytes 3145728 | tf_op jit(solution)/shard_map/enter/pallas_call | solution.py:351
  25.2 0.2 collective-permute-done.7.first_ref
  25.4 1.3 %collective-permute-done.8.second_ref = f32[2,2,128,256]{3,2,1,0:T(8,128)S(1)} collective-permute-done((f32[2,2,128,256]{3,2,1,0:T(8,128)S(1)}, f32[2,2,128,256]{3,2,1,0:T(8,128)S(1)}, u32[]{:S(2)}, u32[]{:S(2)}) %collective-permute-start.8) | collective-permute-done | bytes 524320 | tf_op jit(solution)/shard_map/ppermute | solution.py:313
  26.7 0.6 %slot.1 = (f32[2,2,128,256]{3,2,1,0:T(8,128)S(1)}, f32[2,2,128,256]{3,2,1,0:T(8,128)S(1)}, f32[2,2,128,256]{3,2,1,0:T(8,128)S(1)}, f32[2,2,128,256]{3,2,1,0:T(8,128)S(1)}) custom-call(s32[2,2]{1,0:T(2,128)S(1)} %copy-done.4, s32[1]{0:T(128)S(6)} %copy.7.counts_ref, bf16[2,6,256,256]{3,2,1,0:T(8,128)(2,1)S(1)} %copy-done, ...), custom_call_target="tpu_custom_call" | custom-call | flops 1811939328 | bytes 6291456 | tf_op jit(solution)/shard_map/slot/pallas_call | solution.py:360
  27.3 1.3 %collective-permute-start.9 = (f32[2,2,128,256]{3,2,1,0:T(8,128)S(1)}, f32[2,2,128,256]{3,2,1,0:T(8,128)S(1)}, u32[]{:S(2)}, u32[]{:S(2)}) collective-permute-start(f32[2,2,128,256]{3,2,1,0:T(8,128)S(1)} %get-tuple-element.18), channel_id=1, source_target_pairs={{1,130},{2,129},{3,132},{4,131},{5,134},{6,133},{7,136},{8,135},{9... | collective-permute-start | bytes 1572872 | tf_op jit(solution)/shard_map/ppermute | solution.py:313
  28.6 1.3 %collective-permute-start.11 = (f32[2,2,128,256]{3,2,1,0:T(8,128)S(1)}, f32[2,2,128,256]{3,2,1,0:T(8,128)S(1)}, u32[]{:S(2)}, u32[]{:S(2)}) collective-permute-start(f32[2,2,128,256]{3,2,1,0:T(8,128)S(1)} %get-tuple-element.18), channel_id=1, source_target_pairs={{0,129},{1,128},{2,131},{3,130},{4,133},{5,132},{6,135},{7,134},{8... | collective-permute-start | bytes 1572872 | tf_op jit(solution)/shard_map/ppermute | solution.py:313
  29.9 1.3 %collective-permute-start.13 = (f32[2,2,128,256]{3,2,1,0:T(8,128)S(1)}, f32[2,2,128,256]{3,2,1,0:T(8,128)S(1)}, u32[]{:S(2)}, u32[]{:S(2)}) collective-permute-start(f32[2,2,128,256]{3,2,1,0:T(8,128)S(1)} %get-tuple-element.19), channel_id=1, source_target_pairs={{1,130},{2,129},{3,132},{4,131},{5,134},{6,133},{7,136},{8,135},{9... | collective-permute-start | bytes 1572872 | tf_op jit(solution)/shard_map/ppermute | solution.py:313
  31.2 1.3 %collective-permute-start.14 = (f32[2,2,128,256]{3,2,1,0:T(8,128)S(1)}, f32[2,2,128,256]{3,2,1,0:T(8,128)S(1)}, u32[]{:S(2)}, u32[]{:S(2)}) collective-permute-start(f32[2,2,128,256]{3,2,1,0:T(8,128)S(1)} %get-tuple-element.19), channel_id=1, source_target_pairs={{0,129},{1,128},{2,131},{3,130},{4,133},{5,132},{6,135},{7,134},{8... | collective-permute-start | bytes 1572872 | tf_op jit(solution)/shard_map/ppermute | solution.py:313
  32.5 1.3 %collective-permute-start.15 = (f32[2,2,128,256]{3,2,1,0:T(8,128)S(1)}, f32[2,2,128,256]{3,2,1,0:T(8,128)S(1)}, u32[]{:S(2)}, u32[]{:S(2)}) collective-permute-start(f32[2,2,128,256]{3,2,1,0:T(8,128)S(1)} %get-tuple-element.20), channel_id=1, source_target_pairs={{0,128},{1,129},{2,130},{3,131},{4,132},{5,133},{6,134},{7,135},{8... | collective-permute-start | bytes 1572872 | tf_op jit(solution)/shard_map/ppermute | solution.py:313
  33.8 11.7 %collective-permute-done.9 = f32[2,2,128,256]{3,2,1,0:T(8,128)S(1)} collective-permute-done((f32[2,2,128,256]{3,2,1,0:T(8,128)S(1)}, f32[2,2,128,256]{3,2,1,0:T(8,128)S(1)}, u32[]{:S(2)}, u32[]{:S(2)}) %collective-permute-start.9) | collective-permute-done | bytes 524320 | tf_op jit(solution)/shard_map/ppermute | solution.py:313
  45.5 1.3 %collective-permute-start.10 = (f32[2,2,128,256]{3,2,1,0:T(8,128)S(1)}, f32[2,2,128,256]{3,2,1,0:T(8,128)S(1)}, u32[]{:S(2)}, u32[]{:S(2)}) collective-permute-start(f32[2,2,128,256]{3,2,1,0:T(8,128)S(1)} %collective-permute-done.9), channel_id=1, source_target_pairs={{128,0},{129,1},{130,2},{131,3},{132,4},{133,5},{134,6},{135,7},{1... | collective-permute-start | bytes 1572872 | tf_op jit(solution)/shard_map/ppermute | solution.py:313
  46.8 1.3 %collective-permute-start.12 = (f32[2,2,128,256]{3,2,1,0:T(8,128)S(1)}, f32[2,2,128,256]{3,2,1,0:T(8,128)S(1)}, u32[]{:S(2)}, u32[]{:S(2)}) collective-permute-start(f32[2,2,128,256]{3,2,1,0:T(8,128)S(1)} %collective-permute-done.11), channel_id=1, source_target_pairs={{128,0},{129,1},{130,2},{131,3},{132,4},{133,5},{134,6},{135,7},{1... | collective-permute-start | bytes 1572872 | tf_op jit(solution)/shard_map/ppermute | solution.py:313
  48.2 3.0 %collective-permute-done.13.first_one_ref = f32[2,2,128,256]{3,2,1,0:T(8,128)S(1)} collective-permute-done((f32[2,2,128,256]{3,2,1,0:T(8,128)S(1)}, f32[2,2,128,256]{3,2,1,0:T(8,128)S(1)}, u32[]{:S(2)}, u32[]{:S(2)}) %collective-permute-start.13) | collective-permute-done | bytes 524320 | tf_op jit(solution)/shard_map/ppermute | solution.py:313
  51.1 2.2 %collect.1 = f32[1,2,128,2048]{3,2,1,0:T(8,128)} custom-call(s32[2,2]{1,0:T(2,128)S(1)} %copy-done.4, s32[2,2]{1,0:T(2,128)S(1)} %collective-permute-done.first_ref, s32[2,2]{1,0:T(2,128)S(1)} %collective-permute-done.1.second_ref, s32[2,2]{1,0:T(2,128)S(1)} %collective-permute-done.2.first_copy_ref, s32[2,2]{1,0:T(2,128)S(1)} %collective-permute-done.3.second_copy_ref, ...), custom_call_target="tpu_custom_call" | custom-call | bytes 4194304 | tf_op jit(solution)/shard_map/collect/pallas_call | solution.py:375
  (16 shorter events, 0.0 us)
Async XLA Ops:
  0.0 15.0 %copy-start.1 = (f32[1,2,128,2048]{3,2,1,0:T(8,128)S(1)}, f32[1,2,128,2048]{3,2,1,0:T(8,128)}, u32[]{:S(2)}) copy-start(f32[1,2,128,2048]{3,2,1,0:T(8,128)} %strip_ref.1) | copy-start | bytes 6291460
  0.0 11.6 %collective-permute-start.4 = (f32[1,2,128,2048]{3,2,1,0:T(8,128)}, f32[1,2,128,2048]{3,2,1,0:T(8,128)S(1)}, u32[]{:S(2)}, u32[]{:S(2)}) collective-permute-start(f32[1,2,128,2048]{3,2,1,0:T(8,128)} %strip_ref.1), channel_id=1, source_target_pairs={{0,128},{128,0},{1,129},{129,1},{2,130},{130,2},{3,131},{131,3},{4... | collective-permute-start | bytes 6291464 | tf_op jit(solution)/shard_map/ppermute | solution.py:331
  0.7 9.9 %collective-permute-start = (s32[2,2]{1,0:T(2,128)}, s32[2,2]{1,0:T(2,128)S(1)}, u32[]{:S(2)}, u32[]{:S(2)}) collective-permute-start(s32[2,2]{1,0:T(2,128)} %pos_ref.5), channel_id=1, source_target_pairs={{129,130},{130,129},{131,132},{132,131},{133,134},{134,133},{135,1... | collective-permute-start | bytes 56 | tf_op jit(solution)/shard_map/ppermute | solution.py:313
  7.1 4.5 %collective-permute-start.1 = (s32[2,2]{1,0:T(2,128)}, s32[2,2]{1,0:T(2,128)S(1)}, u32[]{:S(2)}, u32[]{:S(2)}) collective-permute-start(s32[2,2]{1,0:T(2,128)} %pos_ref.5), channel_id=1, source_target_pairs={{128,129},{129,128},{130,131},{131,130},{132,133},{133,132},{134,1... | collective-permute-start | bytes 56 | tf_op jit(solution)/shard_map/ppermute | solution.py:313
  12.4 12.2 %collective-permute-start.5 = (f32[2,2,128,256]{3,2,1,0:T(8,128)S(1)}, f32[2,2,128,256]{3,2,1,0:T(8,128)S(1)}, u32[]{:S(2)}, u32[]{:S(2)}) collective-permute-start(f32[2,2,128,256]{3,2,1,0:T(8,128)S(1)} %get-tuple-element.13), channel_id=1, source_target_pairs={{129,2},{130,1},{131,4},{132,3},{133,6},{134,5},{135,8},{136,7},{1... | collective-permute-start | bytes 1572872 | tf_op jit(solution)/shard_map/ppermute | solution.py:313
  13.7 10.9 %collective-permute-start.6 = (f32[2,2,128,256]{3,2,1,0:T(8,128)S(1)}, f32[2,2,128,256]{3,2,1,0:T(8,128)S(1)}, u32[]{:S(2)}, u32[]{:S(2)}) collective-permute-start(f32[2,2,128,256]{3,2,1,0:T(8,128)S(1)} %get-tuple-element.14), channel_id=1, source_target_pairs={{128,1},{129,0},{130,3},{131,2},{132,5},{133,4},{134,7},{135,6},{1... | collective-permute-start | bytes 1572872 | tf_op jit(solution)/shard_map/ppermute | solution.py:313
  15.2 9.4 %copy-start = (bf16[2,6,256,256]{3,2,1,0:T(8,128)(2,1)S(1)}, bf16[2,6,256,256]{3,2,1,0:T(8,128)(2,1)}, u32[]{:S(2)}) copy-start(bf16[2,6,256,256]{3,2,1,0:T(8,128)(2,1)} %constant.2.clone.table_ref) | copy-start | bytes 4718596
  15.2 9.4 %copy-start.2 = (f32[2,256,256]{2,1,0:T(8,128)S(1)}, f32[2,256,256]{2,1,0:T(8,128)}, u32[]{:S(2)}) copy-start(f32[2,256,256]{2,1,0:T(8,128)} %probe_ref.1) | copy-start | bytes 1572868
  15.2 9.4 %copy-start.4 = (s32[2,2]{1,0:T(2,128)S(1)}, s32[2,2]{1,0:T(2,128)}, u32[]{:S(2)}) copy-start(s32[2,2]{1,0:T(2,128)} %pos_ref.5) | copy-start | bytes 52
  16.0 9.4 %collective-permute-start.7 = (f32[2,2,128,256]{3,2,1,0:T(8,128)S(1)}, f32[2,2,128,256]{3,2,1,0:T(8,128)S(1)}, u32[]{:S(2)}, u32[]{:S(2)}) collective-permute-start(f32[2,2,128,256]{3,2,1,0:T(8,128)S(1)} %get-tuple-element.15), channel_id=1, source_target_pairs={{129,2},{130,1},{131,4},{132,3},{133,6},{134,5},{135,8},{136,7},{1... | collective-permute-start | bytes 1572872 | tf_op jit(solution)/shard_map/ppermute | solution.py:313
  17.4 9.4 %collective-permute-start.8 = (f32[2,2,128,256]{3,2,1,0:T(8,128)S(1)}, f32[2,2,128,256]{3,2,1,0:T(8,128)S(1)}, u32[]{:S(2)}, u32[]{:S(2)}) collective-permute-start(f32[2,2,128,256]{3,2,1,0:T(8,128)S(1)} %get-tuple-element.16), channel_id=1, source_target_pairs={{128,1},{129,0},{130,3},{131,2},{132,5},{133,4},{134,7},{135,6},{1... | collective-permute-start | bytes 1572872 | tf_op jit(solution)/shard_map/ppermute | solution.py:313
  19.3 7.4 %copy-start.3 = (f32[2,256,256]{2,1,0:T(8,128)S(1)}, f32[2,256,256]{2,1,0:T(8,128)}, u32[]{:S(2)}) copy-start(f32[2,256,256]{2,1,0:T(8,128)} %intensity_ref.1) | copy-start | bytes 1572868
  19.4 2.2 %collective-permute-start.2 = (s32[2,2]{1,0:T(2,128)S(1)}, s32[2,2]{1,0:T(2,128)S(1)}, u32[]{:S(2)}, u32[]{:S(2)}) collective-permute-start(s32[2,2]{1,0:T(2,128)S(1)} %collective-permute-done.first_ref), channel_id=1, source_target_pairs={{128,0},{129,1},{130,2},{131,3},{132,4},{133,5},{134,6},{135,7},{1... | collective-permute-start | bytes 56 | tf_op jit(solution)/shard_map/ppermute | solution.py:313
  21.6 3.0 %collective-permute-start.3 = (s32[2,2]{1,0:T(2,128)S(1)}, s32[2,2]{1,0:T(2,128)S(1)}, u32[]{:S(2)}, u32[]{:S(2)}) collective-permute-start(s32[2,2]{1,0:T(2,128)S(1)} %collective-permute-done.1.second_ref), channel_id=1, source_target_pairs={{128,0},{129,1},{130,2},{131,3},{132,4},{133,5},{134,6},{135,7},{1... | collective-permute-start | bytes 56 | tf_op jit(solution)/shard_map/ppermute | solution.py:313
  27.3 18.2 %collective-permute-start.9 = (f32[2,2,128,256]{3,2,1,0:T(8,128)S(1)}, f32[2,2,128,256]{3,2,1,0:T(8,128)S(1)}, u32[]{:S(2)}, u32[]{:S(2)}) collective-permute-start(f32[2,2,128,256]{3,2,1,0:T(8,128)S(1)} %get-tuple-element.18), channel_id=1, source_target_pairs={{1,130},{2,129},{3,132},{4,131},{5,134},{6,133},{7,136},{8,135},{9... | collective-permute-start | bytes 1572872 | tf_op jit(solution)/shard_map/ppermute | solution.py:313
  28.6 18.2 %collective-permute-start.11 = (f32[2,2,128,256]{3,2,1,0:T(8,128)S(1)}, f32[2,2,128,256]{3,2,1,0:T(8,128)S(1)}, u32[]{:S(2)}, u32[]{:S(2)}) collective-permute-start(f32[2,2,128,256]{3,2,1,0:T(8,128)S(1)} %get-tuple-element.18), channel_id=1, source_target_pairs={{0,129},{1,128},{2,131},{3,130},{4,133},{5,132},{6,135},{7,134},{8... | collective-permute-start | bytes 1572872 | tf_op jit(solution)/shard_map/ppermute | solution.py:313
  29.9 21.2 %collective-permute-start.13 = (f32[2,2,128,256]{3,2,1,0:T(8,128)S(1)}, f32[2,2,128,256]{3,2,1,0:T(8,128)S(1)}, u32[]{:S(2)}, u32[]{:S(2)}) collective-permute-start(f32[2,2,128,256]{3,2,1,0:T(8,128)S(1)} %get-tuple-element.19), channel_id=1, source_target_pairs={{1,130},{2,129},{3,132},{4,131},{5,134},{6,133},{7,136},{8,135},{9... | collective-permute-start | bytes 1572872 | tf_op jit(solution)/shard_map/ppermute | solution.py:313
  31.2 19.9 %collective-permute-start.14 = (f32[2,2,128,256]{3,2,1,0:T(8,128)S(1)}, f32[2,2,128,256]{3,2,1,0:T(8,128)S(1)}, u32[]{:S(2)}, u32[]{:S(2)}) collective-permute-start(f32[2,2,128,256]{3,2,1,0:T(8,128)S(1)} %get-tuple-element.19), channel_id=1, source_target_pairs={{0,129},{1,128},{2,131},{3,130},{4,133},{5,132},{6,135},{7,134},{8... | collective-permute-start | bytes 1572872 | tf_op jit(solution)/shard_map/ppermute | solution.py:313
  32.5 18.6 %collective-permute-start.15 = (f32[2,2,128,256]{3,2,1,0:T(8,128)S(1)}, f32[2,2,128,256]{3,2,1,0:T(8,128)S(1)}, u32[]{:S(2)}, u32[]{:S(2)}) collective-permute-start(f32[2,2,128,256]{3,2,1,0:T(8,128)S(1)} %get-tuple-element.20), channel_id=1, source_target_pairs={{0,128},{1,129},{2,130},{3,131},{4,132},{5,133},{6,134},{7,135},{8... | collective-permute-start | bytes 1572872 | tf_op jit(solution)/shard_map/ppermute | solution.py:313
  45.5 5.6 %collective-permute-start.10 = (f32[2,2,128,256]{3,2,1,0:T(8,128)S(1)}, f32[2,2,128,256]{3,2,1,0:T(8,128)S(1)}, u32[]{:S(2)}, u32[]{:S(2)}) collective-permute-start(f32[2,2,128,256]{3,2,1,0:T(8,128)S(1)} %collective-permute-done.9), channel_id=1, source_target_pairs={{128,0},{129,1},{130,2},{131,3},{132,4},{133,5},{134,6},{135,7},{1... | collective-permute-start | bytes 1572872 | tf_op jit(solution)/shard_map/ppermute | solution.py:313
  46.8 4.3 %collective-permute-start.12 = (f32[2,2,128,256]{3,2,1,0:T(8,128)S(1)}, f32[2,2,128,256]{3,2,1,0:T(8,128)S(1)}, u32[]{:S(2)}, u32[]{:S(2)}) collective-permute-start(f32[2,2,128,256]{3,2,1,0:T(8,128)S(1)} %collective-permute-done.11), channel_id=1, source_target_pairs={{128,0},{129,1},{130,2},{131,3},{132,4},{133,5},{134,6},{135,7},{1... | collective-permute-start | bytes 1572872 | tf_op jit(solution)/shard_map/ppermute | solution.py:313

commit v7 on v6

--- a/solution.py
+++ b/solution.py
@@ -15,7 +15,7 @@
 
 def split_tables(real_part, imag_part):
     parts = []
-    for values in (real_part, imag_part - real_part, real_part + imag_part):
+    for values in (real_part, imag_part, -imag_part):
         high = values.astype(ml_dtypes.bfloat16)
         low = (values - high.astype(np.float64)).astype(ml_dtypes.bfloat16)
         parts += [high, low]
@@ -43,24 +43,23 @@
     return jnp.dot(left, right, preferred_element_type=jnp.float32)
 
 
-def product(field, table, which, from_left):
-    high, low = split(field)
-    table_high = table[2 * which]
-    tables = [table_high, table_high, table[2 * which + 1]]
-    if from_left:
-        return dot(jnp.concatenate(tables, axis=1), jnp.concatenate([high, low, high], axis=0))
-    return dot(jnp.concatenate([high, low, high], axis=1), jnp.concatenate(tables, axis=0))
-
-
 def complex_product(real, imag, table, conjugate, from_left):
-    shared = product(real + imag, table, 0, from_left)
-    if conjugate:
-        first = product(real, table, 2, from_left)
-        second = product(imag, table, 1, from_left)
-        return shared + second, shared - first
-    first = product(real, table, 1, from_left)
-    second = product(imag, table, 2, from_left)
-    return shared - second, shared + first
+    real_high, real_low = split(real)
+    imag_high, imag_low = split(imag)
+    fields = [real_high, real_low, real_high, imag_high, imag_low, imag_high]
+
+    def terms(which):
+        return [table[2 * which], table[2 * which], table[2 * which + 1]]
+
+    plus, minus = (2, 1) if conjugate else (1, 2)
+    results = []
+    for parts in (terms(0) + terms(minus), terms(plus) + terms(0)):
+        if from_left:
+            left, right = jnp.concatenate(parts, axis=1), jnp.concatenate(fields, axis=0)
+        else:
+            left, right = jnp.concatenate(fields, axis=1), jnp.concatenate(parts, axis=0)
+        results.append(dot(left, right))
+    return results
 
 
 def sandwich(real, imag, table, conjugate):

time: 53.7 us -> 53.6 us (level)
  no operation moved by 1% of the time
where the time goes in v7:
time: 53.6 us; the launch traced here: 53.3 us
  starting transfers between devices  27 us (50%)
  waiting for transfers between devices  20.3 us (38%)
  Pallas kernels  5.01 us (9%)
  between operations  0.89 us (2%)
    ppermute x15, starting transfers between devices, send(): return lax.ppermute(value, ('cuts', 'tile'), pairs)  26.3 us
    ppermute x15, waiting for transfers between devices, send(): return lax.ppermute(value, ('cuts', 'tile'), pairs)  20.3 us
    pallas_call x1, Pallas kernels, local(): kernel(collect_kernel, 'collect', strip, [SMEM] * 5 + [VMEM] * 6, 0, 4 <<...  2.16 us
    pallas_call x2, Pallas kernels, cut(): kernel(cut_kernel, name, (pieces,) * 2, [SMEM] * 2 + [VMEM], 0, 2 << 20,...  1.56 us
  transfers between devices with their start and end apart: 16, of which 8 were waited for; matrix products, arithmetic and copies ran while one was open for 0% of the time, Pallas kernels for 3%

profile of v7, /device:TPU:129, one launch (start us, length us, event | category | flops | bytes accessed | tf_op | source)
XLA Modules:
  0.0 53.3 jit_solution(126975822818868359)
XLA Ops:
  0.0 0.7 %collective-permute-start.4 = (f32[1,2,128,2048]{3,2,1,0:T(8,128)}, f32[1,2,128,2048]{3,2,1,0:T(8,128)S(1)}, u32[]{:S(2)}, u32[]{:S(2)}) collective-permute-start(f32[1,2,128,2048]{3,2,1,0:T(8,128)} %strip_ref.1), channel_id=1, source_target_pairs={{0,128},{128,0},{1,129},{129,1},{2,130},{130,2},{3,131},{131,3},{4... | collective-permute-start | bytes 6291464 | tf_op jit(solution)/shard_map/ppermute | solution.py:330
  0.7 6.4 %collective-permute-start = (s32[2,2]{1,0:T(2,128)}, s32[2,2]{1,0:T(2,128)S(1)}, u32[]{:S(2)}, u32[]{:S(2)}) collective-permute-start(s32[2,2]{1,0:T(2,128)} %pos_ref.5), channel_id=1, source_target_pairs={{129,130},{130,129},{131,132},{132,131},{133,134},{134,133},{135,1... | collective-permute-start | bytes 56 | tf_op jit(solution)/shard_map/ppermute | solution.py:312
  7.1 1.9 %collective-permute-start.1 = (s32[2,2]{1,0:T(2,128)}, s32[2,2]{1,0:T(2,128)S(1)}, u32[]{:S(2)}, u32[]{:S(2)}) collective-permute-start(s32[2,2]{1,0:T(2,128)} %pos_ref.5), channel_id=1, source_target_pairs={{128,129},{129,128},{130,131},{131,130},{132,133},{133,132},{134,1... | collective-permute-start | bytes 56 | tf_op jit(solution)/shard_map/ppermute | solution.py:312
  9.0 1.6 %collective-permute-done.first_ref = s32[2,2]{1,0:T(2,128)S(1)} collective-permute-done((s32[2,2]{1,0:T(2,128)}, s32[2,2]{1,0:T(2,128)S(1)}, u32[]{:S(2)}, u32[]{:S(2)}) %collective-permute-start) | collective-permute-done | bytes 48 | tf_op jit(solution)/shard_map/ppermute | solution.py:312
  10.6 1.0 %collective-permute-done.1.second_ref = s32[2,2]{1,0:T(2,128)S(1)} collective-permute-done((s32[2,2]{1,0:T(2,128)}, s32[2,2]{1,0:T(2,128)S(1)}, u32[]{:S(2)}, u32[]{:S(2)}) %collective-permute-start.1) | collective-permute-done | bytes 48 | tf_op jit(solution)/shard_map/ppermute | solution.py:312
  11.6 0.8 %cut_zero.1 = (f32[2,2,128,256]{3,2,1,0:T(8,128)S(1)}, f32[2,2,128,256]{3,2,1,0:T(8,128)S(1)}) custom-call(s32[2,2]{1,0:T(2,128)S(1)} %collective-permute-done.first_ref, s32[2,2]{1,0:T(2,128)S(1)} %collective-permute-done.1.second_ref, f32[1,2,128,2048]{3,2,1,0:T(8,128)S(1)} %collective-permute-done.4.strip_ref.other_ref), custom_call_target="tpu_custom_call" | custom-call | bytes 2097152 | tf_op jit(solution)/shard_map/cut_zero/pallas_call | solution.py:338
  12.4 1.3 %collective-permute-start.5 = (f32[2,2,128,256]{3,2,1,0:T(8,128)S(1)}, f32[2,2,128,256]{3,2,1,0:T(8,128)S(1)}, u32[]{:S(2)}, u32[]{:S(2)}) collective-permute-start(f32[2,2,128,256]{3,2,1,0:T(8,128)S(1)} %get-tuple-element.13), channel_id=1, source_target_pairs={{129,2},{130,1},{131,4},{132,3},{133,6},{134,5},{135,8},{136,7},{1... | collective-permute-start | bytes 1572872 | tf_op jit(solution)/shard_map/ppermute | solution.py:312
  13.7 1.3 %collective-permute-start.6 = (f32[2,2,128,256]{3,2,1,0:T(8,128)S(1)}, f32[2,2,128,256]{3,2,1,0:T(8,128)S(1)}, u32[]{:S(2)}, u32[]{:S(2)}) collective-permute-start(f32[2,2,128,256]{3,2,1,0:T(8,128)S(1)} %get-tuple-element.14), channel_id=1, source_target_pairs={{128,1},{129,0},{130,3},{131,2},{132,5},{133,4},{134,7},{135,6},{1... | collective-permute-start | bytes 1572872 | tf_op jit(solution)/shard_map/ppermute | solution.py:312
  15.0 0.2 stage.1.own_ref.strip_ref
  15.2 0.0 copy-start
  15.2 0.0 copy-start.2
  15.2 0.8 %cut_one.1 = (f32[2,2,128,256]{3,2,1,0:T(8,128)S(1)}, f32[2,2,128,256]{3,2,1,0:T(8,128)S(1)}) custom-call(s32[2,2]{1,0:T(2,128)S(1)} %collective-permute-done.first_ref, s32[2,2]{1,0:T(2,128)S(1)} %collective-permute-done.1.second_ref, f32[1,2,128,2048]{3,2,1,0:T(8,128)S(1)} %stage.1.own_ref.strip_ref), custom_call_target="tpu_custom_call" | custom-call | bytes 2097152 | tf_op jit(solution)/shard_map/cut_one/pallas_call | solution.py:338
  16.0 1.3 %collective-permute-start.7 = (f32[2,2,128,256]{3,2,1,0:T(8,128)S(1)}, f32[2,2,128,256]{3,2,1,0:T(8,128)S(1)}, u32[]{:S(2)}, u32[]{:S(2)}) collective-permute-start(f32[2,2,128,256]{3,2,1,0:T(8,128)S(1)} %get-tuple-element.15), channel_id=1, source_target_pairs={{129,2},{130,1},{131,4},{132,3},{133,6},{134,5},{135,8},{136,7},{1... | collective-permute-start | bytes 1572872 | tf_op jit(solution)/shard_map/ppermute | solution.py:312
  17.4 1.3 %collective-permute-start.8 = (f32[2,2,128,256]{3,2,1,0:T(8,128)S(1)}, f32[2,2,128,256]{3,2,1,0:T(8,128)S(1)}, u32[]{:S(2)}, u32[]{:S(2)}) collective-permute-start(f32[2,2,128,256]{3,2,1,0:T(8,128)S(1)} %get-tuple-element.16), channel_id=1, source_target_pairs={{128,1},{129,0},{130,3},{131,2},{132,5},{133,4},{134,7},{135,6},{1... | collective-permute-start | bytes 1572872 | tf_op jit(solution)/shard_map/ppermute | solution.py:312
  19.4 1.4 %collective-permute-start.2 = (s32[2,2]{1,0:T(2,128)S(1)}, s32[2,2]{1,0:T(2,128)S(1)}, u32[]{:S(2)}, u32[]{:S(2)}) collective-permute-start(s32[2,2]{1,0:T(2,128)S(1)} %collective-permute-done.first_ref), channel_id=1, source_target_pairs={{128,0},{129,1},{130,2},{131,3},{132,4},{133,5},{134,6},{135,7},{1... | collective-permute-start | bytes 56 | tf_op jit(solution)/shard_map/ppermute | solution.py:312
  20.8 0.8 %collective-permute-done.2.first_copy_ref = s32[2,2]{1,0:T(2,128)S(1)} collective-permute-done((s32[2,2]{1,0:T(2,128)S(1)}, s32[2,2]{1,0:T(2,128)S(1)}, u32[]{:S(2)}, u32[]{:S(2)}) %collective-permute-start.2) | collective-permute-done | bytes 48 | tf_op jit(solution)/shard_map/ppermute | solution.py:312
  21.6 2.2 %collective-permute-start.3 = (s32[2,2]{1,0:T(2,128)S(1)}, s32[2,2]{1,0:T(2,128)S(1)}, u32[]{:S(2)}, u32[]{:S(2)}) collective-permute-start(s32[2,2]{1,0:T(2,128)S(1)} %collective-permute-done.1.second_ref), channel_id=1, source_target_pairs={{128,0},{129,1},{130,2},{131,3},{132,4},{133,5},{134,6},{135,7},{1... | collective-permute-start | bytes 56 | tf_op jit(solution)/shard_map/ppermute | solution.py:312
  23.8 0.8 %collective-permute-done.3.second_copy_ref = s32[2,2]{1,0:T(2,128)S(1)} collective-permute-done((s32[2,2]{1,0:T(2,128)S(1)}, s32[2,2]{1,0:T(2,128)S(1)}, u32[]{:S(2)}, u32[]{:S(2)}) %collective-permute-start.3) | collective-permute-done | bytes 48 | tf_op jit(solution)/shard_map/ppermute | solution.py:312
  24.6 0.6 %enter.1.wave_ref = f32[2,2,2,256,256]{4,3,2,1,0:T(8,128)S(1)} custom-call(s32[2,2]{1,0:T(2,128)S(1)} %copy-done.4, s32[1]{0:T(128)S(6)} %copy.7.counts_ref, f32[2,256,256]{2,1,0:T(8,128)S(1)} %copy-done.2, bf16[2,6,256,256]{3,2,1,0:T(8,128)(2,1)S(1)} %copy-done, f32[1,2,128,2048]{3,2,1,0:T(8,128)S(1)} %stage.1.own_ref.strip_ref, ...), custom_call_target="tpu_custom_call" | custom-call | flops 603979776 | bytes 3145728 | tf_op jit(solution)/shard_map/enter/pallas_call | solution.py:350
  25.2 0.2 collective-permute-done.7.first_ref
  25.4 1.3 %collective-permute-done.8.second_ref = f32[2,2,128,256]{3,2,1,0:T(8,128)S(1)} collective-permute-done((f32[2,2,128,256]{3,2,1,0:T(8,128)S(1)}, f32[2,2,128,256]{3,2,1,0:T(8,128)S(1)}, u32[]{:S(2)}, u32[]{:S(2)}) %collective-permute-start.8) | collective-permute-done | bytes 524320 | tf_op jit(solution)/shard_map/ppermute | solution.py:312
  26.7 0.6 %slot.1 = (f32[2,2,128,256]{3,2,1,0:T(8,128)S(1)}, f32[2,2,128,256]{3,2,1,0:T(8,128)S(1)}, f32[2,2,128,256]{3,2,1,0:T(8,128)S(1)}, f32[2,2,128,256]{3,2,1,0:T(8,128)S(1)}) custom-call(s32[2,2]{1,0:T(2,128)S(1)} %copy-done.4, s32[1]{0:T(128)S(6)} %copy.7.counts_ref, bf16[2,6,256,256]{3,2,1,0:T(8,128)(2,1)S(1)} %copy-done, ...), custom_call_target="tpu_custom_call" | custom-call | flops 1811939328 | bytes 6291456 | tf_op jit(solution)/shard_map/slot/pallas_call | solution.py:359
  27.3 1.3 %collective-permute-start.9 = (f32[2,2,128,256]{3,2,1,0:T(8,128)S(1)}, f32[2,2,128,256]{3,2,1,0:T(8,128)S(1)}, u32[]{:S(2)}, u32[]{:S(2)}) collective-permute-start(f32[2,2,128,256]{3,2,1,0:T(8,128)S(1)} %get-tuple-element.18), channel_id=1, source_target_pairs={{1,130},{2,129},{3,132},{4,131},{5,134},{6,133},{7,136},{8,135},{9... | collective-permute-start | bytes 1572872 | tf_op jit(solution)/shard_map/ppermute | solution.py:312
  28.6 1.3 %collective-permute-start.11 = (f32[2,2,128,256]{3,2,1,0:T(8,128)S(1)}, f32[2,2,128,256]{3,2,1,0:T(8,128)S(1)}, u32[]{:S(2)}, u32[]{:S(2)}) collective-permute-start(f32[2,2,128,256]{3,2,1,0:T(8,128)S(1)} %get-tuple-element.18), channel_id=1, source_target_pairs={{0,129},{1,128},{2,131},{3,130},{4,133},{5,132},{6,135},{7,134},{8... | collective-permute-start | bytes 1572872 | tf_op jit(solution)/shard_map/ppermute | solution.py:312
  29.9 1.3 %collective-permute-start.13 = (f32[2,2,128,256]{3,2,1,0:T(8,128)S(1)}, f32[2,2,128,256]{3,2,1,0:T(8,128)S(1)}, u32[]{:S(2)}, u32[]{:S(2)}) collective-permute-start(f32[2,2,128,256]{3,2,1,0:T(8,128)S(1)} %get-tuple-element.19), channel_id=1, source_target_pairs={{1,130},{2,129},{3,132},{4,131},{5,134},{6,133},{7,136},{8,135},{9... | collective-permute-start | bytes 1572872 | tf_op jit(solution)/shard_map/ppermute | solution.py:312
  31.2 1.3 %collective-permute-start.14 = (f32[2,2,128,256]{3,2,1,0:T(8,128)S(1)}, f32[2,2,128,256]{3,2,1,0:T(8,128)S(1)}, u32[]{:S(2)}, u32[]{:S(2)}) collective-permute-start(f32[2,2,128,256]{3,2,1,0:T(8,128)S(1)} %get-tuple-element.19), channel_id=1, source_target_pairs={{0,129},{1,128},{2,131},{3,130},{4,133},{5,132},{6,135},{7,134},{8... | collective-permute-start | bytes 1572872 | tf_op jit(solution)/shard_map/ppermute | solution.py:312
  32.5 1.3 %collective-permute-start.15 = (f32[2,2,128,256]{3,2,1,0:T(8,128)S(1)}, f32[2,2,128,256]{3,2,1,0:T(8,128)S(1)}, u32[]{:S(2)}, u32[]{:S(2)}) collective-permute-start(f32[2,2,128,256]{3,2,1,0:T(8,128)S(1)} %get-tuple-element.20), channel_id=1, source_target_pairs={{0,128},{1,129},{2,130},{3,131},{4,132},{5,133},{6,134},{7,135},{8... | collective-permute-start | bytes 1572872 | tf_op jit(solution)/shard_map/ppermute | solution.py:312
  33.8 11.6 %collective-permute-done.9 = f32[2,2,128,256]{3,2,1,0:T(8,128)S(1)} collective-permute-done((f32[2,2,128,256]{3,2,1,0:T(8,128)S(1)}, f32[2,2,128,256]{3,2,1,0:T(8,128)S(1)}, u32[]{:S(2)}, u32[]{:S(2)}) %collective-permute-start.9) | collective-permute-done | bytes 524320 | tf_op jit(solution)/shard_map/ppermute | solution.py:312
  45.5 1.3 %collective-permute-start.10 = (f32[2,2,128,256]{3,2,1,0:T(8,128)S(1)}, f32[2,2,128,256]{3,2,1,0:T(8,128)S(1)}, u32[]{:S(2)}, u32[]{:S(2)}) collective-permute-start(f32[2,2,128,256]{3,2,1,0:T(8,128)S(1)} %collective-permute-done.9), channel_id=1, source_target_pairs={{128,0},{129,1},{130,2},{131,3},{132,4},{133,5},{134,6},{135,7},{1... | collective-permute-start | bytes 1572872 | tf_op jit(solution)/shard_map/ppermute | solution.py:312
  46.8 1.3 %collective-permute-start.12 = (f32[2,2,128,256]{3,2,1,0:T(8,128)S(1)}, f32[2,2,128,256]{3,2,1,0:T(8,128)S(1)}, u32[]{:S(2)}, u32[]{:S(2)}) collective-permute-start(f32[2,2,128,256]{3,2,1,0:T(8,128)S(1)} %collective-permute-done.11), channel_id=1, source_target_pairs={{128,0},{129,1},{130,2},{131,3},{132,4},{133,5},{134,6},{135,7},{1... | collective-permute-start | bytes 1572872 | tf_op jit(solution)/shard_map/ppermute | solution.py:312
  48.1 3.0 %collective-permute-done.13.first_one_ref = f32[2,2,128,256]{3,2,1,0:T(8,128)S(1)} collective-permute-done((f32[2,2,128,256]{3,2,1,0:T(8,128)S(1)}, f32[2,2,128,256]{3,2,1,0:T(8,128)S(1)}, u32[]{:S(2)}, u32[]{:S(2)}) %collective-permute-start.13) | collective-permute-done | bytes 524320 | tf_op jit(solution)/shard_map/ppermute | solution.py:312
  51.1 2.2 %collect.1 = f32[1,2,128,2048]{3,2,1,0:T(8,128)} custom-call(s32[2,2]{1,0:T(2,128)S(1)} %copy-done.4, s32[2,2]{1,0:T(2,128)S(1)} %collective-permute-done.first_ref, s32[2,2]{1,0:T(2,128)S(1)} %collective-permute-done.1.second_ref, s32[2,2]{1,0:T(2,128)S(1)} %collective-permute-done.2.first_copy_ref, s32[2,2]{1,0:T(2,128)S(1)} %collective-permute-done.3.second_copy_ref, ...), custom_call_target="tpu_custom_call" | custom-call | bytes 4194304 | tf_op jit(solution)/shard_map/collect/pallas_call | solution.py:374
  (16 shorter events, 0.0 us)
Async XLA Ops:
  0.0 15.0 %copy-start.1 = (f32[1,2,128,2048]{3,2,1,0:T(8,128)S(1)}, f32[1,2,128,2048]{3,2,1,0:T(8,128)}, u32[]{:S(2)}) copy-start(f32[1,2,128,2048]{3,2,1,0:T(8,128)} %strip_ref.1) | copy-start | bytes 6291460
  0.0 11.6 %collective-permute-start.4 = (f32[1,2,128,2048]{3,2,1,0:T(8,128)}, f32[1,2,128,2048]{3,2,1,0:T(8,128)S(1)}, u32[]{:S(2)}, u32[]{:S(2)}) collective-permute-start(f32[1,2,128,2048]{3,2,1,0:T(8,128)} %strip_ref.1), channel_id=1, source_target_pairs={{0,128},{128,0},{1,129},{129,1},{2,130},{130,2},{3,131},{131,3},{4... | collective-permute-start | bytes 6291464 | tf_op jit(solution)/shard_map/ppermute | solution.py:330
  0.7 9.9 %collective-permute-start = (s32[2,2]{1,0:T(2,128)}, s32[2,2]{1,0:T(2,128)S(1)}, u32[]{:S(2)}, u32[]{:S(2)}) collective-permute-start(s32[2,2]{1,0:T(2,128)} %pos_ref.5), channel_id=1, source_target_pairs={{129,130},{130,129},{131,132},{132,131},{133,134},{134,133},{135,1... | collective-permute-start | bytes 56 | tf_op jit(solution)/shard_map/ppermute | solution.py:312
  7.1 4.5 %collective-permute-start.1 = (s32[2,2]{1,0:T(2,128)}, s32[2,2]{1,0:T(2,128)S(1)}, u32[]{:S(2)}, u32[]{:S(2)}) collective-permute-start(s32[2,2]{1,0:T(2,128)} %pos_ref.5), channel_id=1, source_target_pairs={{128,129},{129,128},{130,131},{131,130},{132,133},{133,132},{134,1... | collective-permute-start | bytes 56 | tf_op jit(solution)/shard_map/ppermute | solution.py:312
  12.4 12.2 %collective-permute-start.5 = (f32[2,2,128,256]{3,2,1,0:T(8,128)S(1)}, f32[2,2,128,256]{3,2,1,0:T(8,128)S(1)}, u32[]{:S(2)}, u32[]{:S(2)}) collective-permute-start(f32[2,2,128,256]{3,2,1,0:T(8,128)S(1)} %get-tuple-element.13), channel_id=1, source_target_pairs={{129,2},{130,1},{131,4},{132,3},{133,6},{134,5},{135,8},{136,7},{1... | collective-permute-start | bytes 1572872 | tf_op jit(solution)/shard_map/ppermute | solution.py:312
  13.7 10.9 %collective-permute-start.6 = (f32[2,2,128,256]{3,2,1,0:T(8,128)S(1)}, f32[2,2,128,256]{3,2,1,0:T(8,128)S(1)}, u32[]{:S(2)}, u32[]{:S(2)}) collective-permute-start(f32[2,2,128,256]{3,2,1,0:T(8,128)S(1)} %get-tuple-element.14), channel_id=1, source_target_pairs={{128,1},{129,0},{130,3},{131,2},{132,5},{133,4},{134,7},{135,6},{1... | collective-permute-start | bytes 1572872 | tf_op jit(solution)/shard_map/ppermute | solution.py:312
  15.2 9.4 %copy-start = (bf16[2,6,256,256]{3,2,1,0:T(8,128)(2,1)S(1)}, bf16[2,6,256,256]{3,2,1,0:T(8,128)(2,1)}, u32[]{:S(2)}) copy-start(bf16[2,6,256,256]{3,2,1,0:T(8,128)(2,1)} %constant.2.clone.table_ref) | copy-start | bytes 4718596
  15.2 9.4 %copy-start.2 = (f32[2,256,256]{2,1,0:T(8,128)S(1)}, f32[2,256,256]{2,1,0:T(8,128)}, u32[]{:S(2)}) copy-start(f32[2,256,256]{2,1,0:T(8,128)} %probe_ref.1) | copy-start | bytes 1572868
  15.2 9.4 %copy-start.4 = (s32[2,2]{1,0:T(2,128)S(1)}, s32[2,2]{1,0:T(2,128)}, u32[]{:S(2)}) copy-start(s32[2,2]{1,0:T(2,128)} %pos_ref.5) | copy-start | bytes 52
  16.0 9.4 %collective-permute-start.7 = (f32[2,2,128,256]{3,2,1,0:T(8,128)S(1)}, f32[2,2,128,256]{3,2,1,0:T(8,128)S(1)}, u32[]{:S(2)}, u32[]{:S(2)}) collective-permute-start(f32[2,2,128,256]{3,2,1,0:T(8,128)S(1)} %get-tuple-element.15), channel_id=1, source_target_pairs={{129,2},{130,1},{131,4},{132,3},{133,6},{134,5},{135,8},{136,7},{1... | collective-permute-start | bytes 1572872 | tf_op jit(solution)/shard_map/ppermute | solution.py:312
  17.4 9.4 %collective-permute-start.8 = (f32[2,2,128,256]{3,2,1,0:T(8,128)S(1)}, f32[2,2,128,256]{3,2,1,0:T(8,128)S(1)}, u32[]{:S(2)}, u32[]{:S(2)}) collective-permute-start(f32[2,2,128,256]{3,2,1,0:T(8,128)S(1)} %get-tuple-element.16), channel_id=1, source_target_pairs={{128,1},{129,0},{130,3},{131,2},{132,5},{133,4},{134,7},{135,6},{1... | collective-permute-start | bytes 1572872 | tf_op jit(solution)/shard_map/ppermute | solution.py:312
  19.3 7.4 %copy-start.3 = (f32[2,256,256]{2,1,0:T(8,128)S(1)}, f32[2,256,256]{2,1,0:T(8,128)}, u32[]{:S(2)}) copy-start(f32[2,256,256]{2,1,0:T(8,128)} %intensity_ref.1) | copy-start | bytes 1572868
  19.4 2.2 %collective-permute-start.2 = (s32[2,2]{1,0:T(2,128)S(1)}, s32[2,2]{1,0:T(2,128)S(1)}, u32[]{:S(2)}, u32[]{:S(2)}) collective-permute-start(s32[2,2]{1,0:T(2,128)S(1)} %collective-permute-done.first_ref), channel_id=1, source_target_pairs={{128,0},{129,1},{130,2},{131,3},{132,4},{133,5},{134,6},{135,7},{1... | collective-permute-start | bytes 56 | tf_op jit(solution)/shard_map/ppermute | solution.py:312
  21.6 3.0 %collective-permute-start.3 = (s32[2,2]{1,0:T(2,128)S(1)}, s32[2,2]{1,0:T(2,128)S(1)}, u32[]{:S(2)}, u32[]{:S(2)}) collective-permute-start(s32[2,2]{1,0:T(2,128)S(1)} %collective-permute-done.1.second_ref), channel_id=1, source_target_pairs={{128,0},{129,1},{130,2},{131,3},{132,4},{133,5},{134,6},{135,7},{1... | collective-permute-start | bytes 56 | tf_op jit(solution)/shard_map/ppermute | solution.py:312
  27.3 18.1 %collective-permute-start.9 = (f32[2,2,128,256]{3,2,1,0:T(8,128)S(1)}, f32[2,2,128,256]{3,2,1,0:T(8,128)S(1)}, u32[]{:S(2)}, u32[]{:S(2)}) collective-permute-start(f32[2,2,128,256]{3,2,1,0:T(8,128)S(1)} %get-tuple-element.18), channel_id=1, source_target_pairs={{1,130},{2,129},{3,132},{4,131},{5,134},{6,133},{7,136},{8,135},{9... | collective-permute-start | bytes 1572872 | tf_op jit(solution)/shard_map/ppermute | solution.py:312
  28.6 18.2 %collective-permute-start.11 = (f32[2,2,128,256]{3,2,1,0:T(8,128)S(1)}, f32[2,2,128,256]{3,2,1,0:T(8,128)S(1)}, u32[]{:S(2)}, u32[]{:S(2)}) collective-permute-start(f32[2,2,128,256]{3,2,1,0:T(8,128)S(1)} %get-tuple-element.18), channel_id=1, source_target_pairs={{0,129},{1,128},{2,131},{3,130},{4,133},{5,132},{6,135},{7,134},{8... | collective-permute-start | bytes 1572872 | tf_op jit(solution)/shard_map/ppermute | solution.py:312
  29.9 21.2 %collective-permute-start.13 = (f32[2,2,128,256]{3,2,1,0:T(8,128)S(1)}, f32[2,2,128,256]{3,2,1,0:T(8,128)S(1)}, u32[]{:S(2)}, u32[]{:S(2)}) collective-permute-start(f32[2,2,128,256]{3,2,1,0:T(8,128)S(1)} %get-tuple-element.19), channel_id=1, source_target_pairs={{1,130},{2,129},{3,132},{4,131},{5,134},{6,133},{7,136},{8,135},{9... | collective-permute-start | bytes 1572872 | tf_op jit(solution)/shard_map/ppermute | solution.py:312
  31.2 19.9 %collective-permute-start.14 = (f32[2,2,128,256]{3,2,1,0:T(8,128)S(1)}, f32[2,2,128,256]{3,2,1,0:T(8,128)S(1)}, u32[]{:S(2)}, u32[]{:S(2)}) collective-permute-start(f32[2,2,128,256]{3,2,1,0:T(8,128)S(1)} %get-tuple-element.19), channel_id=1, source_target_pairs={{0,129},{1,128},{2,131},{3,130},{4,133},{5,132},{6,135},{7,134},{8... | collective-permute-start | bytes 1572872 | tf_op jit(solution)/shard_map/ppermute | solution.py:312
  32.5 18.6 %collective-permute-start.15 = (f32[2,2,128,256]{3,2,1,0:T(8,128)S(1)}, f32[2,2,128,256]{3,2,1,0:T(8,128)S(1)}, u32[]{:S(2)}, u32[]{:S(2)}) collective-permute-start(f32[2,2,128,256]{3,2,1,0:T(8,128)S(1)} %get-tuple-element.20), channel_id=1, source_target_pairs={{0,128},{1,129},{2,130},{3,131},{4,132},{5,133},{6,134},{7,135},{8... | collective-permute-start | bytes 1572872 | tf_op jit(solution)/shard_map/ppermute | solution.py:312
  45.5 5.6 %collective-permute-start.10 = (f32[2,2,128,256]{3,2,1,0:T(8,128)S(1)}, f32[2,2,128,256]{3,2,1,0:T(8,128)S(1)}, u32[]{:S(2)}, u32[]{:S(2)}) collective-permute-start(f32[2,2,128,256]{3,2,1,0:T(8,128)S(1)} %collective-permute-done.9), channel_id=1, source_target_pairs={{128,0},{129,1},{130,2},{131,3},{132,4},{133,5},{134,6},{135,7},{1... | collective-permute-start | bytes 1572872 | tf_op jit(solution)/shard_map/ppermute | solution.py:312
  46.8 4.3 %collective-permute-start.12 = (f32[2,2,128,256]{3,2,1,0:T(8,128)S(1)}, f32[2,2,128,256]{3,2,1,0:T(8,128)S(1)}, u32[]{:S(2)}, u32[]{:S(2)}) collective-permute-start(f32[2,2,128,256]{3,2,1,0:T(8,128)S(1)} %collective-permute-done.11), channel_id=1, source_target_pairs={{128,0},{129,1},{130,2},{131,3},{132,4},{133,5},{134,6},{135,7},{1... | collective-permute-start | bytes 1572872 | tf_op jit(solution)/shard_map/ppermute | solution.py:312

commit v8 on v7

--- a/solution.py
+++ b/solution.py
@@ -43,28 +43,39 @@
     return jnp.dot(left, right, preferred_element_type=jnp.float32)
 
 
-def complex_product(real, imag, table, conjugate, from_left):
+def terms_of(real, imag):
     real_high, real_low = split(real)
     imag_high, imag_low = split(imag)
-    fields = [real_high, real_low, real_high, imag_high, imag_low, imag_high]
-
-    def terms(which):
-        return [table[2 * which], table[2 * which], table[2 * which + 1]]
-
+    return [real_high, real_low, real_high, imag_high, imag_low, imag_high]
+
+
+def sandwich(real, imag, table, conjugate):
     plus, minus = (2, 1) if conjugate else (1, 2)
-    results = []
-    for parts in (terms(0) + terms(minus), terms(plus) + terms(0)):
-        if from_left:
-            left, right = jnp.concatenate(parts, axis=1), jnp.concatenate(fields, axis=0)
-        else:
-            left, right = jnp.concatenate(fields, axis=1), jnp.concatenate(parts, axis=0)
-        results.append(dot(left, right))
-    return results
-
-
-def sandwich(real, imag, table, conjugate):
-    real, imag = complex_product(real, imag, table, conjugate, False)
-    return complex_product(real, imag, table, conjugate, True)
+
+    def weights(which, rows):
+        high, low = table[2 * which, rows], table[2 * which + 1, rows]
+        return [high, high, low]
+
+    every = slice(0, WIN)
+    halves = [slice(0, HALF), slice(HALF, WIN)]
+    right = [
+        jnp.concatenate(weights(0, every) + weights(minus, every), axis=0),
+        jnp.concatenate(weights(plus, every) + weights(0, every), axis=0),
+    ]
+    middle = []
+    for rows in halves:
+        field = jnp.concatenate(terms_of(real[rows], imag[rows]), axis=1)
+        middle.append(terms_of(dot(field, right[0]), dot(field, right[1])))
+    stacked = jnp.concatenate(
+        [jnp.concatenate(pair, axis=0) for pair in zip(*middle)], axis=0
+    )
+    results = [[], []]
+    for rows in halves:
+        left = jnp.concatenate(weights(0, rows) + weights(minus, rows), axis=1)
+        results[0].append(dot(left, stacked))
+        left = jnp.concatenate(weights(plus, rows) + weights(0, rows), axis=1)
+        results[1].append(dot(left, stacked))
+    return [jnp.concatenate(parts, axis=0) for parts in results]
 
 
 def block(number):

time: 53.6 us -> 53.5 us (level)
  no operation moved by 1% of the time
where the time goes in v8:
time: 53.5 us; the launch traced here: 53.2 us
  starting transfers between devices  27 us (50%)
  waiting for transfers between devices  20.2 us (38%)
  Pallas kernels  5.01 us (9%)
  between operations  0.89 us (2%)
    ppermute x15, starting transfers between devices, send(): return lax.ppermute(value, ('cuts', 'tile'), pairs)  26.3 us
    ppermute x15, waiting for transfers between devices, send(): return lax.ppermute(value, ('cuts', 'tile'), pairs)  20.2 us
    pallas_call x1, Pallas kernels, local(): kernel(collect_kernel, 'collect', strip, [SMEM] * 5 + [VMEM] * 6, 0, 4 <<...  2.16 us
    pallas_call x2, Pallas kernels, cut(): kernel(cut_kernel, name, (pieces,) * 2, [SMEM] * 2 + [VMEM], 0, 2 << 20,...  1.56 us
  transfers between devices with their start and end apart: 16, of which 8 were waited for; matrix products, arithmetic and copies ran while one was open for 0% of the time, Pallas kernels for 3%

profile of v8, /device:TPU:129, one launch (start us, length us, event | category | flops | bytes accessed | tf_op | source)
XLA Modules:
  0.0 53.2 jit_solution(9570762403919197018)
XLA Ops:
  0.0 0.7 %collective-permute-start.4 = (f32[1,2,128,2048]{3,2,1,0:T(8,128)}, f32[1,2,128,2048]{3,2,1,0:T(8,128)S(1)}, u32[]{:S(2)}, u32[]{:S(2)}) collective-permute-start(f32[1,2,128,2048]{3,2,1,0:T(8,128)} %strip_ref.1), channel_id=1, source_target_pairs={{0,128},{128,0},{1,129},{129,1},{2,130},{130,2},{3,131},{131,3},{4... | collective-permute-start | bytes 6291464 | tf_op jit(solution)/shard_map/ppermute | solution.py:341
  0.7 6.4 %collective-permute-start = (s32[2,2]{1,0:T(2,128)}, s32[2,2]{1,0:T(2,128)S(1)}, u32[]{:S(2)}, u32[]{:S(2)}) collective-permute-start(s32[2,2]{1,0:T(2,128)} %pos_ref.5), channel_id=1, source_target_pairs={{129,130},{130,129},{131,132},{132,131},{133,134},{134,133},{135,1... | collective-permute-start | bytes 56 | tf_op jit(solution)/shard_map/ppermute | solution.py:323
  7.1 1.9 %collective-permute-start.1 = (s32[2,2]{1,0:T(2,128)}, s32[2,2]{1,0:T(2,128)S(1)}, u32[]{:S(2)}, u32[]{:S(2)}) collective-permute-start(s32[2,2]{1,0:T(2,128)} %pos_ref.5), channel_id=1, source_target_pairs={{128,129},{129,128},{130,131},{131,130},{132,133},{133,132},{134,1... | collective-permute-start | bytes 56 | tf_op jit(solution)/shard_map/ppermute | solution.py:323
  9.0 1.6 %collective-permute-done.first_ref = s32[2,2]{1,0:T(2,128)S(1)} collective-permute-done((s32[2,2]{1,0:T(2,128)}, s32[2,2]{1,0:T(2,128)S(1)}, u32[]{:S(2)}, u32[]{:S(2)}) %collective-permute-start) | collective-permute-done | bytes 48 | tf_op jit(solution)/shard_map/ppermute | solution.py:323
  10.6 1.0 %collective-permute-done.1.second_ref = s32[2,2]{1,0:T(2,128)S(1)} collective-permute-done((s32[2,2]{1,0:T(2,128)}, s32[2,2]{1,0:T(2,128)S(1)}, u32[]{:S(2)}, u32[]{:S(2)}) %collective-permute-start.1) | collective-permute-done | bytes 48 | tf_op jit(solution)/shard_map/ppermute | solution.py:323
  11.6 0.8 %cut_zero.1 = (f32[2,2,128,256]{3,2,1,0:T(8,128)S(1)}, f32[2,2,128,256]{3,2,1,0:T(8,128)S(1)}) custom-call(s32[2,2]{1,0:T(2,128)S(1)} %collective-permute-done.first_ref, s32[2,2]{1,0:T(2,128)S(1)} %collective-permute-done.1.second_ref, f32[1,2,128,2048]{3,2,1,0:T(8,128)S(1)} %collective-permute-done.4.strip_ref.other_ref), custom_call_target="tpu_custom_call" | custom-call | bytes 2097152 | tf_op jit(solution)/shard_map/cut_zero/pallas_call | solution.py:349
  12.4 1.3 %collective-permute-start.5 = (f32[2,2,128,256]{3,2,1,0:T(8,128)S(1)}, f32[2,2,128,256]{3,2,1,0:T(8,128)S(1)}, u32[]{:S(2)}, u32[]{:S(2)}) collective-permute-start(f32[2,2,128,256]{3,2,1,0:T(8,128)S(1)} %get-tuple-element.13), channel_id=1, source_target_pairs={{129,2},{130,1},{131,4},{132,3},{133,6},{134,5},{135,8},{136,7},{1... | collective-permute-start | bytes 1572872 | tf_op jit(solution)/shard_map/ppermute | solution.py:323
  13.7 1.3 %collective-permute-start.6 = (f32[2,2,128,256]{3,2,1,0:T(8,128)S(1)}, f32[2,2,128,256]{3,2,1,0:T(8,128)S(1)}, u32[]{:S(2)}, u32[]{:S(2)}) collective-permute-start(f32[2,2,128,256]{3,2,1,0:T(8,128)S(1)} %get-tuple-element.14), channel_id=1, source_target_pairs={{128,1},{129,0},{130,3},{131,2},{132,5},{133,4},{134,7},{135,6},{1... | collective-permute-start | bytes 1572872 | tf_op jit(solution)/shard_map/ppermute | solution.py:323
  15.0 0.2 stage.1.own_ref.strip_ref
  15.2 0.0 copy-start
  15.2 0.0 copy-start.2
  15.2 0.8 %cut_one.1 = (f32[2,2,128,256]{3,2,1,0:T(8,128)S(1)}, f32[2,2,128,256]{3,2,1,0:T(8,128)S(1)}) custom-call(s32[2,2]{1,0:T(2,128)S(1)} %collective-permute-done.first_ref, s32[2,2]{1,0:T(2,128)S(1)} %collective-permute-done.1.second_ref, f32[1,2,128,2048]{3,2,1,0:T(8,128)S(1)} %stage.1.own_ref.strip_ref), custom_call_target="tpu_custom_call" | custom-call | bytes 2097152 | tf_op jit(solution)/shard_map/cut_one/pallas_call | solution.py:349
  16.0 1.3 %collective-permute-start.7 = (f32[2,2,128,256]{3,2,1,0:T(8,128)S(1)}, f32[2,2,128,256]{3,2,1,0:T(8,128)S(1)}, u32[]{:S(2)}, u32[]{:S(2)}) collective-permute-start(f32[2,2,128,256]{3,2,1,0:T(8,128)S(1)} %get-tuple-element.15), channel_id=1, source_target_pairs={{129,2},{130,1},{131,4},{132,3},{133,6},{134,5},{135,8},{136,7},{1... | collective-permute-start | bytes 1572872 | tf_op jit(solution)/shard_map/ppermute | solution.py:323
  17.4 1.3 %collective-permute-start.8 = (f32[2,2,128,256]{3,2,1,0:T(8,128)S(1)}, f32[2,2,128,256]{3,2,1,0:T(8,128)S(1)}, u32[]{:S(2)}, u32[]{:S(2)}) collective-permute-start(f32[2,2,128,256]{3,2,1,0:T(8,128)S(1)} %get-tuple-element.16), channel_id=1, source_target_pairs={{128,1},{129,0},{130,3},{131,2},{132,5},{133,4},{134,7},{135,6},{1... | collective-permute-start | bytes 1572872 | tf_op jit(solution)/shard_map/ppermute | solution.py:323
  19.4 1.4 %collective-permute-start.2 = (s32[2,2]{1,0:T(2,128)S(1)}, s32[2,2]{1,0:T(2,128)S(1)}, u32[]{:S(2)}, u32[]{:S(2)}) collective-permute-start(s32[2,2]{1,0:T(2,128)S(1)} %collective-permute-done.first_ref), channel_id=1, source_target_pairs={{128,0},{129,1},{130,2},{131,3},{132,4},{133,5},{134,6},{135,7},{1... | collective-permute-start | bytes 56 | tf_op jit(solution)/shard_map/ppermute | solution.py:323
  20.8 0.8 %collective-permute-done.2.first_copy_ref = s32[2,2]{1,0:T(2,128)S(1)} collective-permute-done((s32[2,2]{1,0:T(2,128)S(1)}, s32[2,2]{1,0:T(2,128)S(1)}, u32[]{:S(2)}, u32[]{:S(2)}) %collective-permute-start.2) | collective-permute-done | bytes 48 | tf_op jit(solution)/shard_map/ppermute | solution.py:323
  21.6 2.2 %collective-permute-start.3 = (s32[2,2]{1,0:T(2,128)S(1)}, s32[2,2]{1,0:T(2,128)S(1)}, u32[]{:S(2)}, u32[]{:S(2)}) collective-permute-start(s32[2,2]{1,0:T(2,128)S(1)} %collective-permute-done.1.second_ref), channel_id=1, source_target_pairs={{128,0},{129,1},{130,2},{131,3},{132,4},{133,5},{134,6},{135,7},{1... | collective-permute-start | bytes 56 | tf_op jit(solution)/shard_map/ppermute | solution.py:323
  23.8 0.8 %collective-permute-done.3.second_copy_ref = s32[2,2]{1,0:T(2,128)S(1)} collective-permute-done((s32[2,2]{1,0:T(2,128)S(1)}, s32[2,2]{1,0:T(2,128)S(1)}, u32[]{:S(2)}, u32[]{:S(2)}) %collective-permute-start.3) | collective-permute-done | bytes 48 | tf_op jit(solution)/shard_map/ppermute | solution.py:323
  24.6 0.6 %enter.1.wave_ref = f32[2,2,2,256,256]{4,3,2,1,0:T(8,128)S(1)} custom-call(s32[2,2]{1,0:T(2,128)S(1)} %copy-done.4, s32[1]{0:T(128)S(6)} %copy.7.counts_ref, f32[2,256,256]{2,1,0:T(8,128)S(1)} %copy-done.2, bf16[2,6,256,256]{3,2,1,0:T(8,128)(2,1)S(1)} %copy-done, f32[1,2,128,2048]{3,2,1,0:T(8,128)S(1)} %stage.1.own_ref.strip_ref, ...), custom_call_target="tpu_custom_call" | custom-call | flops 603979776 | bytes 3145728 | tf_op jit(solution)/shard_map/enter/pallas_call | solution.py:361
  25.2 0.2 collective-permute-done.7.first_ref
  25.4 1.3 %collective-permute-done.8.second_ref = f32[2,2,128,256]{3,2,1,0:T(8,128)S(1)} collective-permute-done((f32[2,2,128,256]{3,2,1,0:T(8,128)S(1)}, f32[2,2,128,256]{3,2,1,0:T(8,128)S(1)}, u32[]{:S(2)}, u32[]{:S(2)}) %collective-permute-start.8) | collective-permute-done | bytes 524320 | tf_op jit(solution)/shard_map/ppermute | solution.py:323
  26.7 0.6 %slot.1 = (f32[2,2,128,256]{3,2,1,0:T(8,128)S(1)}, f32[2,2,128,256]{3,2,1,0:T(8,128)S(1)}, f32[2,2,128,256]{3,2,1,0:T(8,128)S(1)}, f32[2,2,128,256]{3,2,1,0:T(8,128)S(1)}) custom-call(s32[2,2]{1,0:T(2,128)S(1)} %copy-done.4, s32[1]{0:T(128)S(6)} %copy.7.counts_ref, bf16[2,6,256,256]{3,2,1,0:T(8,128)(2,1)S(1)} %copy-done, ...), custom_call_target="tpu_custom_call" | custom-call | flops 1811939328 | bytes 6291456 | tf_op jit(solution)/shard_map/slot/pallas_call | solution.py:370
  27.3 1.3 %collective-permute-start.9 = (f32[2,2,128,256]{3,2,1,0:T(8,128)S(1)}, f32[2,2,128,256]{3,2,1,0:T(8,128)S(1)}, u32[]{:S(2)}, u32[]{:S(2)}) collective-permute-start(f32[2,2,128,256]{3,2,1,0:T(8,128)S(1)} %get-tuple-element.18), channel_id=1, source_target_pairs={{1,130},{2,129},{3,132},{4,131},{5,134},{6,133},{7,136},{8,135},{9... | collective-permute-start | bytes 1572872 | tf_op jit(solution)/shard_map/ppermute | solution.py:323
  28.6 1.3 %collective-permute-start.11 = (f32[2,2,128,256]{3,2,1,0:T(8,128)S(1)}, f32[2,2,128,256]{3,2,1,0:T(8,128)S(1)}, u32[]{:S(2)}, u32[]{:S(2)}) collective-permute-start(f32[2,2,128,256]{3,2,1,0:T(8,128)S(1)} %get-tuple-element.18), channel_id=1, source_target_pairs={{0,129},{1,128},{2,131},{3,130},{4,133},{5,132},{6,135},{7,134},{8... | collective-permute-start | bytes 1572872 | tf_op jit(solution)/shard_map/ppermute | solution.py:323
  29.9 1.3 %collective-permute-start.13 = (f32[2,2,128,256]{3,2,1,0:T(8,128)S(1)}, f32[2,2,128,256]{3,2,1,0:T(8,128)S(1)}, u32[]{:S(2)}, u32[]{:S(2)}) collective-permute-start(f32[2,2,128,256]{3,2,1,0:T(8,128)S(1)} %get-tuple-element.19), channel_id=1, source_target_pairs={{1,130},{2,129},{3,132},{4,131},{5,134},{6,133},{7,136},{8,135},{9... | collective-permute-start | bytes 1572872 | tf_op jit(solution)/shard_map/ppermute | solution.py:323
  31.2 1.3 %collective-permute-start.14 = (f32[2,2,128,256]{3,2,1,0:T(8,128)S(1)}, f32[2,2,128,256]{3,2,1,0:T(8,128)S(1)}, u32[]{:S(2)}, u32[]{:S(2)}) collective-permute-start(f32[2,2,128,256]{3,2,1,0:T(8,128)S(1)} %get-tuple-element.19), channel_id=1, source_target_pairs={{0,129},{1,128},{2,131},{3,130},{4,133},{5,132},{6,135},{7,134},{8... | collective-permute-start | bytes 1572872 | tf_op jit(solution)/shard_map/ppermute | solution.py:323
  32.5 1.3 %collective-permute-start.15 = (f32[2,2,128,256]{3,2,1,0:T(8,128)S(1)}, f32[2,2,128,256]{3,2,1,0:T(8,128)S(1)}, u32[]{:S(2)}, u32[]{:S(2)}) collective-permute-start(f32[2,2,128,256]{3,2,1,0:T(8,128)S(1)} %get-tuple-element.20), channel_id=1, source_target_pairs={{0,128},{1,129},{2,130},{3,131},{4,132},{5,133},{6,134},{7,135},{8... | collective-permute-start | bytes 1572872 | tf_op jit(solution)/shard_map/ppermute | solution.py:323
  33.8 11.5 %collective-permute-done.9 = f32[2,2,128,256]{3,2,1,0:T(8,128)S(1)} collective-permute-done((f32[2,2,128,256]{3,2,1,0:T(8,128)S(1)}, f32[2,2,128,256]{3,2,1,0:T(8,128)S(1)}, u32[]{:S(2)}, u32[]{:S(2)}) %collective-permute-start.9) | collective-permute-done | bytes 524320 | tf_op jit(solution)/shard_map/ppermute | solution.py:323
  45.4 1.3 %collective-permute-start.10 = (f32[2,2,128,256]{3,2,1,0:T(8,128)S(1)}, f32[2,2,128,256]{3,2,1,0:T(8,128)S(1)}, u32[]{:S(2)}, u32[]{:S(2)}) collective-permute-start(f32[2,2,128,256]{3,2,1,0:T(8,128)S(1)} %collective-permute-done.9), channel_id=1, source_target_pairs={{128,0},{129,1},{130,2},{131,3},{132,4},{133,5},{134,6},{135,7},{1... | collective-permute-start | bytes 1572872 | tf_op jit(solution)/shard_map/ppermute | solution.py:323
  46.7 1.3 %collective-permute-start.12 = (f32[2,2,128,256]{3,2,1,0:T(8,128)S(1)}, f32[2,2,128,256]{3,2,1,0:T(8,128)S(1)}, u32[]{:S(2)}, u32[]{:S(2)}) collective-permute-start(f32[2,2,128,256]{3,2,1,0:T(8,128)S(1)} %collective-permute-done.11), channel_id=1, source_target_pairs={{128,0},{129,1},{130,2},{131,3},{132,4},{133,5},{134,6},{135,7},{1... | collective-permute-start | bytes 1572872 | tf_op jit(solution)/shard_map/ppermute | solution.py:323
  48.0 3.0 %collective-permute-done.13.first_one_ref = f32[2,2,128,256]{3,2,1,0:T(8,128)S(1)} collective-permute-done((f32[2,2,128,256]{3,2,1,0:T(8,128)S(1)}, f32[2,2,128,256]{3,2,1,0:T(8,128)S(1)}, u32[]{:S(2)}, u32[]{:S(2)}) %collective-permute-start.13) | collective-permute-done | bytes 524320 | tf_op jit(solution)/shard_map/ppermute | solution.py:323
  51.0 2.2 %collect.1 = f32[1,2,128,2048]{3,2,1,0:T(8,128)} custom-call(s32[2,2]{1,0:T(2,128)S(1)} %copy-done.4, s32[2,2]{1,0:T(2,128)S(1)} %collective-permute-done.first_ref, s32[2,2]{1,0:T(2,128)S(1)} %collective-permute-done.1.second_ref, s32[2,2]{1,0:T(2,128)S(1)} %collective-permute-done.2.first_copy_ref, s32[2,2]{1,0:T(2,128)S(1)} %collective-permute-done.3.second_copy_ref, ...), custom_call_target="tpu_custom_call" | custom-call | bytes 4194304 | tf_op jit(solution)/shard_map/collect/pallas_call | solution.py:385
  (16 shorter events, 0.0 us)
Async XLA Ops:
  0.0 15.0 %copy-start.1 = (f32[1,2,128,2048]{3,2,1,0:T(8,128)S(1)}, f32[1,2,128,2048]{3,2,1,0:T(8,128)}, u32[]{:S(2)}) copy-start(f32[1,2,128,2048]{3,2,1,0:T(8,128)} %strip_ref.1) | copy-start | bytes 6291460
  0.0 11.6 %collective-permute-start.4 = (f32[1,2,128,2048]{3,2,1,0:T(8,128)}, f32[1,2,128,2048]{3,2,1,0:T(8,128)S(1)}, u32[]{:S(2)}, u32[]{:S(2)}) collective-permute-start(f32[1,2,128,2048]{3,2,1,0:T(8,128)} %strip_ref.1), channel_id=1, source_target_pairs={{0,128},{128,0},{1,129},{129,1},{2,130},{130,2},{3,131},{131,3},{4... | collective-permute-start | bytes 6291464 | tf_op jit(solution)/shard_map/ppermute | solution.py:341
  0.7 9.9 %collective-permute-start = (s32[2,2]{1,0:T(2,128)}, s32[2,2]{1,0:T(2,128)S(1)}, u32[]{:S(2)}, u32[]{:S(2)}) collective-permute-start(s32[2,2]{1,0:T(2,128)} %pos_ref.5), channel_id=1, source_target_pairs={{129,130},{130,129},{131,132},{132,131},{133,134},{134,133},{135,1... | collective-permute-start | bytes 56 | tf_op jit(solution)/shard_map/ppermute | solution.py:323
  7.1 4.5 %collective-permute-start.1 = (s32[2,2]{1,0:T(2,128)}, s32[2,2]{1,0:T(2,128)S(1)}, u32[]{:S(2)}, u32[]{:S(2)}) collective-permute-start(s32[2,2]{1,0:T(2,128)} %pos_ref.5), channel_id=1, source_target_pairs={{128,129},{129,128},{130,131},{131,130},{132,133},{133,132},{134,1... | collective-permute-start | bytes 56 | tf_op jit(solution)/shard_map/ppermute | solution.py:323
  12.4 12.2 %collective-permute-start.5 = (f32[2,2,128,256]{3,2,1,0:T(8,128)S(1)}, f32[2,2,128,256]{3,2,1,0:T(8,128)S(1)}, u32[]{:S(2)}, u32[]{:S(2)}) collective-permute-start(f32[2,2,128,256]{3,2,1,0:T(8,128)S(1)} %get-tuple-element.13), channel_id=1, source_target_pairs={{129,2},{130,1},{131,4},{132,3},{133,6},{134,5},{135,8},{136,7},{1... | collective-permute-start | bytes 1572872 | tf_op jit(solution)/shard_map/ppermute | solution.py:323
  13.7 10.9 %collective-permute-start.6 = (f32[2,2,128,256]{3,2,1,0:T(8,128)S(1)}, f32[2,2,128,256]{3,2,1,0:T(8,128)S(1)}, u32[]{:S(2)}, u32[]{:S(2)}) collective-permute-start(f32[2,2,128,256]{3,2,1,0:T(8,128)S(1)} %get-tuple-element.14), channel_id=1, source_target_pairs={{128,1},{129,0},{130,3},{131,2},{132,5},{133,4},{134,7},{135,6},{1... | collective-permute-start | bytes 1572872 | tf_op jit(solution)/shard_map/ppermute | solution.py:323
  15.2 9.4 %copy-start = (bf16[2,6,256,256]{3,2,1,0:T(8,128)(2,1)S(1)}, bf16[2,6,256,256]{3,2,1,0:T(8,128)(2,1)}, u32[]{:S(2)}) copy-start(bf16[2,6,256,256]{3,2,1,0:T(8,128)(2,1)} %constant.2.clone.table_ref) | copy-start | bytes 4718596
  15.2 9.4 %copy-start.2 = (f32[2,256,256]{2,1,0:T(8,128)S(1)}, f32[2,256,256]{2,1,0:T(8,128)}, u32[]{:S(2)}) copy-start(f32[2,256,256]{2,1,0:T(8,128)} %probe_ref.1) | copy-start | bytes 1572868
  15.2 9.4 %copy-start.4 = (s32[2,2]{1,0:T(2,128)S(1)}, s32[2,2]{1,0:T(2,128)}, u32[]{:S(2)}) copy-start(s32[2,2]{1,0:T(2,128)} %pos_ref.5) | copy-start | bytes 52
  16.0 9.4 %collective-permute-start.7 = (f32[2,2,128,256]{3,2,1,0:T(8,128)S(1)}, f32[2,2,128,256]{3,2,1,0:T(8,128)S(1)}, u32[]{:S(2)}, u32[]{:S(2)}) collective-permute-start(f32[2,2,128,256]{3,2,1,0:T(8,128)S(1)} %get-tuple-element.15), channel_id=1, source_target_pairs={{129,2},{130,1},{131,4},{132,3},{133,6},{134,5},{135,8},{136,7},{1... | collective-permute-start | bytes 1572872 | tf_op jit(solution)/shard_map/ppermute | solution.py:323
  17.4 9.4 %collective-permute-start.8 = (f32[2,2,128,256]{3,2,1,0:T(8,128)S(1)}, f32[2,2,128,256]{3,2,1,0:T(8,128)S(1)}, u32[]{:S(2)}, u32[]{:S(2)}) collective-permute-start(f32[2,2,128,256]{3,2,1,0:T(8,128)S(1)} %get-tuple-element.16), channel_id=1, source_target_pairs={{128,1},{129,0},{130,3},{131,2},{132,5},{133,4},{134,7},{135,6},{1... | collective-permute-start | bytes 1572872 | tf_op jit(solution)/shard_map/ppermute | solution.py:323
  19.3 7.4 %copy-start.3 = (f32[2,256,256]{2,1,0:T(8,128)S(1)}, f32[2,256,256]{2,1,0:T(8,128)}, u32[]{:S(2)}) copy-start(f32[2,256,256]{2,1,0:T(8,128)} %intensity_ref.1) | copy-start | bytes 1572868
  19.4 2.2 %collective-permute-start.2 = (s32[2,2]{1,0:T(2,128)S(1)}, s32[2,2]{1,0:T(2,128)S(1)}, u32[]{:S(2)}, u32[]{:S(2)}) collective-permute-start(s32[2,2]{1,0:T(2,128)S(1)} %collective-permute-done.first_ref), channel_id=1, source_target_pairs={{128,0},{129,1},{130,2},{131,3},{132,4},{133,5},{134,6},{135,7},{1... | collective-permute-start | bytes 56 | tf_op jit(solution)/shard_map/ppermute | solution.py:323
  21.6 3.0 %collective-permute-start.3 = (s32[2,2]{1,0:T(2,128)S(1)}, s32[2,2]{1,0:T(2,128)S(1)}, u32[]{:S(2)}, u32[]{:S(2)}) collective-permute-start(s32[2,2]{1,0:T(2,128)S(1)} %collective-permute-done.1.second_ref), channel_id=1, source_target_pairs={{128,0},{129,1},{130,2},{131,3},{132,4},{133,5},{134,6},{135,7},{1... | collective-permute-start | bytes 56 | tf_op jit(solution)/shard_map/ppermute | solution.py:323
  27.3 18.0 %collective-permute-start.9 = (f32[2,2,128,256]{3,2,1,0:T(8,128)S(1)}, f32[2,2,128,256]{3,2,1,0:T(8,128)S(1)}, u32[]{:S(2)}, u32[]{:S(2)}) collective-permute-start(f32[2,2,128,256]{3,2,1,0:T(8,128)S(1)} %get-tuple-element.18), channel_id=1, source_target_pairs={{1,130},{2,129},{3,132},{4,131},{5,134},{6,133},{7,136},{8,135},{9... | collective-permute-start | bytes 1572872 | tf_op jit(solution)/shard_map/ppermute | solution.py:323
  28.6 18.1 %collective-permute-start.11 = (f32[2,2,128,256]{3,2,1,0:T(8,128)S(1)}, f32[2,2,128,256]{3,2,1,0:T(8,128)S(1)}, u32[]{:S(2)}, u32[]{:S(2)}) collective-permute-start(f32[2,2,128,256]{3,2,1,0:T(8,128)S(1)} %get-tuple-element.18), channel_id=1, source_target_pairs={{0,129},{1,128},{2,131},{3,130},{4,133},{5,132},{6,135},{7,134},{8... | collective-permute-start | bytes 1572872 | tf_op jit(solution)/shard_map/ppermute | solution.py:323
  29.9 21.1 %collective-permute-start.13 = (f32[2,2,128,256]{3,2,1,0:T(8,128)S(1)}, f32[2,2,128,256]{3,2,1,0:T(8,128)S(1)}, u32[]{:S(2)}, u32[]{:S(2)}) collective-permute-start(f32[2,2,128,256]{3,2,1,0:T(8,128)S(1)} %get-tuple-element.19), channel_id=1, source_target_pairs={{1,130},{2,129},{3,132},{4,131},{5,134},{6,133},{7,136},{8,135},{9... | collective-permute-start | bytes 1572872 | tf_op jit(solution)/shard_map/ppermute | solution.py:323
  31.2 19.8 %collective-permute-start.14 = (f32[2,2,128,256]{3,2,1,0:T(8,128)S(1)}, f32[2,2,128,256]{3,2,1,0:T(8,128)S(1)}, u32[]{:S(2)}, u32[]{:S(2)}) collective-permute-start(f32[2,2,128,256]{3,2,1,0:T(8,128)S(1)} %get-tuple-element.19), channel_id=1, source_target_pairs={{0,129},{1,128},{2,131},{3,130},{4,133},{5,132},{6,135},{7,134},{8... | collective-permute-start | bytes 1572872 | tf_op jit(solution)/shard_map/ppermute | solution.py:323
  32.5 18.5 %collective-permute-start.15 = (f32[2,2,128,256]{3,2,1,0:T(8,128)S(1)}, f32[2,2,128,256]{3,2,1,0:T(8,128)S(1)}, u32[]{:S(2)}, u32[]{:S(2)}) collective-permute-start(f32[2,2,128,256]{3,2,1,0:T(8,128)S(1)} %get-tuple-element.20), channel_id=1, source_target_pairs={{0,128},{1,129},{2,130},{3,131},{4,132},{5,133},{6,134},{7,135},{8... | collective-permute-start | bytes 1572872 | tf_op jit(solution)/shard_map/ppermute | solution.py:323
  45.4 5.6 %collective-permute-start.10 = (f32[2,2,128,256]{3,2,1,0:T(8,128)S(1)}, f32[2,2,128,256]{3,2,1,0:T(8,128)S(1)}, u32[]{:S(2)}, u32[]{:S(2)}) collective-permute-start(f32[2,2,128,256]{3,2,1,0:T(8,128)S(1)} %collective-permute-done.9), channel_id=1, source_target_pairs={{128,0},{129,1},{130,2},{131,3},{132,4},{133,5},{134,6},{135,7},{1... | collective-permute-start | bytes 1572872 | tf_op jit(solution)/shard_map/ppermute | solution.py:323
  46.7 4.3 %collective-permute-start.12 = (f32[2,2,128,256]{3,2,1,0:T(8,128)S(1)}, f32[2,2,128,256]{3,2,1,0:T(8,128)S(1)}, u32[]{:S(2)}, u32[]{:S(2)}) collective-permute-start(f32[2,2,128,256]{3,2,1,0:T(8,128)S(1)} %collective-permute-done.11), channel_id=1, source_target_pairs={{128,0},{129,1},{130,2},{131,3},{132,4},{133,5},{134,6},{135,7},{1... | collective-permute-start | bytes 1572872 | tf_op jit(solution)/shard_map/ppermute | solution.py:323

commit v9 on v7

--- a/solution.py
+++ b/solution.py
@@ -71,6 +71,14 @@
     return pl.ds(pl.multiple_of(number * HALF, HALF), HALF)
 
 
+def entry(ref, slot, which):
+    rows = lax.broadcasted_iota(jnp.int32, (2, 2), 0)
+    columns = lax.broadcasted_iota(jnp.int32, (2, 2), 1)
+    values = ref[...].astype(jnp.float32)
+    chosen = jnp.where((rows == slot) & (columns == which), values, 0.0)
+    return jnp.sum(chosen).astype(jnp.int32)
+
+
 def cut_piece(strip_ref, column, out_ref):
     first = lax.shift_right_logical(column, 7)
     offset = jnp.bitwise_and(column, HALF - 1)
@@ -94,9 +102,9 @@
     @pl.when(lax.axis_index("cuts") == 1)
     def _():
         for slot in range(2):
-            cut_piece(strip_ref, first_ref[slot, 1], to_first_ref.at[slot])
+            cut_piece(strip_ref, entry(first_ref, slot, 1), to_first_ref.at[slot])
         for slot in range(2):
-            cut_piece(strip_ref, second_ref[slot, 1], to_second_ref.at[slot])
+            cut_piece(strip_ref, entry(second_ref, slot, 1), to_second_ref.at[slot])
 
 
 def slots_of_core(counts_ref):
@@ -106,8 +114,8 @@
 def fill_window(pos_ref, slot, strip_ref, first_ref, second_ref, window_ref):
     tile = lax.axis_index("tile")
     odd = jnp.bitwise_and(tile, 1)
-    shift_rows = pos_ref[slot, 0] - (tile - 1) * HALF
-    column = pos_ref[slot, 1]
+    shift_rows = entry(pos_ref, slot, 0) - (tile - 1) * HALF
+    column = entry(pos_ref, slot, 1)
     rows = lax.broadcasted_iota(jnp.int32, (HALF, WIN), 0)
     from_first = (1 - 2 * odd) * (rows - shift_rows) >= odd
     for part in range(2):
@@ -247,20 +255,25 @@
 
     def gather(mid_ref, *nearby):
         copies = []
+        columns = [entry(pos_ref, slot, 1) for slot in range(2)]
+        places = [
+            [(entry(place_ref, slot, 0), entry(place_ref, slot, 1)) for slot in range(2)]
+            for _, place_ref, _ in nearby
+        ]
         for part in range(2):
             for top in range(0, HALF, CHUNK):
                 here = pl.ds(top, CHUNK)
                 total = sum_ref.at[part, here]
                 total[...] = jnp.zeros(total.shape, jnp.float32)
                 for slot in range(2):
-                    add_piece(total, mid_ref.at[slot, part, here], pos_ref[slot, 1], None)
-                for piece_ref, place_ref, above in nearby:
+                    add_piece(total, mid_ref.at[slot, part, here], columns[slot], None)
+                for (piece_ref, _, above), place in zip(nearby, places):
                     sign = 2 * above - 1
                     for slot in range(2):
-                        shift_rows = place_ref[slot, 0] - (tile + sign - 1) * HALF - top
+                        shift_rows = place[slot][0] - (tile + sign - 1) * HALF - top
                         keep = sign * (rows - shift_rows) >= 1 - above
                         piece = piece_ref.at[slot, part, here]
-                        add_piece(total, piece, place_ref[slot, 1], keep)
+                        add_piece(total, piece, place[slot][1], keep)
                 copy = pltpu.make_async_copy(
                     total, out_ref.at[0, part, here], sem.at[len(copies)]
                 )
@@ -336,7 +349,7 @@
 
     def cut(name, source):
         return kernel(
-            cut_kernel, name, (pieces,) * 2, [SMEM] * 2 + [VMEM], 0, 2 << 20, (), (VMEM,) * 2
+            cut_kernel, name, (pieces,) * 2, [VMEM] * 2 + [VMEM], 0, 2 << 20, (), (VMEM,) * 2
         )(pos_first, pos_second, source)
 
     to_first_zero, to_second_zero = cut("cut_zero", other_slice)
@@ -351,7 +364,7 @@
         enter_kernel,
         "enter",
         jax.ShapeDtypeStruct((2, 2, 2, WIN, WIN), jnp.float32),
-        [SMEM] * 2 + [VMEM] * 5 + [ANY] * 2,
+        [VMEM, SMEM] + [VMEM] * 5 + [ANY] * 2,
         18 * 2 * WIN**3,
         3 << 20,
         window,
@@ -360,7 +373,7 @@
         slot_kernel,
         "slot",
         (pieces,) * 4,
-        [SMEM] * 2 + [VMEM] * 6,
+        [VMEM, SMEM] + [VMEM] * 6,
         54 * 2 * WIN**3,
         6 << 20,
         window,
@@ -375,7 +388,7 @@
         collect_kernel,
         "collect",
         strip,
-        [SMEM] * 5 + [VMEM] * 6,
+        [VMEM] * 11,
         0,
         4 << 20,
         (pltpu.VMEM(strip.shape[1:], jnp.float32), pltpu.SemaphoreType.DMA((2 * HALF // CHUNK,))),

time: 53.6 us -> 52.3 us (0.976)
  Pallas kernels: 5.01 us -> 2.47 us
  waiting for transfers between devices: 20.3 us -> 21.4 us
    pallas_call x4, Pallas kernels: 4.29 us -> 2.3 us  [the longest x1 1.63 us: local(): kernel(collect_kernel, 'collect', strip, [VMEM] * 11, 0, 4 << 20, (pltpu....]
    ppermute x15, waiting for transfers between devices: 20.3 us -> 21.4 us  [send(): return lax.ppermute(value, ('cuts', 'tile'), pairs)]
    pallas_call x1, Pallas kernels: 0.57 us -> 0.02 us  [local(): kernel(enter_kernel, 'enter', jax.ShapeDtypeStruct((2, 2, 2, WIN, WIN), j...]
  transfers between devices with their start and end apart: 16 -> 16, of which waited for: 8 -> 8; matrix products, arithmetic and copies ran while one was open for 0% -> 0% of each run, Pallas kernels for 3% -> 1%
where the time goes in v9:
time: 52.3 us; the launch traced here: 51.9 us
  starting transfers between devices  27.1 us (52%)
  waiting for transfers between devices  21.4 us (41%)
  Pallas kernels  2.47 us (5%)
  between operations  0.89 us (2%)
    ppermute x15, starting transfers between devices, send(): return lax.ppermute(value, ('cuts', 'tile'), pairs)  26.4 us
    ppermute x15, waiting for transfers between devices, send(): return lax.ppermute(value, ('cuts', 'tile'), pairs)  21.4 us
    pallas_call x1, Pallas kernels, local(): kernel(collect_kernel, 'collect', strip, [VMEM] * 11, 0, 4 << 20, (pltpu....  1.63 us
  transfers between devices with their start and end apart: 16, of which 8 were waited for; matrix products, arithmetic and copies ran while one was open for 0% of the time, Pallas kernels for 1%

profile of v9, /device:TPU:129, one launch (start us, length us, event | category | flops | bytes accessed | tf_op | source)
XLA Modules:
  0.0 51.9 jit_solution(6168155996038705073)
XLA Ops:
  0.0 0.7 %collective-permute-start.4 = (f32[1,2,128,2048]{3,2,1,0:T(8,128)}, f32[1,2,128,2048]{3,2,1,0:T(8,128)S(1)}, u32[]{:S(2)}, u32[]{:S(2)}) collective-permute-start(f32[1,2,128,2048]{3,2,1,0:T(8,128)} %strip_ref.1), channel_id=1, source_target_pairs={{0,128},{128,0},{1,129},{129,1},{2,130},{130,2},{3,131},{131,3},{4... | collective-permute-start | bytes 6291464 | tf_op jit(solution)/shard_map/ppermute | solution.py:343
  0.7 6.4 %collective-permute-start = (s32[2,2]{1,0:T(2,128)}, s32[2,2]{1,0:T(2,128)S(1)}, u32[]{:S(2)}, u32[]{:S(2)}) collective-permute-start(s32[2,2]{1,0:T(2,128)} %pos_ref.5), channel_id=1, source_target_pairs={{129,130},{130,129},{131,132},{132,131},{133,134},{134,133},{135,1... | collective-permute-start | bytes 56 | tf_op jit(solution)/shard_map/ppermute | solution.py:325
  7.1 1.9 %collective-permute-start.1 = (s32[2,2]{1,0:T(2,128)}, s32[2,2]{1,0:T(2,128)S(1)}, u32[]{:S(2)}, u32[]{:S(2)}) collective-permute-start(s32[2,2]{1,0:T(2,128)} %pos_ref.5), channel_id=1, source_target_pairs={{128,129},{129,128},{130,131},{131,130},{132,133},{133,132},{134,1... | collective-permute-start | bytes 56 | tf_op jit(solution)/shard_map/ppermute | solution.py:325
  9.0 1.6 %collective-permute-done.first_ref = s32[2,2]{1,0:T(2,128)S(1)} collective-permute-done((s32[2,2]{1,0:T(2,128)}, s32[2,2]{1,0:T(2,128)S(1)}, u32[]{:S(2)}, u32[]{:S(2)}) %collective-permute-start) | collective-permute-done | bytes 48 | tf_op jit(solution)/shard_map/ppermute | solution.py:325
  10.6 1.0 %collective-permute-done.1.second_ref = s32[2,2]{1,0:T(2,128)S(1)} collective-permute-done((s32[2,2]{1,0:T(2,128)}, s32[2,2]{1,0:T(2,128)S(1)}, u32[]{:S(2)}, u32[]{:S(2)}) %collective-permute-start.1) | collective-permute-done | bytes 48 | tf_op jit(solution)/shard_map/ppermute | solution.py:325
  11.6 0.3 cut_zero.1
  11.9 1.3 %collective-permute-start.5 = (f32[2,2,128,256]{3,2,1,0:T(8,128)S(1)}, f32[2,2,128,256]{3,2,1,0:T(8,128)S(1)}, u32[]{:S(2)}, u32[]{:S(2)}) collective-permute-start(f32[2,2,128,256]{3,2,1,0:T(8,128)S(1)} %get-tuple-element.13), channel_id=1, source_target_pairs={{129,2},{130,1},{131,4},{132,3},{133,6},{134,5},{135,8},{136,7},{1... | collective-permute-start | bytes 1572872 | tf_op jit(solution)/shard_map/ppermute | solution.py:325
  13.3 1.3 %collective-permute-start.6 = (f32[2,2,128,256]{3,2,1,0:T(8,128)S(1)}, f32[2,2,128,256]{3,2,1,0:T(8,128)S(1)}, u32[]{:S(2)}, u32[]{:S(2)}) collective-permute-start(f32[2,2,128,256]{3,2,1,0:T(8,128)S(1)} %get-tuple-element.14), channel_id=1, source_target_pairs={{128,1},{129,0},{130,3},{131,2},{132,5},{133,4},{134,7},{135,6},{1... | collective-permute-start | bytes 1572872 | tf_op jit(solution)/shard_map/ppermute | solution.py:325
  14.6 0.2 stage.1.own_ref.strip_ref
  14.8 0.0 copy-start
  14.8 0.0 copy-start.2
  14.8 0.0 copy-start.4
  14.8 0.3 cut_one.1
  15.1 1.5 %collective-permute-start.7 = (f32[2,2,128,256]{3,2,1,0:T(8,128)S(1)}, f32[2,2,128,256]{3,2,1,0:T(8,128)S(1)}, u32[]{:S(2)}, u32[]{:S(2)}) collective-permute-start(f32[2,2,128,256]{3,2,1,0:T(8,128)S(1)} %get-tuple-element.15), channel_id=1, source_target_pairs={{129,2},{130,1},{131,4},{132,3},{133,6},{134,5},{135,8},{136,7},{1... | collective-permute-start | bytes 1572872 | tf_op jit(solution)/shard_map/ppermute | solution.py:325
  16.6 1.3 %collective-permute-start.8 = (f32[2,2,128,256]{3,2,1,0:T(8,128)S(1)}, f32[2,2,128,256]{3,2,1,0:T(8,128)S(1)}, u32[]{:S(2)}, u32[]{:S(2)}) collective-permute-start(f32[2,2,128,256]{3,2,1,0:T(8,128)S(1)} %get-tuple-element.16), channel_id=1, source_target_pairs={{128,1},{129,0},{130,3},{131,2},{132,5},{133,4},{134,7},{135,6},{1... | collective-permute-start | bytes 1572872 | tf_op jit(solution)/shard_map/ppermute | solution.py:325
  18.6 0.0 copy-start.3
  18.6 1.4 %collective-permute-start.2 = (s32[2,2]{1,0:T(2,128)S(1)}, s32[2,2]{1,0:T(2,128)S(1)}, u32[]{:S(2)}, u32[]{:S(2)}) collective-permute-start(s32[2,2]{1,0:T(2,128)S(1)} %collective-permute-done.first_ref), channel_id=1, source_target_pairs={{128,0},{129,1},{130,2},{131,3},{132,4},{133,5},{134,6},{135,7},{1... | collective-permute-start | bytes 56 | tf_op jit(solution)/shard_map/ppermute | solution.py:325
  20.0 0.8 %collective-permute-done.2.first_copy_ref = s32[2,2]{1,0:T(2,128)S(1)} collective-permute-done((s32[2,2]{1,0:T(2,128)S(1)}, s32[2,2]{1,0:T(2,128)S(1)}, u32[]{:S(2)}, u32[]{:S(2)}) %collective-permute-start.2) | collective-permute-done | bytes 48 | tf_op jit(solution)/shard_map/ppermute | solution.py:325
  20.8 2.2 %collective-permute-start.3 = (s32[2,2]{1,0:T(2,128)S(1)}, s32[2,2]{1,0:T(2,128)S(1)}, u32[]{:S(2)}, u32[]{:S(2)}) collective-permute-start(s32[2,2]{1,0:T(2,128)S(1)} %collective-permute-done.1.second_ref), channel_id=1, source_target_pairs={{128,0},{129,1},{130,2},{131,3},{132,4},{133,5},{134,6},{135,7},{1... | collective-permute-start | bytes 56 | tf_op jit(solution)/shard_map/ppermute | solution.py:325
  23.0 0.8 %collective-permute-done.3.second_copy_ref = s32[2,2]{1,0:T(2,128)S(1)} collective-permute-done((s32[2,2]{1,0:T(2,128)S(1)}, s32[2,2]{1,0:T(2,128)S(1)}, u32[]{:S(2)}, u32[]{:S(2)}) %collective-permute-start.3) | collective-permute-done | bytes 48 | tf_op jit(solution)/shard_map/ppermute | solution.py:325
  23.9 1.0 %collective-permute-done.7.first_ref = f32[2,2,128,256]{3,2,1,0:T(8,128)S(1)} collective-permute-done((f32[2,2,128,256]{3,2,1,0:T(8,128)S(1)}, f32[2,2,128,256]{3,2,1,0:T(8,128)S(1)}, u32[]{:S(2)}, u32[]{:S(2)}) %collective-permute-start.7) | collective-permute-done | bytes 524320 | tf_op jit(solution)/shard_map/ppermute | solution.py:325
  24.9 1.3 %collective-permute-done.8.second_ref = f32[2,2,128,256]{3,2,1,0:T(8,128)S(1)} collective-permute-done((f32[2,2,128,256]{3,2,1,0:T(8,128)S(1)}, f32[2,2,128,256]{3,2,1,0:T(8,128)S(1)}, u32[]{:S(2)}, u32[]{:S(2)}) %collective-permute-start.8) | collective-permute-done | bytes 524320 | tf_op jit(solution)/shard_map/ppermute | solution.py:325
  26.3 1.3 %collective-permute-start.9 = (f32[2,2,128,256]{3,2,1,0:T(8,128)S(1)}, f32[2,2,128,256]{3,2,1,0:T(8,128)S(1)}, u32[]{:S(2)}, u32[]{:S(2)}) collective-permute-start(f32[2,2,128,256]{3,2,1,0:T(8,128)S(1)} %get-tuple-element.18), channel_id=1, source_target_pairs={{1,130},{2,129},{3,132},{4,131},{5,134},{6,133},{7,136},{8,135},{9... | collective-permute-start | bytes 1572872 | tf_op jit(solution)/shard_map/ppermute | solution.py:325
  27.6 1.3 %collective-permute-start.11 = (f32[2,2,128,256]{3,2,1,0:T(8,128)S(1)}, f32[2,2,128,256]{3,2,1,0:T(8,128)S(1)}, u32[]{:S(2)}, u32[]{:S(2)}) collective-permute-start(f32[2,2,128,256]{3,2,1,0:T(8,128)S(1)} %get-tuple-element.18), channel_id=1, source_target_pairs={{0,129},{1,128},{2,131},{3,130},{4,133},{5,132},{6,135},{7,134},{8... | collective-permute-start | bytes 1572872 | tf_op jit(solution)/shard_map/ppermute | solution.py:325
  28.9 1.3 %collective-permute-start.13 = (f32[2,2,128,256]{3,2,1,0:T(8,128)S(1)}, f32[2,2,128,256]{3,2,1,0:T(8,128)S(1)}, u32[]{:S(2)}, u32[]{:S(2)}) collective-permute-start(f32[2,2,128,256]{3,2,1,0:T(8,128)S(1)} %get-tuple-element.19), channel_id=1, source_target_pairs={{1,130},{2,129},{3,132},{4,131},{5,134},{6,133},{7,136},{8,135},{9... | collective-permute-start | bytes 1572872 | tf_op jit(solution)/shard_map/ppermute | solution.py:325
  30.2 1.3 %collective-permute-start.14 = (f32[2,2,128,256]{3,2,1,0:T(8,128)S(1)}, f32[2,2,128,256]{3,2,1,0:T(8,128)S(1)}, u32[]{:S(2)}, u32[]{:S(2)}) collective-permute-start(f32[2,2,128,256]{3,2,1,0:T(8,128)S(1)} %get-tuple-element.19), channel_id=1, source_target_pairs={{0,129},{1,128},{2,131},{3,130},{4,133},{5,132},{6,135},{7,134},{8... | collective-permute-start | bytes 1572872 | tf_op jit(solution)/shard_map/ppermute | solution.py:325
  31.5 1.3 %collective-permute-start.15 = (f32[2,2,128,256]{3,2,1,0:T(8,128)S(1)}, f32[2,2,128,256]{3,2,1,0:T(8,128)S(1)}, u32[]{:S(2)}, u32[]{:S(2)}) collective-permute-start(f32[2,2,128,256]{3,2,1,0:T(8,128)S(1)} %get-tuple-element.20), channel_id=1, source_target_pairs={{0,128},{1,129},{2,130},{3,131},{4,132},{5,133},{6,134},{7,135},{8... | collective-permute-start | bytes 1572872 | tf_op jit(solution)/shard_map/ppermute | solution.py:325
  32.8 11.8 %collective-permute-done.9 = f32[2,2,128,256]{3,2,1,0:T(8,128)S(1)} collective-permute-done((f32[2,2,128,256]{3,2,1,0:T(8,128)S(1)}, f32[2,2,128,256]{3,2,1,0:T(8,128)S(1)}, u32[]{:S(2)}, u32[]{:S(2)}) %collective-permute-start.9) | collective-permute-done | bytes 524320 | tf_op jit(solution)/shard_map/ppermute | solution.py:325
  44.6 1.3 %collective-permute-start.10 = (f32[2,2,128,256]{3,2,1,0:T(8,128)S(1)}, f32[2,2,128,256]{3,2,1,0:T(8,128)S(1)}, u32[]{:S(2)}, u32[]{:S(2)}) collective-permute-start(f32[2,2,128,256]{3,2,1,0:T(8,128)S(1)} %collective-permute-done.9), channel_id=1, source_target_pairs={{128,0},{129,1},{130,2},{131,3},{132,4},{133,5},{134,6},{135,7},{1... | collective-permute-start | bytes 1572872 | tf_op jit(solution)/shard_map/ppermute | solution.py:325
  45.9 1.3 %collective-permute-start.12 = (f32[2,2,128,256]{3,2,1,0:T(8,128)S(1)}, f32[2,2,128,256]{3,2,1,0:T(8,128)S(1)}, u32[]{:S(2)}, u32[]{:S(2)}) collective-permute-start(f32[2,2,128,256]{3,2,1,0:T(8,128)S(1)} %collective-permute-done.11), channel_id=1, source_target_pairs={{128,0},{129,1},{130,2},{131,3},{132,4},{133,5},{134,6},{135,7},{1... | collective-permute-start | bytes 1572872 | tf_op jit(solution)/shard_map/ppermute | solution.py:325
  47.3 3.0 %collective-permute-done.13.first_one_ref = f32[2,2,128,256]{3,2,1,0:T(8,128)S(1)} collective-permute-done((f32[2,2,128,256]{3,2,1,0:T(8,128)S(1)}, f32[2,2,128,256]{3,2,1,0:T(8,128)S(1)}, u32[]{:S(2)}, u32[]{:S(2)}) %collective-permute-start.13) | collective-permute-done | bytes 524320 | tf_op jit(solution)/shard_map/ppermute | solution.py:325
  50.2 1.6 %collect.1 = f32[1,2,128,2048]{3,2,1,0:T(8,128)} custom-call(s32[2,2]{1,0:T(2,128)S(1)} %copy-done.4, s32[2,2]{1,0:T(2,128)S(1)} %collective-permute-done.first_ref, s32[2,2]{1,0:T(2,128)S(1)} %collective-permute-done.1.second_ref, s32[2,2]{1,0:T(2,128)S(1)} %collective-permute-done.2.first_copy_ref, s32[2,2]{1,0:T(2,128)S(1)} %collective-permute-done.3.second_copy_ref, ...), custom_call_target="tpu_custom_call" | custom-call | bytes 4194304 | tf_op jit(solution)/shard_map/collect/pallas_call | solution.py:387
  (16 shorter events, 0.1 us)
Async XLA Ops:
  0.0 14.6 %copy-start.1 = (f32[1,2,128,2048]{3,2,1,0:T(8,128)S(1)}, f32[1,2,128,2048]{3,2,1,0:T(8,128)}, u32[]{:S(2)}) copy-start(f32[1,2,128,2048]{3,2,1,0:T(8,128)} %strip_ref.1) | copy-start | bytes 6291460
  0.0 11.6 %collective-permute-start.4 = (f32[1,2,128,2048]{3,2,1,0:T(8,128)}, f32[1,2,128,2048]{3,2,1,0:T(8,128)S(1)}, u32[]{:S(2)}, u32[]{:S(2)}) collective-permute-start(f32[1,2,128,2048]{3,2,1,0:T(8,128)} %strip_ref.1), channel_id=1, source_target_pairs={{0,128},{128,0},{1,129},{129,1},{2,130},{130,2},{3,131},{131,3},{4... | collective-permute-start | bytes 6291464 | tf_op jit(solution)/shard_map/ppermute | solution.py:343
  0.7 9.9 %collective-permute-start = (s32[2,2]{1,0:T(2,128)}, s32[2,2]{1,0:T(2,128)S(1)}, u32[]{:S(2)}, u32[]{:S(2)}) collective-permute-start(s32[2,2]{1,0:T(2,128)} %pos_ref.5), channel_id=1, source_target_pairs={{129,130},{130,129},{131,132},{132,131},{133,134},{134,133},{135,1... | collective-permute-start | bytes 56 | tf_op jit(solution)/shard_map/ppermute | solution.py:325
  7.1 4.5 %collective-permute-start.1 = (s32[2,2]{1,0:T(2,128)}, s32[2,2]{1,0:T(2,128)S(1)}, u32[]{:S(2)}, u32[]{:S(2)}) collective-permute-start(s32[2,2]{1,0:T(2,128)} %pos_ref.5), channel_id=1, source_target_pairs={{128,129},{129,128},{130,131},{131,130},{132,133},{133,132},{134,1... | collective-permute-start | bytes 56 | tf_op jit(solution)/shard_map/ppermute | solution.py:325
  11.9 11.9 %collective-permute-start.5 = (f32[2,2,128,256]{3,2,1,0:T(8,128)S(1)}, f32[2,2,128,256]{3,2,1,0:T(8,128)S(1)}, u32[]{:S(2)}, u32[]{:S(2)}) collective-permute-start(f32[2,2,128,256]{3,2,1,0:T(8,128)S(1)} %get-tuple-element.13), channel_id=1, source_target_pairs={{129,2},{130,1},{131,4},{132,3},{133,6},{134,5},{135,8},{136,7},{1... | collective-permute-start | bytes 1572872 | tf_op jit(solution)/shard_map/ppermute | solution.py:325
  13.3 10.6 %collective-permute-start.6 = (f32[2,2,128,256]{3,2,1,0:T(8,128)S(1)}, f32[2,2,128,256]{3,2,1,0:T(8,128)S(1)}, u32[]{:S(2)}, u32[]{:S(2)}) collective-permute-start(f32[2,2,128,256]{3,2,1,0:T(8,128)S(1)} %get-tuple-element.14), channel_id=1, source_target_pairs={{128,1},{129,0},{130,3},{131,2},{132,5},{133,4},{134,7},{135,6},{1... | collective-permute-start | bytes 1572872 | tf_op jit(solution)/shard_map/ppermute | solution.py:325
  14.8 9.1 %copy-start = (bf16[2,6,256,256]{3,2,1,0:T(8,128)(2,1)S(1)}, bf16[2,6,256,256]{3,2,1,0:T(8,128)(2,1)}, u32[]{:S(2)}) copy-start(bf16[2,6,256,256]{3,2,1,0:T(8,128)(2,1)} %constant.2.clone.table_ref) | copy-start | bytes 4718596
  14.8 9.1 %copy-start.2 = (f32[2,256,256]{2,1,0:T(8,128)S(1)}, f32[2,256,256]{2,1,0:T(8,128)}, u32[]{:S(2)}) copy-start(f32[2,256,256]{2,1,0:T(8,128)} %probe_ref.1) | copy-start | bytes 1572868
  14.8 9.1 %copy-start.4 = (s32[2,2]{1,0:T(2,128)S(1)}, s32[2,2]{1,0:T(2,128)}, u32[]{:S(2)}) copy-start(s32[2,2]{1,0:T(2,128)} %pos_ref.5) | copy-start | bytes 52
  15.1 9.8 %collective-permute-start.7 = (f32[2,2,128,256]{3,2,1,0:T(8,128)S(1)}, f32[2,2,128,256]{3,2,1,0:T(8,128)S(1)}, u32[]{:S(2)}, u32[]{:S(2)}) collective-permute-start(f32[2,2,128,256]{3,2,1,0:T(8,128)S(1)} %get-tuple-element.15), channel_id=1, source_target_pairs={{129,2},{130,1},{131,4},{132,3},{133,6},{134,5},{135,8},{136,7},{1... | collective-permute-start | bytes 1572872 | tf_op jit(solution)/shard_map/ppermute | solution.py:325
  16.6 9.7 %collective-permute-start.8 = (f32[2,2,128,256]{3,2,1,0:T(8,128)S(1)}, f32[2,2,128,256]{3,2,1,0:T(8,128)S(1)}, u32[]{:S(2)}, u32[]{:S(2)}) collective-permute-start(f32[2,2,128,256]{3,2,1,0:T(8,128)S(1)} %get-tuple-element.16), channel_id=1, source_target_pairs={{128,1},{129,0},{130,3},{131,2},{132,5},{133,4},{134,7},{135,6},{1... | collective-permute-start | bytes 1572872 | tf_op jit(solution)/shard_map/ppermute | solution.py:325
  18.6 7.7 %copy-start.3 = (f32[2,256,256]{2,1,0:T(8,128)S(1)}, f32[2,256,256]{2,1,0:T(8,128)}, u32[]{:S(2)}) copy-start(f32[2,256,256]{2,1,0:T(8,128)} %intensity_ref.1) | copy-start | bytes 1572868
  18.6 2.2 %collective-permute-start.2 = (s32[2,2]{1,0:T(2,128)S(1)}, s32[2,2]{1,0:T(2,128)S(1)}, u32[]{:S(2)}, u32[]{:S(2)}) collective-permute-start(s32[2,2]{1,0:T(2,128)S(1)} %collective-permute-done.first_ref), channel_id=1, source_target_pairs={{128,0},{129,1},{130,2},{131,3},{132,4},{133,5},{134,6},{135,7},{1... | collective-permute-start | bytes 56 | tf_op jit(solution)/shard_map/ppermute | solution.py:325
  20.8 3.0 %collective-permute-start.3 = (s32[2,2]{1,0:T(2,128)S(1)}, s32[2,2]{1,0:T(2,128)S(1)}, u32[]{:S(2)}, u32[]{:S(2)}) collective-permute-start(s32[2,2]{1,0:T(2,128)S(1)} %collective-permute-done.1.second_ref), channel_id=1, source_target_pairs={{128,0},{129,1},{130,2},{131,3},{132,4},{133,5},{134,6},{135,7},{1... | collective-permute-start | bytes 56 | tf_op jit(solution)/shard_map/ppermute | solution.py:325
  26.3 18.3 %collective-permute-start.9 = (f32[2,2,128,256]{3,2,1,0:T(8,128)S(1)}, f32[2,2,128,256]{3,2,1,0:T(8,128)S(1)}, u32[]{:S(2)}, u32[]{:S(2)}) collective-permute-start(f32[2,2,128,256]{3,2,1,0:T(8,128)S(1)} %get-tuple-element.18), channel_id=1, source_target_pairs={{1,130},{2,129},{3,132},{4,131},{5,134},{6,133},{7,136},{8,135},{9... | collective-permute-start | bytes 1572872 | tf_op jit(solution)/shard_map/ppermute | solution.py:325
  27.6 18.4 %collective-permute-start.11 = (f32[2,2,128,256]{3,2,1,0:T(8,128)S(1)}, f32[2,2,128,256]{3,2,1,0:T(8,128)S(1)}, u32[]{:S(2)}, u32[]{:S(2)}) collective-permute-start(f32[2,2,128,256]{3,2,1,0:T(8,128)S(1)} %get-tuple-element.18), channel_id=1, source_target_pairs={{0,129},{1,128},{2,131},{3,130},{4,133},{5,132},{6,135},{7,134},{8... | collective-permute-start | bytes 1572872 | tf_op jit(solution)/shard_map/ppermute | solution.py:325
  28.9 21.3 %collective-permute-start.13 = (f32[2,2,128,256]{3,2,1,0:T(8,128)S(1)}, f32[2,2,128,256]{3,2,1,0:T(8,128)S(1)}, u32[]{:S(2)}, u32[]{:S(2)}) collective-permute-start(f32[2,2,128,256]{3,2,1,0:T(8,128)S(1)} %get-tuple-element.19), channel_id=1, source_target_pairs={{1,130},{2,129},{3,132},{4,131},{5,134},{6,133},{7,136},{8,135},{9... | collective-permute-start | bytes 1572872 | tf_op jit(solution)/shard_map/ppermute | solution.py:325
  30.2 20.0 %collective-permute-start.14 = (f32[2,2,128,256]{3,2,1,0:T(8,128)S(1)}, f32[2,2,128,256]{3,2,1,0:T(8,128)S(1)}, u32[]{:S(2)}, u32[]{:S(2)}) collective-permute-start(f32[2,2,128,256]{3,2,1,0:T(8,128)S(1)} %get-tuple-element.19), channel_id=1, source_target_pairs={{0,129},{1,128},{2,131},{3,130},{4,133},{5,132},{6,135},{7,134},{8... | collective-permute-start | bytes 1572872 | tf_op jit(solution)/shard_map/ppermute | solution.py:325
  31.5 18.8 %collective-permute-start.15 = (f32[2,2,128,256]{3,2,1,0:T(8,128)S(1)}, f32[2,2,128,256]{3,2,1,0:T(8,128)S(1)}, u32[]{:S(2)}, u32[]{:S(2)}) collective-permute-start(f32[2,2,128,256]{3,2,1,0:T(8,128)S(1)} %get-tuple-element.20), channel_id=1, source_target_pairs={{0,128},{1,129},{2,130},{3,131},{4,132},{5,133},{6,134},{7,135},{8... | collective-permute-start | bytes 1572872 | tf_op jit(solution)/shard_map/ppermute | solution.py:325
  44.6 5.6 %collective-permute-start.10 = (f32[2,2,128,256]{3,2,1,0:T(8,128)S(1)}, f32[2,2,128,256]{3,2,1,0:T(8,128)S(1)}, u32[]{:S(2)}, u32[]{:S(2)}) collective-permute-start(f32[2,2,128,256]{3,2,1,0:T(8,128)S(1)} %collective-permute-done.9), channel_id=1, source_target_pairs={{128,0},{129,1},{130,2},{131,3},{132,4},{133,5},{134,6},{135,7},{1... | collective-permute-start | bytes 1572872 | tf_op jit(solution)/shard_map/ppermute | solution.py:325
  45.9 4.3 %collective-permute-start.12 = (f32[2,2,128,256]{3,2,1,0:T(8,128)S(1)}, f32[2,2,128,256]{3,2,1,0:T(8,128)S(1)}, u32[]{:S(2)}, u32[]{:S(2)}) collective-permute-start(f32[2,2,128,256]{3,2,1,0:T(8,128)S(1)} %collective-permute-done.11), channel_id=1, source_target_pairs={{128,0},{129,1},{130,2},{131,3},{132,4},{133,5},{134,6},{135,7},{1... | collective-permute-start | bytes 1572872 | tf_op jit(solution)/shard_map/ppermute | solution.py:325

commit v10 on v9

--- a/solution.py
+++ b/solution.py
@@ -10,7 +10,7 @@
 
 WIN = 256
 HALF = 128
-CHUNK = 64
+CHUNK = 32
 
 
 def split_tables(real_part, imag_part):

time: 52.3 us -> 53.1 us (1.015)
  the two profiles are of different devices: /device:TPU:129 before, /device:TPU:193 now
where the time goes in v10:
time: 53.1 us; the launch traced here: 53.5 us
  starting transfers between devices  28 us (53%)
  waiting for transfers between devices  22.1 us (42%)
  Pallas kernels  2.52 us (5%)
  between operations  0.88 us (2%)
    ppermute x15, starting transfers between devices, send(): return lax.ppermute(value, ('cuts', 'tile'), pairs)  27.3 us
    ppermute x15, waiting for transfers between devices, send(): return lax.ppermute(value, ('cuts', 'tile'), pairs)  22.1 us
    pallas_call x1, Pallas kernels, local(): kernel(collect_kernel, 'collect', strip, [VMEM] * 11, 0, 4 << 20, (pltpu....  1.68 us
  transfers between devices with their start and end apart: 16, of which 9 were waited for; matrix products, arithmetic and copies ran while one was open for 0% of the time, Pallas kernels for 1%

profile of v10, /device:TPU:193, one launch (start us, length us, event | category | flops | bytes accessed | tf_op | source)
XLA Modules:
  0.0 53.5 jit_solution(14746422262518051728)
XLA Ops:
  0.0 0.7 %collective-permute-start.4 = (f32[1,2,128,2048]{3,2,1,0:T(8,128)}, f32[1,2,128,2048]{3,2,1,0:T(8,128)S(1)}, u32[]{:S(2)}, u32[]{:S(2)}) collective-permute-start(f32[1,2,128,2048]{3,2,1,0:T(8,128)} %strip_ref.1), channel_id=1, source_target_pairs={{0,128},{128,0},{1,129},{129,1},{2,130},{130,2},{3,131},{131,3},{4... | collective-permute-start | bytes 6291464 | tf_op jit(solution)/shard_map/ppermute | solution.py:343
  0.7 7.3 %collective-permute-start = (s32[2,2]{1,0:T(2,128)}, s32[2,2]{1,0:T(2,128)S(1)}, u32[]{:S(2)}, u32[]{:S(2)}) collective-permute-start(s32[2,2]{1,0:T(2,128)} %pos_ref.5), channel_id=1, source_target_pairs={{129,130},{130,129},{131,132},{132,131},{133,134},{134,133},{135,1... | collective-permute-start | bytes 56 | tf_op jit(solution)/shard_map/ppermute | solution.py:325
  8.0 1.9 %collective-permute-start.1 = (s32[2,2]{1,0:T(2,128)}, s32[2,2]{1,0:T(2,128)S(1)}, u32[]{:S(2)}, u32[]{:S(2)}) collective-permute-start(s32[2,2]{1,0:T(2,128)} %pos_ref.5), channel_id=1, source_target_pairs={{128,129},{129,128},{130,131},{131,130},{132,133},{133,132},{134,1... | collective-permute-start | bytes 56 | tf_op jit(solution)/shard_map/ppermute | solution.py:325
  9.9 2.6 %collective-permute-done.1.second_ref = s32[2,2]{1,0:T(2,128)S(1)} collective-permute-done((s32[2,2]{1,0:T(2,128)}, s32[2,2]{1,0:T(2,128)S(1)}, u32[]{:S(2)}, u32[]{:S(2)}) %collective-permute-start.1) | collective-permute-done | bytes 48 | tf_op jit(solution)/shard_map/ppermute | solution.py:325
  12.5 0.3 cut_zero.1
  12.8 1.3 %collective-permute-start.5 = (f32[2,2,128,256]{3,2,1,0:T(8,128)S(1)}, f32[2,2,128,256]{3,2,1,0:T(8,128)S(1)}, u32[]{:S(2)}, u32[]{:S(2)}) collective-permute-start(f32[2,2,128,256]{3,2,1,0:T(8,128)S(1)} %get-tuple-element.13), channel_id=1, source_target_pairs={{129,2},{130,1},{131,4},{132,3},{133,6},{134,5},{135,8},{136,7},{1... | collective-permute-start | bytes 1572872 | tf_op jit(solution)/shard_map/ppermute | solution.py:325
  14.2 1.3 %collective-permute-start.6 = (f32[2,2,128,256]{3,2,1,0:T(8,128)S(1)}, f32[2,2,128,256]{3,2,1,0:T(8,128)S(1)}, u32[]{:S(2)}, u32[]{:S(2)}) collective-permute-start(f32[2,2,128,256]{3,2,1,0:T(8,128)S(1)} %get-tuple-element.14), channel_id=1, source_target_pairs={{128,1},{129,0},{130,3},{131,2},{132,5},{133,4},{134,7},{135,6},{1... | collective-permute-start | bytes 1572872 | tf_op jit(solution)/shard_map/ppermute | solution.py:325
  15.5 0.2 stage.1.own_ref.strip_ref
  15.7 0.0 copy-start
  15.7 0.0 copy-start.2
  15.7 0.3 cut_one.1
  16.0 1.5 %collective-permute-start.7 = (f32[2,2,128,256]{3,2,1,0:T(8,128)S(1)}, f32[2,2,128,256]{3,2,1,0:T(8,128)S(1)}, u32[]{:S(2)}, u32[]{:S(2)}) collective-permute-start(f32[2,2,128,256]{3,2,1,0:T(8,128)S(1)} %get-tuple-element.15), channel_id=1, source_target_pairs={{129,2},{130,1},{131,4},{132,3},{133,6},{134,5},{135,8},{136,7},{1... | collective-permute-start | bytes 1572872 | tf_op jit(solution)/shard_map/ppermute | solution.py:325
  17.5 1.3 %collective-permute-start.8 = (f32[2,2,128,256]{3,2,1,0:T(8,128)S(1)}, f32[2,2,128,256]{3,2,1,0:T(8,128)S(1)}, u32[]{:S(2)}, u32[]{:S(2)}) collective-permute-start(f32[2,2,128,256]{3,2,1,0:T(8,128)S(1)} %get-tuple-element.16), channel_id=1, source_target_pairs={{128,1},{129,0},{130,3},{131,2},{132,5},{133,4},{134,7},{135,6},{1... | collective-permute-start | bytes 1572872 | tf_op jit(solution)/shard_map/ppermute | solution.py:325
  19.5 0.0 copy-start.3
  19.5 1.4 %collective-permute-start.2 = (s32[2,2]{1,0:T(2,128)S(1)}, s32[2,2]{1,0:T(2,128)S(1)}, u32[]{:S(2)}, u32[]{:S(2)}) collective-permute-start(s32[2,2]{1,0:T(2,128)S(1)} %collective-permute-done.first_ref), channel_id=1, source_target_pairs={{128,0},{129,1},{130,2},{131,3},{132,4},{133,5},{134,6},{135,7},{1... | collective-permute-start | bytes 56 | tf_op jit(solution)/shard_map/ppermute | solution.py:325
  20.9 0.8 %collective-permute-done.2.first_copy_ref = s32[2,2]{1,0:T(2,128)S(1)} collective-permute-done((s32[2,2]{1,0:T(2,128)S(1)}, s32[2,2]{1,0:T(2,128)S(1)}, u32[]{:S(2)}, u32[]{:S(2)}) %collective-permute-start.2) | collective-permute-done | bytes 48 | tf_op jit(solution)/shard_map/ppermute | solution.py:325
  21.7 2.2 %collective-permute-start.3 = (s32[2,2]{1,0:T(2,128)S(1)}, s32[2,2]{1,0:T(2,128)S(1)}, u32[]{:S(2)}, u32[]{:S(2)}) collective-permute-start(s32[2,2]{1,0:T(2,128)S(1)} %collective-permute-done.1.second_ref), channel_id=1, source_target_pairs={{128,0},{129,1},{130,2},{131,3},{132,4},{133,5},{134,6},{135,7},{1... | collective-permute-start | bytes 56 | tf_op jit(solution)/shard_map/ppermute | solution.py:325
  23.9 0.8 %collective-permute-done.3.second_copy_ref = s32[2,2]{1,0:T(2,128)S(1)} collective-permute-done((s32[2,2]{1,0:T(2,128)S(1)}, s32[2,2]{1,0:T(2,128)S(1)}, u32[]{:S(2)}, u32[]{:S(2)}) %collective-permute-start.3) | collective-permute-done | bytes 48 | tf_op jit(solution)/shard_map/ppermute | solution.py:325
  24.8 1.0 %collective-permute-done.7.first_ref = f32[2,2,128,256]{3,2,1,0:T(8,128)S(1)} collective-permute-done((f32[2,2,128,256]{3,2,1,0:T(8,128)S(1)}, f32[2,2,128,256]{3,2,1,0:T(8,128)S(1)}, u32[]{:S(2)}, u32[]{:S(2)}) %collective-permute-start.7) | collective-permute-done | bytes 524320 | tf_op jit(solution)/shard_map/ppermute | solution.py:325
  25.8 1.3 %collective-permute-done.8.second_ref = f32[2,2,128,256]{3,2,1,0:T(8,128)S(1)} collective-permute-done((f32[2,2,128,256]{3,2,1,0:T(8,128)S(1)}, f32[2,2,128,256]{3,2,1,0:T(8,128)S(1)}, u32[]{:S(2)}, u32[]{:S(2)}) %collective-permute-start.8) | collective-permute-done | bytes 524320 | tf_op jit(solution)/shard_map/ppermute | solution.py:325
  27.2 1.3 %collective-permute-start.9 = (f32[2,2,128,256]{3,2,1,0:T(8,128)S(1)}, f32[2,2,128,256]{3,2,1,0:T(8,128)S(1)}, u32[]{:S(2)}, u32[]{:S(2)}) collective-permute-start(f32[2,2,128,256]{3,2,1,0:T(8,128)S(1)} %get-tuple-element.18), channel_id=1, source_target_pairs={{1,130},{2,129},{3,132},{4,131},{5,134},{6,133},{7,136},{8,135},{9... | collective-permute-start | bytes 1572872 | tf_op jit(solution)/shard_map/ppermute | solution.py:325
  28.5 1.3 %collective-permute-start.11 = (f32[2,2,128,256]{3,2,1,0:T(8,128)S(1)}, f32[2,2,128,256]{3,2,1,0:T(8,128)S(1)}, u32[]{:S(2)}, u32[]{:S(2)}) collective-permute-start(f32[2,2,128,256]{3,2,1,0:T(8,128)S(1)} %get-tuple-element.18), channel_id=1, source_target_pairs={{0,129},{1,128},{2,131},{3,130},{4,133},{5,132},{6,135},{7,134},{8... | collective-permute-start | bytes 1572872 | tf_op jit(solution)/shard_map/ppermute | solution.py:325
  29.8 1.3 %collective-permute-start.13 = (f32[2,2,128,256]{3,2,1,0:T(8,128)S(1)}, f32[2,2,128,256]{3,2,1,0:T(8,128)S(1)}, u32[]{:S(2)}, u32[]{:S(2)}) collective-permute-start(f32[2,2,128,256]{3,2,1,0:T(8,128)S(1)} %get-tuple-element.19), channel_id=1, source_target_pairs={{1,130},{2,129},{3,132},{4,131},{5,134},{6,133},{7,136},{8,135},{9... | collective-permute-start | bytes 1572872 | tf_op jit(solution)/shard_map/ppermute | solution.py:325
  31.1 1.3 %collective-permute-start.14 = (f32[2,2,128,256]{3,2,1,0:T(8,128)S(1)}, f32[2,2,128,256]{3,2,1,0:T(8,128)S(1)}, u32[]{:S(2)}, u32[]{:S(2)}) collective-permute-start(f32[2,2,128,256]{3,2,1,0:T(8,128)S(1)} %get-tuple-element.19), channel_id=1, source_target_pairs={{0,129},{1,128},{2,131},{3,130},{4,133},{5,132},{6,135},{7,134},{8... | collective-permute-start | bytes 1572872 | tf_op jit(solution)/shard_map/ppermute | solution.py:325
  32.4 1.3 %collective-permute-start.15 = (f32[2,2,128,256]{3,2,1,0:T(8,128)S(1)}, f32[2,2,128,256]{3,2,1,0:T(8,128)S(1)}, u32[]{:S(2)}, u32[]{:S(2)}) collective-permute-start(f32[2,2,128,256]{3,2,1,0:T(8,128)S(1)} %get-tuple-element.20), channel_id=1, source_target_pairs={{0,128},{1,129},{2,130},{3,131},{4,132},{5,133},{6,134},{7,135},{8... | collective-permute-start | bytes 1572872 | tf_op jit(solution)/shard_map/ppermute | solution.py:325
  33.7 10.6 %collective-permute-done.9 = f32[2,2,128,256]{3,2,1,0:T(8,128)S(1)} collective-permute-done((f32[2,2,128,256]{3,2,1,0:T(8,128)S(1)}, f32[2,2,128,256]{3,2,1,0:T(8,128)S(1)}, u32[]{:S(2)}, u32[]{:S(2)}) %collective-permute-start.9) | collective-permute-done | bytes 524320 | tf_op jit(solution)/shard_map/ppermute | solution.py:325
  44.3 1.3 %collective-permute-start.10 = (f32[2,2,128,256]{3,2,1,0:T(8,128)S(1)}, f32[2,2,128,256]{3,2,1,0:T(8,128)S(1)}, u32[]{:S(2)}, u32[]{:S(2)}) collective-permute-start(f32[2,2,128,256]{3,2,1,0:T(8,128)S(1)} %collective-permute-done.9), channel_id=1, source_target_pairs={{128,0},{129,1},{130,2},{131,3},{132,4},{133,5},{134,6},{135,7},{1... | collective-permute-start | bytes 1572872 | tf_op jit(solution)/shard_map/ppermute | solution.py:325
  45.6 0.6 %collective-permute-done.11 = f32[2,2,128,256]{3,2,1,0:T(8,128)S(1)} collective-permute-done((f32[2,2,128,256]{3,2,1,0:T(8,128)S(1)}, f32[2,2,128,256]{3,2,1,0:T(8,128)S(1)}, u32[]{:S(2)}, u32[]{:S(2)}) %collective-permute-start.11) | collective-permute-done | bytes 524320 | tf_op jit(solution)/shard_map/ppermute | solution.py:325
  46.2 1.3 %collective-permute-start.12 = (f32[2,2,128,256]{3,2,1,0:T(8,128)S(1)}, f32[2,2,128,256]{3,2,1,0:T(8,128)S(1)}, u32[]{:S(2)}, u32[]{:S(2)}) collective-permute-start(f32[2,2,128,256]{3,2,1,0:T(8,128)S(1)} %collective-permute-done.11), channel_id=1, source_target_pairs={{128,0},{129,1},{130,2},{131,3},{132,4},{133,5},{134,6},{135,7},{1... | collective-permute-start | bytes 1572872 | tf_op jit(solution)/shard_map/ppermute | solution.py:325
  47.5 2.4 %collective-permute-done.13.first_one_ref = f32[2,2,128,256]{3,2,1,0:T(8,128)S(1)} collective-permute-done((f32[2,2,128,256]{3,2,1,0:T(8,128)S(1)}, f32[2,2,128,256]{3,2,1,0:T(8,128)S(1)}, u32[]{:S(2)}, u32[]{:S(2)}) %collective-permute-start.13) | collective-permute-done | bytes 524320 | tf_op jit(solution)/shard_map/ppermute | solution.py:325
  49.9 1.9 %collective-permute-done.14.second_one_ref = f32[2,2,128,256]{3,2,1,0:T(8,128)S(1)} collective-permute-done((f32[2,2,128,256]{3,2,1,0:T(8,128)S(1)}, f32[2,2,128,256]{3,2,1,0:T(8,128)S(1)}, u32[]{:S(2)}, u32[]{:S(2)}) %collective-permute-start.14) | collective-permute-done | bytes 524320 | tf_op jit(solution)/shard_map/ppermute | solution.py:325
  51.8 1.7 %collect.1 = f32[1,2,128,2048]{3,2,1,0:T(8,128)} custom-call(s32[2,2]{1,0:T(2,128)S(1)} %copy-done.4, s32[2,2]{1,0:T(2,128)S(1)} %collective-permute-done.first_ref, s32[2,2]{1,0:T(2,128)S(1)} %collective-permute-done.1.second_ref, s32[2,2]{1,0:T(2,128)S(1)} %collective-permute-done.2.first_copy_ref, s32[2,2]{1,0:T(2,128)S(1)} %collective-permute-done.3.second_copy_ref, ...), custom_call_target="tpu_custom_call" | custom-call | bytes 4194304 | tf_op jit(solution)/shard_map/collect/pallas_call | solution.py:387
  (16 shorter events, 0.1 us)
Async XLA Ops:
  0.0 15.5 %copy-start.1 = (f32[1,2,128,2048]{3,2,1,0:T(8,128)S(1)}, f32[1,2,128,2048]{3,2,1,0:T(8,128)}, u32[]{:S(2)}) copy-start(f32[1,2,128,2048]{3,2,1,0:T(8,128)} %strip_ref.1) | copy-start | bytes 6291460
  0.0 12.5 %collective-permute-start.4 = (f32[1,2,128,2048]{3,2,1,0:T(8,128)}, f32[1,2,128,2048]{3,2,1,0:T(8,128)S(1)}, u32[]{:S(2)}, u32[]{:S(2)}) collective-permute-start(f32[1,2,128,2048]{3,2,1,0:T(8,128)} %strip_ref.1), channel_id=1, source_target_pairs={{0,128},{128,0},{1,129},{129,1},{2,130},{130,2},{3,131},{131,3},{4... | collective-permute-start | bytes 6291464 | tf_op jit(solution)/shard_map/ppermute | solution.py:343
  0.7 9.2 %collective-permute-start = (s32[2,2]{1,0:T(2,128)}, s32[2,2]{1,0:T(2,128)S(1)}, u32[]{:S(2)}, u32[]{:S(2)}) collective-permute-start(s32[2,2]{1,0:T(2,128)} %pos_ref.5), channel_id=1, source_target_pairs={{129,130},{130,129},{131,132},{132,131},{133,134},{134,133},{135,1... | collective-permute-start | bytes 56 | tf_op jit(solution)/shard_map/ppermute | solution.py:325
  8.0 4.5 %collective-permute-start.1 = (s32[2,2]{1,0:T(2,128)}, s32[2,2]{1,0:T(2,128)S(1)}, u32[]{:S(2)}, u32[]{:S(2)}) collective-permute-start(s32[2,2]{1,0:T(2,128)} %pos_ref.5), channel_id=1, source_target_pairs={{128,129},{129,128},{130,131},{131,130},{132,133},{133,132},{134,1... | collective-permute-start | bytes 56 | tf_op jit(solution)/shard_map/ppermute | solution.py:325
  12.8 11.9 %collective-permute-start.5 = (f32[2,2,128,256]{3,2,1,0:T(8,128)S(1)}, f32[2,2,128,256]{3,2,1,0:T(8,128)S(1)}, u32[]{:S(2)}, u32[]{:S(2)}) collective-permute-start(f32[2,2,128,256]{3,2,1,0:T(8,128)S(1)} %get-tuple-element.13), channel_id=1, source_target_pairs={{129,2},{130,1},{131,4},{132,3},{133,6},{134,5},{135,8},{136,7},{1... | collective-permute-start | bytes 1572872 | tf_op jit(solution)/shard_map/ppermute | solution.py:325
  14.2 10.6 %collective-permute-start.6 = (f32[2,2,128,256]{3,2,1,0:T(8,128)S(1)}, f32[2,2,128,256]{3,2,1,0:T(8,128)S(1)}, u32[]{:S(2)}, u32[]{:S(2)}) collective-permute-start(f32[2,2,128,256]{3,2,1,0:T(8,128)S(1)} %get-tuple-element.14), channel_id=1, source_target_pairs={{128,1},{129,0},{130,3},{131,2},{132,5},{133,4},{134,7},{135,6},{1... | collective-permute-start | bytes 1572872 | tf_op jit(solution)/shard_map/ppermute | solution.py:325
  15.7 9.1 %copy-start = (bf16[2,6,256,256]{3,2,1,0:T(8,128)(2,1)S(1)}, bf16[2,6,256,256]{3,2,1,0:T(8,128)(2,1)}, u32[]{:S(2)}) copy-start(bf16[2,6,256,256]{3,2,1,0:T(8,128)(2,1)} %constant.2.clone.table_ref) | copy-start | bytes 4718596
  15.7 9.1 %copy-start.2 = (f32[2,256,256]{2,1,0:T(8,128)S(1)}, f32[2,256,256]{2,1,0:T(8,128)}, u32[]{:S(2)}) copy-start(f32[2,256,256]{2,1,0:T(8,128)} %probe_ref.1) | copy-start | bytes 1572868
  15.7 9.1 %copy-start.4 = (s32[2,2]{1,0:T(2,128)S(1)}, s32[2,2]{1,0:T(2,128)}, u32[]{:S(2)}) copy-start(s32[2,2]{1,0:T(2,128)} %pos_ref.5) | copy-start | bytes 52
  16.0 9.8 %collective-permute-start.7 = (f32[2,2,128,256]{3,2,1,0:T(8,128)S(1)}, f32[2,2,128,256]{3,2,1,0:T(8,128)S(1)}, u32[]{:S(2)}, u32[]{:S(2)}) collective-permute-start(f32[2,2,128,256]{3,2,1,0:T(8,128)S(1)} %get-tuple-element.15), channel_id=1, source_target_pairs={{129,2},{130,1},{131,4},{132,3},{133,6},{134,5},{135,8},{136,7},{1... | collective-permute-start | bytes 1572872 | tf_op jit(solution)/shard_map/ppermute | solution.py:325
  17.5 9.7 %collective-permute-start.8 = (f32[2,2,128,256]{3,2,1,0:T(8,128)S(1)}, f32[2,2,128,256]{3,2,1,0:T(8,128)S(1)}, u32[]{:S(2)}, u32[]{:S(2)}) collective-permute-start(f32[2,2,128,256]{3,2,1,0:T(8,128)S(1)} %get-tuple-element.16), channel_id=1, source_target_pairs={{128,1},{129,0},{130,3},{131,2},{132,5},{133,4},{134,7},{135,6},{1... | collective-permute-start | bytes 1572872 | tf_op jit(solution)/shard_map/ppermute | solution.py:325
  19.5 7.7 %copy-start.3 = (f32[2,256,256]{2,1,0:T(8,128)S(1)}, f32[2,256,256]{2,1,0:T(8,128)}, u32[]{:S(2)}) copy-start(f32[2,256,256]{2,1,0:T(8,128)} %intensity_ref.1) | copy-start | bytes 1572868
  19.5 2.2 %collective-permute-start.2 = (s32[2,2]{1,0:T(2,128)S(1)}, s32[2,2]{1,0:T(2,128)S(1)}, u32[]{:S(2)}, u32[]{:S(2)}) collective-permute-start(s32[2,2]{1,0:T(2,128)S(1)} %collective-permute-done.first_ref), channel_id=1, source_target_pairs={{128,0},{129,1},{130,2},{131,3},{132,4},{133,5},{134,6},{135,7},{1... | collective-permute-start | bytes 56 | tf_op jit(solution)/shard_map/ppermute | solution.py:325
  21.7 3.0 %collective-permute-start.3 = (s32[2,2]{1,0:T(2,128)S(1)}, s32[2,2]{1,0:T(2,128)S(1)}, u32[]{:S(2)}, u32[]{:S(2)}) collective-permute-start(s32[2,2]{1,0:T(2,128)S(1)} %collective-permute-done.1.second_ref), channel_id=1, source_target_pairs={{128,0},{129,1},{130,2},{131,3},{132,4},{133,5},{134,6},{135,7},{1... | collective-permute-start | bytes 56 | tf_op jit(solution)/shard_map/ppermute | solution.py:325
  27.2 17.1 %collective-permute-start.9 = (f32[2,2,128,256]{3,2,1,0:T(8,128)S(1)}, f32[2,2,128,256]{3,2,1,0:T(8,128)S(1)}, u32[]{:S(2)}, u32[]{:S(2)}) collective-permute-start(f32[2,2,128,256]{3,2,1,0:T(8,128)S(1)} %get-tuple-element.18), channel_id=1, source_target_pairs={{1,130},{2,129},{3,132},{4,131},{5,134},{6,133},{7,136},{8,135},{9... | collective-permute-start | bytes 1572872 | tf_op jit(solution)/shard_map/ppermute | solution.py:325
  28.5 17.7 %collective-permute-start.11 = (f32[2,2,128,256]{3,2,1,0:T(8,128)S(1)}, f32[2,2,128,256]{3,2,1,0:T(8,128)S(1)}, u32[]{:S(2)}, u32[]{:S(2)}) collective-permute-start(f32[2,2,128,256]{3,2,1,0:T(8,128)S(1)} %get-tuple-element.18), channel_id=1, source_target_pairs={{0,129},{1,128},{2,131},{3,130},{4,133},{5,132},{6,135},{7,134},{8... | collective-permute-start | bytes 1572872 | tf_op jit(solution)/shard_map/ppermute | solution.py:325
  29.8 20.1 %collective-permute-start.13 = (f32[2,2,128,256]{3,2,1,0:T(8,128)S(1)}, f32[2,2,128,256]{3,2,1,0:T(8,128)S(1)}, u32[]{:S(2)}, u32[]{:S(2)}) collective-permute-start(f32[2,2,128,256]{3,2,1,0:T(8,128)S(1)} %get-tuple-element.19), channel_id=1, source_target_pairs={{1,130},{2,129},{3,132},{4,131},{5,134},{6,133},{7,136},{8,135},{9... | collective-permute-start | bytes 1572872 | tf_op jit(solution)/shard_map/ppermute | solution.py:325
  31.1 20.7 %collective-permute-start.14 = (f32[2,2,128,256]{3,2,1,0:T(8,128)S(1)}, f32[2,2,128,256]{3,2,1,0:T(8,128)S(1)}, u32[]{:S(2)}, u32[]{:S(2)}) collective-permute-start(f32[2,2,128,256]{3,2,1,0:T(8,128)S(1)} %get-tuple-element.19), channel_id=1, source_target_pairs={{0,129},{1,128},{2,131},{3,130},{4,133},{5,132},{6,135},{7,134},{8... | collective-permute-start | bytes 1572872 | tf_op jit(solution)/shard_map/ppermute | solution.py:325
  32.4 19.4 %collective-permute-start.15 = (f32[2,2,128,256]{3,2,1,0:T(8,128)S(1)}, f32[2,2,128,256]{3,2,1,0:T(8,128)S(1)}, u32[]{:S(2)}, u32[]{:S(2)}) collective-permute-start(f32[2,2,128,256]{3,2,1,0:T(8,128)S(1)} %get-tuple-element.20), channel_id=1, source_target_pairs={{0,128},{1,129},{2,130},{3,131},{4,132},{5,133},{6,134},{7,135},{8... | collective-permute-start | bytes 1572872 | tf_op jit(solution)/shard_map/ppermute | solution.py:325
  44.3 7.5 %collective-permute-start.10 = (f32[2,2,128,256]{3,2,1,0:T(8,128)S(1)}, f32[2,2,128,256]{3,2,1,0:T(8,128)S(1)}, u32[]{:S(2)}, u32[]{:S(2)}) collective-permute-start(f32[2,2,128,256]{3,2,1,0:T(8,128)S(1)} %collective-permute-done.9), channel_id=1, source_target_pairs={{128,0},{129,1},{130,2},{131,3},{132,4},{133,5},{134,6},{135,7},{1... | collective-permute-start | bytes 1572872 | tf_op jit(solution)/shard_map/ppermute | solution.py:325
  46.2 5.6 %collective-permute-start.12 = (f32[2,2,128,256]{3,2,1,0:T(8,128)S(1)}, f32[2,2,128,256]{3,2,1,0:T(8,128)S(1)}, u32[]{:S(2)}, u32[]{:S(2)}) collective-permute-start(f32[2,2,128,256]{3,2,1,0:T(8,128)S(1)} %collective-permute-done.11), channel_id=1, source_target_pairs={{128,0},{129,1},{130,2},{131,3},{132,4},{133,5},{134,6},{135,7},{1... | collective-permute-start | bytes 1572872 | tf_op jit(solution)/shard_map/ppermute | solution.py:325

commit v11 on v10

--- a/solution.py
+++ b/solution.py
@@ -10,7 +10,7 @@
 
 WIN = 256
 HALF = 128
-CHUNK = 32
+CHUNK = 128
 
 
 def split_tables(real_part, imag_part):

time: 53.1 us -> 52.4 us (0.987)
  the two profiles are of different devices: /device:TPU:193 before, /device:TPU:129 now
where the time goes in v11:
time: 52.4 us; the launch traced here: 52 us
  starting transfers between devices  27.1 us (52%)
  waiting for transfers between devices  21.4 us (41%)
  Pallas kernels  2.58 us (5%)
  between operations  0.89 us (2%)
    ppermute x15, starting transfers between devices, send(): return lax.ppermute(value, ('cuts', 'tile'), pairs)  26.4 us
    ppermute x15, waiting for transfers between devices, send(): return lax.ppermute(value, ('cuts', 'tile'), pairs)  21.4 us
    pallas_call x1, Pallas kernels, local(): kernel(collect_kernel, 'collect', strip, [VMEM] * 11, 0, 4 << 20, (pltpu....  1.74 us
  transfers between devices with their start and end apart: 16, of which 8 were waited for; matrix products, arithmetic and copies ran while one was open for 0% of the time, Pallas kernels for 1%

profile of v11, /device:TPU:129, one launch (start us, length us, event | category | flops | bytes accessed | tf_op | source)
XLA Modules:
  0.0 52.0 jit_solution(5495690093906489682)
XLA Ops:
  0.0 0.7 %collective-permute-start.4 = (f32[1,2,128,2048]{3,2,1,0:T(8,128)}, f32[1,2,128,2048]{3,2,1,0:T(8,128)S(1)}, u32[]{:S(2)}, u32[]{:S(2)}) collective-permute-start(f32[1,2,128,2048]{3,2,1,0:T(8,128)} %strip_ref.1), channel_id=1, source_target_pairs={{0,128},{128,0},{1,129},{129,1},{2,130},{130,2},{3,131},{131,3},{4... | collective-permute-start | bytes 6291464 | tf_op jit(solution)/shard_map/ppermute | solution.py:343
  0.7 6.4 %collective-permute-start = (s32[2,2]{1,0:T(2,128)}, s32[2,2]{1,0:T(2,128)S(1)}, u32[]{:S(2)}, u32[]{:S(2)}) collective-permute-start(s32[2,2]{1,0:T(2,128)} %pos_ref.5), channel_id=1, source_target_pairs={{129,130},{130,129},{131,132},{132,131},{133,134},{134,133},{135,1... | collective-permute-start | bytes 56 | tf_op jit(solution)/shard_map/ppermute | solution.py:325
  7.1 1.9 %collective-permute-start.1 = (s32[2,2]{1,0:T(2,128)}, s32[2,2]{1,0:T(2,128)S(1)}, u32[]{:S(2)}, u32[]{:S(2)}) collective-permute-start(s32[2,2]{1,0:T(2,128)} %pos_ref.5), channel_id=1, source_target_pairs={{128,129},{129,128},{130,131},{131,130},{132,133},{133,132},{134,1... | collective-permute-start | bytes 56 | tf_op jit(solution)/shard_map/ppermute | solution.py:325
  9.0 1.6 %collective-permute-done.first_ref = s32[2,2]{1,0:T(2,128)S(1)} collective-permute-done((s32[2,2]{1,0:T(2,128)}, s32[2,2]{1,0:T(2,128)S(1)}, u32[]{:S(2)}, u32[]{:S(2)}) %collective-permute-start) | collective-permute-done | bytes 48 | tf_op jit(solution)/shard_map/ppermute | solution.py:325
  10.6 1.0 %collective-permute-done.1.second_ref = s32[2,2]{1,0:T(2,128)S(1)} collective-permute-done((s32[2,2]{1,0:T(2,128)}, s32[2,2]{1,0:T(2,128)S(1)}, u32[]{:S(2)}, u32[]{:S(2)}) %collective-permute-start.1) | collective-permute-done | bytes 48 | tf_op jit(solution)/shard_map/ppermute | solution.py:325
  11.6 0.3 cut_zero.1
  11.9 1.3 %collective-permute-start.5 = (f32[2,2,128,256]{3,2,1,0:T(8,128)S(1)}, f32[2,2,128,256]{3,2,1,0:T(8,128)S(1)}, u32[]{:S(2)}, u32[]{:S(2)}) collective-permute-start(f32[2,2,128,256]{3,2,1,0:T(8,128)S(1)} %get-tuple-element.13), channel_id=1, source_target_pairs={{129,2},{130,1},{131,4},{132,3},{133,6},{134,5},{135,8},{136,7},{1... | collective-permute-start | bytes 1572872 | tf_op jit(solution)/shard_map/ppermute | solution.py:325
  13.3 1.3 %collective-permute-start.6 = (f32[2,2,128,256]{3,2,1,0:T(8,128)S(1)}, f32[2,2,128,256]{3,2,1,0:T(8,128)S(1)}, u32[]{:S(2)}, u32[]{:S(2)}) collective-permute-start(f32[2,2,128,256]{3,2,1,0:T(8,128)S(1)} %get-tuple-element.14), channel_id=1, source_target_pairs={{128,1},{129,0},{130,3},{131,2},{132,5},{133,4},{134,7},{135,6},{1... | collective-permute-start | bytes 1572872 | tf_op jit(solution)/shard_map/ppermute | solution.py:325
  14.6 0.2 stage.1.own_ref.strip_ref
  14.8 0.0 copy-start
  14.8 0.0 copy-start.2
  14.8 0.0 copy-start.4
  14.8 0.3 cut_one.1
  15.1 1.5 %collective-permute-start.7 = (f32[2,2,128,256]{3,2,1,0:T(8,128)S(1)}, f32[2,2,128,256]{3,2,1,0:T(8,128)S(1)}, u32[]{:S(2)}, u32[]{:S(2)}) collective-permute-start(f32[2,2,128,256]{3,2,1,0:T(8,128)S(1)} %get-tuple-element.15), channel_id=1, source_target_pairs={{129,2},{130,1},{131,4},{132,3},{133,6},{134,5},{135,8},{136,7},{1... | collective-permute-start | bytes 1572872 | tf_op jit(solution)/shard_map/ppermute | solution.py:325
  16.6 1.3 %collective-permute-start.8 = (f32[2,2,128,256]{3,2,1,0:T(8,128)S(1)}, f32[2,2,128,256]{3,2,1,0:T(8,128)S(1)}, u32[]{:S(2)}, u32[]{:S(2)}) collective-permute-start(f32[2,2,128,256]{3,2,1,0:T(8,128)S(1)} %get-tuple-element.16), channel_id=1, source_target_pairs={{128,1},{129,0},{130,3},{131,2},{132,5},{133,4},{134,7},{135,6},{1... | collective-permute-start | bytes 1572872 | tf_op jit(solution)/shard_map/ppermute | solution.py:325
  18.6 0.0 copy-start.3
  18.6 1.4 %collective-permute-start.2 = (s32[2,2]{1,0:T(2,128)S(1)}, s32[2,2]{1,0:T(2,128)S(1)}, u32[]{:S(2)}, u32[]{:S(2)}) collective-permute-start(s32[2,2]{1,0:T(2,128)S(1)} %collective-permute-done.first_ref), channel_id=1, source_target_pairs={{128,0},{129,1},{130,2},{131,3},{132,4},{133,5},{134,6},{135,7},{1... | collective-permute-start | bytes 56 | tf_op jit(solution)/shard_map/ppermute | solution.py:325
  20.0 0.8 %collective-permute-done.2.first_copy_ref = s32[2,2]{1,0:T(2,128)S(1)} collective-permute-done((s32[2,2]{1,0:T(2,128)S(1)}, s32[2,2]{1,0:T(2,128)S(1)}, u32[]{:S(2)}, u32[]{:S(2)}) %collective-permute-start.2) | collective-permute-done | bytes 48 | tf_op jit(solution)/shard_map/ppermute | solution.py:325
  20.8 2.2 %collective-permute-start.3 = (s32[2,2]{1,0:T(2,128)S(1)}, s32[2,2]{1,0:T(2,128)S(1)}, u32[]{:S(2)}, u32[]{:S(2)}) collective-permute-start(s32[2,2]{1,0:T(2,128)S(1)} %collective-permute-done.1.second_ref), channel_id=1, source_target_pairs={{128,0},{129,1},{130,2},{131,3},{132,4},{133,5},{134,6},{135,7},{1... | collective-permute-start | bytes 56 | tf_op jit(solution)/shard_map/ppermute | solution.py:325
  23.0 0.8 %collective-permute-done.3.second_copy_ref = s32[2,2]{1,0:T(2,128)S(1)} collective-permute-done((s32[2,2]{1,0:T(2,128)S(1)}, s32[2,2]{1,0:T(2,128)S(1)}, u32[]{:S(2)}, u32[]{:S(2)}) %collective-permute-start.3) | collective-permute-done | bytes 48 | tf_op jit(solution)/shard_map/ppermute | solution.py:325
  23.9 1.0 %collective-permute-done.7.first_ref = f32[2,2,128,256]{3,2,1,0:T(8,128)S(1)} collective-permute-done((f32[2,2,128,256]{3,2,1,0:T(8,128)S(1)}, f32[2,2,128,256]{3,2,1,0:T(8,128)S(1)}, u32[]{:S(2)}, u32[]{:S(2)}) %collective-permute-start.7) | collective-permute-done | bytes 524320 | tf_op jit(solution)/shard_map/ppermute | solution.py:325
  24.9 1.3 %collective-permute-done.8.second_ref = f32[2,2,128,256]{3,2,1,0:T(8,128)S(1)} collective-permute-done((f32[2,2,128,256]{3,2,1,0:T(8,128)S(1)}, f32[2,2,128,256]{3,2,1,0:T(8,128)S(1)}, u32[]{:S(2)}, u32[]{:S(2)}) %collective-permute-start.8) | collective-permute-done | bytes 524320 | tf_op jit(solution)/shard_map/ppermute | solution.py:325
  26.3 1.3 %collective-permute-start.9 = (f32[2,2,128,256]{3,2,1,0:T(8,128)S(1)}, f32[2,2,128,256]{3,2,1,0:T(8,128)S(1)}, u32[]{:S(2)}, u32[]{:S(2)}) collective-permute-start(f32[2,2,128,256]{3,2,1,0:T(8,128)S(1)} %get-tuple-element.18), channel_id=1, source_target_pairs={{1,130},{2,129},{3,132},{4,131},{5,134},{6,133},{7,136},{8,135},{9... | collective-permute-start | bytes 1572872 | tf_op jit(solution)/shard_map/ppermute | solution.py:325
  27.6 1.3 %collective-permute-start.11 = (f32[2,2,128,256]{3,2,1,0:T(8,128)S(1)}, f32[2,2,128,256]{3,2,1,0:T(8,128)S(1)}, u32[]{:S(2)}, u32[]{:S(2)}) collective-permute-start(f32[2,2,128,256]{3,2,1,0:T(8,128)S(1)} %get-tuple-element.18), channel_id=1, source_target_pairs={{0,129},{1,128},{2,131},{3,130},{4,133},{5,132},{6,135},{7,134},{8... | collective-permute-start | bytes 1572872 | tf_op jit(solution)/shard_map/ppermute | solution.py:325
  28.9 1.3 %collective-permute-start.13 = (f32[2,2,128,256]{3,2,1,0:T(8,128)S(1)}, f32[2,2,128,256]{3,2,1,0:T(8,128)S(1)}, u32[]{:S(2)}, u32[]{:S(2)}) collective-permute-start(f32[2,2,128,256]{3,2,1,0:T(8,128)S(1)} %get-tuple-element.19), channel_id=1, source_target_pairs={{1,130},{2,129},{3,132},{4,131},{5,134},{6,133},{7,136},{8,135},{9... | collective-permute-start | bytes 1572872 | tf_op jit(solution)/shard_map/ppermute | solution.py:325
  30.2 1.3 %collective-permute-start.14 = (f32[2,2,128,256]{3,2,1,0:T(8,128)S(1)}, f32[2,2,128,256]{3,2,1,0:T(8,128)S(1)}, u32[]{:S(2)}, u32[]{:S(2)}) collective-permute-start(f32[2,2,128,256]{3,2,1,0:T(8,128)S(1)} %get-tuple-element.19), channel_id=1, source_target_pairs={{0,129},{1,128},{2,131},{3,130},{4,133},{5,132},{6,135},{7,134},{8... | collective-permute-start | bytes 1572872 | tf_op jit(solution)/shard_map/ppermute | solution.py:325
  31.5 1.3 %collective-permute-start.15 = (f32[2,2,128,256]{3,2,1,0:T(8,128)S(1)}, f32[2,2,128,256]{3,2,1,0:T(8,128)S(1)}, u32[]{:S(2)}, u32[]{:S(2)}) collective-permute-start(f32[2,2,128,256]{3,2,1,0:T(8,128)S(1)} %get-tuple-element.20), channel_id=1, source_target_pairs={{0,128},{1,129},{2,130},{3,131},{4,132},{5,133},{6,134},{7,135},{8... | collective-permute-start | bytes 1572872 | tf_op jit(solution)/shard_map/ppermute | solution.py:325
  32.8 11.8 %collective-permute-done.9 = f32[2,2,128,256]{3,2,1,0:T(8,128)S(1)} collective-permute-done((f32[2,2,128,256]{3,2,1,0:T(8,128)S(1)}, f32[2,2,128,256]{3,2,1,0:T(8,128)S(1)}, u32[]{:S(2)}, u32[]{:S(2)}) %collective-permute-start.9) | collective-permute-done | bytes 524320 | tf_op jit(solution)/shard_map/ppermute | solution.py:325
  44.6 1.3 %collective-permute-start.10 = (f32[2,2,128,256]{3,2,1,0:T(8,128)S(1)}, f32[2,2,128,256]{3,2,1,0:T(8,128)S(1)}, u32[]{:S(2)}, u32[]{:S(2)}) collective-permute-start(f32[2,2,128,256]{3,2,1,0:T(8,128)S(1)} %collective-permute-done.9), channel_id=1, source_target_pairs={{128,0},{129,1},{130,2},{131,3},{132,4},{133,5},{134,6},{135,7},{1... | collective-permute-start | bytes 1572872 | tf_op jit(solution)/shard_map/ppermute | solution.py:325
  45.9 1.3 %collective-permute-start.12 = (f32[2,2,128,256]{3,2,1,0:T(8,128)S(1)}, f32[2,2,128,256]{3,2,1,0:T(8,128)S(1)}, u32[]{:S(2)}, u32[]{:S(2)}) collective-permute-start(f32[2,2,128,256]{3,2,1,0:T(8,128)S(1)} %collective-permute-done.11), channel_id=1, source_target_pairs={{128,0},{129,1},{130,2},{131,3},{132,4},{133,5},{134,6},{135,7},{1... | collective-permute-start | bytes 1572872 | tf_op jit(solution)/shard_map/ppermute | solution.py:325
  47.3 3.0 %collective-permute-done.13.first_one_ref = f32[2,2,128,256]{3,2,1,0:T(8,128)S(1)} collective-permute-done((f32[2,2,128,256]{3,2,1,0:T(8,128)S(1)}, f32[2,2,128,256]{3,2,1,0:T(8,128)S(1)}, u32[]{:S(2)}, u32[]{:S(2)}) %collective-permute-start.13) | collective-permute-done | bytes 524320 | tf_op jit(solution)/shard_map/ppermute | solution.py:325
  50.2 1.7 %collect.1 = f32[1,2,128,2048]{3,2,1,0:T(8,128)} custom-call(s32[2,2]{1,0:T(2,128)S(1)} %copy-done.4, s32[2,2]{1,0:T(2,128)S(1)} %collective-permute-done.first_ref, s32[2,2]{1,0:T(2,128)S(1)} %collective-permute-done.1.second_ref, s32[2,2]{1,0:T(2,128)S(1)} %collective-permute-done.2.first_copy_ref, s32[2,2]{1,0:T(2,128)S(1)} %collective-permute-done.3.second_copy_ref, ...), custom_call_target="tpu_custom_call" | custom-call | bytes 4194304 | tf_op jit(solution)/shard_map/collect/pallas_call | solution.py:387
  (16 shorter events, 0.1 us)
Async XLA Ops:
  0.0 14.6 %copy-start.1 = (f32[1,2,128,2048]{3,2,1,0:T(8,128)S(1)}, f32[1,2,128,2048]{3,2,1,0:T(8,128)}, u32[]{:S(2)}) copy-start(f32[1,2,128,2048]{3,2,1,0:T(8,128)} %strip_ref.1) | copy-start | bytes 6291460
  0.0 11.6 %collective-permute-start.4 = (f32[1,2,128,2048]{3,2,1,0:T(8,128)}, f32[1,2,128,2048]{3,2,1,0:T(8,128)S(1)}, u32[]{:S(2)}, u32[]{:S(2)}) collective-permute-start(f32[1,2,128,2048]{3,2,1,0:T(8,128)} %strip_ref.1), channel_id=1, source_target_pairs={{0,128},{128,0},{1,129},{129,1},{2,130},{130,2},{3,131},{131,3},{4... | collective-permute-start | bytes 6291464 | tf_op jit(solution)/shard_map/ppermute | solution.py:343
  0.7 9.9 %collective-permute-start = (s32[2,2]{1,0:T(2,128)}, s32[2,2]{1,0:T(2,128)S(1)}, u32[]{:S(2)}, u32[]{:S(2)}) collective-permute-start(s32[2,2]{1,0:T(2,128)} %pos_ref.5), channel_id=1, source_target_pairs={{129,130},{130,129},{131,132},{132,131},{133,134},{134,133},{135,1... | collective-permute-start | bytes 56 | tf_op jit(solution)/shard_map/ppermute | solution.py:325
  7.1 4.5 %collective-permute-start.1 = (s32[2,2]{1,0:T(2,128)}, s32[2,2]{1,0:T(2,128)S(1)}, u32[]{:S(2)}, u32[]{:S(2)}) collective-permute-start(s32[2,2]{1,0:T(2,128)} %pos_ref.5), channel_id=1, source_target_pairs={{128,129},{129,128},{130,131},{131,130},{132,133},{133,132},{134,1... | collective-permute-start | bytes 56 | tf_op jit(solution)/shard_map/ppermute | solution.py:325
  11.9 11.9 %collective-permute-start.5 = (f32[2,2,128,256]{3,2,1,0:T(8,128)S(1)}, f32[2,2,128,256]{3,2,1,0:T(8,128)S(1)}, u32[]{:S(2)}, u32[]{:S(2)}) collective-permute-start(f32[2,2,128,256]{3,2,1,0:T(8,128)S(1)} %get-tuple-element.13), channel_id=1, source_target_pairs={{129,2},{130,1},{131,4},{132,3},{133,6},{134,5},{135,8},{136,7},{1... | collective-permute-start | bytes 1572872 | tf_op jit(solution)/shard_map/ppermute | solution.py:325
  13.3 10.6 %collective-permute-start.6 = (f32[2,2,128,256]{3,2,1,0:T(8,128)S(1)}, f32[2,2,128,256]{3,2,1,0:T(8,128)S(1)}, u32[]{:S(2)}, u32[]{:S(2)}) collective-permute-start(f32[2,2,128,256]{3,2,1,0:T(8,128)S(1)} %get-tuple-element.14), channel_id=1, source_target_pairs={{128,1},{129,0},{130,3},{131,2},{132,5},{133,4},{134,7},{135,6},{1... | collective-permute-start | bytes 1572872 | tf_op jit(solution)/shard_map/ppermute | solution.py:325
  14.8 9.1 %copy-start = (bf16[2,6,256,256]{3,2,1,0:T(8,128)(2,1)S(1)}, bf16[2,6,256,256]{3,2,1,0:T(8,128)(2,1)}, u32[]{:S(2)}) copy-start(bf16[2,6,256,256]{3,2,1,0:T(8,128)(2,1)} %constant.2.clone.table_ref) | copy-start | bytes 4718596
  14.8 9.1 %copy-start.2 = (f32[2,256,256]{2,1,0:T(8,128)S(1)}, f32[2,256,256]{2,1,0:T(8,128)}, u32[]{:S(2)}) copy-start(f32[2,256,256]{2,1,0:T(8,128)} %probe_ref.1) | copy-start | bytes 1572868
  14.8 9.1 %copy-start.4 = (s32[2,2]{1,0:T(2,128)S(1)}, s32[2,2]{1,0:T(2,128)}, u32[]{:S(2)}) copy-start(s32[2,2]{1,0:T(2,128)} %pos_ref.5) | copy-start | bytes 52
  15.1 9.8 %collective-permute-start.7 = (f32[2,2,128,256]{3,2,1,0:T(8,128)S(1)}, f32[2,2,128,256]{3,2,1,0:T(8,128)S(1)}, u32[]{:S(2)}, u32[]{:S(2)}) collective-permute-start(f32[2,2,128,256]{3,2,1,0:T(8,128)S(1)} %get-tuple-element.15), channel_id=1, source_target_pairs={{129,2},{130,1},{131,4},{132,3},{133,6},{134,5},{135,8},{136,7},{1... | collective-permute-start | bytes 1572872 | tf_op jit(solution)/shard_map/ppermute | solution.py:325
  16.6 9.7 %collective-permute-start.8 = (f32[2,2,128,256]{3,2,1,0:T(8,128)S(1)}, f32[2,2,128,256]{3,2,1,0:T(8,128)S(1)}, u32[]{:S(2)}, u32[]{:S(2)}) collective-permute-start(f32[2,2,128,256]{3,2,1,0:T(8,128)S(1)} %get-tuple-element.16), channel_id=1, source_target_pairs={{128,1},{129,0},{130,3},{131,2},{132,5},{133,4},{134,7},{135,6},{1... | collective-permute-start | bytes 1572872 | tf_op jit(solution)/shard_map/ppermute | solution.py:325
  18.6 7.7 %copy-start.3 = (f32[2,256,256]{2,1,0:T(8,128)S(1)}, f32[2,256,256]{2,1,0:T(8,128)}, u32[]{:S(2)}) copy-start(f32[2,256,256]{2,1,0:T(8,128)} %intensity_ref.1) | copy-start | bytes 1572868
  18.6 2.2 %collective-permute-start.2 = (s32[2,2]{1,0:T(2,128)S(1)}, s32[2,2]{1,0:T(2,128)S(1)}, u32[]{:S(2)}, u32[]{:S(2)}) collective-permute-start(s32[2,2]{1,0:T(2,128)S(1)} %collective-permute-done.first_ref), channel_id=1, source_target_pairs={{128,0},{129,1},{130,2},{131,3},{132,4},{133,5},{134,6},{135,7},{1... | collective-permute-start | bytes 56 | tf_op jit(solution)/shard_map/ppermute | solution.py:325
  20.8 3.0 %collective-permute-start.3 = (s32[2,2]{1,0:T(2,128)S(1)}, s32[2,2]{1,0:T(2,128)S(1)}, u32[]{:S(2)}, u32[]{:S(2)}) collective-permute-start(s32[2,2]{1,0:T(2,128)S(1)} %collective-permute-done.1.second_ref), channel_id=1, source_target_pairs={{128,0},{129,1},{130,2},{131,3},{132,4},{133,5},{134,6},{135,7},{1... | collective-permute-start | bytes 56 | tf_op jit(solution)/shard_map/ppermute | solution.py:325
  26.3 18.3 %collective-permute-start.9 = (f32[2,2,128,256]{3,2,1,0:T(8,128)S(1)}, f32[2,2,128,256]{3,2,1,0:T(8,128)S(1)}, u32[]{:S(2)}, u32[]{:S(2)}) collective-permute-start(f32[2,2,128,256]{3,2,1,0:T(8,128)S(1)} %get-tuple-element.18), channel_id=1, source_target_pairs={{1,130},{2,129},{3,132},{4,131},{5,134},{6,133},{7,136},{8,135},{9... | collective-permute-start | bytes 1572872 | tf_op jit(solution)/shard_map/ppermute | solution.py:325
  27.6 18.4 %collective-permute-start.11 = (f32[2,2,128,256]{3,2,1,0:T(8,128)S(1)}, f32[2,2,128,256]{3,2,1,0:T(8,128)S(1)}, u32[]{:S(2)}, u32[]{:S(2)}) collective-permute-start(f32[2,2,128,256]{3,2,1,0:T(8,128)S(1)} %get-tuple-element.18), channel_id=1, source_target_pairs={{0,129},{1,128},{2,131},{3,130},{4,133},{5,132},{6,135},{7,134},{8... | collective-permute-start | bytes 1572872 | tf_op jit(solution)/shard_map/ppermute | solution.py:325
  28.9 21.3 %collective-permute-start.13 = (f32[2,2,128,256]{3,2,1,0:T(8,128)S(1)}, f32[2,2,128,256]{3,2,1,0:T(8,128)S(1)}, u32[]{:S(2)}, u32[]{:S(2)}) collective-permute-start(f32[2,2,128,256]{3,2,1,0:T(8,128)S(1)} %get-tuple-element.19), channel_id=1, source_target_pairs={{1,130},{2,129},{3,132},{4,131},{5,134},{6,133},{7,136},{8,135},{9... | collective-permute-start | bytes 1572872 | tf_op jit(solution)/shard_map/ppermute | solution.py:325
  30.2 20.0 %collective-permute-start.14 = (f32[2,2,128,256]{3,2,1,0:T(8,128)S(1)}, f32[2,2,128,256]{3,2,1,0:T(8,128)S(1)}, u32[]{:S(2)}, u32[]{:S(2)}) collective-permute-start(f32[2,2,128,256]{3,2,1,0:T(8,128)S(1)} %get-tuple-element.19), channel_id=1, source_target_pairs={{0,129},{1,128},{2,131},{3,130},{4,133},{5,132},{6,135},{7,134},{8... | collective-permute-start | bytes 1572872 | tf_op jit(solution)/shard_map/ppermute | solution.py:325
  31.5 18.8 %collective-permute-start.15 = (f32[2,2,128,256]{3,2,1,0:T(8,128)S(1)}, f32[2,2,128,256]{3,2,1,0:T(8,128)S(1)}, u32[]{:S(2)}, u32[]{:S(2)}) collective-permute-start(f32[2,2,128,256]{3,2,1,0:T(8,128)S(1)} %get-tuple-element.20), channel_id=1, source_target_pairs={{0,128},{1,129},{2,130},{3,131},{4,132},{5,133},{6,134},{7,135},{8... | collective-permute-start | bytes 1572872 | tf_op jit(solution)/shard_map/ppermute | solution.py:325
  44.6 5.6 %collective-permute-start.10 = (f32[2,2,128,256]{3,2,1,0:T(8,128)S(1)}, f32[2,2,128,256]{3,2,1,0:T(8,128)S(1)}, u32[]{:S(2)}, u32[]{:S(2)}) collective-permute-start(f32[2,2,128,256]{3,2,1,0:T(8,128)S(1)} %collective-permute-done.9), channel_id=1, source_target_pairs={{128,0},{129,1},{130,2},{131,3},{132,4},{133,5},{134,6},{135,7},{1... | collective-permute-start | bytes 1572872 | tf_op jit(solution)/shard_map/ppermute | solution.py:325
  45.9 4.3 %collective-permute-start.12 = (f32[2,2,128,256]{3,2,1,0:T(8,128)S(1)}, f32[2,2,128,256]{3,2,1,0:T(8,128)S(1)}, u32[]{:S(2)}, u32[]{:S(2)}) collective-permute-start(f32[2,2,128,256]{3,2,1,0:T(8,128)S(1)} %collective-permute-done.11), channel_id=1, source_target_pairs={{128,0},{129,1},{130,2},{131,3},{132,4},{133,5},{134,6},{135,7},{1... | collective-permute-start | bytes 1572872 | tf_op jit(solution)/shard_map/ppermute | solution.py:325
